TPU v7x, 32 devices: a whole 2x2x4 slice. The times are simulated.
32 devices in a mesh: gx: 4 (over x, core), gy: 8 (over z, y).
Axes of the slice: x: 2, y: 2, z: 4, core: 2. Of those that a mesh axis runs over, the one named last changes fastest.
Arguments:
- displacement: float32 [6, 262144], P(None, ('gx', 'gy')), may hold values from -4 to 4
- velocity: float32 [6, 262144], P(None, ('gx', 'gy')), may hold values from -6 to 6
- ref_pos: float32 [3, 262144], P(None, ('gx', 'gy')), may hold values from -6 to 6
- normals: float32 [3, 262144], P(None, ('gx', 'gy')), may hold values from -4 to 4
- inv_mass: float32 [6, 262144], P(None, ('gx', 'gy')), may hold values from 0.5 to 2
- connectivity: int32 [4, 262144], P(None, ('gx', 'gy')), may hold values from 0 to 8191, as said below
- stiffness: bfloat16 [24, 24, 262144], P(None, None, ('gx', 'gy'))
- yield_force: float32 [262144], P(('gx', 'gy')), may hold values from 2 to 20
- shared_nodes: int32 [4, 4096], P(None, ('gx', 'gy')), may hold values from 0 to 8191, as said below
- block_slot: int32 [2048], P(('gx', 'gy')), may hold values from 0 to 63, as said below
- edge_slots: int32 [256], P(('gx', 'gy')), may hold values from 0 to 63, as said below
- tile_pairs: int32 [2, 4096], P(None, ('gx', 'gy')), may hold values from 0 to 95, as said below
- tile_count: int32 [32], P(('gx', 'gy')), may hold values from 0 to 128, as said below
- win_start: int32 [4096, 128], P(('gx', 'gy')), may hold values from 0 to 127
- win_len: int32 [4096, 128], P(('gx', 'gy')), may hold values from 1 to 128
Outputs:
- displacement_out: float32 [6, 262144], P(None, ('gx', 'gy'))
- velocity_out: float32 [6, 262144], P(None, ('gx', 'gy'))
Inputs may be any that keep to these rules, and one draw needn't show every extreme that they name: `connectivity`: element e of a partition (e counted within the partition) has its corners among the partition's nodes 128 * (e // 128) to 128 * (e // 128) + 127. `shared_nodes`: the four rows of a partition list distinct local nodes, 128 a row, 512 distinct in all. `block_slot`: entries of one partition are distinct; box = entry // 2 is the receiving box. Every partition fills all 2 places of some boxes, and some boxes receive 2 blocks from every partition. `edge_slots`: places of a box's received blocks. `tile_pairs`: row 0 is a received place; row 1 is a received place or 64 + k for entry k of the neighbours' edge blocks. A box uses its first tile_count tiles; some box uses all 128 in every draw.
All inputs are finite; a program needn't handle non-finite values.
Results may differ from a plain program's by a relative error of at most 0.0003.
Values sent between devices are 32-bit elements; how exact they have to be, the bound alone decides.
No kernel may reach another device: no remote copies, remote signals or barrier semaphores. Data moves between devices by JAX's collectives and lax.ppermute only.
A program may use at most 128 MiB of HBM per device.

v0:
```python
import jax
import jax.numpy as jnp
from jax import lax
from jax.sharding import PartitionSpec as P

BLK = 128
SBLK_DEV = 64
CAP = 2
STEPS = 2


TIME_STEP = 0.5
PENALTY = 32.0
THICKNESS = 0.2
EXACT = lax.Precision.HIGHEST


def padded_2(cells, sides, width):
    for axis, dim in sides:
        count = lax.axis_size(axis)
        ends = count - 1
        head = lax.slice_in_dim(cells, 0, width, axis=dim)
        tail = lax.slice_in_dim(cells, cells.shape[dim] - width, cells.shape[dim], axis=dim)
        cells = jnp.concatenate(
            [
                lax.ppermute(tail, axis, [(i, (i + 1) % count) for i in range(ends)]),
                cells,
                lax.ppermute(head, axis, [((i + 1) % count, i) for i in range(ends)]),
            ],
            axis=dim,
        )
    return cells


def element_forces(displacement, connectivity, stiffness, yield_force):
    node_count = displacement.shape[1]
    block_count = node_count // BLK
    local = (connectivity % BLK).reshape(4, block_count, BLK)
    picker = (local[:, :, :, None] == jnp.arange(BLK, dtype=jnp.int32)[None, None, None, :]).astype(
        jnp.float32
    )
    disp_blocks = displacement.reshape(6, block_count, BLK)
    gathered = jnp.einsum("ckn,aken->cake", disp_blocks, picker, precision=EXACT)
    elem_dofs = gathered.reshape(24, -1)
    trial = jnp.sum(stiffness.astype(jnp.float32) * elem_dofs[None, :, :], axis=1)
    squared = jnp.sum(trial * trial, axis=0)
    factor = 1.0 / jnp.sqrt(1.0 + squared / (yield_force * yield_force))
    element_force = (trial * factor[None, :]).reshape(6, 4, block_count, BLK)
    internal = jnp.einsum("cake,aken->ckn", element_force, picker, precision=EXACT)
    return internal.reshape(6, node_count)


def tile_forces(own_blocks, extended, slaves, masters, starts, lengths, active):
    width = own_blocks.shape[2]
    slave_pick = (
        slaves[:, None] == jnp.arange(own_blocks.shape[1], dtype=jnp.int32)[None, :]
    ).astype(jnp.float32)
    master_pick = (
        masters[:, None] == jnp.arange(extended.shape[1], dtype=jnp.int32)[None, :]
    ).astype(jnp.float32)
    slave_pos = jnp.einsum("csb,ts->ctb", own_blocks[0:3], slave_pick, precision=EXACT)
    master_data = jnp.einsum("csb,ts->ctb", extended, master_pick, precision=EXACT)
    master_pos = master_data[0:3]
    master_nrm = master_data[3:6]
    offset = jnp.sum(master_pos * master_nrm, axis=0)
    gap_matrix = (
        jnp.einsum("cti,ctj->tij", slave_pos, master_nrm, precision=EXACT) - offset[:, None, :]
    )
    column = jnp.arange(width, dtype=jnp.int32)
    inside = (column[None, None, :] - starts[:, :, None]) % width < lengths[:, :, None]
    inside = jnp.logical_and(inside, active[:, None, None])
    pressure = jnp.where(inside, jnp.maximum(THICKNESS - gap_matrix, 0.0), 0.0)
    forces = PENALTY / width * jnp.einsum("tij,ctj->cti", pressure, master_nrm, precision=EXACT)
    return jnp.einsum("cti,ts->csi", forces, slave_pick, precision=EXACT)


def body(
    displacement,
    velocity,
    ref_pos,
    normals,
    inv_mass,
    connectivity,
    stiffness,
    yield_force,
    shared_nodes,
    block_slot,
    edge_slots,
    tile_pairs,
    tile_count,
    win_start,
    win_len,
):
    gx_size = lax.axis_size("gx")
    gy_size = lax.axis_size("gy")
    slot_total = gx_size * gy_size * CAP
    node_count = displacement.shape[1]
    edge_count = edge_slots.shape[0]
    tiles_here = tile_pairs.shape[1]
    tile_group = min(32, tiles_here)
    send_pick = (block_slot[None, :] == jnp.arange(slot_total, dtype=jnp.int32)[:, None]).astype(
        jnp.float32
    )
    for time_step in range(STEPS):
        positions = ref_pos + displacement[0:3]
        surface = jnp.concatenate([positions, normals], axis=0).reshape(6, SBLK_DEV, BLK)
        outgoing = jnp.einsum("ckb,sk->csb", surface, send_pick, precision=EXACT)
        received = lax.all_to_all(outgoing, ("gx", "gy"), split_axis=1, concat_axis=1, tiled=True)
        internal = element_forces(displacement, connectivity, stiffness, yield_force)
        edge_rows = received[:, edge_slots].reshape(6, 1, 1, edge_count, BLK)
        padded = padded_2(edge_rows, (("gx", 1), ("gy", 2)), 1)
        neighbours = jnp.concatenate(
            [padded[:, 0, 1], padded[:, 2, 1], padded[:, 1, 0], padded[:, 1, 2]], axis=1
        )
        extended = jnp.concatenate([received, neighbours], axis=1)
        used_tiles = tile_count[0]
        rounds = (used_tiles + tile_group - 1) // tile_group

        def accumulate(group_index, running):
            first_tile = group_index * tile_group
            slaves = lax.dynamic_slice_in_dim(tile_pairs[0], first_tile, tile_group, 0)
            masters = lax.dynamic_slice_in_dim(tile_pairs[1], first_tile, tile_group, 0)
            starts = lax.dynamic_slice_in_dim(win_start, first_tile, tile_group, 0)
            lengths = lax.dynamic_slice_in_dim(win_len, first_tile, tile_group, 0)
            active = first_tile + jnp.arange(tile_group, dtype=jnp.int32) < used_tiles
            return running + tile_forces(
                received, extended, slaves, masters, starts, lengths, active
            )

        contact = lax.fori_loop(0, rounds, accumulate, jnp.zeros((3, slot_total, BLK), jnp.float32))
        returned = lax.all_to_all(contact, ("gx", "gy"), split_axis=1, concat_axis=1, tiled=True)
        contact_nodes = jnp.einsum("csb,sk->ckb", returned, send_pick, precision=EXACT).reshape(
            3, node_count
        )
        nodal_force = (
            jnp.concatenate([contact_nodes, jnp.zeros_like(contact_nodes)], axis=0) - internal
        )
        side_x = nodal_force[:, shared_nodes[0:2]]
        side_y = nodal_force[:, shared_nodes[2:4]]
        near_x = padded_2(side_x, (("gx", 1),), 1)
        near_y = padded_2(side_y, (("gy", 1),), 1)
        assembled = nodal_force.at[:, shared_nodes[0]].add(near_x[:, 0])
        assembled = assembled.at[:, shared_nodes[1]].add(near_x[:, 3])
        assembled = assembled.at[:, shared_nodes[2]].add(near_y[:, 0])
        assembled = assembled.at[:, shared_nodes[3]].add(near_y[:, 3])
        velocity = velocity + TIME_STEP * inv_mass * assembled
        displacement = displacement + TIME_STEP * velocity
    return (displacement, velocity)


def solution(mesh):
    placed = (
        P(None, ("gx", "gy")),
        P(None, ("gx", "gy")),
        P(None, ("gx", "gy")),
        P(None, ("gx", "gy")),
        P(None, ("gx", "gy")),
        P(None, ("gx", "gy")),
        P(None, None, ("gx", "gy")),
        P(("gx", "gy")),
        P(None, ("gx", "gy")),
        P(("gx", "gy")),
        P(("gx", "gy")),
        P(None, ("gx", "gy")),
        P(("gx", "gy")),
        P(("gx", "gy"), None),
        P(("gx", "gy"), None),
    )
    return jax.shard_map(
        body,
        mesh=mesh,
        in_specs=placed,
        out_specs=(P(None, ("gx", "gy")), P(None, ("gx", "gy"))),
        check_vma=False,
    )
```

profile of v0, /device:TPU:0, one launch (start us, length us, event | category | flops | bytes accessed | tf_op | source)
XLA Modules:
  0.0 336.2 jit_solution(14728144858664974877)
XLA Ops:
  4.6 7.3 %all-to-all-start = ((f32[6,64,128]{2,0,1:T(8,128)}), f32[6,64,128]{2,0,1:T(8,128)S(1)}, u32[]{:S(2)}, u32[]{:S(2)}) async-start(f32[6,64,128]{2,0,1:T(8,128)} %copy.111), calls=%async_computation | async-start | bytes 524288 | tf_op jit(solution)/shard_map/all_to_all | solution.py:108
  13.6 12.7 %fusion.112 = f32[6,4,64,128]{3,0,1,2:T(8,128)S(1)} fusion(s32[4,64,128]{2,0,1:T(4,128)S(1)} %fusion.125, f32[6,8192]{1,0:T(8,128)} %param.19), kind=kOutput, calls=%fused_computation.143 | convolution fusion | flops 306184192 | bytes 1114112 | tf_op jit(solution)/shard_map/ckn,aken->cake/dot_general | solution.py:43
  36.8 12.7 %fusion.106 = f32[6,8192]{1,0:T(8,128)S(1)} fusion(s32[4,64,128]{2,0,1:T(4,128)S(1)} %fusion.125, f32[6,4,64,128]{3,2,1,0:T(8,128)S(1)} %broadcast_multiply_fusion.1), kind=kOutput, calls=%fused_computation.135 | convolution fusion | flops 306184192 | bytes 1114112 | tf_op jit(solution)/shard_map/cake,aken->ckn/dot_general | solution.py:49
  65.2 43.3 %while.24 = (s32[]{:T(128)}, f32[3,64,128]{2,1,0:T(8,128)S(1)}, s32[]{:T(128)}, s32[2,128]{1,0:T(2,128)S(1)}, f32[6,96,128]{2,1,0:T(8,128)S(1)}, /*index=5*/s32[...) while((s32[]{:T(128)}, f32[3,64,128]{2,1,0:T(8,128)S(1)}, ...), condition=%wide.region_2.3_spmd, body=%wide.region_0.2_spmd.sunk | while | flops 94436416 | bytes 5459451 | solution.py:130
  69.9 5.8 %fusion.217 = f32[3,32,128]{2,0,1:T(4,128)S(1)} fusion(f32[32,128,128]{2,1,0:T(8,128)S(1)} %fusion.216, f32[32,128]{1,0:T(8,128)S(1)} %get-tuple-element.474, s32[32,128]{1,0:T(8,128)S(1)} %get-tuple-element.475, s32[32,128]{1,0:T(8,128)S(1)} %get-tuple-element.476, pred[32]{0:T(512)(128)(4,1)S(1)} %add_compare_fusion.4, ...), kind=kOutput, calls=%fused_computation.32.clone.1 | convolution fusion | flops 28323840 | bytes 2244640 | tf_op jit(solution)/shard_map/while/body/tij,ctj->cti/dot_general | solution.py:73
  80.8 5.8 %fusion.217 = f32[3,32,128]{2,0,1:T(4,128)S(1)} fusion(f32[32,128,128]{2,1,0:T(8,128)S(1)} %fusion.216, f32[32,128]{1,0:T(8,128)S(1)} %get-tuple-element.474, s32[32,128]{1,0:T(8,128)S(1)} %get-tuple-element.475, s32[32,128]{1,0:T(8,128)S(1)} %get-tuple-element.476, pred[32]{0:T(512)(128)(4,1)S(1)} %add_compare_fusion.4, ...), kind=kOutput, calls=%fused_computation.32.clone.1 | convolution fusion | flops 28323840 | bytes 2244640 | tf_op jit(solution)/shard_map/while/body/tij,ctj->cti/dot_general | solution.py:73
  91.6 5.8 %fusion.217 = f32[3,32,128]{2,0,1:T(4,128)S(1)} fusion(f32[32,128,128]{2,1,0:T(8,128)S(1)} %fusion.216, f32[32,128]{1,0:T(8,128)S(1)} %get-tuple-element.474, s32[32,128]{1,0:T(8,128)S(1)} %get-tuple-element.475, s32[32,128]{1,0:T(8,128)S(1)} %get-tuple-element.476, pred[32]{0:T(512)(128)(4,1)S(1)} %add_compare_fusion.4, ...), kind=kOutput, calls=%fused_computation.32.clone.1 | convolution fusion | flops 28323840 | bytes 2244640 | tf_op jit(solution)/shard_map/while/body/tij,ctj->cti/dot_general | solution.py:73
  102.4 5.8 %fusion.217 = f32[3,32,128]{2,0,1:T(4,128)S(1)} fusion(f32[32,128,128]{2,1,0:T(8,128)S(1)} %fusion.216, f32[32,128]{1,0:T(8,128)S(1)} %get-tuple-element.474, s32[32,128]{1,0:T(8,128)S(1)} %get-tuple-element.475, s32[32,128]{1,0:T(8,128)S(1)} %get-tuple-element.476, pred[32]{0:T(512)(128)(4,1)S(1)} %add_compare_fusion.4, ...), kind=kOutput, calls=%fused_computation.32.clone.1 | convolution fusion | flops 28323840 | bytes 2244640 | tf_op jit(solution)/shard_map/while/body/tij,ctj->cti/dot_general | solution.py:73
  109.3 8.3 %all-to-all-start.1 = ((f32[3,64,128]{2,0,1:T(4,128)}), f32[3,64,128]{2,0,1:T(4,128)S(1)}, u32[]{:S(2)}, u32[]{:S(2)}) async-start(f32[3,64,128]{2,0,1:T(4,128)} %copy.114), calls=%async_computation.1 | async-start | bytes 262144 | tf_op jit(solution)/shard_map/all_to_all | solution.py:131
  128.1 5.9 %pad_subtract_fusion.1 = f32[6,8192]{0,1:T(8,128)} fusion(f32[6,8192]{0,1:T(8,128)} %copy.121, f32[3,8192]{0,1:T(8,128)} %bitcast.268), kind=kLoop, calls=%fused_computation.142 | loop fusion | flops 49152 | bytes 491520 | tf_op jit(solution)/shard_map/sub | solution.py:136
  156.2 5.3 %scatter_custom_fusion.1 = f32[6,8192]{0,1:T(8,128)} fusion(f32[6,8192]{0,1:T(8,128)} %scatter_custom_fusion, s32[128]{0:T(128)S(1)} %get-tuple-element.344, f32[6,1,128]{0,2,1:T(8,128)S(1)} %collective-permute-done.5), kind=kCustom, calls=%fused_computation.194 | custom fusion | flops 768 | bytes 262144 | tf_op jit(solution)/shard_map/scatter-add | solution.py:143
  166.8 5.4 %scatter_custom_fusion.3 = f32[6,8192]{0,1:T(8,128)} fusion(f32[6,8192]{0,1:T(8,128)} %scatter_custom_fusion.2, s32[128]{0:T(128)S(1)} %get-tuple-element.342, f32[6,1,128]{0,2,1:T(8,128)S(1)} %collective-permute-done.7), kind=kCustom, calls=%fused_computation.190 | custom fusion | flops 768 | bytes 262144 | tf_op jit(solution)/shard_map/scatter-add | solution.py:145
  175.2 14.8 %fusion.113 = f32[6,4,64,128]{3,0,1,2:T(8,128)S(1)} fusion(s32[4,64,128]{2,0,1:T(4,128)S(1)} %fusion.125, f32[6,8192]{1,0:T(8,128)S(1)} %multiply_add_fusion.2), kind=kOutput, calls=%fused_computation.144 | convolution fusion | flops 306184192 | bytes 1114112 | tf_op jit(solution)/shard_map/ckn,aken->cake/dot_general | solution.py:43
  191.3 5.4 %all-to-all-start.2 = ((f32[6,64,128]{2,0,1:T(8,128)}), f32[6,64,128]{2,0,1:T(8,128)S(1)}, u32[]{:S(2)}, u32[]{:S(2)}) async-start(f32[6,64,128]{2,0,1:T(8,128)} %copy.124), calls=%async_computation.2 | async-start | bytes 524288 | tf_op jit(solution)/shard_map/all_to_all | solution.py:108
  197.6 6.9 %fusion.101 = f32[24,8192]{1,0:T(8,128)S(1)} fusion(bf16[24,24,8192]{2,1,0:T(8,128)(2,1)} %param.25, f32[24,8192]{1,0:T(8,128)S(1)} %bitcast.277), kind=kLoop, calls=%fused_computation.129 | loop fusion | flops 13959168 | bytes 11010048 | tf_op jit(solution)/shard_map/reduce_sum | solution.py:45
  222.3 43.6 %while.25 = (s32[]{:T(128)}, f32[3,64,128]{2,1,0:T(8,128)S(1)}, s32[]{:T(128)}, s32[2,128]{1,0:T(2,128)S(1)}, f32[6,96,128]{2,1,0:T(8,128)S(1)}, /*index=5*/s32[...) while((s32[]{:T(128)}, f32[3,64,128]{2,1,0:T(8,128)S(1)}, ...), condition=%wide.region_11.12_spmd, body=%wide.region_9.11_spmd.sunk | while | flops 94436416 | bytes 5459451 | solution.py:130
  227.2 5.8 %fusion.233 = f32[3,32,128]{2,0,1:T(4,128)S(1)} fusion(f32[32,128,128]{2,1,0:T(8,128)S(1)} %fusion.232, f32[32,128]{1,0:T(8,128)S(1)} %get-tuple-element.491, s32[32,128]{1,0:T(8,128)S(1)} %get-tuple-element.492, s32[32,128]{1,0:T(8,128)S(1)} %get-tuple-element.493, pred[32]{0:T(512)(128)(4,1)S(1)} %add_compare_fusion.5, ...), kind=kOutput, calls=%fused_computation.88.clone.1 | convolution fusion | flops 28323840 | bytes 2244640 | tf_op jit(solution)/shard_map/while/body/tij,ctj->cti/dot_general | solution.py:73
  238.0 5.8 %fusion.233 = f32[3,32,128]{2,0,1:T(4,128)S(1)} fusion(f32[32,128,128]{2,1,0:T(8,128)S(1)} %fusion.232, f32[32,128]{1,0:T(8,128)S(1)} %get-tuple-element.491, s32[32,128]{1,0:T(8,128)S(1)} %get-tuple-element.492, s32[32,128]{1,0:T(8,128)S(1)} %get-tuple-element.493, pred[32]{0:T(512)(128)(4,1)S(1)} %add_compare_fusion.5, ...), kind=kOutput, calls=%fused_computation.88.clone.1 | convolution fusion | flops 28323840 | bytes 2244640 | tf_op jit(solution)/shard_map/while/body/tij,ctj->cti/dot_general | solution.py:73
  248.9 5.8 %fusion.233 = f32[3,32,128]{2,0,1:T(4,128)S(1)} fusion(f32[32,128,128]{2,1,0:T(8,128)S(1)} %fusion.232, f32[32,128]{1,0:T(8,128)S(1)} %get-tuple-element.491, s32[32,128]{1,0:T(8,128)S(1)} %get-tuple-element.492, s32[32,128]{1,0:T(8,128)S(1)} %get-tuple-element.493, pred[32]{0:T(512)(128)(4,1)S(1)} %add_compare_fusion.5, ...), kind=kOutput, calls=%fused_computation.88.clone.1 | convolution fusion | flops 28323840 | bytes 2244640 | tf_op jit(solution)/shard_map/while/body/tij,ctj->cti/dot_general | solution.py:73
  259.7 5.8 %fusion.233 = f32[3,32,128]{2,0,1:T(4,128)S(1)} fusion(f32[32,128,128]{2,1,0:T(8,128)S(1)} %fusion.232, f32[32,128]{1,0:T(8,128)S(1)} %get-tuple-element.491, s32[32,128]{1,0:T(8,128)S(1)} %get-tuple-element.492, s32[32,128]{1,0:T(8,128)S(1)} %get-tuple-element.493, pred[32]{0:T(512)(128)(4,1)S(1)} %add_compare_fusion.5, ...), kind=kOutput, calls=%fused_computation.88.clone.1 | convolution fusion | flops 28323840 | bytes 2244640 | tf_op jit(solution)/shard_map/while/body/tij,ctj->cti/dot_general | solution.py:73
  266.6 6.4 %all-to-all-start.3 = ((f32[3,64,128]{2,0,1:T(4,128)}), f32[3,64,128]{2,0,1:T(4,128)S(1)}, u32[]{:S(2)}, u32[]{:S(2)}) async-start(f32[3,64,128]{2,0,1:T(4,128)} %copy.127), calls=%async_computation.3 | async-start | bytes 262144 | tf_op jit(solution)/shard_map/all_to_all | solution.py:131
  273.0 12.7 %fusion.107 = f32[6,8192]{1,0:T(8,128)S(1)} fusion(s32[4,64,128]{2,0,1:T(4,128)S(1)} %fusion.125, f32[6,4,64,128]{3,2,1,0:T(8,128)S(1)} %broadcast_multiply_fusion), kind=kOutput, calls=%fused_computation.136 | convolution fusion | flops 306184192 | bytes 1114112 | tf_op jit(solution)/shard_map/cake,aken->ckn/dot_general | solution.py:49
  291.2 5.9 %pad_subtract_fusion = f32[6,8192]{0,1:T(8,128)} fusion(f32[6,8192]{0,1:T(8,128)} %copy.133, f32[3,8192]{0,1:T(8,128)} %bitcast.269), kind=kLoop, calls=%fused_computation.141 | loop fusion | flops 49152 | bytes 491520 | tf_op jit(solution)/shard_map/sub | solution.py:136
  311.3 5.3 %scatter_custom_fusion.4 = f32[6,8192]{0,1:T(8,128)} fusion(f32[6,8192]{0,1:T(8,128)} %pad_subtract_fusion, s32[128]{0:T(128)S(1)} %get-tuple-element.345, f32[6,1,128]{0,2,1:T(8,128)S(1)} %collective-permute-done.12), kind=kCustom, calls=%fused_computation.188 | custom fusion | flops 768 | bytes 262144 | tf_op jit(solution)/shard_map/scatter-add | solution.py:142
  (209 shorter events, 172.4 us)
Async XLA Ops:
  4.6 44.9 %all-to-all-start = ((f32[6,64,128]{2,0,1:T(8,128)}), f32[6,64,128]{2,0,1:T(8,128)S(1)}, u32[]{:S(2)}, u32[]{:S(2)}) async-start(f32[6,64,128]{2,0,1:T(8,128)} %copy.111), calls=%async_computation | async-start | bytes 524288 | tf_op jit(solution)/shard_map/all_to_all | solution.py:108
  36.8 28.4 %copy-start.5 = (s32[128,128]{1,0:T(8,128)S(1)}, s32[128,128]{1,0:T(8,128)}, u32[]{:S(2)}) copy-start(s32[128,128]{1,0:T(8,128)} %param.32) | copy-start | bytes 196612
  36.8 28.4 %copy-start.6 = (s32[128,128]{1,0:T(8,128)S(1)}, s32[128,128]{1,0:T(8,128)}, u32[]{:S(2)}) copy-start(s32[128,128]{1,0:T(8,128)} %param.33) | copy-start | bytes 196612
  36.8 28.4 %copy-start.8 = (s32[2,128]{1,0:T(2,128)S(1)}, s32[2,128]{1,0:T(2,128)}, u32[]{:S(2)}) copy-start(s32[2,128]{1,0:T(2,128)} %param.30) | copy-start | bytes 3076
  50.1 4.4 %collective-permute-start.1 = (f32[6,1,1,8,128]{4,0,3,2,1:T(8,128)S(1)}, f32[6,1,1,8,128]{4,0,3,2,1:T(8,128)S(1)}, u32[]{:S(2)}, u32[]{:S(2)}) collective-permute-start(f32[6,1,1,8,128]{4,0,3,2,1:T(8,128)S(1)} %bitcast.285), channel_id=1, source_target_pairs={{8,0},{16,8},{24,16},{9,1},{17,9},{25,17},{10,2},{18,10},{26,18},{... | collective-permute-start | bytes 73736 | tf_op jit(solution)/shard_map/ppermute | solution.py:28
  51.4 3.9 %collective-permute-start = (f32[6,1,1,8,128]{4,0,3,2,1:T(8,128)S(1)}, f32[6,1,1,8,128]{4,0,3,2,1:T(8,128)S(1)}, u32[]{:S(2)}, u32[]{:S(2)}) collective-permute-start(f32[6,1,1,8,128]{4,0,3,2,1:T(8,128)S(1)} %bitcast.286), channel_id=1, source_target_pairs={{0,8},{8,16},{16,24},{1,9},{9,17},{17,25},{2,10},{10,18},{18,26},{... | collective-permute-start | bytes 73736 | tf_op jit(solution)/shard_map/ppermute | solution.py:26
  55.3 9.8 %collective-permute-start.3 = (f32[6,3,1,8,128]{4,0,3,2,1:T(8,128)S(1)}, f32[6,3,1,8,128]{4,0,3,2,1:T(8,128)S(1)}, u32[]{:S(2)}, u32[]{:S(2)}) collective-permute-start(f32[6,3,1,8,128]{4,0,3,2,1:T(8,128)S(1)} %pad_maximum_fusion.2), channel_id=1, source_target_pairs={{1,0},{2,1},{3,2},{4,3},{5,4},{6,5},{7,6},{9,8},{10,9},{11,10},{12... | collective-permute-start | bytes 221192 | tf_op jit(solution)/shard_map/ppermute | solution.py:28
  56.6 8.5 %collective-permute-start.2 = (f32[6,3,1,8,128]{4,0,3,2,1:T(8,128)S(1)}, f32[6,3,1,8,128]{4,0,3,2,1:T(8,128)S(1)}, u32[]{:S(2)}, u32[]{:S(2)}) collective-permute-start(f32[6,3,1,8,128]{4,0,3,2,1:T(8,128)S(1)} %pad_maximum_fusion.2), channel_id=1, source_target_pairs={{0,1},{1,2},{2,3},{3,4},{4,5},{5,6},{6,7},{8,9},{9,10},{10,11},{11... | collective-permute-start | bytes 221192 | tf_op jit(solution)/shard_map/ppermute | solution.py:26
  65.2 52.4 %copy-start.10 = (s32[4,128]{1,0:T(4,128)S(1)}, s32[4,128]{1,0:T(4,128)}, u32[]{:S(2)}) copy-start(s32[4,128]{1,0:T(4,128)} %param.27) | copy-start | bytes 6148
  109.3 15.9 %all-to-all-start.1 = ((f32[3,64,128]{2,0,1:T(4,128)}), f32[3,64,128]{2,0,1:T(4,128)S(1)}, u32[]{:S(2)}, u32[]{:S(2)}) async-start(f32[3,64,128]{2,0,1:T(4,128)} %copy.114), calls=%async_computation.1 | async-start | bytes 262144 | tf_op jit(solution)/shard_map/all_to_all | solution.py:131
  136.9 29.9 %collective-permute-start.7 = (f32[6,1,128]{0,2,1:T(8,128)S(1)}, f32[6,1,128]{0,2,1:T(8,128)S(1)}, u32[]{:S(2)}, u32[]{:S(2)}) collective-permute-start(f32[6,1,128]{0,2,1:T(8,128)S(1)} %get-tuple-element.338), channel_id=1, source_target_pairs={{1,0},{2,1},{3,2},{4,3},{5,4},{6,5},{7,6},{9,8},{10,9},{11,10},{12... | collective-permute-start | bytes 9224 | tf_op jit(solution)/shard_map/ppermute | solution.py:28
  138.2 23.3 %collective-permute-start.6 = (f32[6,1,128]{0,2,1:T(8,128)S(1)}, f32[6,1,128]{0,2,1:T(8,128)S(1)}, u32[]{:S(2)}, u32[]{:S(2)}) collective-permute-start(f32[6,1,128]{0,2,1:T(8,128)S(1)} %get-tuple-element.339), channel_id=1, source_target_pairs={{0,1},{1,2},{2,3},{3,4},{4,5},{5,6},{6,7},{8,9},{9,10},{10,11},{11... | collective-permute-start | bytes 9224 | tf_op jit(solution)/shard_map/ppermute | solution.py:26
  145.7 10.5 %collective-permute-start.5 = (f32[6,1,128]{0,2,1:T(8,128)S(1)}, f32[6,1,128]{0,2,1:T(8,128)S(1)}, u32[]{:S(2)}, u32[]{:S(2)}) collective-permute-start(f32[6,1,128]{0,2,1:T(8,128)S(1)} %get-tuple-element.340), channel_id=1, source_target_pairs={{8,0},{16,8},{24,16},{9,1},{17,9},{25,17},{10,2},{18,10},{26,18},{... | collective-permute-start | bytes 9224 | tf_op jit(solution)/shard_map/ppermute | solution.py:28
  147.0 3.9 %collective-permute-start.4 = (f32[6,1,128]{0,2,1:T(8,128)S(1)}, f32[6,1,128]{0,2,1:T(8,128)S(1)}, u32[]{:S(2)}, u32[]{:S(2)}) collective-permute-start(f32[6,1,128]{0,2,1:T(8,128)S(1)} %get-tuple-element.341), channel_id=1, source_target_pairs={{0,8},{8,16},{16,24},{1,9},{9,17},{17,25},{2,10},{10,18},{18,26},{... | collective-permute-start | bytes 9224 | tf_op jit(solution)/shard_map/ppermute | solution.py:26
  191.3 15.8 %all-to-all-start.2 = ((f32[6,64,128]{2,0,1:T(8,128)}), f32[6,64,128]{2,0,1:T(8,128)S(1)}, u32[]{:S(2)}, u32[]{:S(2)}) async-start(f32[6,64,128]{2,0,1:T(8,128)} %copy.124), calls=%async_computation.2 | async-start | bytes 524288 | tf_op jit(solution)/shard_map/all_to_all | solution.py:108
  207.7 4.4 %collective-permute-start.9 = (f32[6,1,1,8,128]{4,0,3,2,1:T(8,128)S(1)}, f32[6,1,1,8,128]{4,0,3,2,1:T(8,128)S(1)}, u32[]{:S(2)}, u32[]{:S(2)}) collective-permute-start(f32[6,1,1,8,128]{4,0,3,2,1:T(8,128)S(1)} %bitcast.282), channel_id=1, source_target_pairs={{8,0},{16,8},{24,16},{9,1},{17,9},{25,17},{10,2},{18,10},{26,18},{... | collective-permute-start | bytes 73736 | tf_op jit(solution)/shard_map/ppermute | solution.py:28
  209.0 3.9 %collective-permute-start.8 = (f32[6,1,1,8,128]{4,0,3,2,1:T(8,128)S(1)}, f32[6,1,1,8,128]{4,0,3,2,1:T(8,128)S(1)}, u32[]{:S(2)}, u32[]{:S(2)}) collective-permute-start(f32[6,1,1,8,128]{4,0,3,2,1:T(8,128)S(1)} %bitcast.283), channel_id=1, source_target_pairs={{0,8},{8,16},{16,24},{1,9},{9,17},{17,25},{2,10},{10,18},{18,26},{... | collective-permute-start | bytes 73736 | tf_op jit(solution)/shard_map/ppermute | solution.py:26
  212.9 9.3 %collective-permute-start.11 = (f32[6,3,1,8,128]{4,0,3,2,1:T(8,128)S(1)}, f32[6,3,1,8,128]{4,0,3,2,1:T(8,128)S(1)}, u32[]{:S(2)}, u32[]{:S(2)}) collective-permute-start(f32[6,3,1,8,128]{4,0,3,2,1:T(8,128)S(1)} %pad_maximum_fusion.3), channel_id=1, source_target_pairs={{1,0},{2,1},{3,2},{4,3},{5,4},{6,5},{7,6},{9,8},{10,9},{11,10},{12... | collective-permute-start | bytes 221192 | tf_op jit(solution)/shard_map/ppermute | solution.py:28
  214.2 8.0 %collective-permute-start.10 = (f32[6,3,1,8,128]{4,0,3,2,1:T(8,128)S(1)}, f32[6,3,1,8,128]{4,0,3,2,1:T(8,128)S(1)}, u32[]{:S(2)}, u32[]{:S(2)}) collective-permute-start(f32[6,3,1,8,128]{4,0,3,2,1:T(8,128)S(1)} %pad_maximum_fusion.3), channel_id=1, source_target_pairs={{0,1},{1,2},{2,3},{3,4},{4,5},{5,6},{6,7},{8,9},{9,10},{10,11},{11... | collective-permute-start | bytes 221192 | tf_op jit(solution)/shard_map/ppermute | solution.py:26
  266.6 21.8 %all-to-all-start.3 = ((f32[3,64,128]{2,0,1:T(4,128)}), f32[3,64,128]{2,0,1:T(4,128)S(1)}, u32[]{:S(2)}, u32[]{:S(2)}) async-start(f32[3,64,128]{2,0,1:T(4,128)} %copy.127), calls=%async_computation.3 | async-start | bytes 262144 | tf_op jit(solution)/shard_map/all_to_all | solution.py:131
  302.9 8.3 %collective-permute-start.12 = (f32[6,1,128]{0,2,1:T(8,128)S(1)}, f32[6,1,128]{0,2,1:T(8,128)S(1)}, u32[]{:S(2)}, u32[]{:S(2)}) collective-permute-start(f32[6,1,128]{0,2,1:T(8,128)S(1)} %get-tuple-element.337), channel_id=1, source_target_pairs={{0,8},{8,16},{16,24},{1,9},{9,17},{17,25},{2,10},{10,18},{18,26},{... | collective-permute-start | bytes 9224 | tf_op jit(solution)/shard_map/ppermute | solution.py:26
  305.1 11.5 %collective-permute-start.13 = (f32[6,1,128]{0,2,1:T(8,128)S(1)}, f32[6,1,128]{0,2,1:T(8,128)S(1)}, u32[]{:S(2)}, u32[]{:S(2)}) collective-permute-start(f32[6,1,128]{0,2,1:T(8,128)S(1)} %get-tuple-element.336), channel_id=1, source_target_pairs={{8,0},{16,8},{24,16},{9,1},{17,9},{25,17},{10,2},{18,10},{26,18},{... | collective-permute-start | bytes 9224 | tf_op jit(solution)/shard_map/ppermute | solution.py:28
  306.4 15.5 %collective-permute-start.14 = (f32[6,1,128]{0,2,1:T(8,128)S(1)}, f32[6,1,128]{0,2,1:T(8,128)S(1)}, u32[]{:S(2)}, u32[]{:S(2)}) collective-permute-start(f32[6,1,128]{0,2,1:T(8,128)S(1)} %get-tuple-element.335), channel_id=1, source_target_pairs={{0,1},{1,2},{2,3},{3,4},{4,5},{5,6},{6,7},{8,9},{9,10},{10,11},{11... | collective-permute-start | bytes 9224 | tf_op jit(solution)/shard_map/ppermute | solution.py:26
  310.0 17.2 %collective-permute-start.15 = (f32[6,1,128]{0,2,1:T(8,128)S(1)}, f32[6,1,128]{0,2,1:T(8,128)S(1)}, u32[]{:S(2)}, u32[]{:S(2)}) collective-permute-start(f32[6,1,128]{0,2,1:T(8,128)S(1)} %get-tuple-element.334), channel_id=1, source_target_pairs={{1,0},{2,1},{3,2},{4,3},{5,4},{6,5},{7,6},{9,8},{10,9},{11,10},{12... | collective-permute-start | bytes 9224 | tf_op jit(solution)/shard_map/ppermute | solution.py:28
  (10 other events, 128.1 us)
where the time goes:
time: 340 us; the launch traced here: 336 us
  matrix products  135 us (40%)
  other arithmetic  78 us (23%)
  starting transfers between devices  66.2 us (19%)
  local copies, waits for them, and re-layouts  37.4 us (11%)
  waiting for transfers between devices  16.9 us (5%)
    dot_general x8, matrix products, tile_forces(): jnp.einsum('tij,ctj->cti', pressure, master_nrm, precision=EXACT)  46.2 us
    ppermute x8, starting transfers between devices, padded_2(): lax.ppermute(tail, axis, [(i, (i + 1) % count) for i in range(ends)])  28.4 us
    dot_general x2, matrix products, element_forces(): jnp.einsum('ckn,aken->cake', disp_blocks, picker, precision=EXACT)  27.6 us
    dot_general x8, matrix products, tile_forces(): jnp.einsum('cti,ctj->tij', slave_pos, master_nrm, precision=EXACT)  27.5 us
    dot_general x2, matrix products, element_forces(): jnp.einsum('cake,aken->ckn', element_force, picker, precision=EXACT)  25.3 us
    all_to_all x2, starting transfers between devices, body(): lax.all_to_all(contact, ('gx', 'gy'), split_axis=1, concat_axis=1, tiled=...  14.7 us
    all_to_all x2, starting transfers between devices, body(): lax.all_to_all(outgoing, ('gx', 'gy'), split_axis=1, concat_axis=1, tiled...  12.7 us
    reduce_sum x2, other arithmetic, element_forces(): jnp.sum(stiffness.astype(jnp.float32) * elem_dofs[None, :, :], axis=1)  12.2 us
  transfers between devices with their start and end apart: 20, of which 7 were waited for; matrix products, arithmetic and copies ran while one was open for 29% of the time, Pallas kernels for 0%

commit v1 on v0

v1 whole, which is shorter than its diff:
```python
import jax
import jax.numpy as jnp
from jax import lax
from jax.experimental import pallas as pl
from jax.experimental.pallas import tpu as pltpu
from jax.sharding import PartitionSpec as P

BLK = 128
CAP = 2
STEPS = 2
ROWS = 8
HALF = 4
EBLK = 8

TIME_STEP = 0.5
PENALTY = 32.0
THICKNESS = 0.2

AXES = ("gx", "gy")
F32 = jnp.float32
BF16 = jnp.bfloat16
VMEM = pltpu.VMEM
SMEM = pltpu.SMEM


def vspec():
    return pl.BlockSpec(memory_space=VMEM)


def sspec():
    return pl.BlockSpec(memory_space=SMEM)


def lane_gather(data, index):
    return jnp.take_along_axis(data, index, axis=1, mode="promise_in_bounds")


def split(x):
    high = x.astype(BF16).astype(F32)
    return high, x - high


def prep_kernel(slot_ref, disp_ref, pos_ref, nrm_ref, out_ref):
    places = out_ref.shape[0]
    blocks = slot_ref.shape[0]
    if places != blocks:
        out_ref[...] = jnp.zeros(out_ref.shape, F32)
    pad = jnp.zeros((ROWS - 6, BLK), F32)
    for k in range(blocks):
        lanes = slice(k * BLK, (k + 1) * BLK)
        position = pos_ref[:, lanes] + disp_ref[0:3, lanes]
        out_ref[slot_ref[k]] = jnp.concatenate([position, nrm_ref[:, lanes], pad], axis=0)


def prep(block_slot, displacement, ref_pos, normals, places):
    return pl.pallas_call(
        prep_kernel,
        out_shape=jax.ShapeDtypeStruct((places, ROWS, BLK), F32),
        in_specs=[sspec(), vspec(), vspec(), vspec()],
        out_specs=vspec(),
        name="prep",
    )(block_slot, displacement, ref_pos, normals)


def fold_rows(tiles, row):
    low4 = row < 4
    low2 = (row & 2) == 0
    low1 = (row & 1) == 0
    four = []
    for i in range(4):
        a, b = tiles[i], tiles[i + 4]
        four.append(jnp.where(low4, a, b) + pltpu.roll(jnp.where(low4, b, a), 4, 0))
    two = []
    for i in range(2):
        a, b = four[i], four[i + 2]
        two.append(jnp.where(low2, a + pltpu.roll(a, 6, 0), b + pltpu.roll(b, 2, 0)))
    a, b = two
    return jnp.where(low1, a + pltpu.roll(a, 7, 0), b + pltpu.roll(b, 1, 0))


def element_kernel(disp_ref, conn_ref, stiff_ref, yield_ref, out_ref):
    row = lax.broadcasted_iota(jnp.int32, (ROWS, BLK), 0)
    row48 = lax.broadcasted_iota(jnp.int32, (48, BLK), 0)
    node = lax.broadcasted_iota(jnp.int32, (BLK, BLK), 0)
    for k in range(out_ref.shape[0]):
        lanes = slice(k * BLK, (k + 1) * BLK)
        local = conn_ref[:, lanes] & (BLK - 1)
        index = jnp.concatenate([local, local], axis=0)
        dofs = []
        for t in range(3):
            first = jnp.broadcast_to(disp_ref[2 * t : 2 * t + 1, lanes], (4, BLK))
            second = jnp.broadcast_to(disp_ref[2 * t + 1 : 2 * t + 2, lanes], (4, BLK))
            dofs.append(lane_gather(jnp.concatenate([first, second], axis=0), index))
        trial = []
        for g in range(3):
            tiles = []
            for i in range(8 * g, 8 * g + 8):
                line = stiff_ref[i, :, lanes].astype(F32)
                tiles.append(line[0:8] * dofs[0] + line[8:16] * dofs[1] + line[16:24] * dofs[2])
            trial.append(fold_rows(tiles, row))
        squared = trial[0] * trial[0] + trial[1] * trial[1] + trial[2] * trial[2]
        squared = squared + pltpu.roll(squared, 4, 0)
        squared = squared + pltpu.roll(squared, 2, 0)
        squared = squared + pltpu.roll(squared, 1, 0)
        level = yield_ref[0, k : k + 1, :]
        factor = lax.rsqrt(1.0 + squared / (level * level))
        forces = jnp.concatenate([t * factor for t in trial], axis=0)
        high, low = split(forces)
        stacked = jnp.concatenate([high, low], axis=0)
        total = jnp.zeros((48, BLK), F32)
        for a in range(4):
            corner = jnp.where((row48 & 3) == a, stacked, 0.0).astype(BF16)
            picker = jnp.where(node == local[a : a + 1, :], 1.0, 0.0).astype(BF16)
            total = total + lax.dot_general(
                corner, picker, (((1,), (1,)), ((), ())), preferred_element_type=F32
            )
        total = total[0:24] + total[24:48]
        pieces = []
        for t in range(3):
            x = total[8 * t : 8 * t + 8]
            x = x + pltpu.roll(x, 7, 0)
            x = x + pltpu.roll(x, 6, 0)
            pieces += [x[0:1], x[4:5]]
        out_ref[k] = jnp.concatenate(pieces + [jnp.zeros((2, BLK), F32)], axis=0)


def element_forces(displacement, connectivity, stiffness, yield_force):
    nodes = displacement.shape[1]
    blocks = nodes // BLK
    wide = EBLK * BLK
    return pl.pallas_call(
        element_kernel,
        out_shape=jax.ShapeDtypeStruct((blocks, ROWS, BLK), F32),
        grid=(blocks // EBLK,),
        in_specs=[
            pl.BlockSpec((6, wide), lambda i: (0, i)),
            pl.BlockSpec((4, wide), lambda i: (0, i)),
            pl.BlockSpec((24, 24, wide), lambda i: (0, 0, i)),
            pl.BlockSpec((1, EBLK, BLK), lambda i: (i, 0, 0)),
        ],
        out_specs=pl.BlockSpec((EBLK, ROWS, BLK), lambda i: (i, 0, 0)),
        cost_estimate=pl.CostEstimate(
            flops=2 * 576 * nodes, transcendentals=nodes, bytes_accessed=2 * 576 * nodes
        ),
        name="element",
    )(displacement, connectivity, stiffness, yield_force.reshape(-1, EBLK, BLK))


def contact_kernel(
    count_ref, pairs_ref, valid_ref, *refs, places, edges, fresh
):
    if fresh:
        recv_ref = refs[0]
        edge_refs = refs[1:5]
        rest = refs[5:]
    else:
        recv_ref, pos_ref = refs[0:2]
        edge_refs = refs[2:6]
        edge_pos_refs = refs[6:10]
        rest = refs[10:]
    start_ref, length_ref, out_ref, slave_tab, master_tab, force_tab, total_ref = rest
    zero1 = jnp.zeros((1, BLK), F32)
    ones = jnp.ones((3, BLK), F32)
    zero10 = jnp.zeros((10, BLK), F32)

    def master_entry(where, position, normal):
        n_high, n_low = split(normal)
        product = position * normal
        offset = THICKNESS + (product[0:1] + product[1:2] + product[2:3])
        o_high, o_rest = split(offset)
        o_mid, o_low = split(o_rest)
        negative = jnp.concatenate([-n_high, -n_low], axis=0)
        master_tab[where] = jnp.concatenate(
            [negative, negative, o_high, o_mid, o_low, zero1], axis=0
        ).astype(BF16)
        force_tab[where] = jnp.concatenate([n_high, n_low, zero10], axis=0).astype(BF16)

    def own_entry(p, carry):
        tile = recv_ref[p]
        position = tile[0:3] if fresh else pos_ref[p][0:3]
        p_high, p_low = split(position)
        slave_tab[p] = jnp.concatenate(
            [p_high, p_high, p_low, p_low, ones, zero1], axis=0
        ).astype(BF16)
        master_entry(p, position, tile[3:6])
        total_ref[p] = jnp.zeros((16, BLK), F32)
        return carry

    lax.fori_loop(0, places, own_entry, 0, unroll=4)
    for side in range(4):
        valid = valid_ref[side] > 0
        for e in range(edges):
            tile = jnp.where(valid, edge_refs[side][e], 0.0)
            if fresh:
                position = tile[0:3]
            else:
                position = jnp.where(valid, edge_pos_refs[side][e], 0.0)[0:3]
            master_entry(places + side * edges + e, position, tile[3:6])

    facet = lax.broadcasted_iota(jnp.int32, (BLK, BLK), 0)
    count = count_ref[0]

    def one_tile(t, live):
        slave = pairs_ref[0, t]
        master = pairs_ref[1, t]
        depth = lax.dot_general(
            master_tab[master],
            slave_tab[slave],
            (((0,), (0,)), ((), ())),
            preferred_element_type=F32,
        )
        start = start_ref[pl.ds(t, 1), :]
        length = jnp.where(live, length_ref[pl.ds(t, 1), :], 0)
        inside = ((facet - start) & (BLK - 1)) < length
        pressure = jnp.where(inside, jnp.maximum(depth, 0.0), 0.0)
        high = pressure.astype(BF16)
        low = (pressure - high.astype(F32)).astype(BF16)
        rows = force_tab[master]
        force = jnp.dot(rows, high, preferred_element_type=F32) + jnp.dot(
            rows, low, preferred_element_type=F32
        )
        total_ref[slave] = total_ref[slave] + force

    unroll = 4

    def body(r, carry):
        for d in range(unroll):
            t = r * unroll + d
            one_tile(t, t < count)
        return carry

    lax.fori_loop(0, (count + unroll - 1) // unroll, body, 0)

    def finish(p, carry):
        tile = total_ref[p]
        out_ref[p] = (PENALTY / BLK) * jnp.concatenate([tile[0:3] + tile[3:6], zero1], axis=0)
        return carry

    lax.fori_loop(0, places, finish, 0, unroll=8)


def contact(count, pairs, valid, received, positions, edges, edge_positions, start, length):
    places = received.shape[0]
    edge_count = edges[0].shape[0]
    extended = places + 4 * edge_count
    fresh = positions is None
    arrays = [received] + ([] if fresh else [positions]) + list(edges)
    arrays += [] if fresh else list(edge_positions)
    arrays += [start, length]
    tiles = start.shape[0]

    def kernel(*refs):
        contact_kernel(*refs, places=places, edges=edge_count, fresh=fresh)

    return pl.pallas_call(
        kernel,
        out_shape=jax.ShapeDtypeStruct((places, HALF, BLK), F32),
        in_specs=[sspec()] * 3 + [vspec()] * len(arrays),
        out_specs=vspec(),
        scratch_shapes=[
            VMEM((places, 16, BLK), BF16),
            VMEM((extended, 16, BLK), BF16),
            VMEM((extended, 16, BLK), BF16),
            VMEM((places, 16, BLK), F32),
        ],
        cost_estimate=pl.CostEstimate(
            flops=tiles * BLK * BLK * 64, transcendentals=0, bytes_accessed=tiles * BLK * 8
        ),
        name="contact",
    )(count, pairs, valid, *arrays)


def inverse_kernel(valid_ref, list_ref, out_ref):
    blocks = out_ref.shape[0]
    block_id = lax.broadcasted_iota(jnp.int32, (blocks, BLK), 0)
    lane_id = lax.broadcasted_iota(jnp.int32, (BLK, BLK), 0)
    rank = (lax.broadcasted_iota(jnp.int32, (BLK, BLK), 1) + 1).astype(F32)
    code = jnp.full((blocks, BLK), -1, jnp.int32)
    for side in range(4):
        nodes = list_ref[side : side + 1, :]
        valid = valid_ref[side] > 0
        in_block = jnp.where(
            jnp.logical_and(block_id == nodes // BLK, valid), 1.0, 0.0
        ).astype(BF16)
        at_lane = jnp.where(lane_id == (nodes & (BLK - 1)), rank, 0.0).astype(BF16)
        found = lax.dot_general(
            in_block, at_lane, (((1,), (1,)), ((), ())), preferred_element_type=F32
        ).astype(jnp.int32)
        code = jnp.where(found > 0, found - 1 + side * BLK, code)
    out_ref[...] = code


def inverse(valid, lists, blocks):
    return pl.pallas_call(
        inverse_kernel,
        out_shape=jax.ShapeDtypeStruct((blocks, BLK), jnp.int32),
        in_specs=[sspec(), vspec()],
        out_specs=vspec(),
        name="inverse",
    )(valid, lists)


def force_kernel(slot_ref, back_ref, internal_ref, list_ref, force_ref, *side_refs):
    blocks = slot_ref.shape[0]
    pad = jnp.zeros((ROWS - HALF, BLK), F32)
    lanes = []
    owners = []
    for side in range(4):
        nodes = jnp.broadcast_to(list_ref[side : side + 1, :], (ROWS, BLK))
        lanes.append(nodes & (BLK - 1))
        owners.append(nodes // BLK)
    sums = [jnp.zeros((ROWS, BLK), F32) for _ in range(4)]
    for k in range(blocks):
        tile = jnp.concatenate([back_ref[slot_ref[k]], pad], axis=0) - internal_ref[k]
        force_ref[k] = tile
        for side in range(4):
            sums[side] = jnp.where(
                owners[side] == k, lane_gather(tile, lanes[side]), sums[side]
            )
    for side in range(4):
        side_refs[side][...] = sums[side]


def nodal_force(block_slot, returned, internal, lists):
    blocks = internal.shape[0]
    return pl.pallas_call(
        force_kernel,
        out_shape=[jax.ShapeDtypeStruct((blocks, ROWS, BLK), F32)]
        + [jax.ShapeDtypeStruct((ROWS, BLK), F32)] * 4,
        in_specs=[sspec(), vspec(), vspec(), vspec()],
        out_specs=[vspec()] * 5,
        name="force",
    )(block_slot, returned, internal, lists)


def update_kernel(
    slot_ref,
    force_ref,
    near0_ref,
    near1_ref,
    near2_ref,
    near3_ref,
    code_ref,
    mass_ref,
    vel_ref,
    disp_ref,
    pos_ref,
    vel_out,
    disp_out,
    *send_refs,
):
    blocks = force_ref.shape[0]
    near = [r[...] for r in (near0_ref, near1_ref, near2_ref, near3_ref)]
    if send_refs and send_refs[0].shape[0] != blocks:
        send_refs[0][...] = jnp.zeros(send_refs[0].shape, F32)
    zero1 = jnp.zeros((1, BLK), F32)
    for k in range(blocks):
        lanes = slice(k * BLK, (k + 1) * BLK)
        code = jnp.broadcast_to(code_ref[k : k + 1, :], (ROWS, BLK))
        index = code & (BLK - 1)
        extra = jnp.zeros((ROWS, BLK), F32)
        for side in range(4):
            inside = jnp.logical_and(code >= side * BLK, code < (side + 1) * BLK)
            extra = jnp.where(inside, lane_gather(near[side], index), extra)
        assembled = (force_ref[k] + extra)[0:6]
        vel = vel_ref[:, lanes] + TIME_STEP * mass_ref[:, lanes] * assembled
        disp = disp_ref[:, lanes] + TIME_STEP * vel
        vel_out[:, lanes] = vel
        disp_out[:, lanes] = disp
        if send_refs:
            send_refs[0][slot_ref[k]] = jnp.concatenate(
                [pos_ref[:, lanes] + disp[0:3], zero1], axis=0
            )


def update(block_slot, force, near, code, inv_mass, velocity, displacement, ref_pos, places):
    nodes = displacement.shape[1]
    out = [jax.ShapeDtypeStruct((6, nodes), F32)] * 2
    if places:
        out = out + [jax.ShapeDtypeStruct((places, HALF, BLK), F32)]
    return pl.pallas_call(
        update_kernel,
        out_shape=out,
        in_specs=[sspec()] + [vspec()] * 10,
        out_specs=[vspec()] * len(out),
        name="update",
    )(block_slot, force, *near, code, inv_mass, velocity, displacement, ref_pos)


def pair_lists(size):
    first = [(i, i ^ 1) for i in range(size)]
    second = [(i, (i + 1) % size if i % 2 else (i - 1) % size) for i in range(size)]
    return first, second


def swap(values, sizes):
    out = []
    for at, axis in enumerate(AXES):
        for stage, pairs in enumerate(pair_lists(sizes[at])):
            out.append(lax.ppermute(values[2 * at + stage], axis, pairs))
    return out


def body(
    displacement,
    velocity,
    ref_pos,
    normals,
    inv_mass,
    connectivity,
    stiffness,
    yield_force,
    shared_nodes,
    block_slot,
    edge_slots,
    tile_pairs,
    tile_count,
    win_start,
    win_len,
):
    sizes = [lax.axis_size(axis) for axis in AXES]
    if any(size % 2 for size in sizes):
        raise ValueError("odd axis")
    places = sizes[0] * sizes[1] * CAP
    blocks = displacement.shape[1] // BLK
    edge_count = edge_slots.shape[0]
    at = [lax.axis_index(axis) for axis in AXES]
    even = [1 - i % 2 for i in at]
    valid = []
    for i, size in zip(at, sizes):
        valid += [jnp.int32(1), jnp.where((i == 0) | (i == size - 1), 0, 1).astype(jnp.int32)]
    valid = jnp.stack(valid)
    lists = []
    for axis in range(2):
        low, high = shared_nodes[2 * axis], shared_nodes[2 * axis + 1]
        is_even = even[axis] == 1
        lists += [jnp.where(is_even, high, low), jnp.where(is_even, low, high)]
    lists = jnp.stack(lists)
    far = tile_pairs[1] - places
    side = far // edge_count
    flip = jnp.where(side < 2, even[0], even[1])
    masters = jnp.where(
        far < 0, tile_pairs[1], places + (side ^ flip) * edge_count + far % edge_count
    )
    pairs = jnp.stack([tile_pairs[0], masters])
    code = inverse(valid, lists, blocks)

    def exchange(blocks_out):
        return lax.all_to_all(blocks_out, AXES, split_axis=0, concat_axis=0, tiled=True)

    outgoing = prep(block_slot, displacement, ref_pos, normals, places)
    first = None
    for step in range(STEPS):
        received = exchange(outgoing)
        internal = element_forces(displacement, connectivity, stiffness, yield_force)
        rows = received[edge_slots]
        near = swap([rows] * 4, sizes)
        if step == 0:
            first = (received, near)
            box_force = contact(
                tile_count, pairs, valid, received, None, near, None, win_start, win_len
            )
        else:
            box_force = contact(
                tile_count, pairs, valid, first[0], received, first[1], near, win_start, win_len
            )
        returned = exchange(box_force)
        force, *sides = nodal_force(block_slot, returned, internal, lists)
        incoming = swap(sides, sizes)
        last = step == STEPS - 1
        out = update(
            block_slot,
            force,
            incoming,
            code,
            inv_mass,
            velocity,
            displacement,
            ref_pos,
            0 if last else places,
        )
        velocity, displacement = out[0:2]
        if not last:
            outgoing = out[2]
    return (displacement, velocity)


def solution(mesh):
    split_last = P(None, AXES)
    placed = (
        split_last,
        split_last,
        split_last,
        split_last,
        split_last,
        split_last,
        P(None, None, AXES),
        P(AXES),
        split_last,
        P(AXES),
        P(AXES),
        split_last,
        P(AXES),
        P(AXES, None),
        P(AXES, None),
    )
    return jax.shard_map(
        body,
        mesh=mesh,
        in_specs=placed,
        out_specs=(split_last, split_last),
        check_vma=False,
    )
```

time: 340 us -> 169 us (0.50)
  matrix products: 135 us -> 0 us
  Pallas kernels: 0 us -> 88.5 us
  other arithmetic: 78 us -> 3.32 us
  starting transfers between devices: 66.2 us -> 32.9 us
  local copies, waits for them, and re-layouts: 37.4 us -> 5.43 us
  blocking collectives: 0 us -> 10.5 us
  waiting for transfers between devices: 16.9 us -> 25.8 us
    dot_general x48 -> x0, matrix products: 135 us -> none  [the longest x8 46.2 us: tile_forces(): jnp.einsum('tij,ctj->cti', pressure, master_nrm, precision=EXACT)]
    pallas_call x0 -> x10, Pallas kernels: none -> 88.5 us  [the longest x2 52.9 us: contact(): pl.pallas_call(kernel, out_shape=jax.ShapeDtypeStruct((places, HALF, BLK)...]
    scatter-add x8 -> x0, other arithmetic: 42.5 us -> none  [the longest x2 10.7 us: body(): assembled = assembled.at[:, shared_nodes[3]].add(near_y[:, 3])]
    ppermute x16, starting transfers between devices: 38.8 us -> 19.4 us  [swap(): out.append(lax.ppermute(values[2 * at + stage], axis, pairs))]
    all_to_all x4 -> x3, starting transfers between devices: 27.4 us -> 13.5 us  [exchange(): lax.all_to_all(blocks_out, AXES, split_axis=0, concat_axis=0, tiled=True)]
    reduce_sum x12 -> x0, other arithmetic: 13.6 us -> none  [the longest x2 12.2 us: element_forces(): jnp.sum(stiffness.astype(jnp.float32) * elem_dofs[None, :, :], axis=1)]
    sub x2 -> x0, other arithmetic: 11.7 us -> none  [body(): jnp.concatenate([contact_nodes, jnp.zeros_like(contact_nodes)], axis=0)]
    gather x6 -> x2, local copies, waits for them, and re-layouts: 12.7 us -> 1.13 us  [body(): rows = received[edge_slots]]
  transfers between devices with their start and end apart: 20 -> 19, of which waited for: 7 -> 6; matrix products, arithmetic and copies ran while one was open for 29% -> 2% of each run, Pallas kernels for 0% -> 14%
where the time goes in v1:
time: 169 us; the launch traced here: 168 us
  Pallas kernels  88.5 us (52%)
  starting transfers between devices  32.9 us (19%)
  waiting for transfers between devices  25.8 us (15%)
  blocking collectives  10.5 us (6%)
  local copies, waits for them, and re-layouts  5.43 us (3%)
  other arithmetic  3.32 us (2%)
    pallas_call x2, Pallas kernels, contact(): pl.pallas_call(kernel, out_shape=jax.ShapeDtypeStruct((places, HALF, BLK)...  52.9 us
    pallas_call x2, Pallas kernels, element_forces(): pl.pallas_call(element_kernel, out_shape=jax.ShapeDtypeStruct((blocks, RO...  22.3 us
    ppermute x16, starting transfers between devices, swap(): out.append(lax.ppermute(values[2 * at + stage], axis, pairs))  19.4 us
    all_to_all x3, waiting for transfers between devices, exchange(): lax.all_to_all(blocks_out, AXES, split_axis=0, concat_axis=0, tiled=True)  15.5 us
    all_to_all x3, starting transfers between devices, exchange(): lax.all_to_all(blocks_out, AXES, split_axis=0, concat_axis=0, tiled=True)  13.5 us
    all_to_all x1, blocking collectives, exchange(): lax.all_to_all(blocks_out, AXES, split_axis=0, concat_axis=0, tiled=True)  10.5 us
    ppermute x16, waiting for transfers between devices, swap(): out.append(lax.ppermute(values[2 * at + stage], axis, pairs))  10.3 us
    pallas_call x2, Pallas kernels, update(): pl.pallas_call(update_kernel, out_shape=out, in_specs=[sspec()] + [vspec(...  5.28 us
  transfers between devices with their start and end apart: 19, of which 6 were waited for; matrix products, arithmetic and copies ran while one was open for 2% of the time, Pallas kernels for 14%

profile of v1, /device:TPU:0, one launch (start us, length us, event | category | flops | bytes accessed | tf_op | source)
XLA Modules:
  0.0 168.0 jit_solution(3474678024846090784)
XLA Ops:
  0.6 1.8 %prep.1 = f32[64,8,128]{2,1,0:T(8,128)} custom-call(s32[64]{0:T(128)} %slot_ref.9, f32[6,8192]{1,0:T(8,128)} %disp_ref.5, f32[3,8192]{1,0:T(4,128)} %pos_ref.5, f32[3,8192]{1,0:T(4,128)} %nrm_ref.1), custom_call_target="tpu_custom_call" | custom-call | tf_op jit(solution)/shard_map/prep/pallas_call | solution.py:56
  2.5 7.3 %all-to-all-start = ((f32[64,8,128]{2,1,0:T(8,128)}), f32[64,8,128]{2,1,0:T(8,128)S(1)}, u32[]{:S(2)}, u32[]{:S(2)}) async-start(f32[64,8,128]{2,1,0:T(8,128)} %prep.1), calls=%async_computation | async-start | bytes 524288 | tf_op jit(solution)/shard_map/all_to_all | solution.py:449
  11.9 8.4 %all-to-all-done.refs_3_ = f32[64,8,128]{2,1,0:T(8,128)S(1)} async-done(((f32[64,8,128]{2,1,0:T(8,128)}), f32[64,8,128]{2,1,0:T(8,128)S(1)}, u32[]{:S(2)}, u32[]{:S(2)}) %all-to-all-start) | async-done | bytes 262176 | tf_op jit(solution)/shard_map/all_to_all | solution.py:449
  22.7 2.4 %collective-permute-start.3 = (f32[8,8,128]{2,1,0:T(8,128)S(1)}, f32[8,8,128]{2,1,0:T(8,128)S(1)}, u32[]{:S(2)}, u32[]{:S(2)}) collective-permute-start(f32[8,8,128]{2,1,0:T(8,128)S(1)} %gather_fusion), channel_id=1, source_target_pairs={{0,7},{1,2},{2,1},{3,4},{4,3},{5,6},{6,5},{7,0},{8,15},{9,10},{10,... | collective-permute-start | bytes 98312 | tf_op jit(solution)/shard_map/ppermute | solution.py:400
  26.5 11.1 %element.2.internal_ref = f32[64,8,128]{2,1,0:T(8,128)} custom-call(f32[6,8192]{1,0:T(8,128)} %disp_ref.5, s32[4,8192]{1,0:T(4,128)} %conn_ref.3, bf16[24,24,8192]{2,1,0:T(8,128)(2,1)} %stiff_ref.3, f32[8,8,128]{2,1,0:T(8,128)} %bitcast.3), custom_call_target="tpu_custom_call" | custom-call | flops 9437184 | bytes 9437184 | tf_op jit(solution)/shard_map/element/pallas_call | solution.py:131
  38.9 26.4 %contact.2 = f32[64,4,128]{2,1,0:T(4,128)} custom-call(s32[1]{0:T(128)S(6)} %copy.17.refs_0_, s32[2,128]{1,0:T(2,128)} %pad_add_fusion.1.refs_1_, s32[4]{0:T(128)} %pad_add_fusion.2.refs_2_.valid_ref, f32[64,8,128]{2,1,0:T(8,128)} %copy-done, f32[8,8,128]{2,1,0:T(8,128)} %copy-done.6, f32[8,8,128]{2,1,0:T(8,128)} %copy-done.5, f32[8,8,128]{2,1,0:T(8,128)} %copy-done.4, ...), custom_call_target="tpu_custom_call" | custom-call | flops 134217728 | bytes 131072 | tf_op jit(solution)/shard_map/contact/pallas_call | solution.py:255
  65.3 3.6 %all-to-all-start.1 = ((f32[64,4,128]{2,1,0:T(4,128)}), f32[64,4,128]{2,1,0:T(4,128)S(1)}, u32[]{:S(2)}, u32[]{:S(2)}) async-start(f32[64,4,128]{2,1,0:T(4,128)} %contact.2), calls=%async_computation.1 | async-start | bytes 262144 | tf_op jit(solution)/shard_map/all_to_all | solution.py:449
  69.4 7.2 %all-to-all-done.1.back_ref = f32[64,4,128]{2,1,0:T(4,128)S(1)} async-done(((f32[64,4,128]{2,1,0:T(4,128)}), f32[64,4,128]{2,1,0:T(4,128)S(1)}, u32[]{:S(2)}, u32[]{:S(2)}) %all-to-all-start.1) | async-done | bytes 131104 | tf_op jit(solution)/shard_map/all_to_all | solution.py:449
  77.3 2.4 %force.2 = (f32[64,8,128]{2,1,0:T(8,128)}, f32[8,128]{1,0:T(8,128)}, f32[8,128]{1,0:T(8,128)}, f32[8,128]{1,0:T(8,128)}, f32[8,128]{1,0:T(8,128)}) custom-call(s32[64]{0:T(128)} %slot_ref.9, f32[64,4,128]{2,1,0:T(4,128)} %copy-done.2, f32[64,8,128]{2,1,0:T(8,128)} %element.2.internal_ref, s32[4,128]{1,0:T(4,128)} %pad_add_fusion.list_ref), custom_call_target="tpu_custom_call" | custom-call | tf_op jit(solution)/shard_map/force/pallas_call | solution.py:326
  81.6 2.1 %collective-permute-start.7 = (f32[8,128]{1,0:T(8,128)}, f32[8,128]{1,0:T(8,128)S(1)}, u32[]{:S(2)}, u32[]{:S(2)}) collective-permute-start(f32[8,128]{1,0:T(8,128)} %get-tuple-element.21), channel_id=1, source_target_pairs={{0,7},{1,2},{2,1},{3,4},{4,3},{5,6},{6,5},{7,0},{8,15},{9,10},{10,... | collective-permute-start | bytes 12296 | tf_op jit(solution)/shard_map/ppermute | solution.py:400
  83.8 1.5 inverse.1.code_ref
  85.3 2.8 %collective-permute-done.7.near3_ref = f32[8,128]{1,0:T(8,128)S(1)} collective-permute-done((f32[8,128]{1,0:T(8,128)}, f32[8,128]{1,0:T(8,128)S(1)}, u32[]{:S(2)}, u32[]{:S(2)}) %collective-permute-start.7) | collective-permute-done | bytes 4128 | tf_op jit(solution)/shard_map/ppermute | solution.py:400
  88.8 2.7 %update.2 = (f32[6,8192]{1,0:T(8,128)}, f32[6,8192]{1,0:T(8,128)}, f32[64,4,128]{2,1,0:T(4,128)}) custom-call(s32[64]{0:T(128)} %slot_ref.9, f32[64,8,128]{2,1,0:T(8,128)} %get-tuple-element.17.force_ref, f32[8,128]{1,0:T(8,128)} %copy-done.13, f32[8,128]{1,0:T(8,128)} %copy-done.15, f32[8,128]{1,0:T(8,128)} %copy-done.17, f32[8,128]{1,0:T(8,128)} %copy-done.19, ...), custom_call_target="tpu_custom_call" | custom-call | tf_op jit(solution)/shard_map/update/pallas_call | solution.py:381
  91.4 10.5 %all_to_all.20.refs_4_ = f32[64,4,128]{2,1,0:T(4,128)S(1)} all-to-all(f32[64,4,128]{2,1,0:T(4,128)} %get-tuple-element.22), channel_id=1, replica_groups=mesh['gx'=4,'gy'=8] {'gx','gy'}, dimensions={0} | all-to-all | bytes 262144 | tf_op jit(solution)/shard_map/all_to_all | solution.py:449
  104.5 2.1 %collective-permute-start.11 = (f32[8,4,128]{2,1,0:T(4,128)S(1)}, f32[8,4,128]{2,1,0:T(4,128)S(1)}, u32[]{:S(2)}, u32[]{:S(2)}) collective-permute-start(f32[8,4,128]{2,1,0:T(4,128)S(1)} %gather_fusion.1), channel_id=1, source_target_pairs={{0,7},{1,2},{2,1},{3,4},{4,3},{5,6},{6,5},{7,0},{8,15},{9,10},{10,... | collective-permute-start | bytes 49160 | tf_op jit(solution)/shard_map/ppermute | solution.py:400
  107.0 4.0 %collective-permute-done.11.refs_12_ = f32[8,4,128]{2,1,0:T(4,128)S(1)} collective-permute-done((f32[8,4,128]{2,1,0:T(4,128)S(1)}, f32[8,4,128]{2,1,0:T(4,128)S(1)}, u32[]{:S(2)}, u32[]{:S(2)}) %collective-permute-start.11) | collective-permute-done | bytes 16416 | tf_op jit(solution)/shard_map/ppermute | solution.py:400
  111.6 26.5 %contact.3 = f32[64,4,128]{2,1,0:T(4,128)} custom-call(s32[1]{0:T(128)S(6)} %copy.17.refs_0_, s32[2,128]{1,0:T(2,128)} %pad_add_fusion.1.refs_1_, s32[4]{0:T(128)} %pad_add_fusion.2.refs_2_.valid_ref, f32[64,8,128]{2,1,0:T(8,128)} %copy-done, f32[64,4,128]{2,1,0:T(4,128)} %copy-done.1, f32[8,8,128]{2,1,0:T(8,128)} %copy-done.6, f32[8,8,128]{2,1,0:T(8,128)} %copy-done.5, ...), custom_call_target="tpu_custom_call" | custom-call | flops 134217728 | bytes 131072 | tf_op jit(solution)/shard_map/contact/pallas_call | solution.py:255
  138.1 2.7 %all-to-all-start.3 = ((f32[64,4,128]{2,1,0:T(4,128)}), f32[64,4,128]{2,1,0:T(4,128)S(1)}, u32[]{:S(2)}, u32[]{:S(2)}) async-start(f32[64,4,128]{2,1,0:T(4,128)} %contact.3), calls=%async_computation.3 | async-start | bytes 262144 | tf_op jit(solution)/shard_map/all_to_all | solution.py:449
  140.7 11.1 %element.3.internal_ref = f32[64,8,128]{2,1,0:T(8,128)} custom-call(f32[6,8192]{1,0:T(8,128)} %get-tuple-element.23.disp_ref, s32[4,8192]{1,0:T(4,128)} %conn_ref.3, bf16[24,24,8192]{2,1,0:T(8,128)(2,1)} %stiff_ref.3, f32[8,8,128]{2,1,0:T(8,128)} %bitcast.4), custom_call_target="tpu_custom_call" | custom-call | flops 9437184 | bytes 9437184 | tf_op jit(solution)/shard_map/element/pallas_call | solution.py:131
  152.5 2.4 %force.3 = (f32[64,8,128]{2,1,0:T(8,128)}, f32[8,128]{1,0:T(8,128)}, f32[8,128]{1,0:T(8,128)}, f32[8,128]{1,0:T(8,128)}, f32[8,128]{1,0:T(8,128)}) custom-call(s32[64]{0:T(128)} %slot_ref.9, f32[64,4,128]{2,1,0:T(4,128)} %copy-done.3, f32[64,8,128]{2,1,0:T(8,128)} %element.3.internal_ref, s32[4,128]{1,0:T(4,128)} %pad_add_fusion.list_ref), custom_call_target="tpu_custom_call" | custom-call | tf_op jit(solution)/shard_map/force/pallas_call | solution.py:326
  155.2 1.6 collective-permute-start.13
  158.3 3.3 %collective-permute-start.15 = (f32[8,128]{1,0:T(8,128)}, f32[8,128]{1,0:T(8,128)S(1)}, u32[]{:S(2)}, u32[]{:S(2)}) collective-permute-start(f32[8,128]{1,0:T(8,128)} %get-tuple-element.28), channel_id=1, source_target_pairs={{0,7},{1,2},{2,1},{3,4},{4,3},{5,6},{6,5},{7,0},{8,15},{9,10},{10,... | collective-permute-start | bytes 12296 | tf_op jit(solution)/shard_map/ppermute | solution.py:400
  161.6 3.1 %collective-permute-done.15.near3_ref = f32[8,128]{1,0:T(8,128)S(1)} collective-permute-done((f32[8,128]{1,0:T(8,128)}, f32[8,128]{1,0:T(8,128)S(1)}, u32[]{:S(2)}, u32[]{:S(2)}) %collective-permute-start.15) | collective-permute-done | bytes 4128 | tf_op jit(solution)/shard_map/ppermute | solution.py:400
  165.4 2.6 %update.3 = (f32[6,8192]{1,0:T(8,128)}, f32[6,8192]{1,0:T(8,128)}) custom-call(s32[64]{0:T(128)} %slot_ref.9, f32[64,8,128]{2,1,0:T(8,128)} %get-tuple-element.24.force_ref, f32[8,128]{1,0:T(8,128)} %copy-done.12, f32[8,128]{1,0:T(8,128)} %copy-done.14, f32[8,128]{1,0:T(8,128)} %copy-done.16, f32[8,128]{1,0:T(8,128)} %copy-done.18, ...), custom_call_target="tpu_custom_call" | custom-call | tf_op jit(solution)/shard_map/update/pallas_call | solution.py:381
  (76 shorter events, 16.8 us)
Async XLA Ops:
  0.6 68.2 %copy-start.20 = (s32[4,128]{1,0:T(4,128)S(1)}, s32[4,128]{1,0:T(4,128)}, u32[]{:S(2)}) copy-start(s32[4,128]{1,0:T(4,128)} %param.23) | copy-start | bytes 6148
  2.5 17.8 %all-to-all-start = ((f32[64,8,128]{2,1,0:T(8,128)}), f32[64,8,128]{2,1,0:T(8,128)S(1)}, u32[]{:S(2)}, u32[]{:S(2)}) async-start(f32[64,8,128]{2,1,0:T(8,128)} %prep.1), calls=%async_computation | async-start | bytes 524288 | tf_op jit(solution)/shard_map/all_to_all | solution.py:449
  20.2 17.4 %copy-start = (f32[64,8,128]{2,1,0:T(8,128)}, f32[64,8,128]{2,1,0:T(8,128)S(1)}, u32[]{:S(2)}) copy-start(f32[64,8,128]{2,1,0:T(8,128)S(1)} %all-to-all-done.refs_3_) | copy-start | bytes 786436
  20.8 16.8 %collective-permute-start.2 = (f32[8,8,128]{2,1,0:T(8,128)S(1)}, f32[8,8,128]{2,1,0:T(8,128)S(1)}, u32[]{:S(2)}, u32[]{:S(2)}) collective-permute-start(f32[8,8,128]{2,1,0:T(8,128)S(1)} %gather_fusion), channel_id=1, source_target_pairs={{0,1},{1,0},{2,3},{3,2},{4,5},{5,4},{6,7},{7,6},{8,9},{9,8},{10,11... | collective-permute-start | bytes 98312 | tf_op jit(solution)/shard_map/ppermute | solution.py:400
  22.1 15.6 %collective-permute-start.1 = (f32[8,8,128]{2,1,0:T(8,128)S(1)}, f32[8,8,128]{2,1,0:T(8,128)S(1)}, u32[]{:S(2)}, u32[]{:S(2)}) collective-permute-start(f32[8,8,128]{2,1,0:T(8,128)S(1)} %gather_fusion), channel_id=1, source_target_pairs={{0,24},{8,16},{16,8},{24,0},{1,25},{9,17},{17,9},{25,1},{2,26},{10... | collective-permute-start | bytes 98312 | tf_op jit(solution)/shard_map/ppermute | solution.py:400
  22.1 15.6 %collective-permute-start = (f32[8,8,128]{2,1,0:T(8,128)S(1)}, f32[8,8,128]{2,1,0:T(8,128)S(1)}, u32[]{:S(2)}, u32[]{:S(2)}) collective-permute-start(f32[8,8,128]{2,1,0:T(8,128)S(1)} %gather_fusion), channel_id=1, source_target_pairs={{0,8},{8,0},{16,24},{24,16},{1,9},{9,1},{17,25},{25,17},{2,10},{10... | collective-permute-start | bytes 98312 | tf_op jit(solution)/shard_map/ppermute | solution.py:400
  22.7 14.9 %collective-permute-start.3 = (f32[8,8,128]{2,1,0:T(8,128)S(1)}, f32[8,8,128]{2,1,0:T(8,128)S(1)}, u32[]{:S(2)}, u32[]{:S(2)}) collective-permute-start(f32[8,8,128]{2,1,0:T(8,128)S(1)} %gather_fusion), channel_id=1, source_target_pairs={{0,7},{1,2},{2,1},{3,4},{4,3},{5,6},{6,5},{7,0},{8,15},{9,10},{10,... | collective-permute-start | bytes 98312 | tf_op jit(solution)/shard_map/ppermute | solution.py:400
  65.3 11.4 %all-to-all-start.1 = ((f32[64,4,128]{2,1,0:T(4,128)}), f32[64,4,128]{2,1,0:T(4,128)S(1)}, u32[]{:S(2)}, u32[]{:S(2)}) async-start(f32[64,4,128]{2,1,0:T(4,128)} %contact.2), calls=%async_computation.1 | async-start | bytes 262144 | tf_op jit(solution)/shard_map/all_to_all | solution.py:449
  79.7 5.7 %collective-permute-start.4 = (f32[8,128]{1,0:T(8,128)}, f32[8,128]{1,0:T(8,128)S(1)}, u32[]{:S(2)}, u32[]{:S(2)}) collective-permute-start(f32[8,128]{1,0:T(8,128)} %get-tuple-element.18), channel_id=1, source_target_pairs={{0,8},{8,0},{16,24},{24,16},{1,9},{9,1},{17,25},{25,17},{2,10},{10... | collective-permute-start | bytes 12296 | tf_op jit(solution)/shard_map/ppermute | solution.py:400
  79.8 5.5 %collective-permute-start.5 = (f32[8,128]{1,0:T(8,128)}, f32[8,128]{1,0:T(8,128)S(1)}, u32[]{:S(2)}, u32[]{:S(2)}) collective-permute-start(f32[8,128]{1,0:T(8,128)} %get-tuple-element.19), channel_id=1, source_target_pairs={{0,24},{8,16},{16,8},{24,0},{1,25},{9,17},{17,9},{25,1},{2,26},{10... | collective-permute-start | bytes 12296 | tf_op jit(solution)/shard_map/ppermute | solution.py:400
  80.7 4.6 %collective-permute-start.6 = (f32[8,128]{1,0:T(8,128)}, f32[8,128]{1,0:T(8,128)S(1)}, u32[]{:S(2)}, u32[]{:S(2)}) collective-permute-start(f32[8,128]{1,0:T(8,128)} %get-tuple-element.20), channel_id=1, source_target_pairs={{0,1},{1,0},{2,3},{3,2},{4,5},{5,4},{6,7},{7,6},{8,9},{9,8},{10,11... | collective-permute-start | bytes 12296 | tf_op jit(solution)/shard_map/ppermute | solution.py:400
  81.6 6.5 %collective-permute-start.7 = (f32[8,128]{1,0:T(8,128)}, f32[8,128]{1,0:T(8,128)S(1)}, u32[]{:S(2)}, u32[]{:S(2)}) collective-permute-start(f32[8,128]{1,0:T(8,128)} %get-tuple-element.21), channel_id=1, source_target_pairs={{0,7},{1,2},{2,1},{3,4},{4,3},{5,6},{6,5},{7,0},{8,15},{9,10},{10,... | collective-permute-start | bytes 12296 | tf_op jit(solution)/shard_map/ppermute | solution.py:400
  101.9 9.1 %copy-start.1 = (f32[64,4,128]{2,1,0:T(4,128)}, f32[64,4,128]{2,1,0:T(4,128)S(1)}, u32[]{:S(2)}) copy-start(f32[64,4,128]{2,1,0:T(4,128)S(1)} %all_to_all.20.refs_4_) | copy-start | bytes 393220
  102.5 4.2 %collective-permute-start.10 = (f32[8,4,128]{2,1,0:T(4,128)S(1)}, f32[8,4,128]{2,1,0:T(4,128)S(1)}, u32[]{:S(2)}, u32[]{:S(2)}) collective-permute-start(f32[8,4,128]{2,1,0:T(4,128)S(1)} %gather_fusion.1), channel_id=1, source_target_pairs={{0,1},{1,0},{2,3},{3,2},{4,5},{5,4},{6,7},{7,6},{8,9},{9,8},{10,11... | collective-permute-start | bytes 49160 | tf_op jit(solution)/shard_map/ppermute | solution.py:400
  103.7 3.3 %collective-permute-start.9 = (f32[8,4,128]{2,1,0:T(4,128)S(1)}, f32[8,4,128]{2,1,0:T(4,128)S(1)}, u32[]{:S(2)}, u32[]{:S(2)}) collective-permute-start(f32[8,4,128]{2,1,0:T(4,128)S(1)} %gather_fusion.1), channel_id=1, source_target_pairs={{0,24},{8,16},{16,8},{24,0},{1,25},{9,17},{17,9},{25,1},{2,26},{10... | collective-permute-start | bytes 49160 | tf_op jit(solution)/shard_map/ppermute | solution.py:400
  103.7 3.3 %collective-permute-start.8 = (f32[8,4,128]{2,1,0:T(4,128)S(1)}, f32[8,4,128]{2,1,0:T(4,128)S(1)}, u32[]{:S(2)}, u32[]{:S(2)}) collective-permute-start(f32[8,4,128]{2,1,0:T(4,128)S(1)} %gather_fusion.1), channel_id=1, source_target_pairs={{0,8},{8,0},{16,24},{24,16},{1,9},{9,1},{17,25},{25,17},{2,10},{10... | collective-permute-start | bytes 49160 | tf_op jit(solution)/shard_map/ppermute | solution.py:400
  104.5 6.4 %collective-permute-start.11 = (f32[8,4,128]{2,1,0:T(4,128)S(1)}, f32[8,4,128]{2,1,0:T(4,128)S(1)}, u32[]{:S(2)}, u32[]{:S(2)}) collective-permute-start(f32[8,4,128]{2,1,0:T(4,128)S(1)} %gather_fusion.1), channel_id=1, source_target_pairs={{0,7},{1,2},{2,1},{3,4},{4,3},{5,6},{6,5},{7,0},{8,15},{9,10},{10,... | collective-permute-start | bytes 49160 | tf_op jit(solution)/shard_map/ppermute | solution.py:400
  106.7 4.3 %copy-start.8 = (f32[8,4,128]{2,1,0:T(4,128)}, f32[8,4,128]{2,1,0:T(4,128)S(1)}, u32[]{:S(2)}) copy-start(f32[8,4,128]{2,1,0:T(4,128)S(1)} %collective-permute-done.10.refs_11_) | copy-start | bytes 49156
  107.0 4.0 %copy-start.9 = (f32[8,4,128]{2,1,0:T(4,128)}, f32[8,4,128]{2,1,0:T(4,128)S(1)}, u32[]{:S(2)}) copy-start(f32[8,4,128]{2,1,0:T(4,128)S(1)} %collective-permute-done.9.refs_10_) | copy-start | bytes 49156
  138.1 13.8 %all-to-all-start.3 = ((f32[64,4,128]{2,1,0:T(4,128)}), f32[64,4,128]{2,1,0:T(4,128)S(1)}, u32[]{:S(2)}, u32[]{:S(2)}) async-start(f32[64,4,128]{2,1,0:T(4,128)} %contact.3), calls=%async_computation.3 | async-start | bytes 262144 | tf_op jit(solution)/shard_map/all_to_all | solution.py:449
  154.9 6.7 %collective-permute-start.12 = (f32[8,128]{1,0:T(8,128)}, f32[8,128]{1,0:T(8,128)S(1)}, u32[]{:S(2)}, u32[]{:S(2)}) collective-permute-start(f32[8,128]{1,0:T(8,128)} %get-tuple-element.25), channel_id=1, source_target_pairs={{0,8},{8,0},{16,24},{24,16},{1,9},{9,1},{17,25},{25,17},{2,10},{10... | collective-permute-start | bytes 12296 | tf_op jit(solution)/shard_map/ppermute | solution.py:400
  155.2 6.4 %collective-permute-start.13 = (f32[8,128]{1,0:T(8,128)}, f32[8,128]{1,0:T(8,128)S(1)}, u32[]{:S(2)}, u32[]{:S(2)}) collective-permute-start(f32[8,128]{1,0:T(8,128)} %get-tuple-element.26), channel_id=1, source_target_pairs={{0,24},{8,16},{16,8},{24,0},{1,25},{9,17},{17,9},{25,1},{2,26},{10... | collective-permute-start | bytes 12296 | tf_op jit(solution)/shard_map/ppermute | solution.py:400
  156.8 4.8 %collective-permute-start.14 = (f32[8,128]{1,0:T(8,128)}, f32[8,128]{1,0:T(8,128)S(1)}, u32[]{:S(2)}, u32[]{:S(2)}) collective-permute-start(f32[8,128]{1,0:T(8,128)} %get-tuple-element.27), channel_id=1, source_target_pairs={{0,1},{1,0},{2,3},{3,2},{4,5},{5,4},{6,7},{7,6},{8,9},{9,8},{10,11... | collective-permute-start | bytes 12296 | tf_op jit(solution)/shard_map/ppermute | solution.py:400
  158.3 6.5 %collective-permute-start.15 = (f32[8,128]{1,0:T(8,128)}, f32[8,128]{1,0:T(8,128)S(1)}, u32[]{:S(2)}, u32[]{:S(2)}) collective-permute-start(f32[8,128]{1,0:T(8,128)} %get-tuple-element.28), channel_id=1, source_target_pairs={{0,7},{1,2},{2,1},{3,4},{4,3},{5,6},{6,5},{7,0},{8,15},{9,10},{10,... | collective-permute-start | bytes 12296 | tf_op jit(solution)/shard_map/ppermute | solution.py:400
  (16 other events, 27.6 us)

commit v2 on v1

--- a/solution.py
+++ b/solution.py
@@ -11,6 +11,7 @@
 ROWS = 8
 HALF = 4
 EBLK = 8
+GROUP = 16
 
 TIME_STEP = 0.5
 PENALTY = 32.0
@@ -81,7 +82,10 @@
 def element_kernel(disp_ref, conn_ref, stiff_ref, yield_ref, out_ref):
     row = lax.broadcasted_iota(jnp.int32, (ROWS, BLK), 0)
     row48 = lax.broadcasted_iota(jnp.int32, (48, BLK), 0)
-    node = lax.broadcasted_iota(jnp.int32, (BLK, BLK), 0)
+    node = lax.broadcasted_iota(jnp.int32, (BLK, BLK), 0).astype(jnp.int16)
+    unit = jnp.ones((), BF16)
+    zero = jnp.zeros((), BF16)
+    row48 = row48.astype(jnp.int16) & 3
     for k in range(out_ref.shape[0]):
         lanes = slice(k * BLK, (k + 1) * BLK)
         local = conn_ref[:, lanes] & (BLK - 1)
@@ -106,11 +110,12 @@
         factor = lax.rsqrt(1.0 + squared / (level * level))
         forces = jnp.concatenate([t * factor for t in trial], axis=0)
         high, low = split(forces)
-        stacked = jnp.concatenate([high, low], axis=0)
+        stacked = jnp.concatenate([high, low], axis=0).astype(BF16)
+        small = local.astype(jnp.int16)
         total = jnp.zeros((48, BLK), F32)
         for a in range(4):
-            corner = jnp.where((row48 & 3) == a, stacked, 0.0).astype(BF16)
-            picker = jnp.where(node == local[a : a + 1, :], 1.0, 0.0).astype(BF16)
+            corner = jnp.where(row48 == a, stacked, zero)
+            picker = jnp.where(node == small[a : a + 1, :], unit, zero)
             total = total + lax.dot_general(
                 corner, picker, (((1,), (1,)), ((), ())), preferred_element_type=F32
             )
@@ -124,19 +129,21 @@
         out_ref[k] = jnp.concatenate(pieces + [jnp.zeros((2, BLK), F32)], axis=0)
 
 
-def element_forces(displacement, connectivity, stiffness, yield_force):
+def element_forces(displacement, connectivity, stiffness, yield_force, part=0, parts=1):
     nodes = displacement.shape[1]
-    blocks = nodes // BLK
+    blocks = nodes // BLK // parts
     wide = EBLK * BLK
+    steps = blocks // EBLK
+    first = part * steps
     return pl.pallas_call(
         element_kernel,
         out_shape=jax.ShapeDtypeStruct((blocks, ROWS, BLK), F32),
-        grid=(blocks // EBLK,),
+        grid=(steps,),
         in_specs=[
-            pl.BlockSpec((6, wide), lambda i: (0, i)),
-            pl.BlockSpec((4, wide), lambda i: (0, i)),
-            pl.BlockSpec((24, 24, wide), lambda i: (0, 0, i)),
-            pl.BlockSpec((1, EBLK, BLK), lambda i: (i, 0, 0)),
+            pl.BlockSpec((6, wide), lambda i: (0, i + first)),
+            pl.BlockSpec((4, wide), lambda i: (0, i + first)),
+            pl.BlockSpec((24, 24, wide), lambda i: (0, 0, i + first)),
+            pl.BlockSpec((1, EBLK, BLK), lambda i: (i + first, 0, 0)),
         ],
         out_specs=pl.BlockSpec((EBLK, ROWS, BLK), lambda i: (i, 0, 0)),
         cost_estimate=pl.CostEstimate(
@@ -146,90 +153,177 @@
     )(displacement, connectivity, stiffness, yield_force.reshape(-1, EBLK, BLK))
 
 
-def contact_kernel(
-    count_ref, pairs_ref, valid_ref, *refs, places, edges, fresh
+def plan_kernel(count_ref, pairs_ref, even_ref, plan_ref, *, places, edges):
+    for row, value in enumerate((0, 0, 0, 0, 0, places)):
+        plan_ref[row, 0] = value
+
+    def sort(t, numbers):
+        own, far = numbers
+        slave = pairs_ref[0, t]
+        master = pairs_ref[1, t]
+        is_own = master < places
+        entry = jnp.maximum(master - places, 0)
+        side = entry // edges
+        flip = jnp.where(side < 2, even_ref[0], even_ref[1])
+        moved = places + (side ^ flip) * edges + entry % edges
+
+        @pl.when(is_own)
+        def _():
+            plan_ref[0, own] = t
+            plan_ref[1, own] = slave
+            plan_ref[2, own] = master
+
+        @pl.when(jnp.logical_not(is_own))
+        def _():
+            plan_ref[3, far] = t
+            plan_ref[4, far] = slave
+            plan_ref[5, far] = moved
+
+        return own + is_own.astype(jnp.int32), far + 1 - is_own.astype(jnp.int32)
+
+    own, far = lax.fori_loop(0, count_ref[0], sort, (jnp.int32(0), jnp.int32(0)))
+    plan_ref[6, 0] = own
+    plan_ref[7, 0] = far
+
+
+def plan_tiles(tile_count, tile_pairs, even, places, edges):
+    def kernel(*refs):
+        plan_kernel(*refs, places=places, edges=edges)
+
+    return pl.pallas_call(
+        kernel,
+        out_shape=jax.ShapeDtypeStruct((8, tile_pairs.shape[1]), jnp.int32),
+        in_specs=[sspec()] * 3,
+        out_specs=sspec(),
+        name="plan",
+    )(tile_count, tile_pairs, even)
+
+
+def master_entry(where, position, normal, master_tab, force_tab):
+    zero1 = jnp.zeros((1, BLK), F32)
+    zero2 = jnp.zeros((2, BLK), F32)
+    n_high, n_low = split(normal)
+    product = position * normal
+    offset = THICKNESS + (product[0:1] + product[1:2] + product[2:3])
+    o_high, o_rest = split(offset)
+    o_mid, o_low = split(o_rest)
+    negative = jnp.concatenate([-n_high, -n_low], axis=0)
+    master_tab[where] = jnp.concatenate(
+        [negative, negative, o_high, o_mid, o_low, zero1], axis=0
+    ).astype(BF16)
+    lines = [n_high, n_low, zero2]
+    force_tab[where] = jnp.concatenate(lines + lines, axis=0).astype(BF16)
+
+
+def run_tiles(
+    plan_ref, row, number, base, start_ref, length_ref, slave_tab, master_tab, force_tab,
+    total_ref, depth_ref,
 ):
-    if fresh:
-        recv_ref = refs[0]
-        edge_refs = refs[1:5]
-        rest = refs[5:]
-    else:
-        recv_ref, pos_ref = refs[0:2]
-        edge_refs = refs[2:6]
-        edge_pos_refs = refs[6:10]
-        rest = refs[10:]
-    start_ref, length_ref, out_ref, slave_tab, master_tab, force_tab, total_ref = rest
+    facet = lax.broadcasted_iota(jnp.int32, (BLK, 2 * BLK), 0).astype(jnp.int16)
+    upper = lax.broadcasted_iota(jnp.int32, (16, BLK), 0) < 8
+    blank = jnp.zeros((16, BLK), BF16)
+    small = jnp.int16
+    last = jnp.maximum(number - 1, 0)
+
+    def at(group, d):
+        i = group * GROUP + d
+        return jnp.clip(i, 0, last), jnp.logical_and(i >= 0, i < number)
+
+    def body(r, carry):
+        forces = []
+        for d in range(0, GROUP, 2):
+            starts, lengths, rows = [], [], []
+            for e in range(2):
+                i, live = at(r - 1, d + e)
+                t = plan_ref[row, i]
+                starts.append(start_ref[pl.ds(t, 1), :])
+                lengths.append(jnp.where(live, length_ref[pl.ds(t, 1), :], 0))
+                rows.append(force_tab[plan_ref[row + 2, i] - base])
+            start = jnp.concatenate(starts, axis=1).astype(small)
+            length = jnp.concatenate(lengths, axis=1).astype(small)
+            inside = ((facet - start) & (BLK - 1)) < length
+            pressure = jnp.maximum(depth_ref[d // 2], 0.0)
+            high = pressure.astype(BF16)
+            low = (pressure - high.astype(F32)).astype(BF16)
+            high = jnp.where(inside, high, jnp.zeros((), BF16))
+            low = jnp.where(inside, low, jnp.zeros((), BF16))
+            both = jnp.where(upper, rows[0], rows[1])
+            forces.append(
+                jnp.dot(
+                    jnp.concatenate([both, both], axis=1),
+                    jnp.concatenate([high, low], axis=0),
+                    preferred_element_type=F32,
+                )
+            )
+        for d in range(0, GROUP, 2):
+            facets, nodes = [], []
+            for e in range(2):
+                i, _ = at(r, d + e)
+                facets.append(master_tab[plan_ref[row + 2, i] - base])
+                nodes.append(slave_tab[plan_ref[row + 1, i]])
+            left = jnp.concatenate([nodes[0], blank], axis=0)
+            right = jnp.concatenate([blank, nodes[1]], axis=0)
+            depth_ref[d // 2] = lax.dot_general(
+                jnp.concatenate(facets, axis=0),
+                jnp.concatenate([left, right], axis=1),
+                (((0,), (0,)), ((), ())),
+                preferred_element_type=F32,
+            )
+        for d in range(GROUP):
+            i, _ = at(r - 1, d)
+            e = d % 2
+            slave = plan_ref[row + 1, i]
+            part = forces[d // 2][8 * e : 8 * e + 8, e * BLK : (e + 1) * BLK]
+            total_ref[slave] = total_ref[slave] + part
+        return carry
+
+    lax.fori_loop(0, (number + GROUP - 1) // GROUP + 1, body, 0)
+
+
+def own_kernel(plan_ref, recv_ref, *refs, fresh):
+    pos_ref = recv_ref if fresh else refs[0]
+    refs = refs if fresh else refs[1:]
+    start_ref, length_ref, total_ref, slave_tab, master_tab, force_tab, depth_ref = refs
+    ones = jnp.ones((3, BLK), F32)
     zero1 = jnp.zeros((1, BLK), F32)
-    ones = jnp.ones((3, BLK), F32)
-    zero10 = jnp.zeros((10, BLK), F32)
-
-    def master_entry(where, position, normal):
-        n_high, n_low = split(normal)
-        product = position * normal
-        offset = THICKNESS + (product[0:1] + product[1:2] + product[2:3])
-        o_high, o_rest = split(offset)
-        o_mid, o_low = split(o_rest)
-        negative = jnp.concatenate([-n_high, -n_low], axis=0)
-        master_tab[where] = jnp.concatenate(
-            [negative, negative, o_high, o_mid, o_low, zero1], axis=0
-        ).astype(BF16)
-        force_tab[where] = jnp.concatenate([n_high, n_low, zero10], axis=0).astype(BF16)
-
-    def own_entry(p, carry):
-        tile = recv_ref[p]
-        position = tile[0:3] if fresh else pos_ref[p][0:3]
+    places = recv_ref.shape[0]
+
+    def entry(p, carry):
+        position = pos_ref[p][0:3]
         p_high, p_low = split(position)
         slave_tab[p] = jnp.concatenate(
             [p_high, p_high, p_low, p_low, ones, zero1], axis=0
         ).astype(BF16)
-        master_entry(p, position, tile[3:6])
-        total_ref[p] = jnp.zeros((16, BLK), F32)
+        master_entry(p, position, recv_ref[p][3:6], master_tab, force_tab)
+        total_ref[p] = jnp.zeros((ROWS, BLK), F32)
         return carry
 
-    lax.fori_loop(0, places, own_entry, 0, unroll=4)
+    lax.fori_loop(0, places, entry, 0, unroll=8)
+    run_tiles(
+        plan_ref, 0, plan_ref[6, 0], 0, start_ref, length_ref, slave_tab, master_tab, force_tab,
+        total_ref, depth_ref,
+    )
+
+
+def far_kernel(plan_ref, valid_ref, *refs, edges, fresh):
+    edge_refs = refs[0:4]
+    pos_refs = edge_refs if fresh else refs[4:8]
+    refs = refs[4:] if fresh else refs[8:]
+    start_ref, length_ref, own_ref, slave_tab, out_ref = refs[0:5]
+    master_tab, force_tab, total_ref, depth_ref = refs[5:9]
+    places = own_ref.shape[0]
+    zero1 = jnp.zeros((1, BLK), F32)
+    total_ref[...] = own_ref[...]
     for side in range(4):
         valid = valid_ref[side] > 0
         for e in range(edges):
-            tile = jnp.where(valid, edge_refs[side][e], 0.0)
-            if fresh:
-                position = tile[0:3]
-            else:
-                position = jnp.where(valid, edge_pos_refs[side][e], 0.0)[0:3]
-            master_entry(places + side * edges + e, position, tile[3:6])
-
-    facet = lax.broadcasted_iota(jnp.int32, (BLK, BLK), 0)
-    count = count_ref[0]
-
-    def one_tile(t, live):
-        slave = pairs_ref[0, t]
-        master = pairs_ref[1, t]
-        depth = lax.dot_general(
-            master_tab[master],
-            slave_tab[slave],
-            (((0,), (0,)), ((), ())),
-            preferred_element_type=F32,
-        )
-        start = start_ref[pl.ds(t, 1), :]
-        length = jnp.where(live, length_ref[pl.ds(t, 1), :], 0)
-        inside = ((facet - start) & (BLK - 1)) < length
-        pressure = jnp.where(inside, jnp.maximum(depth, 0.0), 0.0)
-        high = pressure.astype(BF16)
-        low = (pressure - high.astype(F32)).astype(BF16)
-        rows = force_tab[master]
-        force = jnp.dot(rows, high, preferred_element_type=F32) + jnp.dot(
-            rows, low, preferred_element_type=F32
-        )
-        total_ref[slave] = total_ref[slave] + force
-
-    unroll = 4
-
-    def body(r, carry):
-        for d in range(unroll):
-            t = r * unroll + d
-            one_tile(t, t < count)
-        return carry
-
-    lax.fori_loop(0, (count + unroll - 1) // unroll, body, 0)
+            normal = jnp.where(valid, edge_refs[side][e], 0.0)[3:6]
+            position = jnp.where(valid, pos_refs[side][e], 0.0)[0:3]
+            master_entry(side * edges + e, position, normal, master_tab, force_tab)
+    run_tiles(
+        plan_ref, 3, plan_ref[7, 0], places, start_ref, length_ref, slave_tab, master_tab,
+        force_tab, total_ref, depth_ref,
+    )
 
     def finish(p, carry):
         tile = total_ref[p]
@@ -239,35 +333,62 @@
     lax.fori_loop(0, places, finish, 0, unroll=8)
 
 
-def contact(count, pairs, valid, received, positions, edges, edge_positions, start, length):
+def tile_cost(tiles):
+    return pl.CostEstimate(
+        flops=tiles * BLK * BLK * 64, transcendentals=0, bytes_accessed=tiles * BLK * 8
+    )
+
+
+def own_contact(plan, received, positions, start, length):
     places = received.shape[0]
+    fresh = positions is None
+    arrays = [received] + ([] if fresh else [positions]) + [start, length]
+
+    def kernel(*refs):
+        own_kernel(*refs, fresh=fresh)
+
+    return pl.pallas_call(
+        kernel,
+        out_shape=[
+            jax.ShapeDtypeStruct((places, ROWS, BLK), F32),
+            jax.ShapeDtypeStruct((places, 16, BLK), BF16),
+        ],
+        in_specs=[sspec()] + [vspec()] * len(arrays),
+        out_specs=[vspec()] * 2,
+        scratch_shapes=[
+            VMEM((places, 16, BLK), BF16),
+            VMEM((places, 16, BLK), BF16),
+            VMEM((GROUP // 2, BLK, 2 * BLK), F32),
+        ],
+        cost_estimate=tile_cost(start.shape[0] // 2),
+        name="own_contact",
+    )(plan, *arrays)
+
+
+def far_contact(plan, valid, edges, edge_positions, start, length, total, slave_tab):
+    places = total.shape[0]
+    fresh = edge_positions is None
     edge_count = edges[0].shape[0]
-    extended = places + 4 * edge_count
-    fresh = positions is None
-    arrays = [received] + ([] if fresh else [positions]) + list(edges)
-    arrays += [] if fresh else list(edge_positions)
-    arrays += [start, length]
-    tiles = start.shape[0]
+    arrays = list(edges) + ([] if fresh else list(edge_positions))
+    arrays += [start, length, total, slave_tab]
 
     def kernel(*refs):
-        contact_kernel(*refs, places=places, edges=edge_count, fresh=fresh)
+        far_kernel(*refs, edges=edge_count, fresh=fresh)
 
     return pl.pallas_call(
         kernel,
         out_shape=jax.ShapeDtypeStruct((places, HALF, BLK), F32),
-        in_specs=[sspec()] * 3 + [vspec()] * len(arrays),
+        in_specs=[sspec()] * 2 + [vspec()] * len(arrays),
         out_specs=vspec(),
         scratch_shapes=[
-            VMEM((places, 16, BLK), BF16),
-            VMEM((extended, 16, BLK), BF16),
-            VMEM((extended, 16, BLK), BF16),
-            VMEM((places, 16, BLK), F32),
+            VMEM((4 * edge_count, 16, BLK), BF16),
+            VMEM((4 * edge_count, 16, BLK), BF16),
+            VMEM((places, ROWS, BLK), F32),
+            VMEM((GROUP // 2, BLK, 2 * BLK), F32),
         ],
-        cost_estimate=pl.CostEstimate(
-            flops=tiles * BLK * BLK * 64, transcendentals=0, bytes_accessed=tiles * BLK * 8
-        ),
-        name="contact",
-    )(count, pairs, valid, *arrays)
+        cost_estimate=tile_cost(start.shape[0] // 2),
+        name="far_contact",
+    )(plan, valid, *arrays)
 
 
 def inverse_kernel(valid_ref, list_ref, out_ref):
@@ -300,7 +421,8 @@
     )(valid, lists)
 
 
-def force_kernel(slot_ref, back_ref, internal_ref, list_ref, force_ref, *side_refs):
+def force_kernel(slot_ref, back_ref, first_ref, second_ref, list_ref, force_ref, *side_refs):
+    half = first_ref.shape[0]
     blocks = slot_ref.shape[0]
     pad = jnp.zeros((ROWS - HALF, BLK), F32)
     lanes = []
@@ -311,7 +433,8 @@
         owners.append(nodes // BLK)
     sums = [jnp.zeros((ROWS, BLK), F32) for _ in range(4)]
     for k in range(blocks):
-        tile = jnp.concatenate([back_ref[slot_ref[k]], pad], axis=0) - internal_ref[k]
+        internal = first_ref[k] if k < half else second_ref[k - half]
+        tile = jnp.concatenate([back_ref[slot_ref[k]], pad], axis=0) - internal
         force_ref[k] = tile
         for side in range(4):
             sums[side] = jnp.where(
@@ -322,15 +445,15 @@
 
 
 def nodal_force(block_slot, returned, internal, lists):
-    blocks = internal.shape[0]
+    blocks = 2 * internal[0].shape[0]
     return pl.pallas_call(
         force_kernel,
         out_shape=[jax.ShapeDtypeStruct((blocks, ROWS, BLK), F32)]
         + [jax.ShapeDtypeStruct((ROWS, BLK), F32)] * 4,
-        in_specs=[sspec(), vspec(), vspec(), vspec()],
+        in_specs=[sspec()] + [vspec()] * 4,
         out_specs=[vspec()] * 5,
         name="force",
-    )(block_slot, returned, internal, lists)
+    )(block_slot, returned, *internal, lists)
 
 
 def update_kernel(
@@ -425,47 +548,48 @@
     blocks = displacement.shape[1] // BLK
     edge_count = edge_slots.shape[0]
     at = [lax.axis_index(axis) for axis in AXES]
-    even = [1 - i % 2 for i in at]
+    even = jnp.stack([1 - i % 2 for i in at]).astype(jnp.int32)
     valid = []
     for i, size in zip(at, sizes):
         valid += [jnp.int32(1), jnp.where((i == 0) | (i == size - 1), 0, 1).astype(jnp.int32)]
     valid = jnp.stack(valid)
+    plan = plan_tiles(tile_count, tile_pairs, even, places, edge_count)
     lists = []
     for axis in range(2):
         low, high = shared_nodes[2 * axis], shared_nodes[2 * axis + 1]
         is_even = even[axis] == 1
         lists += [jnp.where(is_even, high, low), jnp.where(is_even, low, high)]
     lists = jnp.stack(lists)
-    far = tile_pairs[1] - places
-    side = far // edge_count
-    flip = jnp.where(side < 2, even[0], even[1])
-    masters = jnp.where(
-        far < 0, tile_pairs[1], places + (side ^ flip) * edge_count + far % edge_count
-    )
-    pairs = jnp.stack([tile_pairs[0], masters])
     code = inverse(valid, lists, blocks)
 
     def exchange(blocks_out):
         return lax.all_to_all(blocks_out, AXES, split_axis=0, concat_axis=0, tiled=True)
+
+    def half(disp, part):
+        return element_forces(disp, connectivity, stiffness, yield_force, part, 2)
 
     outgoing = prep(block_slot, displacement, ref_pos, normals, places)
     first = None
     for step in range(STEPS):
+        fresh = step == 0
         received = exchange(outgoing)
-        internal = element_forces(displacement, connectivity, stiffness, yield_force)
-        rows = received[edge_slots]
-        near = swap([rows] * 4, sizes)
-        if step == 0:
+        internal0 = half(displacement, 0)
+        received, internal0, plan, code = lax.optimization_barrier(
+            (received, internal0, plan, code)
+        )
+        near = swap([received[edge_slots]] * 4, sizes)
+        if fresh:
             first = (received, near)
-            box_force = contact(
-                tile_count, pairs, valid, received, None, near, None, win_start, win_len
-            )
-        else:
-            box_force = contact(
-                tile_count, pairs, valid, first[0], received, first[1], near, win_start, win_len
-            )
+        total, slave_tab = own_contact(
+            plan, first[0], None if fresh else received, win_start, win_len
+        )
+        box_force = far_contact(
+            plan, valid, first[1], None if fresh else near, win_start, win_len, total, slave_tab
+        )
+        box_force, later = lax.optimization_barrier((box_force, displacement))
         returned = exchange(box_force)
-        force, *sides = nodal_force(block_slot, returned, internal, lists)
+        internal1 = half(later, 1)
+        force, *sides = nodal_force(block_slot, returned, (internal0, internal1), lists)
         incoming = swap(sides, sizes)
         last = step == STEPS - 1
         out = update(

time: 169 us -> 121 us (0.72)
  Pallas kernels: 88.5 us -> 61.8 us
  waiting for transfers between devices: 25.8 us -> 11.1 us
  blocking collectives: 10.5 us -> 0 us
  starting transfers between devices: 32.9 us -> 38.5 us
    pallas_call x2 -> x5, Pallas kernels: 52.9 us -> 23.1 us  [the longest x2 9.82 us: own_contact(): pl.pallas_call(kernel, out_shape=[jax.ShapeDtypeStruct((places, ROWS, BLK...]
    all_to_all x3 -> x4, waiting for transfers between devices: 15.5 us -> 4.48 us  [exchange(): lax.all_to_all(blocks_out, AXES, split_axis=0, concat_axis=0, tiled=True)]
    all_to_all x1 -> x0, blocking collectives: 10.5 us -> none  [exchange(): lax.all_to_all(blocks_out, AXES, split_axis=0, concat_axis=0, tiled=True)]
    ppermute x16, waiting for transfers between devices: 10.3 us -> 6.58 us  [swap(): out.append(lax.ppermute(values[2 * at + stage], axis, pairs))]
    ppermute x16, starting transfers between devices: 19.4 us -> 22.4 us  [swap(): out.append(lax.ppermute(values[2 * at + stage], axis, pairs))]
    pallas_call x2 -> x4, Pallas kernels: 22.3 us -> 25.2 us  [element_forces(): pl.pallas_call(element_kernel, out_shape=jax.ShapeDtypeStruct((blocks, RO...]
    all_to_all x3 -> x4, starting transfers between devices: 13.5 us -> 16.1 us  [exchange(): lax.all_to_all(blocks_out, AXES, split_axis=0, concat_axis=0, tiled=True)]
  transfers between devices with their start and end apart: 19 -> 20, of which waited for: 6 -> 5; matrix products, arithmetic and copies ran while one was open for 2% -> 2% of each run, Pallas kernels for 14% -> 33%
where the time goes in v2:
time: 121 us; the launch traced here: 120 us
  Pallas kernels  61.8 us (51%)
  starting transfers between devices  38.5 us (32%)
  waiting for transfers between devices  11.1 us (9%)
  local copies, waits for them, and re-layouts  4.83 us (4%)
  other arithmetic  2.69 us (2%)
  between operations  1.58 us (1%)
    pallas_call x4, Pallas kernels, element_forces(): pl.pallas_call(element_kernel, out_shape=jax.ShapeDtypeStruct((blocks, RO...  25.2 us
    ppermute x16, starting transfers between devices, swap(): out.append(lax.ppermute(values[2 * at + stage], axis, pairs))  22.4 us
    all_to_all x4, starting transfers between devices, exchange(): lax.all_to_all(blocks_out, AXES, split_axis=0, concat_axis=0, tiled=True)  16.1 us
    pallas_call x2, Pallas kernels, own_contact(): pl.pallas_call(kernel, out_shape=[jax.ShapeDtypeStruct((places, ROWS, BLK...  9.82 us
    pallas_call x2, Pallas kernels, far_contact(): pl.pallas_call(kernel, out_shape=jax.ShapeDtypeStruct((places, HALF, BLK)...  9.58 us
    ppermute x16, waiting for transfers between devices, swap(): out.append(lax.ppermute(values[2 * at + stage], axis, pairs))  6.58 us
    pallas_call x2, Pallas kernels, update(): pl.pallas_call(update_kernel, out_shape=out, in_specs=[sspec()] + [vspec(...  5.3 us
    pallas_call x2, Pallas kernels, nodal_force(): pl.pallas_call(force_kernel, out_shape=[jax.ShapeDtypeStruct((blocks, ROW...  4.84 us
  transfers between devices with their start and end apart: 20, of which 5 were waited for; matrix products, arithmetic and copies ran while one was open for 2% of the time, Pallas kernels for 33%

profile of v2, /device:TPU:0, one launch (start us, length us, event | category | flops | bytes accessed | tf_op | source)
XLA Modules:
  0.0 120.5 jit_solution(9413833309499598458)
XLA Ops:
  0.6 1.8 %prep.1 = f32[64,8,128]{2,1,0:T(8,128)} custom-call(s32[64]{0:T(128)} %slot_ref.9, f32[6,8192]{1,0:T(8,128)} %disp_ref.6, f32[3,8192]{1,0:T(4,128)} %pos_ref.5, f32[3,8192]{1,0:T(4,128)} %nrm_ref.1), custom_call_target="tpu_custom_call" | custom-call | tf_op jit(solution)/shard_map/prep/pallas_call | solution.py:57
  2.5 7.3 %all-to-all-start = ((f32[64,8,128]{2,1,0:T(8,128)}), f32[64,8,128]{2,1,0:T(8,128)S(1)}, u32[]{:S(2)}, u32[]{:S(2)}) async-start(f32[64,8,128]{2,1,0:T(8,128)} %prep.1), calls=%async_computation | async-start | bytes 524288 | tf_op jit(solution)/shard_map/all_to_all | solution.py:566
  14.7 3.7 %plan.1.refs_0_ = s32[8,128]{1,0:T(8,128)} custom-call(s32[1]{0:T(128)S(6)} %copy.17.refs_0_, s32[2,128]{1,0:T(2,128)} %refs_1_.1, s32[2]{0:T(128)} %pad_add_fusion.1.refs_2_), custom_call_target="tpu_custom_call" | custom-call | tf_op jit(solution)/shard_map/plan/pallas_call | solution.py:193
  18.4 6.3 %element.4.first_ref = f32[32,8,128]{2,1,0:T(8,128)} custom-call(f32[6,8192]{1,0:T(8,128)} %disp_ref.6, s32[4,8192]{1,0:T(4,128)} %conn_ref.7, bf16[24,24,8192]{2,1,0:T(8,128)(2,1)} %stiff_ref.7, f32[8,8,128]{2,1,0:T(8,128)} %bitcast.5), custom_call_target="tpu_custom_call" | custom-call | flops 9437184 | bytes 9437184 | tf_op jit(solution)/shard_map/element/pallas_call | solution.py:138
  28.7 3.3 %collective-permute-start.3 = (f32[8,8,128]{2,1,0:T(8,128)S(1)}, f32[8,8,128]{2,1,0:T(8,128)S(1)}, u32[]{:S(2)}, u32[]{:S(2)}) collective-permute-start(f32[8,8,128]{2,1,0:T(8,128)S(1)} %gather_fusion), channel_id=1, source_target_pairs={{0,7},{1,2},{2,1},{3,4},{4,3},{5,6},{6,5},{7,0},{8,15},{9,10},{10,... | collective-permute-start | bytes 98312 | tf_op jit(solution)/shard_map/ppermute | solution.py:523
  32.1 4.9 %own_contact.2 = (f32[64,8,128]{2,1,0:T(8,128)}, bf16[64,16,128]{2,1,0:T(8,128)(2,1)}) custom-call(s32[8,128]{1,0:T(8,128)} %plan.1.refs_0_, f32[64,8,128]{2,1,0:T(8,128)} %copy-done, s32[128,128]{1,0:T(8,128)} %refs_10_.1, s32[128,128]{1,0:T(8,128)} %refs_11_.1), custom_call_target="tpu_custom_call" | custom-call | flops 67108864 | bytes 65536 | tf_op jit(solution)/shard_map/own_contact/pallas_call | solution.py:350
  37.6 4.8 %far_contact.2 = f32[64,4,128]{2,1,0:T(4,128)} custom-call(s32[8,128]{1,0:T(8,128)} %plan.1.refs_0_, s32[4]{0:T(128)} %pad_add_fusion.2.valid_ref.refs_1_, f32[8,8,128]{2,1,0:T(8,128)} %copy-done.4, f32[8,8,128]{2,1,0:T(8,128)} %copy-done.5, f32[8,8,128]{2,1,0:T(8,128)} %copy-done.6, f32[8,8,128]{2,1,0:T(8,128)} %copy-done.7, s32[128,128]{1,0:T(8,128)} %refs_10_.1, ...), custom_call_target="tpu_custom_call" | custom-call | flops 67108864 | bytes 65536 | tf_op jit(solution)/shard_map/far_contact/pallas_call | solution.py:378
  42.3 2.6 %all-to-all-start.1 = ((f32[64,4,128]{2,1,0:T(4,128)}), f32[64,4,128]{2,1,0:T(4,128)S(1)}, u32[]{:S(2)}, u32[]{:S(2)}) async-start(f32[64,4,128]{2,1,0:T(4,128)} %far_contact.2), calls=%async_computation.1 | async-start | bytes 262144 | tf_op jit(solution)/shard_map/all_to_all | solution.py:566
  44.9 6.3 %element.5.second_ref = f32[32,8,128]{2,1,0:T(8,128)} custom-call(f32[6,8192]{1,0:T(8,128)} %disp_ref.6, s32[4,8192]{1,0:T(4,128)} %conn_ref.7, bf16[24,24,8192]{2,1,0:T(8,128)(2,1)} %stiff_ref.7, f32[8,8,128]{2,1,0:T(8,128)} %bitcast.6), custom_call_target="tpu_custom_call" | custom-call | flops 9437184 | bytes 9437184 | tf_op jit(solution)/shard_map/element/pallas_call | solution.py:138
  53.4 2.4 %force.2 = (f32[64,8,128]{2,1,0:T(8,128)}, f32[8,128]{1,0:T(8,128)}, f32[8,128]{1,0:T(8,128)}, f32[8,128]{1,0:T(8,128)}, f32[8,128]{1,0:T(8,128)}) custom-call(s32[64]{0:T(128)} %slot_ref.9, f32[64,4,128]{2,1,0:T(4,128)} %copy-done.3, f32[32,8,128]{2,1,0:T(8,128)} %element.4.first_ref, f32[32,8,128]{2,1,0:T(8,128)} %element.5.second_ref, ...), custom_call_target="tpu_custom_call" | custom-call | tf_op jit(solution)/shard_map/force/pallas_call | solution.py:449
  57.8 3.2 %collective-permute-start.7 = (f32[8,128]{1,0:T(8,128)}, f32[8,128]{1,0:T(8,128)S(1)}, u32[]{:S(2)}, u32[]{:S(2)}) collective-permute-start(f32[8,128]{1,0:T(8,128)} %get-tuple-element.44), channel_id=1, source_target_pairs={{0,7},{1,2},{2,1},{3,4},{4,3},{5,6},{6,5},{7,0},{8,15},{9,10},{10,... | collective-permute-start | bytes 12296 | tf_op jit(solution)/shard_map/ppermute | solution.py:523
  61.0 3.3 %collective-permute-done.7.near3_ref = f32[8,128]{1,0:T(8,128)S(1)} collective-permute-done((f32[8,128]{1,0:T(8,128)}, f32[8,128]{1,0:T(8,128)S(1)}, u32[]{:S(2)}, u32[]{:S(2)}) %collective-permute-start.7) | collective-permute-done | bytes 4128 | tf_op jit(solution)/shard_map/ppermute | solution.py:523
  64.9 2.7 %update.2 = (f32[6,8192]{1,0:T(8,128)}, f32[6,8192]{1,0:T(8,128)}, f32[64,4,128]{2,1,0:T(4,128)}) custom-call(s32[64]{0:T(128)} %slot_ref.9, f32[64,8,128]{2,1,0:T(8,128)} %get-tuple-element.40.force_ref, f32[8,128]{1,0:T(8,128)} %copy-done.13, f32[8,128]{1,0:T(8,128)} %copy-done.15, f32[8,128]{1,0:T(8,128)} %copy-done.17, f32[8,128]{1,0:T(8,128)} %copy-done.19, ...), custom_call_target="tpu_custom_call" | custom-call | tf_op jit(solution)/shard_map/update/pallas_call | solution.py:504
  67.6 3.6 %all-to-all-start.2 = ((f32[64,4,128]{2,1,0:T(4,128)}), f32[64,4,128]{2,1,0:T(4,128)S(1)}, u32[]{:S(2)}, u32[]{:S(2)}) async-start(f32[64,4,128]{2,1,0:T(4,128)} %get-tuple-element.46), calls=%async_computation.2 | async-start | bytes 262144 | tf_op jit(solution)/shard_map/all_to_all | solution.py:566
  71.1 6.3 %element.6.first_ref = f32[32,8,128]{2,1,0:T(8,128)} custom-call(f32[6,8192]{1,0:T(8,128)} %get-tuple-element.54.disp_ref, s32[4,8192]{1,0:T(4,128)} %conn_ref.7, bf16[24,24,8192]{2,1,0:T(8,128)(2,1)} %stiff_ref.7, f32[8,8,128]{2,1,0:T(8,128)} %bitcast.7), custom_call_target="tpu_custom_call" | custom-call | flops 9437184 | bytes 9437184 | tf_op jit(solution)/shard_map/element/pallas_call | solution.py:138
  80.7 2.4 %collective-permute-start.11 = (f32[8,4,128]{2,1,0:T(4,128)S(1)}, f32[8,4,128]{2,1,0:T(4,128)S(1)}, u32[]{:S(2)}, u32[]{:S(2)}) collective-permute-start(f32[8,4,128]{2,1,0:T(4,128)S(1)} %gather_fusion.1), channel_id=1, source_target_pairs={{0,7},{1,2},{2,1},{3,4},{4,3},{5,6},{6,5},{7,0},{8,15},{9,10},{10,... | collective-permute-start | bytes 49160 | tf_op jit(solution)/shard_map/ppermute | solution.py:523
  84.8 5.0 %own_contact.3 = (f32[64,8,128]{2,1,0:T(8,128)}, bf16[64,16,128]{2,1,0:T(8,128)(2,1)}) custom-call(s32[8,128]{1,0:T(8,128)} %plan.1.refs_0_, f32[64,8,128]{2,1,0:T(8,128)} %copy-done, f32[64,4,128]{2,1,0:T(4,128)} %copy-done.1, s32[128,128]{1,0:T(8,128)} %refs_10_.1, s32[128,128]{1,0:T(8,128)} %refs_11_.1), custom_call_target="tpu_custom_call" | custom-call | flops 67108864 | bytes 65536 | tf_op jit(solution)/shard_map/own_contact/pallas_call | solution.py:350
  90.4 4.8 %far_contact.3 = f32[64,4,128]{2,1,0:T(4,128)} custom-call(s32[8,128]{1,0:T(8,128)} %plan.1.refs_0_, s32[4]{0:T(128)} %pad_add_fusion.2.valid_ref.refs_1_, f32[8,8,128]{2,1,0:T(8,128)} %copy-done.4, f32[8,8,128]{2,1,0:T(8,128)} %copy-done.5, f32[8,8,128]{2,1,0:T(8,128)} %copy-done.6, f32[8,8,128]{2,1,0:T(8,128)} %copy-done.7, f32[8,4,128]{2,1,0:T(4,128)} %copy-done.10, ...), custom_call_target="tpu_custom_call" | custom-call | flops 67108864 | bytes 65536 | tf_op jit(solution)/shard_map/far_contact/pallas_call | solution.py:378
  95.2 2.6 %all-to-all-start.3 = ((f32[64,4,128]{2,1,0:T(4,128)}), f32[64,4,128]{2,1,0:T(4,128)S(1)}, u32[]{:S(2)}, u32[]{:S(2)}) async-start(f32[64,4,128]{2,1,0:T(4,128)} %far_contact.3), calls=%async_computation.3 | async-start | bytes 262144 | tf_op jit(solution)/shard_map/all_to_all | solution.py:566
  97.8 6.3 %element.7.second_ref = f32[32,8,128]{2,1,0:T(8,128)} custom-call(f32[6,8192]{1,0:T(8,128)} %get-tuple-element.54.disp_ref, s32[4,8192]{1,0:T(4,128)} %conn_ref.7, bf16[24,24,8192]{2,1,0:T(8,128)(2,1)} %stiff_ref.7, f32[8,8,128]{2,1,0:T(8,128)} %bitcast.8), custom_call_target="tpu_custom_call" | custom-call | flops 9437184 | bytes 9437184 | tf_op jit(solution)/shard_map/element/pallas_call | solution.py:138
  106.3 2.4 %force.3 = (f32[64,8,128]{2,1,0:T(8,128)}, f32[8,128]{1,0:T(8,128)}, f32[8,128]{1,0:T(8,128)}, f32[8,128]{1,0:T(8,128)}, f32[8,128]{1,0:T(8,128)}) custom-call(s32[64]{0:T(128)} %slot_ref.9, f32[64,4,128]{2,1,0:T(4,128)} %copy-done.2, f32[32,8,128]{2,1,0:T(8,128)} %element.6.first_ref, f32[32,8,128]{2,1,0:T(8,128)} %element.7.second_ref, ...), custom_call_target="tpu_custom_call" | custom-call | tf_op jit(solution)/shard_map/force/pallas_call | solution.py:449
  110.7 3.2 %collective-permute-start.15 = (f32[8,128]{1,0:T(8,128)}, f32[8,128]{1,0:T(8,128)S(1)}, u32[]{:S(2)}, u32[]{:S(2)}) collective-permute-start(f32[8,128]{1,0:T(8,128)} %get-tuple-element.59), channel_id=1, source_target_pairs={{0,7},{1,2},{2,1},{3,4},{4,3},{5,6},{6,5},{7,0},{8,15},{9,10},{10,... | collective-permute-start | bytes 12296 | tf_op jit(solution)/shard_map/ppermute | solution.py:523
  114.0 3.3 %collective-permute-done.15.near3_ref = f32[8,128]{1,0:T(8,128)S(1)} collective-permute-done((f32[8,128]{1,0:T(8,128)}, f32[8,128]{1,0:T(8,128)S(1)}, u32[]{:S(2)}, u32[]{:S(2)}) %collective-permute-start.15) | collective-permute-done | bytes 4128 | tf_op jit(solution)/shard_map/ppermute | solution.py:523
  117.8 2.6 %update.3 = (f32[6,8192]{1,0:T(8,128)}, f32[6,8192]{1,0:T(8,128)}) custom-call(s32[64]{0:T(128)} %slot_ref.9, f32[64,8,128]{2,1,0:T(8,128)} %get-tuple-element.55.force_ref, f32[8,128]{1,0:T(8,128)} %copy-done.12, f32[8,128]{1,0:T(8,128)} %copy-done.14, f32[8,128]{1,0:T(8,128)} %copy-done.16, f32[8,128]{1,0:T(8,128)} %copy-done.18, ...), custom_call_target="tpu_custom_call" | custom-call | tf_op jit(solution)/shard_map/update/pallas_call | solution.py:504
  (81 shorter events, 23.7 us)
Async XLA Ops:
  0.6 24.1 %copy-start.20 = (s32[8]{0:T(128)S(1)}, s32[8]{0:T(128)}, u32[]{:S(2)}) copy-start(s32[8]{0:T(128)} %param.25) | copy-start | bytes 100
  2.5 22.3 %all-to-all-start = ((f32[64,8,128]{2,1,0:T(8,128)}), f32[64,8,128]{2,1,0:T(8,128)S(1)}, u32[]{:S(2)}, u32[]{:S(2)}) async-start(f32[64,8,128]{2,1,0:T(8,128)} %prep.1), calls=%async_computation | async-start | bytes 524288 | tf_op jit(solution)/shard_map/all_to_all | solution.py:566
  24.7 7.3 %copy-start = (f32[64,8,128]{2,1,0:T(8,128)}, f32[64,8,128]{2,1,0:T(8,128)S(1)}, u32[]{:S(2)}) copy-start(f32[64,8,128]{2,1,0:T(8,128)S(1)} %all-to-all-done.refs_1_) | copy-start | bytes 786436
  25.3 11.6 %collective-permute-start = (f32[8,8,128]{2,1,0:T(8,128)S(1)}, f32[8,8,128]{2,1,0:T(8,128)S(1)}, u32[]{:S(2)}, u32[]{:S(2)}) collective-permute-start(f32[8,8,128]{2,1,0:T(8,128)S(1)} %gather_fusion), channel_id=1, source_target_pairs={{0,8},{8,0},{16,24},{24,16},{1,9},{9,1},{17,25},{25,17},{2,10},{10... | collective-permute-start | bytes 98312 | tf_op jit(solution)/shard_map/ppermute | solution.py:523
  25.6 11.3 %collective-permute-start.1 = (f32[8,8,128]{2,1,0:T(8,128)S(1)}, f32[8,8,128]{2,1,0:T(8,128)S(1)}, u32[]{:S(2)}, u32[]{:S(2)}) collective-permute-start(f32[8,8,128]{2,1,0:T(8,128)S(1)} %gather_fusion), channel_id=1, source_target_pairs={{0,24},{8,16},{16,8},{24,0},{1,25},{9,17},{17,9},{25,1},{2,26},{10... | collective-permute-start | bytes 98312 | tf_op jit(solution)/shard_map/ppermute | solution.py:523
  27.3 9.7 %collective-permute-start.2 = (f32[8,8,128]{2,1,0:T(8,128)S(1)}, f32[8,8,128]{2,1,0:T(8,128)S(1)}, u32[]{:S(2)}, u32[]{:S(2)}) collective-permute-start(f32[8,8,128]{2,1,0:T(8,128)S(1)} %gather_fusion), channel_id=1, source_target_pairs={{0,1},{1,0},{2,3},{3,2},{4,5},{5,4},{6,7},{7,6},{8,9},{9,8},{10,11... | collective-permute-start | bytes 98312 | tf_op jit(solution)/shard_map/ppermute | solution.py:523
  28.7 8.2 %collective-permute-start.3 = (f32[8,8,128]{2,1,0:T(8,128)S(1)}, f32[8,8,128]{2,1,0:T(8,128)S(1)}, u32[]{:S(2)}, u32[]{:S(2)}) collective-permute-start(f32[8,8,128]{2,1,0:T(8,128)S(1)} %gather_fusion), channel_id=1, source_target_pairs={{0,7},{1,2},{2,1},{3,4},{4,3},{5,6},{6,5},{7,0},{8,15},{9,10},{10,... | collective-permute-start | bytes 98312 | tf_op jit(solution)/shard_map/ppermute | solution.py:523
  42.3 10.4 %all-to-all-start.1 = ((f32[64,4,128]{2,1,0:T(4,128)}), f32[64,4,128]{2,1,0:T(4,128)S(1)}, u32[]{:S(2)}, u32[]{:S(2)}) async-start(f32[64,4,128]{2,1,0:T(4,128)} %far_contact.2), calls=%async_computation.1 | async-start | bytes 262144 | tf_op jit(solution)/shard_map/all_to_all | solution.py:566
  55.8 5.2 %collective-permute-start.4 = (f32[8,128]{1,0:T(8,128)}, f32[8,128]{1,0:T(8,128)S(1)}, u32[]{:S(2)}, u32[]{:S(2)}) collective-permute-start(f32[8,128]{1,0:T(8,128)} %get-tuple-element.41), channel_id=1, source_target_pairs={{0,8},{8,0},{16,24},{24,16},{1,9},{9,1},{17,25},{25,17},{2,10},{10... | collective-permute-start | bytes 12296 | tf_op jit(solution)/shard_map/ppermute | solution.py:523
  55.9 5.1 %collective-permute-start.5 = (f32[8,128]{1,0:T(8,128)}, f32[8,128]{1,0:T(8,128)S(1)}, u32[]{:S(2)}, u32[]{:S(2)}) collective-permute-start(f32[8,128]{1,0:T(8,128)} %get-tuple-element.42), channel_id=1, source_target_pairs={{0,24},{8,16},{16,8},{24,0},{1,25},{9,17},{17,9},{25,1},{2,26},{10... | collective-permute-start | bytes 12296 | tf_op jit(solution)/shard_map/ppermute | solution.py:523
  56.9 4.1 %collective-permute-start.6 = (f32[8,128]{1,0:T(8,128)}, f32[8,128]{1,0:T(8,128)S(1)}, u32[]{:S(2)}, u32[]{:S(2)}) collective-permute-start(f32[8,128]{1,0:T(8,128)} %get-tuple-element.43), channel_id=1, source_target_pairs={{0,1},{1,0},{2,3},{3,2},{4,5},{5,4},{6,7},{7,6},{8,9},{9,8},{10,11... | collective-permute-start | bytes 12296 | tf_op jit(solution)/shard_map/ppermute | solution.py:523
  57.8 6.5 %collective-permute-start.7 = (f32[8,128]{1,0:T(8,128)}, f32[8,128]{1,0:T(8,128)S(1)}, u32[]{:S(2)}, u32[]{:S(2)}) collective-permute-start(f32[8,128]{1,0:T(8,128)} %get-tuple-element.44), channel_id=1, source_target_pairs={{0,7},{1,2},{2,1},{3,4},{4,3},{5,6},{6,5},{7,0},{8,15},{9,10},{10,... | collective-permute-start | bytes 12296 | tf_op jit(solution)/shard_map/ppermute | solution.py:523
  61.0 3.3 %copy-start.13 = (f32[8,128]{1,0:T(8,128)}, f32[8,128]{1,0:T(8,128)S(1)}, u32[]{:S(2)}) copy-start(f32[8,128]{1,0:T(8,128)S(1)} %collective-permute-done.4.near0_ref) | copy-start | bytes 12292
  67.6 11.4 %all-to-all-start.2 = ((f32[64,4,128]{2,1,0:T(4,128)}), f32[64,4,128]{2,1,0:T(4,128)S(1)}, u32[]{:S(2)}, u32[]{:S(2)}) async-start(f32[64,4,128]{2,1,0:T(4,128)} %get-tuple-element.46), calls=%async_computation.2 | async-start | bytes 262144 | tf_op jit(solution)/shard_map/all_to_all | solution.py:566
  78.9 5.8 %copy-start.1 = (f32[64,4,128]{2,1,0:T(4,128)}, f32[64,4,128]{2,1,0:T(4,128)S(1)}, u32[]{:S(2)}) copy-start(f32[64,4,128]{2,1,0:T(4,128)S(1)} %all-to-all-done.2.refs_2_) | copy-start | bytes 393220
  79.5 10.2 %collective-permute-start.10 = (f32[8,4,128]{2,1,0:T(4,128)S(1)}, f32[8,4,128]{2,1,0:T(4,128)S(1)}, u32[]{:S(2)}, u32[]{:S(2)}) collective-permute-start(f32[8,4,128]{2,1,0:T(4,128)S(1)} %gather_fusion.1), channel_id=1, source_target_pairs={{0,1},{1,0},{2,3},{3,2},{4,5},{5,4},{6,7},{7,6},{8,9},{9,8},{10,11... | collective-permute-start | bytes 49160 | tf_op jit(solution)/shard_map/ppermute | solution.py:523
  80.7 9.0 %collective-permute-start.11 = (f32[8,4,128]{2,1,0:T(4,128)S(1)}, f32[8,4,128]{2,1,0:T(4,128)S(1)}, u32[]{:S(2)}, u32[]{:S(2)}) collective-permute-start(f32[8,4,128]{2,1,0:T(4,128)S(1)} %gather_fusion.1), channel_id=1, source_target_pairs={{0,7},{1,2},{2,1},{3,4},{4,3},{5,6},{6,5},{7,0},{8,15},{9,10},{10,... | collective-permute-start | bytes 49160 | tf_op jit(solution)/shard_map/ppermute | solution.py:523
  83.2 6.6 %collective-permute-start.8 = (f32[8,4,128]{2,1,0:T(4,128)S(1)}, f32[8,4,128]{2,1,0:T(4,128)S(1)}, u32[]{:S(2)}, u32[]{:S(2)}) collective-permute-start(f32[8,4,128]{2,1,0:T(4,128)S(1)} %gather_fusion.1), channel_id=1, source_target_pairs={{0,8},{8,0},{16,24},{24,16},{1,9},{9,1},{17,25},{25,17},{2,10},{10... | collective-permute-start | bytes 49160 | tf_op jit(solution)/shard_map/ppermute | solution.py:523
  83.2 6.6 %collective-permute-start.9 = (f32[8,4,128]{2,1,0:T(4,128)S(1)}, f32[8,4,128]{2,1,0:T(4,128)S(1)}, u32[]{:S(2)}, u32[]{:S(2)}) collective-permute-start(f32[8,4,128]{2,1,0:T(4,128)S(1)} %gather_fusion.1), channel_id=1, source_target_pairs={{0,24},{8,16},{16,8},{24,0},{1,25},{9,17},{17,9},{25,1},{2,26},{10... | collective-permute-start | bytes 49160 | tf_op jit(solution)/shard_map/ppermute | solution.py:523
  95.2 10.4 %all-to-all-start.3 = ((f32[64,4,128]{2,1,0:T(4,128)}), f32[64,4,128]{2,1,0:T(4,128)S(1)}, u32[]{:S(2)}, u32[]{:S(2)}) async-start(f32[64,4,128]{2,1,0:T(4,128)} %far_contact.3), calls=%async_computation.3 | async-start | bytes 262144 | tf_op jit(solution)/shard_map/all_to_all | solution.py:566
  108.7 5.2 %collective-permute-start.12 = (f32[8,128]{1,0:T(8,128)}, f32[8,128]{1,0:T(8,128)S(1)}, u32[]{:S(2)}, u32[]{:S(2)}) collective-permute-start(f32[8,128]{1,0:T(8,128)} %get-tuple-element.56), channel_id=1, source_target_pairs={{0,8},{8,0},{16,24},{24,16},{1,9},{9,1},{17,25},{25,17},{2,10},{10... | collective-permute-start | bytes 12296 | tf_op jit(solution)/shard_map/ppermute | solution.py:523
  108.8 5.1 %collective-permute-start.13 = (f32[8,128]{1,0:T(8,128)}, f32[8,128]{1,0:T(8,128)S(1)}, u32[]{:S(2)}, u32[]{:S(2)}) collective-permute-start(f32[8,128]{1,0:T(8,128)} %get-tuple-element.57), channel_id=1, source_target_pairs={{0,24},{8,16},{16,8},{24,0},{1,25},{9,17},{17,9},{25,1},{2,26},{10... | collective-permute-start | bytes 12296 | tf_op jit(solution)/shard_map/ppermute | solution.py:523
  109.8 4.2 %collective-permute-start.14 = (f32[8,128]{1,0:T(8,128)}, f32[8,128]{1,0:T(8,128)S(1)}, u32[]{:S(2)}, u32[]{:S(2)}) collective-permute-start(f32[8,128]{1,0:T(8,128)} %get-tuple-element.58), channel_id=1, source_target_pairs={{0,1},{1,0},{2,3},{3,2},{4,5},{5,4},{6,7},{7,6},{8,9},{9,8},{10,11... | collective-permute-start | bytes 12296 | tf_op jit(solution)/shard_map/ppermute | solution.py:523
  110.7 6.5 %collective-permute-start.15 = (f32[8,128]{1,0:T(8,128)}, f32[8,128]{1,0:T(8,128)S(1)}, u32[]{:S(2)}, u32[]{:S(2)}) collective-permute-start(f32[8,128]{1,0:T(8,128)} %get-tuple-element.59), channel_id=1, source_target_pairs={{0,7},{1,2},{2,1},{3,4},{4,3},{5,6},{6,5},{7,0},{8,15},{9,10},{10,... | collective-permute-start | bytes 12296 | tf_op jit(solution)/shard_map/ppermute | solution.py:523
  (17 other events, 23.8 us)

commit v3 on v2

--- a/solution.py
+++ b/solution.py
@@ -30,6 +30,10 @@
 
 def sspec():
     return pl.BlockSpec(memory_space=SMEM)
+
+
+def limit(mebibytes):
+    return pltpu.CompilerParams(vmem_limit_bytes=mebibytes << 20)
 
 
 def lane_gather(data, index):
@@ -59,6 +63,7 @@
         out_shape=jax.ShapeDtypeStruct((places, ROWS, BLK), F32),
         in_specs=[sspec(), vspec(), vspec(), vspec()],
         out_specs=vspec(),
+        compiler_params=limit(4),
         name="prep",
     )(block_slot, displacement, ref_pos, normals)
 
@@ -149,54 +154,56 @@
         cost_estimate=pl.CostEstimate(
             flops=2 * 576 * nodes, transcendentals=nodes, bytes_accessed=2 * 576 * nodes
         ),
+        compiler_params=limit(10),
         name="element",
-    )(displacement, connectivity, stiffness, yield_force.reshape(-1, EBLK, BLK))
-
-
-def plan_kernel(count_ref, pairs_ref, even_ref, plan_ref, *, places, edges):
-    for row, value in enumerate((0, 0, 0, 0, 0, places)):
-        plan_ref[row, 0] = value
-
-    def sort(t, numbers):
-        own, far = numbers
+    )(
+        displacement,
+        connectivity,
+        pltpu.with_memory_space_constraint(stiffness, pltpu.HBM),
+        yield_force.reshape(-1, EBLK, BLK),
+    )
+
+
+def plan_kernel(count_ref, pairs_ref, meta_ref, plan_ref, *, places, edges):
+    tiles = pairs_ref.shape[1]
+    for first, master in ((0, 0), (tiles, places)):
+        plan_ref[0, first] = 0
+        plan_ref[1, first] = 0
+        plan_ref[2, first] = master
+    log = edges.bit_length() - 1
+    power = edges == 1 << log
+
+    def sort(t, own):
         slave = pairs_ref[0, t]
         master = pairs_ref[1, t]
         is_own = master < places
-        entry = jnp.maximum(master - places, 0)
-        side = entry // edges
-        flip = jnp.where(side < 2, even_ref[0], even_ref[1])
-        moved = places + (side ^ flip) * edges + entry % edges
-
-        @pl.when(is_own)
-        def _():
-            plan_ref[0, own] = t
-            plan_ref[1, own] = slave
-            plan_ref[2, own] = master
-
-        @pl.when(jnp.logical_not(is_own))
-        def _():
-            plan_ref[3, far] = t
-            plan_ref[4, far] = slave
-            plan_ref[5, far] = moved
-
-        return own + is_own.astype(jnp.int32), far + 1 - is_own.astype(jnp.int32)
-
-    own, far = lax.fori_loop(0, count_ref[0], sort, (jnp.int32(0), jnp.int32(0)))
-    plan_ref[6, 0] = own
-    plan_ref[7, 0] = far
-
-
-def plan_tiles(tile_count, tile_pairs, even, places, edges):
+        entry = master - places
+        side = entry >> log if power else entry // edges
+        flip = jnp.where(side < 2, meta_ref[0], meta_ref[1])
+        moved = entry + edges * ((side ^ flip) - side)
+        where = jnp.where(is_own, own, tiles + t - own)
+        plan_ref[0, where] = t
+        plan_ref[1, where] = slave
+        plan_ref[2, where] = jnp.where(is_own, master, places + moved)
+        return own + is_own.astype(jnp.int32)
+
+    own = lax.fori_loop(0, count_ref[0], sort, jnp.int32(0))
+    plan_ref[3, 0] = own
+    plan_ref[3, 1] = count_ref[0] - own
+
+
+def plan_tiles(tile_count, tile_pairs, meta, places, edges):
     def kernel(*refs):
         plan_kernel(*refs, places=places, edges=edges)
 
     return pl.pallas_call(
         kernel,
-        out_shape=jax.ShapeDtypeStruct((8, tile_pairs.shape[1]), jnp.int32),
+        out_shape=jax.ShapeDtypeStruct((4, 2 * tile_pairs.shape[1]), jnp.int32),
         in_specs=[sspec()] * 3,
         out_specs=sspec(),
+        compiler_params=limit(1),
         name="plan",
-    )(tile_count, tile_pairs, even)
+    )(tile_count, tile_pairs, meta)
 
 
 def master_entry(where, position, normal, master_tab, force_tab):
@@ -216,7 +223,7 @@
 
 
 def run_tiles(
-    plan_ref, row, number, base, start_ref, length_ref, slave_tab, master_tab, force_tab,
+    plan_ref, first, number, base, start_ref, length_ref, slave_tab, master_tab, force_tab,
     total_ref, depth_ref,
 ):
     facet = lax.broadcasted_iota(jnp.int32, (BLK, 2 * BLK), 0).astype(jnp.int16)
@@ -227,7 +234,7 @@
 
     def at(group, d):
         i = group * GROUP + d
-        return jnp.clip(i, 0, last), jnp.logical_and(i >= 0, i < number)
+        return first + jnp.clip(i, 0, last), jnp.logical_and(i >= 0, i < number)
 
     def body(r, carry):
         forces = []
@@ -235,10 +242,10 @@
             starts, lengths, rows = [], [], []
             for e in range(2):
                 i, live = at(r - 1, d + e)
-                t = plan_ref[row, i]
+                t = plan_ref[0, i]
                 starts.append(start_ref[pl.ds(t, 1), :])
                 lengths.append(jnp.where(live, length_ref[pl.ds(t, 1), :], 0))
-                rows.append(force_tab[plan_ref[row + 2, i] - base])
+                rows.append(force_tab[plan_ref[2, i] - base])
             start = jnp.concatenate(starts, axis=1).astype(small)
             length = jnp.concatenate(lengths, axis=1).astype(small)
             inside = ((facet - start) & (BLK - 1)) < length
@@ -259,8 +266,8 @@
             facets, nodes = [], []
             for e in range(2):
                 i, _ = at(r, d + e)
-                facets.append(master_tab[plan_ref[row + 2, i] - base])
-                nodes.append(slave_tab[plan_ref[row + 1, i]])
+                facets.append(master_tab[plan_ref[2, i] - base])
+                nodes.append(slave_tab[plan_ref[1, i]])
             left = jnp.concatenate([nodes[0], blank], axis=0)
             right = jnp.concatenate([blank, nodes[1]], axis=0)
             depth_ref[d // 2] = lax.dot_general(
@@ -272,7 +279,7 @@
         for d in range(GROUP):
             i, _ = at(r - 1, d)
             e = d % 2
-            slave = plan_ref[row + 1, i]
+            slave = plan_ref[1, i]
             part = forces[d // 2][8 * e : 8 * e + 8, e * BLK : (e + 1) * BLK]
             total_ref[slave] = total_ref[slave] + part
         return carry
@@ -300,12 +307,12 @@
 
     lax.fori_loop(0, places, entry, 0, unroll=8)
     run_tiles(
-        plan_ref, 0, plan_ref[6, 0], 0, start_ref, length_ref, slave_tab, master_tab, force_tab,
+        plan_ref, 0, plan_ref[3, 0], 0, start_ref, length_ref, slave_tab, master_tab, force_tab,
         total_ref, depth_ref,
     )
 
 
-def far_kernel(plan_ref, valid_ref, *refs, edges, fresh):
+def far_kernel(plan_ref, meta_ref, *refs, edges, fresh):
     edge_refs = refs[0:4]
     pos_refs = edge_refs if fresh else refs[4:8]
     refs = refs[4:] if fresh else refs[8:]
@@ -315,13 +322,13 @@
     zero1 = jnp.zeros((1, BLK), F32)
     total_ref[...] = own_ref[...]
     for side in range(4):
-        valid = valid_ref[side] > 0
+        valid = meta_ref[2 + side] > 0
         for e in range(edges):
             normal = jnp.where(valid, edge_refs[side][e], 0.0)[3:6]
             position = jnp.where(valid, pos_refs[side][e], 0.0)[0:3]
             master_entry(side * edges + e, position, normal, master_tab, force_tab)
     run_tiles(
-        plan_ref, 3, plan_ref[7, 0], places, start_ref, length_ref, slave_tab, master_tab,
+        plan_ref, plan_ref.shape[1] // 2, plan_ref[3, 1], places, start_ref, length_ref, slave_tab, master_tab,
         force_tab, total_ref, depth_ref,
     )
 
@@ -361,11 +368,12 @@
             VMEM((GROUP // 2, BLK, 2 * BLK), F32),
         ],
         cost_estimate=tile_cost(start.shape[0] // 2),
+        compiler_params=limit(8),
         name="own_contact",
     )(plan, *arrays)
 
 
-def far_contact(plan, valid, edges, edge_positions, start, length, total, slave_tab):
+def far_contact(plan, meta, edges, edge_positions, start, length, total, slave_tab):
     places = total.shape[0]
     fresh = edge_positions is None
     edge_count = edges[0].shape[0]
@@ -387,19 +395,27 @@
             VMEM((GROUP // 2, BLK, 2 * BLK), F32),
         ],
         cost_estimate=tile_cost(start.shape[0] // 2),
+        compiler_params=limit(8),
         name="far_contact",
-    )(plan, valid, *arrays)
-
-
-def inverse_kernel(valid_ref, list_ref, out_ref):
+    )(plan, meta, *arrays)
+
+
+def side_list(list_ref, meta_ref, side):
+    axis = side // 2
+    low = list_ref[2 * axis : 2 * axis + 1, :]
+    high = list_ref[2 * axis + 1 : 2 * axis + 2, :]
+    return jnp.where(meta_ref[axis] != side % 2, high, low)
+
+
+def inverse_kernel(meta_ref, list_ref, out_ref):
     blocks = out_ref.shape[0]
     block_id = lax.broadcasted_iota(jnp.int32, (blocks, BLK), 0)
     lane_id = lax.broadcasted_iota(jnp.int32, (BLK, BLK), 0)
     rank = (lax.broadcasted_iota(jnp.int32, (BLK, BLK), 1) + 1).astype(F32)
     code = jnp.full((blocks, BLK), -1, jnp.int32)
     for side in range(4):
-        nodes = list_ref[side : side + 1, :]
-        valid = valid_ref[side] > 0
+        nodes = side_list(list_ref, meta_ref, side)
+        valid = meta_ref[2 + side] > 0
         in_block = jnp.where(
             jnp.logical_and(block_id == nodes // BLK, valid), 1.0, 0.0
         ).astype(BF16)
@@ -411,24 +427,25 @@
     out_ref[...] = code
 
 
-def inverse(valid, lists, blocks):
+def inverse(meta, lists, blocks):
     return pl.pallas_call(
         inverse_kernel,
         out_shape=jax.ShapeDtypeStruct((blocks, BLK), jnp.int32),
         in_specs=[sspec(), vspec()],
         out_specs=vspec(),
+        compiler_params=limit(2),
         name="inverse",
-    )(valid, lists)
-
-
-def force_kernel(slot_ref, back_ref, first_ref, second_ref, list_ref, force_ref, *side_refs):
+    )(meta, lists)
+
+
+def force_kernel(slot_ref, meta_ref, back_ref, first_ref, second_ref, list_ref, force_ref, *side_refs):
     half = first_ref.shape[0]
     blocks = slot_ref.shape[0]
     pad = jnp.zeros((ROWS - HALF, BLK), F32)
     lanes = []
     owners = []
     for side in range(4):
-        nodes = jnp.broadcast_to(list_ref[side : side + 1, :], (ROWS, BLK))
+        nodes = jnp.broadcast_to(side_list(list_ref, meta_ref, side), (ROWS, BLK))
         lanes.append(nodes & (BLK - 1))
         owners.append(nodes // BLK)
     sums = [jnp.zeros((ROWS, BLK), F32) for _ in range(4)]
@@ -444,16 +461,17 @@
         side_refs[side][...] = sums[side]
 
 
-def nodal_force(block_slot, returned, internal, lists):
+def nodal_force(block_slot, meta, returned, internal, lists):
     blocks = 2 * internal[0].shape[0]
     return pl.pallas_call(
         force_kernel,
         out_shape=[jax.ShapeDtypeStruct((blocks, ROWS, BLK), F32)]
         + [jax.ShapeDtypeStruct((ROWS, BLK), F32)] * 4,
-        in_specs=[sspec()] + [vspec()] * 4,
+        in_specs=[sspec()] * 2 + [vspec()] * 4,
         out_specs=[vspec()] * 5,
+        compiler_params=limit(4),
         name="force",
-    )(block_slot, returned, *internal, lists)
+    )(block_slot, meta, returned, *internal, lists)
 
 
 def update_kernel(
@@ -506,22 +524,30 @@
         out_shape=out,
         in_specs=[sspec()] + [vspec()] * 10,
         out_specs=[vspec()] * len(out),
+        compiler_params=limit(6),
         name="update",
     )(block_slot, force, *near, code, inv_mass, velocity, displacement, ref_pos)
 
 
-def pair_lists(size):
-    first = [(i, i ^ 1) for i in range(size)]
-    second = [(i, (i + 1) % size if i % 2 else (i - 1) % size) for i in range(size)]
-    return first, second
+def pair_lists(sizes):
+    rows, columns = sizes
+    near = [[(i, i ^ 1) for i in range(size)] for size in sizes]
+    other = [(i, (i + 1) % rows if i % 2 else (i - 1) % rows) for i in range(rows)]
+    flat = []
+    for i in range(rows):
+        for j in range(columns):
+            k = j + 1 if j % 2 else j - 1
+            inside = 0 <= k < columns
+            flat.append((i * columns + j, i * columns + k if inside else (i ^ 1) * columns + j))
+    return [("gx", near[0]), ("gx", other), ("gy", near[1]), (AXES, flat)]
 
 
 def swap(values, sizes):
-    out = []
-    for at, axis in enumerate(AXES):
-        for stage, pairs in enumerate(pair_lists(sizes[at])):
-            out.append(lax.ppermute(values[2 * at + stage], axis, pairs))
-    return out
+    moved = [
+        lax.ppermute(value, axis, pairs)
+        for value, (axis, pairs) in reversed(list(zip(values, pair_lists(sizes))))
+    ]
+    return moved[::-1]
 
 
 def body(
@@ -548,19 +574,14 @@
     blocks = displacement.shape[1] // BLK
     edge_count = edge_slots.shape[0]
     at = [lax.axis_index(axis) for axis in AXES]
-    even = jnp.stack([1 - i % 2 for i in at]).astype(jnp.int32)
-    valid = []
-    for i, size in zip(at, sizes):
-        valid += [jnp.int32(1), jnp.where((i == 0) | (i == size - 1), 0, 1).astype(jnp.int32)]
-    valid = jnp.stack(valid)
-    plan = plan_tiles(tile_count, tile_pairs, even, places, edge_count)
-    lists = []
-    for axis in range(2):
-        low, high = shared_nodes[2 * axis], shared_nodes[2 * axis + 1]
-        is_even = even[axis] == 1
-        lists += [jnp.where(is_even, high, low), jnp.where(is_even, low, high)]
-    lists = jnp.stack(lists)
-    code = inverse(valid, lists, blocks)
+    odd = [i % 2 for i in at]
+    inner = [((i > 0) & (i < size - 1)).astype(jnp.int32) for i, size in zip(at, sizes)]
+    slot = jnp.arange(8, dtype=jnp.int32)
+    meta = jnp.ones((8,), jnp.int32)
+    for i, value in ((0, 1 - odd[0]), (1, 1 - odd[1]), (3, inner[0]), (5, inner[1])):
+        meta = jnp.where(slot == i, value, meta)
+    plan = plan_tiles(tile_count, tile_pairs, meta, places, edge_count)
+    code = None
 
     def exchange(blocks_out):
         return lax.all_to_all(blocks_out, AXES, split_axis=0, concat_axis=0, tiled=True)
@@ -574,9 +595,7 @@
         fresh = step == 0
         received = exchange(outgoing)
         internal0 = half(displacement, 0)
-        received, internal0, plan, code = lax.optimization_barrier(
-            (received, internal0, plan, code)
-        )
+        received, internal0, plan = lax.optimization_barrier((received, internal0, plan))
         near = swap([received[edge_slots]] * 4, sizes)
         if fresh:
             first = (received, near)
@@ -584,12 +603,17 @@
             plan, first[0], None if fresh else received, win_start, win_len
         )
         box_force = far_contact(
-            plan, valid, first[1], None if fresh else near, win_start, win_len, total, slave_tab
+            plan, meta, first[1], None if fresh else near, win_start, win_len, total, slave_tab
         )
         box_force, later = lax.optimization_barrier((box_force, displacement))
         returned = exchange(box_force)
         internal1 = half(later, 1)
-        force, *sides = nodal_force(block_slot, returned, (internal0, internal1), lists)
+        force, *sides = nodal_force(
+            block_slot, meta, returned, (internal0, internal1), shared_nodes
+        )
+        if code is None:
+            sides, lists = lax.optimization_barrier((sides, shared_nodes))
+            code = inverse(meta, lists, blocks)
         incoming = swap(sides, sizes)
         last = step == STEPS - 1
         out = update(

time: 121 us -> 103 us (0.85)
  Pallas kernels: 61.8 us -> 50.3 us
  starting transfers between devices: 38.5 us -> 31.2 us
  local copies, waits for them, and re-layouts: 4.83 us -> 7.86 us
  other arithmetic: 2.69 us -> 0.02 us
    ppermute x16, starting transfers between devices: 22.4 us -> 9.57 us  [swap(): lax.ppermute(value, axis, pairs)]
    all_to_all x4, starting transfers between devices: 16.1 us -> 21.7 us  [exchange(): lax.all_to_all(blocks_out, AXES, split_axis=0, concat_axis=0, tiled=True)]
    unnamed x42 -> x38, local copies, waits for them, and re-layouts: 3.71 us -> 6.74 us
    pallas_call x4, Pallas kernels: 25.2 us -> 22.6 us  [element_forces(): pl.pallas_call(element_kernel, out_shape=jax.ShapeDtypeStruct((blocks, RO...]
    pallas_call x2, Pallas kernels: 9.82 us -> 7.47 us  [own_contact(): pl.pallas_call(kernel, out_shape=[jax.ShapeDtypeStruct((places, ROWS, BLK...]
    pallas_call x2, Pallas kernels: 4.84 us -> 2.64 us  [nodal_force(): pl.pallas_call(force_kernel, out_shape=[jax.ShapeDtypeStruct((blocks, ROW...]
    all_to_all x4, waiting for transfers between devices: 4.48 us -> 6.51 us  [exchange(): lax.all_to_all(blocks_out, AXES, split_axis=0, concat_axis=0, tiled=True)]
    ppermute x16, waiting for transfers between devices: 6.58 us -> 4.62 us  [swap(): lax.ppermute(value, axis, pairs)]
  transfers between devices with their start and end apart: 20 -> 20, of which waited for: 5 -> 7; matrix products, arithmetic and copies ran while one was open for 2% -> 0% of each run, Pallas kernels for 33% -> 34%
where the time goes in v3:
time: 103 us; the launch traced here: 102 us
  Pallas kernels  50.3 us (49%)
  starting transfers between devices  31.2 us (30%)
  waiting for transfers between devices  11.1 us (11%)
  local copies, waits for them, and re-layouts  7.86 us (8%)
  between operations  1.65 us (2%)
    pallas_call x4, Pallas kernels, element_forces(): pl.pallas_call(element_kernel, out_shape=jax.ShapeDtypeStruct((blocks, RO...  22.6 us
    all_to_all x4, starting transfers between devices, exchange(): lax.all_to_all(blocks_out, AXES, split_axis=0, concat_axis=0, tiled=True)  21.7 us
    ppermute x16, starting transfers between devices, swap(): lax.ppermute(value, axis, pairs)  9.57 us
    pallas_call x2, Pallas kernels, far_contact(): pl.pallas_call(kernel, out_shape=jax.ShapeDtypeStruct((places, HALF, BLK)...  8.36 us
    pallas_call x2, Pallas kernels, own_contact(): pl.pallas_call(kernel, out_shape=[jax.ShapeDtypeStruct((places, ROWS, BLK...  7.47 us
    unnamed x38, local copies, waits for them, and re-layouts  6.74 us
    all_to_all x4, waiting for transfers between devices, exchange(): lax.all_to_all(blocks_out, AXES, split_axis=0, concat_axis=0, tiled=True)  6.51 us
    ppermute x16, waiting for transfers between devices, swap(): lax.ppermute(value, axis, pairs)  4.62 us
  transfers between devices with their start and end apart: 20, of which 7 were waited for; matrix products, arithmetic and copies ran while one was open for 0% of the time, Pallas kernels for 34%

profile of v3, /device:TPU:0, one launch (start us, length us, event | category | flops | bytes accessed | tf_op | source)
XLA Modules:
  0.0 102.2 jit_solution(14151290608413940875)
XLA Ops:
  5.4 7.3 %all-to-all-start = ((f32[64,8,128]{2,1,0:T(8,128)}), f32[64,8,128]{2,1,0:T(8,128)S(1)}, u32[]{:S(2)}, u32[]{:S(2)}) async-start(f32[64,8,128]{2,1,0:T(8,128)} %prep.1), calls=%async_computation | async-start | bytes 524288 | tf_op jit(solution)/shard_map/all_to_all | solution.py:587
  14.1 3.6 %plan.1.refs_0_ = s32[4,256]{1,0:T(4,128)S(1)} custom-call(s32[1]{0:T(128)S(6)} %copy.17.refs_0_, s32[2,128]{1,0:T(2,128)S(1)} %copy-done.17, s32[8]{0:T(128)S(1)} %compare_select_fusion.4.refs_2_.refs_1_.meta_ref), custom_call_target="tpu_custom_call" | custom-call | tf_op jit(solution)/shard_map/plan/pallas_call | solution.py:199
  20.3 5.7 %element.4.first_ref = f32[32,8,128]{2,1,0:T(8,128)S(1)} custom-call(f32[6,8192]{1,0:T(8,128)S(1)} %copy-done.1, s32[4,8192]{1,0:T(4,128)S(1)} %copy-done.3, bf16[24,24,8192]{2,1,0:T(8,128)(2,1)} %stiff_ref.7, f32[8,8,128]{2,1,0:T(8,128)S(1)} %bitcast.1), custom_call_target="tpu_custom_call" | custom-call | flops 9437184 | bytes 9437184 | tf_op jit(solution)/shard_map/element/pallas_call | solution.py:143
  26.9 1.6 %collective-permute-start.1 = (f32[8,8,128]{2,1,0:T(8,128)S(1)}, f32[8,8,128]{2,1,0:T(8,128)S(1)}, u32[]{:S(2)}, u32[]{:S(2)}) collective-permute-start(f32[8,8,128]{2,1,0:T(8,128)S(1)} %gather_fusion), channel_id=1, source_target_pairs={{0,24},{8,16},{16,8},{24,0},{1,25},{9,17},{17,9},{25,1},{2,26},{10... | collective-permute-start | bytes 98312 | tf_op jit(solution)/shard_map/ppermute | solution.py:547
  28.6 1.5 %collective-permute-start.2 = (f32[8,8,128]{2,1,0:T(8,128)S(1)}, f32[8,8,128]{2,1,0:T(8,128)S(1)}, u32[]{:S(2)}, u32[]{:S(2)}) collective-permute-start(f32[8,8,128]{2,1,0:T(8,128)S(1)} %gather_fusion), channel_id=1, source_target_pairs={{0,1},{1,0},{2,3},{3,2},{4,5},{5,4},{6,7},{7,6},{8,9},{9,8},{10,11... | collective-permute-start | bytes 98312 | tf_op jit(solution)/shard_map/ppermute | solution.py:547
  30.0 3.7 %own_contact.2 = (f32[64,8,128]{2,1,0:T(8,128)S(1)}, bf16[64,16,128]{2,1,0:T(8,128)(2,1)S(1)}) custom-call(s32[4,256]{1,0:T(4,128)S(1)} %plan.1.refs_0_, f32[64,8,128]{2,1,0:T(8,128)S(1)} %all-to-all-done.refs_1_, s32[128,128]{1,0:T(8,128)S(1)} %copy-done.7, s32[128,128]{1,0:T(8,128)S(1)} %copy-done.8), custom_call_target="tpu_custom_call" | custom-call | flops 67108864 | bytes 65536 | tf_op jit(solution)/shard_map/own_contact/pallas_call | solution.py:357
  33.8 4.2 %far_contact.2 = f32[64,4,128]{2,1,0:T(4,128)} custom-call(s32[4,256]{1,0:T(4,128)S(1)} %plan.1.refs_0_, s32[8]{0:T(128)S(1)} %compare_select_fusion.4.refs_2_.refs_1_.meta_ref, f32[8,8,128]{2,1,0:T(8,128)S(1)} %collective-permute-done.refs_2_, f32[8,8,128]{2,1,0:T(8,128)S(1)} %collective-permute-done.1.refs_3_, ...), custom_call_target="tpu_custom_call" | custom-call | flops 67108864 | bytes 65536 | tf_op jit(solution)/shard_map/far_contact/pallas_call | solution.py:386
  38.0 5.2 %all-to-all-start.1 = ((f32[64,4,128]{2,1,0:T(4,128)}), f32[64,4,128]{2,1,0:T(4,128)S(1)}, u32[]{:S(2)}, u32[]{:S(2)}) async-start(f32[64,4,128]{2,1,0:T(4,128)} %far_contact.2), calls=%async_computation.1 | async-start | bytes 262144 | tf_op jit(solution)/shard_map/all_to_all | solution.py:587
  43.2 5.6 %element.5.second_ref = f32[32,8,128]{2,1,0:T(8,128)S(1)} custom-call(f32[6,8192]{1,0:T(8,128)S(1)} %copy-done.2, s32[4,8192]{1,0:T(4,128)S(1)} %copy-done.4, bf16[24,24,8192]{2,1,0:T(8,128)(2,1)} %stiff_ref.7, f32[8,8,128]{2,1,0:T(8,128)S(1)} %bitcast.2), custom_call_target="tpu_custom_call" | custom-call | flops 9437184 | bytes 9437184 | tf_op jit(solution)/shard_map/element/pallas_call | solution.py:143
  48.8 2.2 %all-to-all-done.1.back_ref = f32[64,4,128]{2,1,0:T(4,128)S(1)} async-done(((f32[64,4,128]{2,1,0:T(4,128)}), f32[64,4,128]{2,1,0:T(4,128)S(1)}, u32[]{:S(2)}, u32[]{:S(2)}) %all-to-all-start.1) | async-done | bytes 131104 | tf_op jit(solution)/shard_map/all_to_all | solution.py:587
  51.0 1.3 %force.2 = (f32[64,8,128]{2,1,0:T(8,128)S(1)}, f32[8,128]{1,0:T(8,128)S(1)}, f32[8,128]{1,0:T(8,128)S(1)}, f32[8,128]{1,0:T(8,128)S(1)}, f32[8,128]{1,0:T(8,128)S(1)}) custom-call(s32[64]{0:T(128)S(1)} %copy-done.16, s32[8]{0:T(128)S(1)} %compare_select_fusion.4.refs_2_.refs_1_.meta_ref, f32[64,4,128]{2,1,0:T(4,128)S(1)} %all-to-all-done.1.back_ref, ...), custom_call_target="tpu_custom_call" | custom-call | tf_op jit(solution)/shard_map/force/pallas_call | solution.py:466
  55.5 1.5 %collective-permute-done.6.near2_ref = f32[8,128]{1,0:T(8,128)S(1)} collective-permute-done((f32[8,128]{1,0:T(8,128)S(1)}, f32[8,128]{1,0:T(8,128)S(1)}, u32[]{:S(2)}, u32[]{:S(2)}) %collective-permute-start.6) | collective-permute-done | bytes 4128 | tf_op jit(solution)/shard_map/ppermute | solution.py:547
  57.1 1.8 %update.2 = (f32[6,8192]{1,0:T(8,128)S(1)}, f32[6,8192]{1,0:T(8,128)S(1)}, f32[64,4,128]{2,1,0:T(4,128)}) custom-call(s32[64]{0:T(128)S(1)} %copy-done.16, f32[64,8,128]{2,1,0:T(8,128)S(1)} %get-tuple-element.43.force_ref, f32[8,128]{1,0:T(8,128)S(1)} %collective-permute-done.4.near0_ref, f32[8,128]{1,0:T(8,128)S(1)} %collective-permute-done.5.near1_ref, ...), custom_call_target="tpu_custom_call" | custom-call | tf_op jit(solution)/shard_map/update/pallas_call | solution.py:522
  58.9 4.8 %all-to-all-start.2 = ((f32[64,4,128]{2,1,0:T(4,128)}), f32[64,4,128]{2,1,0:T(4,128)S(1)}, u32[]{:S(2)}, u32[]{:S(2)}) async-start(f32[64,4,128]{2,1,0:T(4,128)} %get-tuple-element.53), calls=%async_computation.2 | async-start | bytes 262144 | tf_op jit(solution)/shard_map/all_to_all | solution.py:587
  63.6 5.6 %element.6.first_ref = f32[32,8,128]{2,1,0:T(8,128)S(1)} custom-call(f32[6,8192]{1,0:T(8,128)S(1)} %get-tuple-element.61.disp_ref, s32[4,8192]{1,0:T(4,128)S(1)} %copy-done.4, bf16[24,24,8192]{2,1,0:T(8,128)(2,1)} %stiff_ref.7, f32[8,8,128]{2,1,0:T(8,128)S(1)} %bitcast.3), custom_call_target="tpu_custom_call" | custom-call | flops 9437184 | bytes 9437184 | tf_op jit(solution)/shard_map/element/pallas_call | solution.py:143
  69.3 2.2 %all-to-all-done.2.refs_2_ = f32[64,4,128]{2,1,0:T(4,128)S(1)} async-done(((f32[64,4,128]{2,1,0:T(4,128)}), f32[64,4,128]{2,1,0:T(4,128)S(1)}, u32[]{:S(2)}, u32[]{:S(2)}) %all-to-all-start.2) | async-done | bytes 131104 | tf_op jit(solution)/shard_map/all_to_all | solution.py:587
  74.1 3.8 %own_contact.3 = (f32[64,8,128]{2,1,0:T(8,128)S(1)}, bf16[64,16,128]{2,1,0:T(8,128)(2,1)S(1)}) custom-call(s32[4,256]{1,0:T(4,128)S(1)} %plan.1.refs_0_, f32[64,8,128]{2,1,0:T(8,128)S(1)} %all-to-all-done.refs_1_, f32[64,4,128]{2,1,0:T(4,128)S(1)} %all-to-all-done.2.refs_2_, s32[128,128]{1,0:T(8,128)S(1)} %copy-done.7, s32[128,128]{1,0:T(8,128)S(1)} %copy-done.8), custom_call_target="tpu_custom_call" | custom-call | flops 67108864 | bytes 65536 | tf_op jit(solution)/shard_map/own_contact/pallas_call | solution.py:357
  77.9 4.2 %far_contact.3 = f32[64,4,128]{2,1,0:T(4,128)} custom-call(s32[4,256]{1,0:T(4,128)S(1)} %plan.1.refs_0_, s32[8]{0:T(128)S(1)} %compare_select_fusion.4.refs_2_.refs_1_.meta_ref, f32[8,8,128]{2,1,0:T(8,128)S(1)} %collective-permute-done.refs_2_, f32[8,8,128]{2,1,0:T(8,128)S(1)} %collective-permute-done.1.refs_3_, ...), custom_call_target="tpu_custom_call" | custom-call | flops 67108864 | bytes 65536 | tf_op jit(solution)/shard_map/far_contact/pallas_call | solution.py:386
  82.1 4.4 %all-to-all-start.3 = ((f32[64,4,128]{2,1,0:T(4,128)}), f32[64,4,128]{2,1,0:T(4,128)S(1)}, u32[]{:S(2)}, u32[]{:S(2)}) async-start(f32[64,4,128]{2,1,0:T(4,128)} %far_contact.3), calls=%async_computation.3 | async-start | bytes 262144 | tf_op jit(solution)/shard_map/all_to_all | solution.py:587
  86.5 5.6 %element.7.second_ref = f32[32,8,128]{2,1,0:T(8,128)S(1)} custom-call(f32[6,8192]{1,0:T(8,128)S(1)} %get-tuple-element.61.disp_ref, s32[4,8192]{1,0:T(4,128)S(1)} %copy-done.4, bf16[24,24,8192]{2,1,0:T(8,128)(2,1)} %stiff_ref.7, f32[8,8,128]{2,1,0:T(8,128)S(1)} %bitcast.4), custom_call_target="tpu_custom_call" | custom-call | flops 9437184 | bytes 9437184 | tf_op jit(solution)/shard_map/element/pallas_call | solution.py:143
  92.1 2.2 %all-to-all-done.3.back_ref = f32[64,4,128]{2,1,0:T(4,128)S(1)} async-done(((f32[64,4,128]{2,1,0:T(4,128)}), f32[64,4,128]{2,1,0:T(4,128)S(1)}, u32[]{:S(2)}, u32[]{:S(2)}) %all-to-all-start.3) | async-done | bytes 131104 | tf_op jit(solution)/shard_map/all_to_all | solution.py:587
  94.3 1.3 %force.3 = (f32[64,8,128]{2,1,0:T(8,128)S(1)}, f32[8,128]{1,0:T(8,128)S(1)}, f32[8,128]{1,0:T(8,128)S(1)}, f32[8,128]{1,0:T(8,128)S(1)}, f32[8,128]{1,0:T(8,128)S(1)}) custom-call(s32[64]{0:T(128)S(1)} %copy-done.16, s32[8]{0:T(128)S(1)} %compare_select_fusion.4.refs_2_.refs_1_.meta_ref, f32[64,4,128]{2,1,0:T(4,128)S(1)} %all-to-all-done.3.back_ref, ...), custom_call_target="tpu_custom_call" | custom-call | tf_op jit(solution)/shard_map/force/pallas_call | solution.py:466
  98.8 1.5 %collective-permute-done.14.near2_ref = f32[8,128]{1,0:T(8,128)S(1)} collective-permute-done((f32[8,128]{1,0:T(8,128)S(1)}, f32[8,128]{1,0:T(8,128)S(1)}, u32[]{:S(2)}, u32[]{:S(2)}) %collective-permute-start.14) | collective-permute-done | bytes 4128 | tf_op jit(solution)/shard_map/ppermute | solution.py:547
  100.3 1.9 %update.3 = (f32[6,8192]{1,0:T(8,128)}, f32[6,8192]{1,0:T(8,128)}) custom-call(s32[64]{0:T(128)S(1)} %copy-done.16, f32[64,8,128]{2,1,0:T(8,128)S(1)} %get-tuple-element.62.force_ref, f32[8,128]{1,0:T(8,128)S(1)} %collective-permute-done.12.near0_ref, f32[8,128]{1,0:T(8,128)S(1)} %collective-permute-done.13.near1_ref, ...), custom_call_target="tpu_custom_call" | custom-call | tf_op jit(solution)/shard_map/update/pallas_call | solution.py:522
  (74 shorter events, 18.0 us)
Async XLA Ops:
  4.1 39.1 %copy-start.2 = (f32[6,8192]{1,0:T(8,128)S(1)}, f32[6,8192]{1,0:T(8,128)}, u32[]{:S(2)}) copy-start(f32[6,8192]{1,0:T(8,128)} %disp_ref.6) | copy-start | bytes 589828
  4.1 39.1 %copy-start.4 = (s32[4,8192]{1,0:T(4,128)S(1)}, s32[4,8192]{1,0:T(4,128)}, u32[]{:S(2)}) copy-start(s32[4,8192]{1,0:T(4,128)} %conn_ref.7) | copy-start | bytes 393220
  4.1 39.1 %copy-start.11 = (f32[8192]{0:T(1024)S(1)}, f32[8192]{0:T(1024)}, u32[]{:S(2)}) copy-start(f32[8192]{0:T(1024)} %param.22) | copy-start | bytes 98308
  5.4 20.7 %all-to-all-start = ((f32[64,8,128]{2,1,0:T(8,128)}), f32[64,8,128]{2,1,0:T(8,128)S(1)}, u32[]{:S(2)}, u32[]{:S(2)}) async-start(f32[64,8,128]{2,1,0:T(8,128)} %prep.1), calls=%async_computation | async-start | bytes 524288 | tf_op jit(solution)/shard_map/all_to_all | solution.py:587
  20.3 36.8 %copy-start.12 = (f32[6,8192]{1,0:T(8,128)S(1)}, f32[6,8192]{1,0:T(8,128)}, u32[]{:S(2)}) copy-start(f32[6,8192]{1,0:T(8,128)} %vel_ref.1) | copy-start | bytes 589828
  26.6 7.1 %collective-permute-start = (f32[8,8,128]{2,1,0:T(8,128)S(1)}, f32[8,8,128]{2,1,0:T(8,128)S(1)}, u32[]{:S(2)}, u32[]{:S(2)}) collective-permute-start(f32[8,8,128]{2,1,0:T(8,128)S(1)} %gather_fusion), channel_id=1, source_target_pairs={{0,8},{8,0},{16,24},{24,16},{1,9},{9,1},{17,25},{25,17},{2,10},{10... | collective-permute-start | bytes 98312 | tf_op jit(solution)/shard_map/ppermute | solution.py:547
  26.9 6.8 %collective-permute-start.1 = (f32[8,8,128]{2,1,0:T(8,128)S(1)}, f32[8,8,128]{2,1,0:T(8,128)S(1)}, u32[]{:S(2)}, u32[]{:S(2)}) collective-permute-start(f32[8,8,128]{2,1,0:T(8,128)S(1)} %gather_fusion), channel_id=1, source_target_pairs={{0,24},{8,16},{16,8},{24,0},{1,25},{9,17},{17,9},{25,1},{2,26},{10... | collective-permute-start | bytes 98312 | tf_op jit(solution)/shard_map/ppermute | solution.py:547
  28.6 5.2 %collective-permute-start.2 = (f32[8,8,128]{2,1,0:T(8,128)S(1)}, f32[8,8,128]{2,1,0:T(8,128)S(1)}, u32[]{:S(2)}, u32[]{:S(2)}) collective-permute-start(f32[8,8,128]{2,1,0:T(8,128)S(1)} %gather_fusion), channel_id=1, source_target_pairs={{0,1},{1,0},{2,3},{3,2},{4,5},{5,4},{6,7},{7,6},{8,9},{9,8},{10,11... | collective-permute-start | bytes 98312 | tf_op jit(solution)/shard_map/ppermute | solution.py:547
  30.0 3.8 %collective-permute-start.3 = (f32[8,8,128]{2,1,0:T(8,128)S(1)}, f32[8,8,128]{2,1,0:T(8,128)S(1)}, u32[]{:S(2)}, u32[]{:S(2)}) collective-permute-start(f32[8,8,128]{2,1,0:T(8,128)S(1)} %gather_fusion), channel_id=1, source_target_pairs={{0,8},{1,2},{2,1},{3,4},{4,3},{5,6},{6,5},{7,15},{8,0},{9,10},{10,... | collective-permute-start | bytes 98312 | tf_op jit(solution)/shard_map/ppermute | solution.py:547
  38.0 13.0 %all-to-all-start.1 = ((f32[64,4,128]{2,1,0:T(4,128)}), f32[64,4,128]{2,1,0:T(4,128)S(1)}, u32[]{:S(2)}, u32[]{:S(2)}) async-start(f32[64,4,128]{2,1,0:T(4,128)} %far_contact.2), calls=%async_computation.1 | async-start | bytes 262144 | tf_op jit(solution)/shard_map/all_to_all | solution.py:587
  52.3 2.8 %collective-permute-start.4 = (f32[8,128]{1,0:T(8,128)S(1)}, f32[8,128]{1,0:T(8,128)S(1)}, u32[]{:S(2)}, u32[]{:S(2)}) collective-permute-start(f32[8,128]{1,0:T(8,128)S(1)} %get-tuple-element.48), channel_id=1, source_target_pairs={{0,8},{8,0},{16,24},{24,16},{1,9},{9,1},{17,25},{25,17},{2,10},{10... | collective-permute-start | bytes 12296 | tf_op jit(solution)/shard_map/ppermute | solution.py:547
  52.5 3.0 %collective-permute-start.5 = (f32[8,128]{1,0:T(8,128)S(1)}, f32[8,128]{1,0:T(8,128)S(1)}, u32[]{:S(2)}, u32[]{:S(2)}) collective-permute-start(f32[8,128]{1,0:T(8,128)S(1)} %get-tuple-element.49), channel_id=1, source_target_pairs={{0,24},{8,16},{16,8},{24,0},{1,25},{9,17},{17,9},{25,1},{2,26},{10... | collective-permute-start | bytes 12296 | tf_op jit(solution)/shard_map/ppermute | solution.py:547
  53.5 3.6 %collective-permute-start.6 = (f32[8,128]{1,0:T(8,128)S(1)}, f32[8,128]{1,0:T(8,128)S(1)}, u32[]{:S(2)}, u32[]{:S(2)}) collective-permute-start(f32[8,128]{1,0:T(8,128)S(1)} %get-tuple-element.50), channel_id=1, source_target_pairs={{0,1},{1,0},{2,3},{3,2},{4,5},{5,4},{6,7},{7,6},{8,9},{9,8},{10,11... | collective-permute-start | bytes 12296 | tf_op jit(solution)/shard_map/ppermute | solution.py:547
  54.4 2.7 %collective-permute-start.7 = (f32[8,128]{1,0:T(8,128)S(1)}, f32[8,128]{1,0:T(8,128)S(1)}, u32[]{:S(2)}, u32[]{:S(2)}) collective-permute-start(f32[8,128]{1,0:T(8,128)S(1)} %get-tuple-element.51), channel_id=1, source_target_pairs={{0,8},{1,2},{2,1},{3,4},{4,3},{5,6},{6,5},{7,15},{8,0},{9,10},{10,... | collective-permute-start | bytes 12296 | tf_op jit(solution)/shard_map/ppermute | solution.py:547
  58.9 12.6 %all-to-all-start.2 = ((f32[64,4,128]{2,1,0:T(4,128)}), f32[64,4,128]{2,1,0:T(4,128)S(1)}, u32[]{:S(2)}, u32[]{:S(2)}) async-start(f32[64,4,128]{2,1,0:T(4,128)} %get-tuple-element.53), calls=%async_computation.2 | async-start | bytes 262144 | tf_op jit(solution)/shard_map/all_to_all | solution.py:587
  72.0 5.8 %collective-permute-start.10 = (f32[8,4,128]{2,1,0:T(4,128)S(1)}, f32[8,4,128]{2,1,0:T(4,128)S(1)}, u32[]{:S(2)}, u32[]{:S(2)}) collective-permute-start(f32[8,4,128]{2,1,0:T(4,128)S(1)} %gather_fusion.1), channel_id=1, source_target_pairs={{0,1},{1,0},{2,3},{3,2},{4,5},{5,4},{6,7},{7,6},{8,9},{9,8},{10,11... | collective-permute-start | bytes 49160 | tf_op jit(solution)/shard_map/ppermute | solution.py:547
  73.2 4.6 %collective-permute-start.11 = (f32[8,4,128]{2,1,0:T(4,128)S(1)}, f32[8,4,128]{2,1,0:T(4,128)S(1)}, u32[]{:S(2)}, u32[]{:S(2)}) collective-permute-start(f32[8,4,128]{2,1,0:T(4,128)S(1)} %gather_fusion.1), channel_id=1, source_target_pairs={{0,8},{1,2},{2,1},{3,4},{4,3},{5,6},{6,5},{7,15},{8,0},{9,10},{10,... | collective-permute-start | bytes 49160 | tf_op jit(solution)/shard_map/ppermute | solution.py:547
  73.2 4.6 %collective-permute-start.8 = (f32[8,4,128]{2,1,0:T(4,128)S(1)}, f32[8,4,128]{2,1,0:T(4,128)S(1)}, u32[]{:S(2)}, u32[]{:S(2)}) collective-permute-start(f32[8,4,128]{2,1,0:T(4,128)S(1)} %gather_fusion.1), channel_id=1, source_target_pairs={{0,8},{8,0},{16,24},{24,16},{1,9},{9,1},{17,25},{25,17},{2,10},{10... | collective-permute-start | bytes 49160 | tf_op jit(solution)/shard_map/ppermute | solution.py:547
  73.7 4.1 %collective-permute-start.9 = (f32[8,4,128]{2,1,0:T(4,128)S(1)}, f32[8,4,128]{2,1,0:T(4,128)S(1)}, u32[]{:S(2)}, u32[]{:S(2)}) collective-permute-start(f32[8,4,128]{2,1,0:T(4,128)S(1)} %gather_fusion.1), channel_id=1, source_target_pairs={{0,24},{8,16},{16,8},{24,0},{1,25},{9,17},{17,9},{25,1},{2,26},{10... | collective-permute-start | bytes 49160 | tf_op jit(solution)/shard_map/ppermute | solution.py:547
  82.1 12.2 %all-to-all-start.3 = ((f32[64,4,128]{2,1,0:T(4,128)}), f32[64,4,128]{2,1,0:T(4,128)S(1)}, u32[]{:S(2)}, u32[]{:S(2)}) async-start(f32[64,4,128]{2,1,0:T(4,128)} %far_contact.3), calls=%async_computation.3 | async-start | bytes 262144 | tf_op jit(solution)/shard_map/all_to_all | solution.py:587
  95.6 2.1 %collective-permute-start.12 = (f32[8,128]{1,0:T(8,128)S(1)}, f32[8,128]{1,0:T(8,128)S(1)}, u32[]{:S(2)}, u32[]{:S(2)}) collective-permute-start(f32[8,128]{1,0:T(8,128)S(1)} %get-tuple-element.63), channel_id=1, source_target_pairs={{0,8},{8,0},{16,24},{24,16},{1,9},{9,1},{17,25},{25,17},{2,10},{10... | collective-permute-start | bytes 12296 | tf_op jit(solution)/shard_map/ppermute | solution.py:547
  95.8 3.0 %collective-permute-start.13 = (f32[8,128]{1,0:T(8,128)S(1)}, f32[8,128]{1,0:T(8,128)S(1)}, u32[]{:S(2)}, u32[]{:S(2)}) collective-permute-start(f32[8,128]{1,0:T(8,128)S(1)} %get-tuple-element.64), channel_id=1, source_target_pairs={{0,24},{8,16},{16,8},{24,0},{1,25},{9,17},{17,9},{25,1},{2,26},{10... | collective-permute-start | bytes 12296 | tf_op jit(solution)/shard_map/ppermute | solution.py:547
  96.7 3.6 %collective-permute-start.14 = (f32[8,128]{1,0:T(8,128)S(1)}, f32[8,128]{1,0:T(8,128)S(1)}, u32[]{:S(2)}, u32[]{:S(2)}) collective-permute-start(f32[8,128]{1,0:T(8,128)S(1)} %get-tuple-element.65), channel_id=1, source_target_pairs={{0,1},{1,0},{2,3},{3,2},{4,5},{5,4},{6,7},{7,6},{8,9},{9,8},{10,11... | collective-permute-start | bytes 12296 | tf_op jit(solution)/shard_map/ppermute | solution.py:547
  97.6 2.7 %collective-permute-start.15 = (f32[8,128]{1,0:T(8,128)S(1)}, f32[8,128]{1,0:T(8,128)S(1)}, u32[]{:S(2)}, u32[]{:S(2)}) collective-permute-start(f32[8,128]{1,0:T(8,128)S(1)} %get-tuple-element.66), channel_id=1, source_target_pairs={{0,8},{1,2},{2,1},{3,4},{4,3},{5,6},{6,5},{7,15},{8,0},{9,10},{10,... | collective-permute-start | bytes 12296 | tf_op jit(solution)/shard_map/ppermute | solution.py:547
  (15 other events, 215.7 us)

commit v4 on v3

--- a/solution.py
+++ b/solution.py
@@ -34,6 +34,14 @@
 
 def limit(mebibytes):
     return pltpu.CompilerParams(vmem_limit_bytes=mebibytes << 20)
+
+
+def held(x):
+    return pltpu.with_memory_space_constraint(x, pltpu.VMEM)
+
+
+def left(x):
+    return pltpu.with_memory_space_constraint(x, pltpu.HBM)
 
 
 def lane_gather(data, index):
@@ -65,7 +73,7 @@
         out_specs=vspec(),
         compiler_params=limit(4),
         name="prep",
-    )(block_slot, displacement, ref_pos, normals)
+    )(block_slot, left(displacement), left(ref_pos), left(normals))
 
 
 def fold_rows(tiles, row):
@@ -84,15 +92,28 @@
     return jnp.where(low1, a + pltpu.roll(a, 7, 0), b + pltpu.roll(b, 1, 0))
 
 
-def element_kernel(disp_ref, conn_ref, stiff_ref, yield_ref, out_ref):
+def element_kernel(
+    disp_ref, conn_ref, hbm_ref, yield_ref, out_ref, stiff_ref, sems, *, origin
+):
+    wide = EBLK * BLK
+    turns = out_ref.shape[0] // EBLK
+
+    def load(r):
+        return pltpu.make_async_copy(
+            hbm_ref.at[:, :, pl.ds(origin * BLK + r * wide, wide)], stiff_ref.at[r], sems.at[r]
+        )
+
+    for r in range(turns):
+        load(r).start()
     row = lax.broadcasted_iota(jnp.int32, (ROWS, BLK), 0)
     row48 = lax.broadcasted_iota(jnp.int32, (48, BLK), 0)
     node = lax.broadcasted_iota(jnp.int32, (BLK, BLK), 0).astype(jnp.int16)
     unit = jnp.ones((), BF16)
     zero = jnp.zeros((), BF16)
     row48 = row48.astype(jnp.int16) & 3
-    for k in range(out_ref.shape[0]):
-        lanes = slice(k * BLK, (k + 1) * BLK)
+    def one_block(r, d):
+        k = r * EBLK + d
+        lanes = pl.ds(pl.multiple_of((origin + k) * BLK, BLK), BLK)
         local = conn_ref[:, lanes] & (BLK - 1)
         index = jnp.concatenate([local, local], axis=0)
         dofs = []
@@ -104,14 +125,14 @@
         for g in range(3):
             tiles = []
             for i in range(8 * g, 8 * g + 8):
-                line = stiff_ref[i, :, lanes].astype(F32)
+                line = stiff_ref[r, i, :, d * BLK : (d + 1) * BLK].astype(F32)
                 tiles.append(line[0:8] * dofs[0] + line[8:16] * dofs[1] + line[16:24] * dofs[2])
             trial.append(fold_rows(tiles, row))
         squared = trial[0] * trial[0] + trial[1] * trial[1] + trial[2] * trial[2]
         squared = squared + pltpu.roll(squared, 4, 0)
         squared = squared + pltpu.roll(squared, 2, 0)
         squared = squared + pltpu.roll(squared, 1, 0)
-        level = yield_ref[0, k : k + 1, :]
+        level = yield_ref[pl.ds(origin + k, 1), :]
         factor = lax.rsqrt(1.0 + squared / (level * level))
         forces = jnp.concatenate([t * factor for t in trial], axis=0)
         high, low = split(forces)
@@ -133,35 +154,37 @@
             pieces += [x[0:1], x[4:5]]
         out_ref[k] = jnp.concatenate(pieces + [jnp.zeros((2, BLK), F32)], axis=0)
 
+    def body(r, carry):
+        load(r).wait()
+        for d in range(EBLK):
+            one_block(r, d)
+        return carry
+
+    lax.fori_loop(0, turns, body, 0)
+
 
 def element_forces(displacement, connectivity, stiffness, yield_force, part=0, parts=1):
     nodes = displacement.shape[1]
     blocks = nodes // BLK // parts
-    wide = EBLK * BLK
-    steps = blocks // EBLK
-    first = part * steps
-    return pl.pallas_call(
-        element_kernel,
+
+    def kernel(*refs):
+        element_kernel(*refs, origin=part * blocks)
+
+    return pl.pallas_call(
+        kernel,
         out_shape=jax.ShapeDtypeStruct((blocks, ROWS, BLK), F32),
-        grid=(steps,),
-        in_specs=[
-            pl.BlockSpec((6, wide), lambda i: (0, i + first)),
-            pl.BlockSpec((4, wide), lambda i: (0, i + first)),
-            pl.BlockSpec((24, 24, wide), lambda i: (0, 0, i + first)),
-            pl.BlockSpec((1, EBLK, BLK), lambda i: (i + first, 0, 0)),
+        in_specs=[vspec()] * 2 + [pl.BlockSpec(memory_space=pltpu.HBM)] + [vspec()],
+        out_specs=vspec(),
+        scratch_shapes=[
+            VMEM((blocks // EBLK, 24, 24, EBLK * BLK), BF16),
+            pltpu.SemaphoreType.DMA((blocks // EBLK,)),
         ],
-        out_specs=pl.BlockSpec((EBLK, ROWS, BLK), lambda i: (i, 0, 0)),
         cost_estimate=pl.CostEstimate(
             flops=2 * 576 * nodes, transcendentals=nodes, bytes_accessed=2 * 576 * nodes
         ),
-        compiler_params=limit(10),
+        compiler_params=limit(12),
         name="element",
-    )(
-        displacement,
-        connectivity,
-        pltpu.with_memory_space_constraint(stiffness, pltpu.HBM),
-        yield_force.reshape(-1, EBLK, BLK),
-    )
+    )(displacement, connectivity, left(stiffness), yield_force.reshape(-1, BLK))
 
 
 def plan_kernel(count_ref, pairs_ref, meta_ref, plan_ref, *, places, edges):
@@ -187,7 +210,13 @@
         plan_ref[2, where] = jnp.where(is_own, master, places + moved)
         return own + is_own.astype(jnp.int32)
 
-    own = lax.fori_loop(0, count_ref[0], sort, jnp.int32(0))
+    def several(r, own):
+        for d in range(8):
+            own = sort(8 * r + d, own)
+        return own
+
+    own = lax.fori_loop(0, count_ref[0] // 8, several, jnp.int32(0))
+    own = lax.fori_loop(count_ref[0] // 8 * 8, count_ref[0], sort, own)
     plan_ref[3, 0] = own
     plan_ref[3, 1] = count_ref[0] - own
 
@@ -234,14 +263,30 @@
 
     def at(group, d):
         i = group * GROUP + d
-        return first + jnp.clip(i, 0, last), jnp.logical_and(i >= 0, i < number)
-
-    def body(r, carry):
+        return first + jnp.minimum(i, last), i < number
+
+    def depths(group):
+        for d in range(0, GROUP, 2):
+            facets, nodes = [], []
+            for e in range(2):
+                i, _ = at(group, d + e)
+                facets.append(master_tab[plan_ref[2, i] - base])
+                nodes.append(slave_tab[plan_ref[1, i]])
+            left = jnp.concatenate([nodes[0], blank], axis=0)
+            right = jnp.concatenate([blank, nodes[1]], axis=0)
+            depth_ref[d // 2] = lax.dot_general(
+                jnp.concatenate(facets, axis=0),
+                jnp.concatenate([left, right], axis=1),
+                (((0,), (0,)), ((), ())),
+                preferred_element_type=F32,
+            )
+
+    def body(group, carry):
         forces = []
         for d in range(0, GROUP, 2):
             starts, lengths, rows = [], [], []
             for e in range(2):
-                i, live = at(r - 1, d + e)
+                i, live = at(group, d + e)
                 t = plan_ref[0, i]
                 starts.append(start_ref[pl.ds(t, 1), :])
                 lengths.append(jnp.where(live, length_ref[pl.ds(t, 1), :], 0))
@@ -262,29 +307,17 @@
                     preferred_element_type=F32,
                 )
             )
-        for d in range(0, GROUP, 2):
-            facets, nodes = [], []
-            for e in range(2):
-                i, _ = at(r, d + e)
-                facets.append(master_tab[plan_ref[2, i] - base])
-                nodes.append(slave_tab[plan_ref[1, i]])
-            left = jnp.concatenate([nodes[0], blank], axis=0)
-            right = jnp.concatenate([blank, nodes[1]], axis=0)
-            depth_ref[d // 2] = lax.dot_general(
-                jnp.concatenate(facets, axis=0),
-                jnp.concatenate([left, right], axis=1),
-                (((0,), (0,)), ((), ())),
-                preferred_element_type=F32,
-            )
+        depths(group + 1)
         for d in range(GROUP):
-            i, _ = at(r - 1, d)
+            i, _ = at(group, d)
             e = d % 2
             slave = plan_ref[1, i]
             part = forces[d // 2][8 * e : 8 * e + 8, e * BLK : (e + 1) * BLK]
             total_ref[slave] = total_ref[slave] + part
         return carry
 
-    lax.fori_loop(0, (number + GROUP - 1) // GROUP + 1, body, 0)
+    depths(0)
+    lax.fori_loop(0, (number + GROUP - 1) // GROUP, body, 0)
 
 
 def own_kernel(plan_ref, recv_ref, *refs, fresh):

time: 103 us -> 97.7 us (0.949)
  Pallas kernels: 50.3 us -> 47.4 us
  local copies, waits for them, and re-layouts: 7.86 us -> 5.16 us
  waiting for transfers between devices: 11.1 us -> 12.3 us
    unnamed x38 -> x32, local copies, waits for them, and re-layouts: 6.74 us -> 4.03 us
    pallas_call x4, Pallas kernels: 22.6 us -> 21 us  [element_forces(): pl.pallas_call(kernel, out_shape=jax.ShapeDtypeStruct((blocks, ROWS, BLK)...]
    all_to_all x4, waiting for transfers between devices: 6.51 us -> 7.64 us  [exchange(): lax.all_to_all(blocks_out, AXES, split_axis=0, concat_axis=0, tiled=True)]
  transfers between devices with their start and end apart: 20 -> 20, of which waited for: 7 -> 7; matrix products, arithmetic and copies ran while one was open for 0% -> 0% of each run, Pallas kernels for 34% -> 32%
where the time goes in v4:
time: 97.7 us; the launch traced here: 97.2 us
  Pallas kernels  47.4 us (49%)
  starting transfers between devices  30.7 us (31%)
  waiting for transfers between devices  12.3 us (13%)
  local copies, waits for them, and re-layouts  5.16 us (5%)
  between operations  1.67 us (2%)
    all_to_all x4, starting transfers between devices, exchange(): lax.all_to_all(blocks_out, AXES, split_axis=0, concat_axis=0, tiled=True)  21.1 us
    pallas_call x4, Pallas kernels, element_forces(): pl.pallas_call(kernel, out_shape=jax.ShapeDtypeStruct((blocks, ROWS, BLK)...  21 us
    ppermute x16, starting transfers between devices, swap(): lax.ppermute(value, axis, pairs)  9.59 us
    pallas_call x2, Pallas kernels, far_contact(): pl.pallas_call(kernel, out_shape=jax.ShapeDtypeStruct((places, HALF, BLK)...  7.88 us
    all_to_all x4, waiting for transfers between devices, exchange(): lax.all_to_all(blocks_out, AXES, split_axis=0, concat_axis=0, tiled=True)  7.64 us
    pallas_call x2, Pallas kernels, own_contact(): pl.pallas_call(kernel, out_shape=[jax.ShapeDtypeStruct((places, ROWS, BLK...  6.97 us
    ppermute x16, waiting for transfers between devices, swap(): lax.ppermute(value, axis, pairs)  4.62 us
    unnamed x32, local copies, waits for them, and re-layouts  4.03 us
  transfers between devices with their start and end apart: 20, of which 7 were waited for; matrix products, arithmetic and copies ran while one was open for 0% of the time, Pallas kernels for 32%

profile of v4, /device:TPU:0, one launch (start us, length us, event | category | flops | bytes accessed | tf_op | source)
XLA Modules:
  0.0 97.2 jit_solution(10731225534429027489)
XLA Ops:
  1.4 1.8 %prep.1 = f32[64,8,128]{2,1,0:T(8,128)} custom-call(s32[64]{0:T(128)S(1)} %copy-done.12, f32[6,8192]{1,0:T(8,128)} %disp_ref.3, f32[3,8192]{1,0:T(4,128)} %pos_ref.5, f32[3,8192]{1,0:T(4,128)} %nrm_ref.1), custom_call_target="tpu_custom_call" | custom-call | tf_op jit(solution)/shard_map/prep/pallas_call | solution.py:69
  3.2 7.3 %all-to-all-start = ((f32[64,8,128]{2,1,0:T(8,128)}), f32[64,8,128]{2,1,0:T(8,128)S(1)}, u32[]{:S(2)}, u32[]{:S(2)}) async-start(f32[64,8,128]{2,1,0:T(8,128)} %prep.1), calls=%async_computation | async-start | bytes 524288 | tf_op jit(solution)/shard_map/all_to_all | solution.py:620
  11.9 2.6 %plan.1.refs_0_ = s32[4,256]{1,0:T(4,128)S(1)} custom-call(s32[1]{0:T(128)S(6)} %copy.17.refs_0_, s32[2,128]{1,0:T(2,128)S(1)} %copy-done.14, s32[8]{0:T(128)S(1)} %compare_select_fusion.4.refs_2_.refs_1_.meta_ref), custom_call_target="tpu_custom_call" | custom-call | tf_op jit(solution)/shard_map/plan/pallas_call | solution.py:228
  17.2 5.3 %element.4.first_ref = f32[32,8,128]{2,1,0:T(8,128)S(1)} custom-call(f32[6,8192]{1,0:T(8,128)S(1)} %copy-done, s32[4,8192]{1,0:T(4,128)S(1)} %copy-done.2, bf16[24,24,8192]{2,1,0:T(8,128)(2,1)} %refs_2_.9, f32[64,128]{1,0:T(8,128)S(1)} %bitcast.1), custom_call_target="tpu_custom_call" | custom-call | flops 9437184 | bytes 9437184 | tf_op jit(solution)/shard_map/element/pallas_call | solution.py:173
  23.4 1.6 %collective-permute-start.1 = (f32[8,8,128]{2,1,0:T(8,128)S(1)}, f32[8,8,128]{2,1,0:T(8,128)S(1)}, u32[]{:S(2)}, u32[]{:S(2)}) collective-permute-start(f32[8,8,128]{2,1,0:T(8,128)S(1)} %gather_fusion), channel_id=1, source_target_pairs={{0,24},{8,16},{16,8},{24,0},{1,25},{9,17},{17,9},{25,1},{2,26},{10... | collective-permute-start | bytes 98312 | tf_op jit(solution)/shard_map/ppermute | solution.py:580
  25.1 1.5 %collective-permute-start.2 = (f32[8,8,128]{2,1,0:T(8,128)S(1)}, f32[8,8,128]{2,1,0:T(8,128)S(1)}, u32[]{:S(2)}, u32[]{:S(2)}) collective-permute-start(f32[8,8,128]{2,1,0:T(8,128)S(1)} %gather_fusion), channel_id=1, source_target_pairs={{0,1},{1,0},{2,3},{3,2},{4,5},{5,4},{6,7},{7,6},{8,9},{9,8},{10,11... | collective-permute-start | bytes 98312 | tf_op jit(solution)/shard_map/ppermute | solution.py:580
  26.6 3.5 %own_contact.2 = (f32[64,8,128]{2,1,0:T(8,128)S(1)}, bf16[64,16,128]{2,1,0:T(8,128)(2,1)S(1)}) custom-call(s32[4,256]{1,0:T(4,128)S(1)} %plan.1.refs_0_, f32[64,8,128]{2,1,0:T(8,128)S(1)} %all-to-all-done.refs_1_, s32[128,128]{1,0:T(8,128)S(1)} %copy-done.5, s32[128,128]{1,0:T(8,128)S(1)} %copy-done.6), custom_call_target="tpu_custom_call" | custom-call | flops 67108864 | bytes 65536 | tf_op jit(solution)/shard_map/own_contact/pallas_call | solution.py:390
  30.1 3.9 %far_contact.2 = f32[64,4,128]{2,1,0:T(4,128)} custom-call(s32[4,256]{1,0:T(4,128)S(1)} %plan.1.refs_0_, s32[8]{0:T(128)S(1)} %compare_select_fusion.4.refs_2_.refs_1_.meta_ref, f32[8,8,128]{2,1,0:T(8,128)S(1)} %collective-permute-done.refs_2_, f32[8,8,128]{2,1,0:T(8,128)S(1)} %collective-permute-done.1.refs_3_, ...), custom_call_target="tpu_custom_call" | custom-call | flops 67108864 | bytes 65536 | tf_op jit(solution)/shard_map/far_contact/pallas_call | solution.py:419
  34.0 5.2 %all-to-all-start.1 = ((f32[64,4,128]{2,1,0:T(4,128)}), f32[64,4,128]{2,1,0:T(4,128)S(1)}, u32[]{:S(2)}, u32[]{:S(2)}) async-start(f32[64,4,128]{2,1,0:T(4,128)} %far_contact.2), calls=%async_computation.1 | async-start | bytes 262144 | tf_op jit(solution)/shard_map/all_to_all | solution.py:620
  39.2 5.2 %element.5.second_ref = f32[32,8,128]{2,1,0:T(8,128)S(1)} custom-call(f32[6,8192]{1,0:T(8,128)S(1)} %copy-done.1, s32[4,8192]{1,0:T(4,128)S(1)} %copy-done.3, bf16[24,24,8192]{2,1,0:T(8,128)(2,1)} %refs_2_.9, f32[64,128]{1,0:T(8,128)S(1)} %bitcast.2), custom_call_target="tpu_custom_call" | custom-call | flops 9437184 | bytes 9437184 | tf_op jit(solution)/shard_map/element/pallas_call | solution.py:173
  44.5 2.5 %all-to-all-done.1.back_ref = f32[64,4,128]{2,1,0:T(4,128)S(1)} async-done(((f32[64,4,128]{2,1,0:T(4,128)}), f32[64,4,128]{2,1,0:T(4,128)S(1)}, u32[]{:S(2)}, u32[]{:S(2)}) %all-to-all-start.1) | async-done | bytes 131104 | tf_op jit(solution)/shard_map/all_to_all | solution.py:620
  47.0 1.3 %force.2 = (f32[64,8,128]{2,1,0:T(8,128)S(1)}, f32[8,128]{1,0:T(8,128)S(1)}, f32[8,128]{1,0:T(8,128)S(1)}, f32[8,128]{1,0:T(8,128)S(1)}, f32[8,128]{1,0:T(8,128)S(1)}) custom-call(s32[64]{0:T(128)S(1)} %copy-done.13, s32[8]{0:T(128)S(1)} %compare_select_fusion.4.refs_2_.refs_1_.meta_ref, f32[64,4,128]{2,1,0:T(4,128)S(1)} %all-to-all-done.1.back_ref, ...), custom_call_target="tpu_custom_call" | custom-call | tf_op jit(solution)/shard_map/force/pallas_call | solution.py:499
  51.5 1.5 %collective-permute-done.6.near2_ref = f32[8,128]{1,0:T(8,128)S(1)} collective-permute-done((f32[8,128]{1,0:T(8,128)S(1)}, f32[8,128]{1,0:T(8,128)S(1)}, u32[]{:S(2)}, u32[]{:S(2)}) %collective-permute-start.6) | collective-permute-done | bytes 4128 | tf_op jit(solution)/shard_map/ppermute | solution.py:580
  53.1 1.8 %update.2 = (f32[6,8192]{1,0:T(8,128)S(1)}, f32[6,8192]{1,0:T(8,128)S(1)}, f32[64,4,128]{2,1,0:T(4,128)}) custom-call(s32[64]{0:T(128)S(1)} %copy-done.13, f32[64,8,128]{2,1,0:T(8,128)S(1)} %get-tuple-element.43.force_ref, f32[8,128]{1,0:T(8,128)S(1)} %collective-permute-done.4.near0_ref, f32[8,128]{1,0:T(8,128)S(1)} %collective-permute-done.5.near1_ref, ...), custom_call_target="tpu_custom_call" | custom-call | tf_op jit(solution)/shard_map/update/pallas_call | solution.py:555
  54.9 4.5 %all-to-all-start.2 = ((f32[64,4,128]{2,1,0:T(4,128)}), f32[64,4,128]{2,1,0:T(4,128)S(1)}, u32[]{:S(2)}, u32[]{:S(2)}) async-start(f32[64,4,128]{2,1,0:T(4,128)} %get-tuple-element.53), calls=%async_computation.2 | async-start | bytes 262144 | tf_op jit(solution)/shard_map/all_to_all | solution.py:620
  59.4 5.2 %element.6.first_ref = f32[32,8,128]{2,1,0:T(8,128)S(1)} custom-call(f32[6,8192]{1,0:T(8,128)S(1)} %get-tuple-element.61.refs_0_.disp_ref, s32[4,8192]{1,0:T(4,128)S(1)} %copy-done.3, bf16[24,24,8192]{2,1,0:T(8,128)(2,1)} %refs_2_.9, f32[64,128]{1,0:T(8,128)S(1)} %bitcast.3), custom_call_target="tpu_custom_call" | custom-call | flops 9437184 | bytes 9437184 | tf_op jit(solution)/shard_map/element/pallas_call | solution.py:173
  64.6 2.6 %all-to-all-done.2.refs_2_ = f32[64,4,128]{2,1,0:T(4,128)S(1)} async-done(((f32[64,4,128]{2,1,0:T(4,128)}), f32[64,4,128]{2,1,0:T(4,128)S(1)}, u32[]{:S(2)}, u32[]{:S(2)}) %all-to-all-start.2) | async-done | bytes 131104 | tf_op jit(solution)/shard_map/all_to_all | solution.py:620
  69.8 3.5 %own_contact.3 = (f32[64,8,128]{2,1,0:T(8,128)S(1)}, bf16[64,16,128]{2,1,0:T(8,128)(2,1)S(1)}) custom-call(s32[4,256]{1,0:T(4,128)S(1)} %plan.1.refs_0_, f32[64,8,128]{2,1,0:T(8,128)S(1)} %all-to-all-done.refs_1_, f32[64,4,128]{2,1,0:T(4,128)S(1)} %all-to-all-done.2.refs_2_, s32[128,128]{1,0:T(8,128)S(1)} %copy-done.5, s32[128,128]{1,0:T(8,128)S(1)} %copy-done.6), custom_call_target="tpu_custom_call" | custom-call | flops 67108864 | bytes 65536 | tf_op jit(solution)/shard_map/own_contact/pallas_call | solution.py:390
  73.4 3.9 %far_contact.3 = f32[64,4,128]{2,1,0:T(4,128)} custom-call(s32[4,256]{1,0:T(4,128)S(1)} %plan.1.refs_0_, s32[8]{0:T(128)S(1)} %compare_select_fusion.4.refs_2_.refs_1_.meta_ref, f32[8,8,128]{2,1,0:T(8,128)S(1)} %collective-permute-done.refs_2_, f32[8,8,128]{2,1,0:T(8,128)S(1)} %collective-permute-done.1.refs_3_, ...), custom_call_target="tpu_custom_call" | custom-call | flops 67108864 | bytes 65536 | tf_op jit(solution)/shard_map/far_contact/pallas_call | solution.py:419
  77.3 4.1 %all-to-all-start.3 = ((f32[64,4,128]{2,1,0:T(4,128)}), f32[64,4,128]{2,1,0:T(4,128)S(1)}, u32[]{:S(2)}, u32[]{:S(2)}) async-start(f32[64,4,128]{2,1,0:T(4,128)} %far_contact.3), calls=%async_computation.3 | async-start | bytes 262144 | tf_op jit(solution)/shard_map/all_to_all | solution.py:620
  81.5 5.2 %element.7.second_ref = f32[32,8,128]{2,1,0:T(8,128)S(1)} custom-call(f32[6,8192]{1,0:T(8,128)S(1)} %get-tuple-element.61.refs_0_.disp_ref, s32[4,8192]{1,0:T(4,128)S(1)} %copy-done.3, bf16[24,24,8192]{2,1,0:T(8,128)(2,1)} %refs_2_.9, f32[64,128]{1,0:T(8,128)S(1)} %bitcast.4), custom_call_target="tpu_custom_call" | custom-call | flops 9437184 | bytes 9437184 | tf_op jit(solution)/shard_map/element/pallas_call | solution.py:173
  86.7 2.6 %all-to-all-done.3.back_ref = f32[64,4,128]{2,1,0:T(4,128)S(1)} async-done(((f32[64,4,128]{2,1,0:T(4,128)}), f32[64,4,128]{2,1,0:T(4,128)S(1)}, u32[]{:S(2)}, u32[]{:S(2)}) %all-to-all-start.3) | async-done | bytes 131104 | tf_op jit(solution)/shard_map/all_to_all | solution.py:620
  93.8 1.5 %collective-permute-done.14.near2_ref = f32[8,128]{1,0:T(8,128)S(1)} collective-permute-done((f32[8,128]{1,0:T(8,128)S(1)}, f32[8,128]{1,0:T(8,128)S(1)}, u32[]{:S(2)}, u32[]{:S(2)}) %collective-permute-start.14) | collective-permute-done | bytes 4128 | tf_op jit(solution)/shard_map/ppermute | solution.py:580
  95.3 1.9 %update.3 = (f32[6,8192]{1,0:T(8,128)}, f32[6,8192]{1,0:T(8,128)}) custom-call(s32[64]{0:T(128)S(1)} %copy-done.13, f32[64,8,128]{2,1,0:T(8,128)S(1)} %get-tuple-element.62.force_ref, f32[8,128]{1,0:T(8,128)S(1)} %collective-permute-done.12.near0_ref, f32[8,128]{1,0:T(8,128)S(1)} %collective-permute-done.13.near1_ref, ...), custom_call_target="tpu_custom_call" | custom-call | tf_op jit(solution)/shard_map/update/pallas_call | solution.py:555
  (68 shorter events, 15.3 us)
Async XLA Ops:
  0.6 38.6 %copy-start.1 = (f32[6,8192]{1,0:T(8,128)S(1)}, f32[6,8192]{1,0:T(8,128)}, u32[]{:S(2)}) copy-start(f32[6,8192]{1,0:T(8,128)} %disp_ref.3) | copy-start | bytes 589828
  0.6 38.6 %copy-start.9 = (f32[8192]{0:T(1024)S(1)}, f32[8192]{0:T(1024)}, u32[]{:S(2)}) copy-start(f32[8192]{0:T(1024)} %param.22) | copy-start | bytes 98308
  0.7 38.6 %copy-start.3 = (s32[4,8192]{1,0:T(4,128)S(1)}, s32[4,8192]{1,0:T(4,128)}, u32[]{:S(2)}) copy-start(s32[4,8192]{1,0:T(4,128)} %refs_1_.9) | copy-start | bytes 393220
  3.2 19.3 %all-to-all-start = ((f32[64,8,128]{2,1,0:T(8,128)}), f32[64,8,128]{2,1,0:T(8,128)S(1)}, u32[]{:S(2)}, u32[]{:S(2)}) async-start(f32[64,8,128]{2,1,0:T(8,128)} %prep.1), calls=%async_computation | async-start | bytes 524288 | tf_op jit(solution)/shard_map/all_to_all | solution.py:620
  17.2 35.9 %copy-start.10 = (f32[6,8192]{1,0:T(8,128)S(1)}, f32[6,8192]{1,0:T(8,128)}, u32[]{:S(2)}) copy-start(f32[6,8192]{1,0:T(8,128)} %vel_ref.1) | copy-start | bytes 589828
  23.1 6.9 %collective-permute-start = (f32[8,8,128]{2,1,0:T(8,128)S(1)}, f32[8,8,128]{2,1,0:T(8,128)S(1)}, u32[]{:S(2)}, u32[]{:S(2)}) collective-permute-start(f32[8,8,128]{2,1,0:T(8,128)S(1)} %gather_fusion), channel_id=1, source_target_pairs={{0,8},{8,0},{16,24},{24,16},{1,9},{9,1},{17,25},{25,17},{2,10},{10... | collective-permute-start | bytes 98312 | tf_op jit(solution)/shard_map/ppermute | solution.py:580
  23.4 6.6 %collective-permute-start.1 = (f32[8,8,128]{2,1,0:T(8,128)S(1)}, f32[8,8,128]{2,1,0:T(8,128)S(1)}, u32[]{:S(2)}, u32[]{:S(2)}) collective-permute-start(f32[8,8,128]{2,1,0:T(8,128)S(1)} %gather_fusion), channel_id=1, source_target_pairs={{0,24},{8,16},{16,8},{24,0},{1,25},{9,17},{17,9},{25,1},{2,26},{10... | collective-permute-start | bytes 98312 | tf_op jit(solution)/shard_map/ppermute | solution.py:580
  25.1 5.0 %collective-permute-start.2 = (f32[8,8,128]{2,1,0:T(8,128)S(1)}, f32[8,8,128]{2,1,0:T(8,128)S(1)}, u32[]{:S(2)}, u32[]{:S(2)}) collective-permute-start(f32[8,8,128]{2,1,0:T(8,128)S(1)} %gather_fusion), channel_id=1, source_target_pairs={{0,1},{1,0},{2,3},{3,2},{4,5},{5,4},{6,7},{7,6},{8,9},{9,8},{10,11... | collective-permute-start | bytes 98312 | tf_op jit(solution)/shard_map/ppermute | solution.py:580
  26.5 3.5 %collective-permute-start.3 = (f32[8,8,128]{2,1,0:T(8,128)S(1)}, f32[8,8,128]{2,1,0:T(8,128)S(1)}, u32[]{:S(2)}, u32[]{:S(2)}) collective-permute-start(f32[8,8,128]{2,1,0:T(8,128)S(1)} %gather_fusion), channel_id=1, source_target_pairs={{0,8},{1,2},{2,1},{3,4},{4,3},{5,6},{6,5},{7,15},{8,0},{9,10},{10,... | collective-permute-start | bytes 98312 | tf_op jit(solution)/shard_map/ppermute | solution.py:580
  34.0 13.0 %all-to-all-start.1 = ((f32[64,4,128]{2,1,0:T(4,128)}), f32[64,4,128]{2,1,0:T(4,128)S(1)}, u32[]{:S(2)}, u32[]{:S(2)}) async-start(f32[64,4,128]{2,1,0:T(4,128)} %far_contact.2), calls=%async_computation.1 | async-start | bytes 262144 | tf_op jit(solution)/shard_map/all_to_all | solution.py:620
  48.3 2.8 %collective-permute-start.4 = (f32[8,128]{1,0:T(8,128)S(1)}, f32[8,128]{1,0:T(8,128)S(1)}, u32[]{:S(2)}, u32[]{:S(2)}) collective-permute-start(f32[8,128]{1,0:T(8,128)S(1)} %get-tuple-element.48), channel_id=1, source_target_pairs={{0,8},{8,0},{16,24},{24,16},{1,9},{9,1},{17,25},{25,17},{2,10},{10... | collective-permute-start | bytes 12296 | tf_op jit(solution)/shard_map/ppermute | solution.py:580
  48.5 3.0 %collective-permute-start.5 = (f32[8,128]{1,0:T(8,128)S(1)}, f32[8,128]{1,0:T(8,128)S(1)}, u32[]{:S(2)}, u32[]{:S(2)}) collective-permute-start(f32[8,128]{1,0:T(8,128)S(1)} %get-tuple-element.49), channel_id=1, source_target_pairs={{0,24},{8,16},{16,8},{24,0},{1,25},{9,17},{17,9},{25,1},{2,26},{10... | collective-permute-start | bytes 12296 | tf_op jit(solution)/shard_map/ppermute | solution.py:580
  49.5 3.6 %collective-permute-start.6 = (f32[8,128]{1,0:T(8,128)S(1)}, f32[8,128]{1,0:T(8,128)S(1)}, u32[]{:S(2)}, u32[]{:S(2)}) collective-permute-start(f32[8,128]{1,0:T(8,128)S(1)} %get-tuple-element.50), channel_id=1, source_target_pairs={{0,1},{1,0},{2,3},{3,2},{4,5},{5,4},{6,7},{7,6},{8,9},{9,8},{10,11... | collective-permute-start | bytes 12296 | tf_op jit(solution)/shard_map/ppermute | solution.py:580
  50.4 2.7 %collective-permute-start.7 = (f32[8,128]{1,0:T(8,128)S(1)}, f32[8,128]{1,0:T(8,128)S(1)}, u32[]{:S(2)}, u32[]{:S(2)}) collective-permute-start(f32[8,128]{1,0:T(8,128)S(1)} %get-tuple-element.51), channel_id=1, source_target_pairs={{0,8},{1,2},{2,1},{3,4},{4,3},{5,6},{6,5},{7,15},{8,0},{9,10},{10,... | collective-permute-start | bytes 12296 | tf_op jit(solution)/shard_map/ppermute | solution.py:580
  54.9 12.3 %all-to-all-start.2 = ((f32[64,4,128]{2,1,0:T(4,128)}), f32[64,4,128]{2,1,0:T(4,128)S(1)}, u32[]{:S(2)}, u32[]{:S(2)}) async-start(f32[64,4,128]{2,1,0:T(4,128)} %get-tuple-element.53), calls=%async_computation.2 | async-start | bytes 262144 | tf_op jit(solution)/shard_map/all_to_all | solution.py:620
  67.7 5.6 %collective-permute-start.10 = (f32[8,4,128]{2,1,0:T(4,128)S(1)}, f32[8,4,128]{2,1,0:T(4,128)S(1)}, u32[]{:S(2)}, u32[]{:S(2)}) collective-permute-start(f32[8,4,128]{2,1,0:T(4,128)S(1)} %gather_fusion.1), channel_id=1, source_target_pairs={{0,1},{1,0},{2,3},{3,2},{4,5},{5,4},{6,7},{7,6},{8,9},{9,8},{10,11... | collective-permute-start | bytes 49160 | tf_op jit(solution)/shard_map/ppermute | solution.py:580
  69.0 4.4 %collective-permute-start.11 = (f32[8,4,128]{2,1,0:T(4,128)S(1)}, f32[8,4,128]{2,1,0:T(4,128)S(1)}, u32[]{:S(2)}, u32[]{:S(2)}) collective-permute-start(f32[8,4,128]{2,1,0:T(4,128)S(1)} %gather_fusion.1), channel_id=1, source_target_pairs={{0,8},{1,2},{2,1},{3,4},{4,3},{5,6},{6,5},{7,15},{8,0},{9,10},{10,... | collective-permute-start | bytes 49160 | tf_op jit(solution)/shard_map/ppermute | solution.py:580
  69.0 4.4 %collective-permute-start.8 = (f32[8,4,128]{2,1,0:T(4,128)S(1)}, f32[8,4,128]{2,1,0:T(4,128)S(1)}, u32[]{:S(2)}, u32[]{:S(2)}) collective-permute-start(f32[8,4,128]{2,1,0:T(4,128)S(1)} %gather_fusion.1), channel_id=1, source_target_pairs={{0,8},{8,0},{16,24},{24,16},{1,9},{9,1},{17,25},{25,17},{2,10},{10... | collective-permute-start | bytes 49160 | tf_op jit(solution)/shard_map/ppermute | solution.py:580
  69.5 3.9 %collective-permute-start.9 = (f32[8,4,128]{2,1,0:T(4,128)S(1)}, f32[8,4,128]{2,1,0:T(4,128)S(1)}, u32[]{:S(2)}, u32[]{:S(2)}) collective-permute-start(f32[8,4,128]{2,1,0:T(4,128)S(1)} %gather_fusion.1), channel_id=1, source_target_pairs={{0,24},{8,16},{16,8},{24,0},{1,25},{9,17},{17,9},{25,1},{2,26},{10... | collective-permute-start | bytes 49160 | tf_op jit(solution)/shard_map/ppermute | solution.py:580
  77.3 12.0 %all-to-all-start.3 = ((f32[64,4,128]{2,1,0:T(4,128)}), f32[64,4,128]{2,1,0:T(4,128)S(1)}, u32[]{:S(2)}, u32[]{:S(2)}) async-start(f32[64,4,128]{2,1,0:T(4,128)} %far_contact.3), calls=%async_computation.3 | async-start | bytes 262144 | tf_op jit(solution)/shard_map/all_to_all | solution.py:620
  90.6 2.1 %collective-permute-start.12 = (f32[8,128]{1,0:T(8,128)S(1)}, f32[8,128]{1,0:T(8,128)S(1)}, u32[]{:S(2)}, u32[]{:S(2)}) collective-permute-start(f32[8,128]{1,0:T(8,128)S(1)} %get-tuple-element.63), channel_id=1, source_target_pairs={{0,8},{8,0},{16,24},{24,16},{1,9},{9,1},{17,25},{25,17},{2,10},{10... | collective-permute-start | bytes 12296 | tf_op jit(solution)/shard_map/ppermute | solution.py:580
  90.8 3.0 %collective-permute-start.13 = (f32[8,128]{1,0:T(8,128)S(1)}, f32[8,128]{1,0:T(8,128)S(1)}, u32[]{:S(2)}, u32[]{:S(2)}) collective-permute-start(f32[8,128]{1,0:T(8,128)S(1)} %get-tuple-element.64), channel_id=1, source_target_pairs={{0,24},{8,16},{16,8},{24,0},{1,25},{9,17},{17,9},{25,1},{2,26},{10... | collective-permute-start | bytes 12296 | tf_op jit(solution)/shard_map/ppermute | solution.py:580
  91.7 3.6 %collective-permute-start.14 = (f32[8,128]{1,0:T(8,128)S(1)}, f32[8,128]{1,0:T(8,128)S(1)}, u32[]{:S(2)}, u32[]{:S(2)}) collective-permute-start(f32[8,128]{1,0:T(8,128)S(1)} %get-tuple-element.65), channel_id=1, source_target_pairs={{0,1},{1,0},{2,3},{3,2},{4,5},{5,4},{6,7},{7,6},{8,9},{9,8},{10,11... | collective-permute-start | bytes 12296 | tf_op jit(solution)/shard_map/ppermute | solution.py:580
  92.6 2.7 %collective-permute-start.15 = (f32[8,128]{1,0:T(8,128)S(1)}, f32[8,128]{1,0:T(8,128)S(1)}, u32[]{:S(2)}, u32[]{:S(2)}) collective-permute-start(f32[8,128]{1,0:T(8,128)S(1)} %get-tuple-element.66), channel_id=1, source_target_pairs={{0,8},{1,2},{2,1},{3,4},{4,3},{5,6},{6,5},{7,15},{8,0},{9,10},{10,... | collective-permute-start | bytes 12296 | tf_op jit(solution)/shard_map/ppermute | solution.py:580
  (12 other events, 208.4 us)

commit v5 on v4

--- a/solution.py
+++ b/solution.py
@@ -12,6 +12,7 @@
 HALF = 4
 EBLK = 8
 GROUP = 16
+FIELD = 10
 
 TIME_STEP = 0.5
 PENALTY = 32.0
@@ -34,10 +35,6 @@
 
 def limit(mebibytes):
     return pltpu.CompilerParams(vmem_limit_bytes=mebibytes << 20)
-
-
-def held(x):
-    return pltpu.with_memory_space_constraint(x, pltpu.VMEM)
 
 
 def left(x):
@@ -73,7 +70,7 @@
         out_specs=vspec(),
         compiler_params=limit(4),
         name="prep",
-    )(block_slot, left(displacement), left(ref_pos), left(normals))
+    )(left(block_slot), left(displacement), left(ref_pos), left(normals))
 
 
 def fold_rows(tiles, row):
@@ -92,11 +89,16 @@
     return jnp.where(low1, a + pltpu.roll(a, 7, 0), b + pltpu.roll(b, 1, 0))
 
 
-def element_kernel(
-    disp_ref, conn_ref, hbm_ref, yield_ref, out_ref, stiff_ref, sems, *, origin
-):
+def element_kernel(*refs, origin, places):
+    disp_ref, conn_ref, hbm_ref, yield_ref = refs[0:4]
+    out_ref = refs[6] if places else refs[4]
+    stiff_ref, sems = refs[-2:]
     wide = EBLK * BLK
     turns = out_ref.shape[0] // EBLK
+    if places:
+        plan_ref = refs[7]
+        sort = tile_sorter(*refs[4:6], plan_ref, places)
+        share = -(-refs[5].shape[1] // turns)
 
     def load(r):
         return pltpu.make_async_copy(
@@ -154,27 +156,43 @@
             pieces += [x[0:1], x[4:5]]
         out_ref[k] = jnp.concatenate(pieces + [jnp.zeros((2, BLK), F32)], axis=0)
 
-    def body(r, carry):
+    def body(r, own):
         load(r).wait()
         for d in range(EBLK):
+            if places:
+                for q in range(share * d // EBLK, share * (d + 1) // EBLK):
+                    own = sort(r * share + q, own)
             one_block(r, d)
-        return carry
-
-    lax.fori_loop(0, turns, body, 0)
-
-
-def element_forces(displacement, connectivity, stiffness, yield_force, part=0, parts=1):
+        return own
+
+    own = lax.fori_loop(0, turns, body, jnp.int32(0))
+    if places:
+        plan_ref[plan_ref.shape[0] - 2] = own
+        plan_ref[plan_ref.shape[0] - 1] = refs[4][0] - own
+
+
+def element_forces(
+    displacement, connectivity, stiffness, yield_force, part=0, parts=1, tiles=(), places=0
+):
     nodes = displacement.shape[1]
     blocks = nodes // BLK // parts
 
     def kernel(*refs):
-        element_kernel(*refs, origin=part * blocks)
-
+        element_kernel(*refs, origin=part * blocks, places=places)
+
+    out = jax.ShapeDtypeStruct((blocks, ROWS, BLK), F32)
+    out_spec = vspec()
+    if places:
+        out = [out, jax.ShapeDtypeStruct((2 * tiles[1].shape[1] + 8,), jnp.int32)]
+        out_spec = [out_spec, sspec()]
     return pl.pallas_call(
         kernel,
-        out_shape=jax.ShapeDtypeStruct((blocks, ROWS, BLK), F32),
-        in_specs=[vspec()] * 2 + [pl.BlockSpec(memory_space=pltpu.HBM)] + [vspec()],
-        out_specs=vspec(),
+        out_shape=out,
+        in_specs=[vspec()] * 2
+        + [pl.BlockSpec(memory_space=pltpu.HBM)]
+        + [vspec()]
+        + [sspec()] * len(tiles),
+        out_specs=out_spec,
         scratch_shapes=[
             VMEM((blocks // EBLK, 24, 24, EBLK * BLK), BF16),
             pltpu.SemaphoreType.DMA((blocks // EBLK,)),
@@ -184,55 +202,35 @@
         ),
         compiler_params=limit(12),
         name="element",
-    )(displacement, connectivity, left(stiffness), yield_force.reshape(-1, BLK))
-
-
-def plan_kernel(count_ref, pairs_ref, meta_ref, plan_ref, *, places, edges):
+    )(displacement, connectivity, left(stiffness), yield_force, *tiles)
+
+
+def packed(tile, slave, master):
+    return tile | slave << FIELD | master << (2 * FIELD)
+
+
+def unpacked(entry):
+    mask = (1 << FIELD) - 1
+    return entry & mask, (entry >> FIELD) & mask, entry >> (2 * FIELD)
+
+
+def tile_sorter(count_ref, pairs_ref, plan_ref, places):
     tiles = pairs_ref.shape[1]
-    for first, master in ((0, 0), (tiles, places)):
-        plan_ref[0, first] = 0
-        plan_ref[1, first] = 0
-        plan_ref[2, first] = master
-    log = edges.bit_length() - 1
-    power = edges == 1 << log
+    plan_ref[0] = packed(0, 0, 0)
+    plan_ref[tiles] = packed(0, 0, places)
+    count = count_ref[0]
 
     def sort(t, own):
-        slave = pairs_ref[0, t]
-        master = pairs_ref[1, t]
+        live = t < count
+        at = jnp.minimum(t, tiles - 1)
+        master = pairs_ref[1, at]
         is_own = master < places
-        entry = master - places
-        side = entry >> log if power else entry // edges
-        flip = jnp.where(side < 2, meta_ref[0], meta_ref[1])
-        moved = entry + edges * ((side ^ flip) - side)
         where = jnp.where(is_own, own, tiles + t - own)
-        plan_ref[0, where] = t
-        plan_ref[1, where] = slave
-        plan_ref[2, where] = jnp.where(is_own, master, places + moved)
-        return own + is_own.astype(jnp.int32)
-
-    def several(r, own):
-        for d in range(8):
-            own = sort(8 * r + d, own)
-        return own
-
-    own = lax.fori_loop(0, count_ref[0] // 8, several, jnp.int32(0))
-    own = lax.fori_loop(count_ref[0] // 8 * 8, count_ref[0], sort, own)
-    plan_ref[3, 0] = own
-    plan_ref[3, 1] = count_ref[0] - own
-
-
-def plan_tiles(tile_count, tile_pairs, meta, places, edges):
-    def kernel(*refs):
-        plan_kernel(*refs, places=places, edges=edges)
-
-    return pl.pallas_call(
-        kernel,
-        out_shape=jax.ShapeDtypeStruct((4, 2 * tile_pairs.shape[1]), jnp.int32),
-        in_specs=[sspec()] * 3,
-        out_specs=sspec(),
-        compiler_params=limit(1),
-        name="plan",
-    )(tile_count, tile_pairs, meta)
+        where = jnp.where(live, where, 2 * tiles)
+        plan_ref[where] = packed(at, pairs_ref[0, at], master)
+        return own + jnp.where(jnp.logical_and(live, is_own), 1, 0)
+
+    return sort
 
 
 def master_entry(where, position, normal, master_tab, force_tab):
@@ -263,15 +261,16 @@
 
     def at(group, d):
         i = group * GROUP + d
-        return first + jnp.minimum(i, last), i < number
+        return plan_ref[first + jnp.minimum(i, last)], i < number
 
     def depths(group):
         for d in range(0, GROUP, 2):
             facets, nodes = [], []
             for e in range(2):
-                i, _ = at(group, d + e)
-                facets.append(master_tab[plan_ref[2, i] - base])
-                nodes.append(slave_tab[plan_ref[1, i]])
+                entry, _ = at(group, d + e)
+                _, slave, master = unpacked(entry)
+                facets.append(master_tab[master - base])
+                nodes.append(slave_tab[slave])
             left = jnp.concatenate([nodes[0], blank], axis=0)
             right = jnp.concatenate([blank, nodes[1]], axis=0)
             depth_ref[d // 2] = lax.dot_general(
@@ -286,11 +285,11 @@
         for d in range(0, GROUP, 2):
             starts, lengths, rows = [], [], []
             for e in range(2):
-                i, live = at(group, d + e)
-                t = plan_ref[0, i]
+                entry, live = at(group, d + e)
+                t, _, master = unpacked(entry)
                 starts.append(start_ref[pl.ds(t, 1), :])
                 lengths.append(jnp.where(live, length_ref[pl.ds(t, 1), :], 0))
-                rows.append(force_tab[plan_ref[2, i] - base])
+                rows.append(force_tab[master - base])
             start = jnp.concatenate(starts, axis=1).astype(small)
             length = jnp.concatenate(lengths, axis=1).astype(small)
             inside = ((facet - start) & (BLK - 1)) < length
@@ -309,9 +308,8 @@
             )
         depths(group + 1)
         for d in range(GROUP):
-            i, _ = at(group, d)
+            _, slave, _ = unpacked(at(group, d)[0])
             e = d % 2
-            slave = plan_ref[1, i]
             part = forces[d // 2][8 * e : 8 * e + 8, e * BLK : (e + 1) * BLK]
             total_ref[slave] = total_ref[slave] + part
         return carry
@@ -340,7 +338,7 @@
 
     lax.fori_loop(0, places, entry, 0, unroll=8)
     run_tiles(
-        plan_ref, 0, plan_ref[3, 0], 0, start_ref, length_ref, slave_tab, master_tab, force_tab,
+        plan_ref, 0, plan_ref[plan_ref.shape[0] - 2], 0, start_ref, length_ref, slave_tab, master_tab, force_tab,
         total_ref, depth_ref,
     )
 
@@ -356,13 +354,14 @@
     total_ref[...] = own_ref[...]
     for side in range(4):
         valid = meta_ref[2 + side] > 0
+        base = (side ^ meta_ref[side // 2]) * edges
         for e in range(edges):
             normal = jnp.where(valid, edge_refs[side][e], 0.0)[3:6]
             position = jnp.where(valid, pos_refs[side][e], 0.0)[0:3]
-            master_entry(side * edges + e, position, normal, master_tab, force_tab)
+            master_entry(base + e, position, normal, master_tab, force_tab)
     run_tiles(
-        plan_ref, plan_ref.shape[1] // 2, plan_ref[3, 1], places, start_ref, length_ref, slave_tab, master_tab,
-        force_tab, total_ref, depth_ref,
+        plan_ref, start_ref.shape[0], plan_ref[plan_ref.shape[0] - 1], places, start_ref, length_ref,
+        slave_tab, master_tab, force_tab, total_ref, depth_ref,
     )
 
     def finish(p, carry):
@@ -486,9 +485,10 @@
         internal = first_ref[k] if k < half else second_ref[k - half]
         tile = jnp.concatenate([back_ref[slot_ref[k]], pad], axis=0) - internal
         force_ref[k] = tile
-        for side in range(4):
+    for side in range(4):
+        for k in range(blocks):
             sums[side] = jnp.where(
-                owners[side] == k, lane_gather(tile, lanes[side]), sums[side]
+                owners[side] == k, lane_gather(force_ref[k], lanes[side]), sums[side]
             )
     for side in range(4):
         side_refs[side][...] = sums[side]
@@ -606,6 +606,8 @@
     places = sizes[0] * sizes[1] * CAP
     blocks = displacement.shape[1] // BLK
     edge_count = edge_slots.shape[0]
+    if max(tile_pairs.shape[1], places + 4 * edge_count) >= 1 << FIELD:
+        raise ValueError("field width")
     at = [lax.axis_index(axis) for axis in AXES]
     odd = [i % 2 for i in at]
     inner = [((i > 0) & (i < size - 1)).astype(jnp.int32) for i, size in zip(at, sizes)]
@@ -613,21 +615,34 @@
     meta = jnp.ones((8,), jnp.int32)
     for i, value in ((0, 1 - odd[0]), (1, 1 - odd[1]), (3, inner[0]), (5, inner[1])):
         meta = jnp.where(slot == i, value, meta)
-    plan = plan_tiles(tile_count, tile_pairs, meta, places, edge_count)
+    levels = yield_force.reshape(-1, BLK)
+    plan = None
     code = None
 
     def exchange(blocks_out):
         return lax.all_to_all(blocks_out, AXES, split_axis=0, concat_axis=0, tiled=True)
 
     def half(disp, part):
-        return element_forces(disp, connectivity, stiffness, yield_force, part, 2)
+        return element_forces(disp, connectivity, stiffness, levels, part, 2)
 
     outgoing = prep(block_slot, displacement, ref_pos, normals, places)
     first = None
     for step in range(STEPS):
         fresh = step == 0
         received = exchange(outgoing)
-        internal0 = half(displacement, 0)
+        if fresh:
+            internal0, plan = element_forces(
+                left(displacement),
+                left(connectivity),
+                stiffness,
+                left(levels),
+                0,
+                2,
+                (tile_count, left(tile_pairs)),
+                places,
+            )
+        else:
+            internal0 = half(displacement, 0)
         received, internal0, plan = lax.optimization_barrier((received, internal0, plan))
         near = swap([received[edge_slots]] * 4, sizes)
         if fresh:

time: 97.7 us -> 92.1 us (0.943)
  local copies, waits for them, and re-layouts: 5.16 us -> 1.19 us
  starting transfers between devices: 30.7 us -> 28.4 us
  waiting for transfers between devices: 12.3 us -> 14.6 us
  Pallas kernels: 47.4 us -> 45.9 us
    unnamed x32 -> x22, local copies, waits for them, and re-layouts: 4.03 us -> 0.06 us
    all_to_all x4, waiting for transfers between devices: 7.64 us -> 9.93 us  [exchange(): lax.all_to_all(blocks_out, AXES, split_axis=0, concat_axis=0, tiled=True)]
    ppermute x16, starting transfers between devices: 9.59 us -> 8.1 us  [swap(): lax.ppermute(value, axis, pairs)]
    pallas_call x5 -> x4, Pallas kernels: 23.7 us -> 23.1 us  [element_forces(): pl.pallas_call(kernel, out_shape=out, in_specs=[vspec()] * 2 + [pl.BlockS...]
  transfers between devices with their start and end apart: 20 -> 20, of which waited for: 7 -> 8; matrix products, arithmetic and copies ran while one was open for 0% -> 0% of each run, Pallas kernels for 32% -> 34%
where the time goes in v5:
time: 92.1 us; the launch traced here: 91.7 us
  Pallas kernels  45.9 us (50%)
  starting transfers between devices  28.4 us (31%)
  waiting for transfers between devices  14.6 us (16%)
  between operations  1.68 us (2%)
  local copies, waits for them, and re-layouts  1.19 us (1%)
    pallas_call x4, Pallas kernels, element_forces(): pl.pallas_call(kernel, out_shape=out, in_specs=[vspec()] * 2 + [pl.BlockS...  23.1 us
    all_to_all x4, starting transfers between devices, exchange(): lax.all_to_all(blocks_out, AXES, split_axis=0, concat_axis=0, tiled=True)  20.3 us
    all_to_all x4, waiting for transfers between devices, exchange(): lax.all_to_all(blocks_out, AXES, split_axis=0, concat_axis=0, tiled=True)  9.93 us
    ppermute x16, starting transfers between devices, swap(): lax.ppermute(value, axis, pairs)  8.1 us
    pallas_call x2, Pallas kernels, far_contact(): pl.pallas_call(kernel, out_shape=jax.ShapeDtypeStruct((places, HALF, BLK)...  7.79 us
    pallas_call x2, Pallas kernels, own_contact(): pl.pallas_call(kernel, out_shape=[jax.ShapeDtypeStruct((places, ROWS, BLK...  6.86 us
    ppermute x16, waiting for transfers between devices, swap(): lax.ppermute(value, axis, pairs)  4.62 us
    pallas_call x2, Pallas kernels, update(): pl.pallas_call(update_kernel, out_shape=out, in_specs=[sspec()] + [vspec(...  3.66 us
  transfers between devices with their start and end apart: 20, of which 8 were waited for; matrix products, arithmetic and copies ran while one was open for 0% of the time, Pallas kernels for 34%

profile of v5, /device:TPU:0, one launch (start us, length us, event | category | flops | bytes accessed | tf_op | source)
XLA Modules:
  0.0 91.7 jit_solution(10163955406041490081)
XLA Ops:
  0.7 1.9 %prep.1 = f32[64,8,128]{2,1,0:T(8,128)} custom-call(s32[64]{0:T(128)} %slot_ref.9, f32[6,8192]{1,0:T(8,128)} %disp_ref.3, f32[3,8192]{1,0:T(4,128)} %pos_ref.5, f32[3,8192]{1,0:T(4,128)} %nrm_ref.1), custom_call_target="tpu_custom_call" | custom-call | tf_op jit(solution)/shard_map/prep/pallas_call | solution.py:66
  2.6 7.3 %all-to-all-start = ((f32[64,8,128]{2,1,0:T(8,128)}), f32[64,8,128]{2,1,0:T(8,128)S(1)}, u32[]{:S(2)}, u32[]{:S(2)}) async-start(f32[64,8,128]{2,1,0:T(8,128)} %prep.1), calls=%async_computation | async-start | bytes 524288 | tf_op jit(solution)/shard_map/all_to_all | solution.py:623
  10.7 7.4 %element.4 = (f32[32,8,128]{2,1,0:T(8,128)S(1)}, s32[264]{0:T(512)S(1)}) custom-call(f32[6,8192]{1,0:T(8,128)} %disp_ref.3, s32[4,8192]{1,0:T(4,128)} %refs_1_.7, bf16[24,24,8192]{2,1,0:T(8,128)(2,1)} %refs_2_.9, f32[64,128]{1,0:T(8,128)} %bitcast.1, s32[1]{0:T(128)S(6)} %copy.17.refs_4_, s32[2,128]{1,0:T(2,128)} %refs_5_.1), custom_call_target="tpu_custom_call" | custom-call | flops 9437184 | bytes 9437184 | tf_op jit(solution)/shard_map/element/pallas_call | solution.py:188
  18.1 2.3 %all-to-all-done.refs_1_ = f32[64,8,128]{2,1,0:T(8,128)S(1)} async-done(((f32[64,8,128]{2,1,0:T(8,128)}), f32[64,8,128]{2,1,0:T(8,128)S(1)}, u32[]{:S(2)}, u32[]{:S(2)}) %all-to-all-start) | async-done | bytes 262176 | tf_op jit(solution)/shard_map/all_to_all | solution.py:623
  21.8 1.0 %collective-permute-start.2 = (f32[8,8,128]{2,1,0:T(8,128)S(1)}, f32[8,8,128]{2,1,0:T(8,128)S(1)}, u32[]{:S(2)}, u32[]{:S(2)}) collective-permute-start(f32[8,8,128]{2,1,0:T(8,128)S(1)} %gather_fusion), channel_id=1, source_target_pairs={{0,1},{1,0},{2,3},{3,2},{4,5},{5,4},{6,7},{7,6},{8,9},{9,8},{10,11... | collective-permute-start | bytes 98312 | tf_op jit(solution)/shard_map/ppermute | solution.py:580
  22.9 3.4 %own_contact.2 = (f32[64,8,128]{2,1,0:T(8,128)S(1)}, bf16[64,16,128]{2,1,0:T(8,128)(2,1)S(1)}) custom-call(s32[264]{0:T(512)S(1)} %get-tuple-element.59.refs_0_, f32[64,8,128]{2,1,0:T(8,128)S(1)} %all-to-all-done.refs_1_, s32[128,128]{1,0:T(8,128)S(1)} %copy-done.3, s32[128,128]{1,0:T(8,128)S(1)} %copy-done.4), custom_call_target="tpu_custom_call" | custom-call | flops 67108864 | bytes 65536 | tf_op jit(solution)/shard_map/own_contact/pallas_call | solution.py:389
  26.3 3.9 %far_contact.2 = f32[64,4,128]{2,1,0:T(4,128)} custom-call(s32[264]{0:T(512)S(1)} %get-tuple-element.59.refs_0_, s32[8]{0:T(128)S(1)} %compare_select_fusion.4.refs_1_.meta_ref, f32[8,8,128]{2,1,0:T(8,128)S(1)} %collective-permute-done.refs_2_, f32[8,8,128]{2,1,0:T(8,128)S(1)} %collective-permute-done.1.refs_3_, ...), custom_call_target="tpu_custom_call" | custom-call | flops 67108864 | bytes 65536 | tf_op jit(solution)/shard_map/far_contact/pallas_call | solution.py:418
  30.2 4.4 %all-to-all-start.1 = ((f32[64,4,128]{2,1,0:T(4,128)}), f32[64,4,128]{2,1,0:T(4,128)S(1)}, u32[]{:S(2)}, u32[]{:S(2)}) async-start(f32[64,4,128]{2,1,0:T(4,128)} %far_contact.2), calls=%async_computation.1 | async-start | bytes 262144 | tf_op jit(solution)/shard_map/all_to_all | solution.py:623
  34.7 5.2 %element.5.second_ref = f32[32,8,128]{2,1,0:T(8,128)S(1)} custom-call(f32[6,8192]{1,0:T(8,128)S(1)} %copy-done, s32[4,8192]{1,0:T(4,128)S(1)} %copy-done.1, bf16[24,24,8192]{2,1,0:T(8,128)(2,1)} %refs_2_.9, f32[64,128]{1,0:T(8,128)S(1)} %bitcast.2), custom_call_target="tpu_custom_call" | custom-call | flops 9437184 | bytes 9437184 | tf_op jit(solution)/shard_map/element/pallas_call | solution.py:188
  39.9 2.5 %all-to-all-done.1.back_ref = f32[64,4,128]{2,1,0:T(4,128)S(1)} async-done(((f32[64,4,128]{2,1,0:T(4,128)}), f32[64,4,128]{2,1,0:T(4,128)S(1)}, u32[]{:S(2)}, u32[]{:S(2)}) %all-to-all-start.1) | async-done | bytes 131104 | tf_op jit(solution)/shard_map/all_to_all | solution.py:623
  46.6 1.5 %collective-permute-done.6.near2_ref = f32[8,128]{1,0:T(8,128)S(1)} collective-permute-done((f32[8,128]{1,0:T(8,128)S(1)}, f32[8,128]{1,0:T(8,128)S(1)}, u32[]{:S(2)}, u32[]{:S(2)}) %collective-permute-start.6) | collective-permute-done | bytes 4128 | tf_op jit(solution)/shard_map/ppermute | solution.py:580
  48.1 1.8 %update.2 = (f32[6,8192]{1,0:T(8,128)S(1)}, f32[6,8192]{1,0:T(8,128)S(1)}, f32[64,4,128]{2,1,0:T(4,128)}) custom-call(s32[64]{0:T(128)S(1)} %copy-done.9, f32[64,8,128]{2,1,0:T(8,128)S(1)} %get-tuple-element.47.force_ref, f32[8,128]{1,0:T(8,128)S(1)} %collective-permute-done.4.near0_ref, f32[8,128]{1,0:T(8,128)S(1)} %collective-permute-done.5.near1_ref, ...), custom_call_target="tpu_custom_call" | custom-call | tf_op jit(solution)/shard_map/update/pallas_call | solution.py:555
  49.9 4.5 %all-to-all-start.2 = ((f32[64,4,128]{2,1,0:T(4,128)}), f32[64,4,128]{2,1,0:T(4,128)S(1)}, u32[]{:S(2)}, u32[]{:S(2)}) async-start(f32[64,4,128]{2,1,0:T(4,128)} %get-tuple-element.57), calls=%async_computation.2 | async-start | bytes 262144 | tf_op jit(solution)/shard_map/all_to_all | solution.py:623
  54.4 5.2 %element.6.first_ref = f32[32,8,128]{2,1,0:T(8,128)S(1)} custom-call(f32[6,8192]{1,0:T(8,128)S(1)} %get-tuple-element.65.refs_0_.disp_ref, s32[4,8192]{1,0:T(4,128)S(1)} %copy-done.1, bf16[24,24,8192]{2,1,0:T(8,128)(2,1)} %refs_2_.9, f32[64,128]{1,0:T(8,128)S(1)} %bitcast.3), custom_call_target="tpu_custom_call" | custom-call | flops 9437184 | bytes 9437184 | tf_op jit(solution)/shard_map/element/pallas_call | solution.py:188
  59.6 2.6 %all-to-all-done.2.refs_2_ = f32[64,4,128]{2,1,0:T(4,128)S(1)} async-done(((f32[64,4,128]{2,1,0:T(4,128)}), f32[64,4,128]{2,1,0:T(4,128)S(1)}, u32[]{:S(2)}, u32[]{:S(2)}) %all-to-all-start.2) | async-done | bytes 131104 | tf_op jit(solution)/shard_map/all_to_all | solution.py:623
  62.8 1.2 %collective-permute-start.10 = (f32[8,4,128]{2,1,0:T(4,128)S(1)}, f32[8,4,128]{2,1,0:T(4,128)S(1)}, u32[]{:S(2)}, u32[]{:S(2)}) collective-permute-start(f32[8,4,128]{2,1,0:T(4,128)S(1)} %gather_fusion.1), channel_id=1, source_target_pairs={{0,1},{1,0},{2,3},{3,2},{4,5},{5,4},{6,7},{7,6},{8,9},{9,8},{10,11... | collective-permute-start | bytes 49160 | tf_op jit(solution)/shard_map/ppermute | solution.py:580
  64.8 3.4 %own_contact.3 = (f32[64,8,128]{2,1,0:T(8,128)S(1)}, bf16[64,16,128]{2,1,0:T(8,128)(2,1)S(1)}) custom-call(s32[264]{0:T(512)S(1)} %get-tuple-element.59.refs_0_, f32[64,8,128]{2,1,0:T(8,128)S(1)} %all-to-all-done.refs_1_, f32[64,4,128]{2,1,0:T(4,128)S(1)} %all-to-all-done.2.refs_2_, s32[128,128]{1,0:T(8,128)S(1)} %copy-done.3, s32[128,128]{1,0:T(8,128)S(1)} %copy-done.4), custom_call_target="tpu_custom_call" | custom-call | flops 67108864 | bytes 65536 | tf_op jit(solution)/shard_map/own_contact/pallas_call | solution.py:389
  68.3 3.9 %far_contact.3 = f32[64,4,128]{2,1,0:T(4,128)} custom-call(s32[264]{0:T(512)S(1)} %get-tuple-element.59.refs_0_, s32[8]{0:T(128)S(1)} %compare_select_fusion.4.refs_1_.meta_ref, f32[8,8,128]{2,1,0:T(8,128)S(1)} %collective-permute-done.refs_2_, f32[8,8,128]{2,1,0:T(8,128)S(1)} %collective-permute-done.1.refs_3_, ...), custom_call_target="tpu_custom_call" | custom-call | flops 67108864 | bytes 65536 | tf_op jit(solution)/shard_map/far_contact/pallas_call | solution.py:418
  72.2 4.2 %all-to-all-start.3 = ((f32[64,4,128]{2,1,0:T(4,128)}), f32[64,4,128]{2,1,0:T(4,128)S(1)}, u32[]{:S(2)}, u32[]{:S(2)}) async-start(f32[64,4,128]{2,1,0:T(4,128)} %far_contact.3), calls=%async_computation.3 | async-start | bytes 262144 | tf_op jit(solution)/shard_map/all_to_all | solution.py:623
  76.4 5.2 %element.7.second_ref = f32[32,8,128]{2,1,0:T(8,128)S(1)} custom-call(f32[6,8192]{1,0:T(8,128)S(1)} %get-tuple-element.65.refs_0_.disp_ref, s32[4,8192]{1,0:T(4,128)S(1)} %copy-done.1, bf16[24,24,8192]{2,1,0:T(8,128)(2,1)} %refs_2_.9, f32[64,128]{1,0:T(8,128)S(1)} %bitcast.4), custom_call_target="tpu_custom_call" | custom-call | flops 9437184 | bytes 9437184 | tf_op jit(solution)/shard_map/element/pallas_call | solution.py:188
  81.6 2.6 %all-to-all-done.3.back_ref = f32[64,4,128]{2,1,0:T(4,128)S(1)} async-done(((f32[64,4,128]{2,1,0:T(4,128)}), f32[64,4,128]{2,1,0:T(4,128)S(1)}, u32[]{:S(2)}, u32[]{:S(2)}) %all-to-all-start.3) | async-done | bytes 131104 | tf_op jit(solution)/shard_map/all_to_all | solution.py:623
  87.2 1.1 %collective-permute-done.13.near1_ref = f32[8,128]{1,0:T(8,128)S(1)} collective-permute-done((f32[8,128]{1,0:T(8,128)S(1)}, f32[8,128]{1,0:T(8,128)S(1)}, u32[]{:S(2)}, u32[]{:S(2)}) %collective-permute-start.13) | collective-permute-done | bytes 4128 | tf_op jit(solution)/shard_map/ppermute | solution.py:580
  88.3 1.5 %collective-permute-done.14.near2_ref = f32[8,128]{1,0:T(8,128)S(1)} collective-permute-done((f32[8,128]{1,0:T(8,128)S(1)}, f32[8,128]{1,0:T(8,128)S(1)}, u32[]{:S(2)}, u32[]{:S(2)}) %collective-permute-start.14) | collective-permute-done | bytes 4128 | tf_op jit(solution)/shard_map/ppermute | solution.py:580
  89.8 1.9 %update.3 = (f32[6,8192]{1,0:T(8,128)}, f32[6,8192]{1,0:T(8,128)}) custom-call(s32[64]{0:T(128)S(1)} %copy-done.9, f32[64,8,128]{2,1,0:T(8,128)S(1)} %get-tuple-element.66.force_ref, f32[8,128]{1,0:T(8,128)S(1)} %collective-permute-done.12.near0_ref, f32[8,128]{1,0:T(8,128)S(1)} %collective-permute-done.13.near1_ref, ...), custom_call_target="tpu_custom_call" | custom-call | tf_op jit(solution)/shard_map/update/pallas_call | solution.py:555
  (57 shorter events, 10.0 us)
Async XLA Ops:
  0.6 34.0 %copy-start = (f32[6,8192]{1,0:T(8,128)S(1)}, f32[6,8192]{1,0:T(8,128)}, u32[]{:S(2)}) copy-start(f32[6,8192]{1,0:T(8,128)} %disp_ref.3) | copy-start | bytes 589828
  2.6 17.8 %all-to-all-start = ((f32[64,8,128]{2,1,0:T(8,128)}), f32[64,8,128]{2,1,0:T(8,128)S(1)}, u32[]{:S(2)}, u32[]{:S(2)}) async-start(f32[64,8,128]{2,1,0:T(8,128)} %prep.1), calls=%async_computation | async-start | bytes 524288 | tf_op jit(solution)/shard_map/all_to_all | solution.py:623
  10.6 37.5 %copy-start.2 = (f32[3,8192]{1,0:T(4,128)S(1)}, f32[3,8192]{1,0:T(4,128)}, u32[]{:S(2)}) copy-start(f32[3,8192]{1,0:T(4,128)} %pos_ref.5) | copy-start | bytes 294916
  10.6 37.5 %copy-start.5 = (f32[6,8192]{1,0:T(8,128)S(1)}, f32[6,8192]{1,0:T(8,128)}, u32[]{:S(2)}) copy-start(f32[6,8192]{1,0:T(8,128)} %mass_ref.3) | copy-start | bytes 589828
  10.6 37.5 %copy-start.7 = (f32[6,8192]{1,0:T(8,128)S(1)}, f32[6,8192]{1,0:T(8,128)}, u32[]{:S(2)}) copy-start(f32[6,8192]{1,0:T(8,128)} %vel_ref.1) | copy-start | bytes 589828
  20.9 5.4 %collective-permute-start = (f32[8,8,128]{2,1,0:T(8,128)S(1)}, f32[8,8,128]{2,1,0:T(8,128)S(1)}, u32[]{:S(2)}, u32[]{:S(2)}) collective-permute-start(f32[8,8,128]{2,1,0:T(8,128)S(1)} %gather_fusion), channel_id=1, source_target_pairs={{0,8},{8,0},{16,24},{24,16},{1,9},{9,1},{17,25},{25,17},{2,10},{10... | collective-permute-start | bytes 98312 | tf_op jit(solution)/shard_map/ppermute | solution.py:580
  21.0 5.3 %collective-permute-start.1 = (f32[8,8,128]{2,1,0:T(8,128)S(1)}, f32[8,8,128]{2,1,0:T(8,128)S(1)}, u32[]{:S(2)}, u32[]{:S(2)}) collective-permute-start(f32[8,8,128]{2,1,0:T(8,128)S(1)} %gather_fusion), channel_id=1, source_target_pairs={{0,24},{8,16},{16,8},{24,0},{1,25},{9,17},{17,9},{25,1},{2,26},{10... | collective-permute-start | bytes 98312 | tf_op jit(solution)/shard_map/ppermute | solution.py:580
  21.8 4.5 %collective-permute-start.2 = (f32[8,8,128]{2,1,0:T(8,128)S(1)}, f32[8,8,128]{2,1,0:T(8,128)S(1)}, u32[]{:S(2)}, u32[]{:S(2)}) collective-permute-start(f32[8,8,128]{2,1,0:T(8,128)S(1)} %gather_fusion), channel_id=1, source_target_pairs={{0,1},{1,0},{2,3},{3,2},{4,5},{5,4},{6,7},{7,6},{8,9},{9,8},{10,11... | collective-permute-start | bytes 98312 | tf_op jit(solution)/shard_map/ppermute | solution.py:580
  22.9 3.5 %collective-permute-start.3 = (f32[8,8,128]{2,1,0:T(8,128)S(1)}, f32[8,8,128]{2,1,0:T(8,128)S(1)}, u32[]{:S(2)}, u32[]{:S(2)}) collective-permute-start(f32[8,8,128]{2,1,0:T(8,128)S(1)} %gather_fusion), channel_id=1, source_target_pairs={{0,8},{1,2},{2,1},{3,4},{4,3},{5,6},{6,5},{7,15},{8,0},{9,10},{10,... | collective-permute-start | bytes 98312 | tf_op jit(solution)/shard_map/ppermute | solution.py:580
  30.2 12.2 %all-to-all-start.1 = ((f32[64,4,128]{2,1,0:T(4,128)}), f32[64,4,128]{2,1,0:T(4,128)S(1)}, u32[]{:S(2)}, u32[]{:S(2)}) async-start(f32[64,4,128]{2,1,0:T(4,128)} %far_contact.2), calls=%async_computation.1 | async-start | bytes 262144 | tf_op jit(solution)/shard_map/all_to_all | solution.py:623
  43.3 2.8 %collective-permute-start.4 = (f32[8,128]{1,0:T(8,128)S(1)}, f32[8,128]{1,0:T(8,128)S(1)}, u32[]{:S(2)}, u32[]{:S(2)}) collective-permute-start(f32[8,128]{1,0:T(8,128)S(1)} %get-tuple-element.52), channel_id=1, source_target_pairs={{0,8},{8,0},{16,24},{24,16},{1,9},{9,1},{17,25},{25,17},{2,10},{10... | collective-permute-start | bytes 12296 | tf_op jit(solution)/shard_map/ppermute | solution.py:580
  43.5 3.0 %collective-permute-start.5 = (f32[8,128]{1,0:T(8,128)S(1)}, f32[8,128]{1,0:T(8,128)S(1)}, u32[]{:S(2)}, u32[]{:S(2)}) collective-permute-start(f32[8,128]{1,0:T(8,128)S(1)} %get-tuple-element.53), channel_id=1, source_target_pairs={{0,24},{8,16},{16,8},{24,0},{1,25},{9,17},{17,9},{25,1},{2,26},{10... | collective-permute-start | bytes 12296 | tf_op jit(solution)/shard_map/ppermute | solution.py:580
  44.5 3.6 %collective-permute-start.6 = (f32[8,128]{1,0:T(8,128)S(1)}, f32[8,128]{1,0:T(8,128)S(1)}, u32[]{:S(2)}, u32[]{:S(2)}) collective-permute-start(f32[8,128]{1,0:T(8,128)S(1)} %get-tuple-element.54), channel_id=1, source_target_pairs={{0,1},{1,0},{2,3},{3,2},{4,5},{5,4},{6,7},{7,6},{8,9},{9,8},{10,11... | collective-permute-start | bytes 12296 | tf_op jit(solution)/shard_map/ppermute | solution.py:580
  45.4 2.7 %collective-permute-start.7 = (f32[8,128]{1,0:T(8,128)S(1)}, f32[8,128]{1,0:T(8,128)S(1)}, u32[]{:S(2)}, u32[]{:S(2)}) collective-permute-start(f32[8,128]{1,0:T(8,128)S(1)} %get-tuple-element.55), channel_id=1, source_target_pairs={{0,8},{1,2},{2,1},{3,4},{4,3},{5,6},{6,5},{7,15},{8,0},{9,10},{10,... | collective-permute-start | bytes 12296 | tf_op jit(solution)/shard_map/ppermute | solution.py:580
  49.9 12.3 %all-to-all-start.2 = ((f32[64,4,128]{2,1,0:T(4,128)}), f32[64,4,128]{2,1,0:T(4,128)S(1)}, u32[]{:S(2)}, u32[]{:S(2)}) async-start(f32[64,4,128]{2,1,0:T(4,128)} %get-tuple-element.57), calls=%async_computation.2 | async-start | bytes 262144 | tf_op jit(solution)/shard_map/all_to_all | solution.py:623
  62.8 5.5 %collective-permute-start.10 = (f32[8,4,128]{2,1,0:T(4,128)S(1)}, f32[8,4,128]{2,1,0:T(4,128)S(1)}, u32[]{:S(2)}, u32[]{:S(2)}) collective-permute-start(f32[8,4,128]{2,1,0:T(4,128)S(1)} %gather_fusion.1), channel_id=1, source_target_pairs={{0,1},{1,0},{2,3},{3,2},{4,5},{5,4},{6,7},{7,6},{8,9},{9,8},{10,11... | collective-permute-start | bytes 49160 | tf_op jit(solution)/shard_map/ppermute | solution.py:580
  64.0 4.3 %collective-permute-start.11 = (f32[8,4,128]{2,1,0:T(4,128)S(1)}, f32[8,4,128]{2,1,0:T(4,128)S(1)}, u32[]{:S(2)}, u32[]{:S(2)}) collective-permute-start(f32[8,4,128]{2,1,0:T(4,128)S(1)} %gather_fusion.1), channel_id=1, source_target_pairs={{0,8},{1,2},{2,1},{3,4},{4,3},{5,6},{6,5},{7,15},{8,0},{9,10},{10,... | collective-permute-start | bytes 49160 | tf_op jit(solution)/shard_map/ppermute | solution.py:580
  64.0 4.3 %collective-permute-start.8 = (f32[8,4,128]{2,1,0:T(4,128)S(1)}, f32[8,4,128]{2,1,0:T(4,128)S(1)}, u32[]{:S(2)}, u32[]{:S(2)}) collective-permute-start(f32[8,4,128]{2,1,0:T(4,128)S(1)} %gather_fusion.1), channel_id=1, source_target_pairs={{0,8},{8,0},{16,24},{24,16},{1,9},{9,1},{17,25},{25,17},{2,10},{10... | collective-permute-start | bytes 49160 | tf_op jit(solution)/shard_map/ppermute | solution.py:580
  64.5 3.8 %collective-permute-start.9 = (f32[8,4,128]{2,1,0:T(4,128)S(1)}, f32[8,4,128]{2,1,0:T(4,128)S(1)}, u32[]{:S(2)}, u32[]{:S(2)}) collective-permute-start(f32[8,4,128]{2,1,0:T(4,128)S(1)} %gather_fusion.1), channel_id=1, source_target_pairs={{0,24},{8,16},{16,8},{24,0},{1,25},{9,17},{17,9},{25,1},{2,26},{10... | collective-permute-start | bytes 49160 | tf_op jit(solution)/shard_map/ppermute | solution.py:580
  72.2 12.0 %all-to-all-start.3 = ((f32[64,4,128]{2,1,0:T(4,128)}), f32[64,4,128]{2,1,0:T(4,128)S(1)}, u32[]{:S(2)}, u32[]{:S(2)}) async-start(f32[64,4,128]{2,1,0:T(4,128)} %far_contact.3), calls=%async_computation.3 | async-start | bytes 262144 | tf_op jit(solution)/shard_map/all_to_all | solution.py:623
  85.1 2.1 %collective-permute-start.12 = (f32[8,128]{1,0:T(8,128)S(1)}, f32[8,128]{1,0:T(8,128)S(1)}, u32[]{:S(2)}, u32[]{:S(2)}) collective-permute-start(f32[8,128]{1,0:T(8,128)S(1)} %get-tuple-element.67), channel_id=1, source_target_pairs={{0,8},{8,0},{16,24},{24,16},{1,9},{9,1},{17,25},{25,17},{2,10},{10... | collective-permute-start | bytes 12296 | tf_op jit(solution)/shard_map/ppermute | solution.py:580
  85.3 3.0 %collective-permute-start.13 = (f32[8,128]{1,0:T(8,128)S(1)}, f32[8,128]{1,0:T(8,128)S(1)}, u32[]{:S(2)}, u32[]{:S(2)}) collective-permute-start(f32[8,128]{1,0:T(8,128)S(1)} %get-tuple-element.68), channel_id=1, source_target_pairs={{0,24},{8,16},{16,8},{24,0},{1,25},{9,17},{17,9},{25,1},{2,26},{10... | collective-permute-start | bytes 12296 | tf_op jit(solution)/shard_map/ppermute | solution.py:580
  86.2 3.6 %collective-permute-start.14 = (f32[8,128]{1,0:T(8,128)S(1)}, f32[8,128]{1,0:T(8,128)S(1)}, u32[]{:S(2)}, u32[]{:S(2)}) collective-permute-start(f32[8,128]{1,0:T(8,128)S(1)} %get-tuple-element.69), channel_id=1, source_target_pairs={{0,1},{1,0},{2,3},{3,2},{4,5},{5,4},{6,7},{7,6},{8,9},{9,8},{10,11... | collective-permute-start | bytes 12296 | tf_op jit(solution)/shard_map/ppermute | solution.py:580
  87.1 2.7 %collective-permute-start.15 = (f32[8,128]{1,0:T(8,128)S(1)}, f32[8,128]{1,0:T(8,128)S(1)}, u32[]{:S(2)}, u32[]{:S(2)}) collective-permute-start(f32[8,128]{1,0:T(8,128)S(1)} %get-tuple-element.70), channel_id=1, source_target_pairs={{0,8},{1,2},{2,1},{3,4},{4,3},{5,6},{6,5},{7,15},{8,0},{9,10},{10,... | collective-permute-start | bytes 12296 | tf_op jit(solution)/shard_map/ppermute | solution.py:580
  (7 other events, 193.4 us)

commit v6 on v5

--- a/solution.py
+++ b/solution.py
@@ -9,7 +9,6 @@
 CAP = 2
 STEPS = 2
 ROWS = 8
-HALF = 4
 EBLK = 8
 GROUP = 16
 FIELD = 10
@@ -41,6 +40,16 @@
     return pltpu.with_memory_space_constraint(x, pltpu.HBM)
 
 
+def load_rows(ref, place, first, count):
+    rows = [ref[place, :, r * BLK : (r + 1) * BLK] for r in range(first, first + count)]
+    return jnp.concatenate(rows, axis=0)
+
+
+def store_rows(ref, place, rows):
+    for r in range(rows.shape[0]):
+        ref[place, :, r * BLK : (r + 1) * BLK] = rows[r : r + 1]
+
+
 def lane_gather(data, index):
     return jnp.take_along_axis(data, index, axis=1, mode="promise_in_bounds")
 
@@ -55,17 +64,17 @@
     blocks = slot_ref.shape[0]
     if places != blocks:
         out_ref[...] = jnp.zeros(out_ref.shape, F32)
-    pad = jnp.zeros((ROWS - 6, BLK), F32)
     for k in range(blocks):
         lanes = slice(k * BLK, (k + 1) * BLK)
         position = pos_ref[:, lanes] + disp_ref[0:3, lanes]
-        out_ref[slot_ref[k]] = jnp.concatenate([position, nrm_ref[:, lanes], pad], axis=0)
+        both = jnp.concatenate([position, nrm_ref[:, lanes]], axis=0)
+        store_rows(out_ref, slot_ref[k], both)
 
 
 def prep(block_slot, displacement, ref_pos, normals, places):
     return pl.pallas_call(
         prep_kernel,
-        out_shape=jax.ShapeDtypeStruct((places, ROWS, BLK), F32),
+        out_shape=jax.ShapeDtypeStruct((places, 1, 6 * BLK), F32),
         in_specs=[sspec(), vspec(), vspec(), vspec()],
         out_specs=vspec(),
         compiler_params=limit(4),
@@ -327,12 +336,12 @@
     places = recv_ref.shape[0]
 
     def entry(p, carry):
-        position = pos_ref[p][0:3]
+        position = load_rows(pos_ref, p, 0, 3)
         p_high, p_low = split(position)
         slave_tab[p] = jnp.concatenate(
             [p_high, p_high, p_low, p_low, ones, zero1], axis=0
         ).astype(BF16)
-        master_entry(p, position, recv_ref[p][3:6], master_tab, force_tab)
+        master_entry(p, position, load_rows(recv_ref, p, 3, 3), master_tab, force_tab)
         total_ref[p] = jnp.zeros((ROWS, BLK), F32)
         return carry
 
@@ -350,14 +359,13 @@
     start_ref, length_ref, own_ref, slave_tab, out_ref = refs[0:5]
     master_tab, force_tab, total_ref, depth_ref = refs[5:9]
     places = own_ref.shape[0]
-    zero1 = jnp.zeros((1, BLK), F32)
     total_ref[...] = own_ref[...]
     for side in range(4):
         valid = meta_ref[2 + side] > 0
         base = (side ^ meta_ref[side // 2]) * edges
         for e in range(edges):
-            normal = jnp.where(valid, edge_refs[side][e], 0.0)[3:6]
-            position = jnp.where(valid, pos_refs[side][e], 0.0)[0:3]
+            normal = jnp.where(valid, load_rows(edge_refs[side], e, 3, 3), 0.0)
+            position = jnp.where(valid, load_rows(pos_refs[side], e, 0, 3), 0.0)
             master_entry(base + e, position, normal, master_tab, force_tab)
     run_tiles(
         plan_ref, start_ref.shape[0], plan_ref[plan_ref.shape[0] - 1], places, start_ref, length_ref,
@@ -366,10 +374,26 @@
 
     def finish(p, carry):
         tile = total_ref[p]
-        out_ref[p] = (PENALTY / BLK) * jnp.concatenate([tile[0:3] + tile[3:6], zero1], axis=0)
+        store_rows(out_ref, p, (PENALTY / BLK) * (tile[0:3] + tile[3:6]))
         return carry
 
     lax.fori_loop(0, places, finish, 0, unroll=8)
+
+
+def edge_kernel(slot_ref, recv_ref, out_ref):
+    for e in range(slot_ref.shape[0]):
+        out_ref[e] = recv_ref[slot_ref[e]]
+
+
+def edge_rows(edge_slots, received):
+    return pl.pallas_call(
+        edge_kernel,
+        out_shape=jax.ShapeDtypeStruct((edge_slots.shape[0],) + received.shape[1:], F32),
+        in_specs=[sspec(), vspec()],
+        out_specs=vspec(),
+        compiler_params=limit(1),
+        name="edges",
+    )(edge_slots, received)
 
 
 def tile_cost(tiles):
@@ -417,7 +441,7 @@
 
     return pl.pallas_call(
         kernel,
-        out_shape=jax.ShapeDtypeStruct((places, HALF, BLK), F32),
+        out_shape=jax.ShapeDtypeStruct((places, 1, 3 * BLK), F32),
         in_specs=[sspec()] * 2 + [vspec()] * len(arrays),
         out_specs=vspec(),
         scratch_shapes=[
@@ -473,7 +497,7 @@
 def force_kernel(slot_ref, meta_ref, back_ref, first_ref, second_ref, list_ref, force_ref, *side_refs):
     half = first_ref.shape[0]
     blocks = slot_ref.shape[0]
-    pad = jnp.zeros((ROWS - HALF, BLK), F32)
+    pad = jnp.zeros((ROWS - 3, BLK), F32)
     lanes = []
     owners = []
     for side in range(4):
@@ -483,7 +507,7 @@
     sums = [jnp.zeros((ROWS, BLK), F32) for _ in range(4)]
     for k in range(blocks):
         internal = first_ref[k] if k < half else second_ref[k - half]
-        tile = jnp.concatenate([back_ref[slot_ref[k]], pad], axis=0) - internal
+        tile = jnp.concatenate([load_rows(back_ref, slot_ref[k], 0, 3), pad], axis=0) - internal
         force_ref[k] = tile
     for side in range(4):
         for k in range(blocks):
@@ -527,7 +551,6 @@
     near = [r[...] for r in (near0_ref, near1_ref, near2_ref, near3_ref)]
     if send_refs and send_refs[0].shape[0] != blocks:
         send_refs[0][...] = jnp.zeros(send_refs[0].shape, F32)
-    zero1 = jnp.zeros((1, BLK), F32)
     for k in range(blocks):
         lanes = slice(k * BLK, (k + 1) * BLK)
         code = jnp.broadcast_to(code_ref[k : k + 1, :], (ROWS, BLK))
@@ -542,16 +565,14 @@
         vel_out[:, lanes] = vel
         disp_out[:, lanes] = disp
         if send_refs:
-            send_refs[0][slot_ref[k]] = jnp.concatenate(
-                [pos_ref[:, lanes] + disp[0:3], zero1], axis=0
-            )
+            store_rows(send_refs[0], slot_ref[k], pos_ref[:, lanes] + disp[0:3])
 
 
 def update(block_slot, force, near, code, inv_mass, velocity, displacement, ref_pos, places):
     nodes = displacement.shape[1]
     out = [jax.ShapeDtypeStruct((6, nodes), F32)] * 2
     if places:
-        out = out + [jax.ShapeDtypeStruct((places, HALF, BLK), F32)]
+        out = out + [jax.ShapeDtypeStruct((places, 1, 3 * BLK), F32)]
     return pl.pallas_call(
         update_kernel,
         out_shape=out,
@@ -644,7 +665,7 @@
         else:
             internal0 = half(displacement, 0)
         received, internal0, plan = lax.optimization_barrier((received, internal0, plan))
-        near = swap([received[edge_slots]] * 4, sizes)
+        near = swap([edge_rows(edge_slots, received)] * 4, sizes)
         if fresh:
             first = (received, near)
         total, slave_tab = own_contact(

time: 92.1 us -> 91.6 us (level)
  waiting for transfers between devices: 14.6 us -> 11.9 us
  starting transfers between devices: 28.4 us -> 30.4 us
  Pallas kernels: 45.9 us -> 47.2 us
  local copies, waits for them, and re-layouts: 1.19 us -> 0.06 us
    all_to_all x4, waiting for transfers between devices: 9.93 us -> 7.1 us  [exchange(): lax.all_to_all(blocks_out, AXES, split_axis=0, concat_axis=0, tiled=True)]
    all_to_all x4, starting transfers between devices: 20.3 us -> 21.8 us  [exchange(): lax.all_to_all(blocks_out, AXES, split_axis=0, concat_axis=0, tiled=True)]
    pallas_call x3 -> x5, Pallas kernels: 9.67 us -> 10.9 us  [the longest x2 7.85 us: far_contact(): pl.pallas_call(kernel, out_shape=jax.ShapeDtypeStruct((places, 1, 3 * BLK...]
    gather x2 -> x0, local copies, waits for them, and re-layouts: 1.13 us -> none  [body(): near = swap([received[edge_slots]] * 4, sizes)]
where the time goes in v6:
time: 91.6 us; the launch traced here: 91.2 us
  Pallas kernels  47.2 us (52%)
  starting transfers between devices  30.4 us (33%)
  waiting for transfers between devices  11.9 us (13%)
  between operations  1.65 us (2%)
    pallas_call x4, Pallas kernels, element_forces(): pl.pallas_call(kernel, out_shape=out, in_specs=[vspec()] * 2 + [pl.BlockS...  23.1 us
    all_to_all x4, starting transfers between devices, exchange(): lax.all_to_all(blocks_out, AXES, split_axis=0, concat_axis=0, tiled=True)  21.8 us
    ppermute x16, starting transfers between devices, swap(): lax.ppermute(value, axis, pairs)  8.62 us
    pallas_call x2, Pallas kernels, far_contact(): pl.pallas_call(kernel, out_shape=jax.ShapeDtypeStruct((places, 1, 3 * BLK...  7.85 us
    all_to_all x4, waiting for transfers between devices, exchange(): lax.all_to_all(blocks_out, AXES, split_axis=0, concat_axis=0, tiled=True)  7.1 us
    pallas_call x2, Pallas kernels, own_contact(): pl.pallas_call(kernel, out_shape=[jax.ShapeDtypeStruct((places, ROWS, BLK...  6.98 us
    ppermute x16, waiting for transfers between devices, swap(): lax.ppermute(value, axis, pairs)  4.8 us
    pallas_call x2, Pallas kernels, update(): pl.pallas_call(update_kernel, out_shape=out, in_specs=[sspec()] + [vspec(...  3.65 us
  transfers between devices with their start and end apart: 20, of which 8 were waited for; matrix products, arithmetic and copies ran while one was open for 0% of the time, Pallas kernels for 34%

profile of v6, /device:TPU:0, one launch (start us, length us, event | category | flops | bytes accessed | tf_op | source)
XLA Modules:
  0.0 91.2 jit_solution(14496647606037944782)
XLA Ops:
  0.7 1.9 %prep.1 = f32[64,1,768]{2,1,0:T(1,128)} custom-call(s32[64]{0:T(128)} %slot_ref.13, f32[6,8192]{1,0:T(8,128)} %disp_ref.3, f32[3,8192]{1,0:T(4,128)} %pos_ref.5, f32[3,8192]{1,0:T(4,128)} %nrm_ref.1), custom_call_target="tpu_custom_call" | custom-call | tf_op jit(solution)/shard_map/prep/pallas_call | solution.py:75
  2.6 7.3 %all-to-all-start = ((f32[64,1,768]{2,1,0:T(1,128)}), f32[64,1,768]{2,1,0:T(1,128)S(1)}, u32[]{:S(2)}, u32[]{:S(2)}) async-start(f32[64,1,768]{2,1,0:T(1,128)} %prep.1), calls=%async_computation | async-start | bytes 393216 | tf_op jit(solution)/shard_map/all_to_all | solution.py:644
  10.7 7.4 %element.4 = (f32[32,8,128]{2,1,0:T(8,128)S(1)}, s32[264]{0:T(512)S(1)}) custom-call(f32[6,8192]{1,0:T(8,128)} %disp_ref.3, s32[4,8192]{1,0:T(4,128)} %refs_1_.7, bf16[24,24,8192]{2,1,0:T(8,128)(2,1)} %refs_2_.9, f32[64,128]{1,0:T(8,128)} %bitcast.1, s32[1]{0:T(128)S(6)} %copy.17.refs_4_, s32[2,128]{1,0:T(2,128)} %refs_5_.1), custom_call_target="tpu_custom_call" | custom-call | flops 9437184 | bytes 9437184 | tf_op jit(solution)/shard_map/element/pallas_call | solution.py:197
  19.3 1.3 %collective-permute-start.1 = (f32[8,1,768]{2,1,0:T(1,128)S(1)}, f32[8,1,768]{2,1,0:T(1,128)S(1)}, u32[]{:S(2)}, u32[]{:S(2)}) collective-permute-start(f32[8,1,768]{2,1,0:T(1,128)S(1)} %edges.2), channel_id=1, source_target_pairs={{0,24},{8,16},{16,8},{24,0},{1,25},{9,17},{17,9},{25,1},{2,26},{10... | collective-permute-start | bytes 73736 | tf_op jit(solution)/shard_map/ppermute | solution.py:601
  20.6 1.5 %collective-permute-start.2 = (f32[8,1,768]{2,1,0:T(1,128)S(1)}, f32[8,1,768]{2,1,0:T(1,128)S(1)}, u32[]{:S(2)}, u32[]{:S(2)}) collective-permute-start(f32[8,1,768]{2,1,0:T(1,128)S(1)} %edges.2), channel_id=1, source_target_pairs={{0,1},{1,0},{2,3},{3,2},{4,5},{5,4},{6,7},{7,6},{8,9},{9,8},{10,11... | collective-permute-start | bytes 73736 | tf_op jit(solution)/shard_map/ppermute | solution.py:601
  22.1 3.5 %own_contact.2 = (f32[64,8,128]{2,1,0:T(8,128)S(1)}, bf16[64,16,128]{2,1,0:T(8,128)(2,1)S(1)}) custom-call(s32[264]{0:T(512)S(1)} %get-tuple-element.59.refs_0_, f32[64,1,768]{2,1,0:T(1,128)S(1)} %all-to-all-done.recv_ref.refs_1_, s32[128,128]{1,0:T(8,128)S(1)} %copy-done.3, s32[128,128]{1,0:T(8,128)S(1)} %copy-done.4), custom_call_target="tpu_custom_call" | custom-call | flops 67108864 | bytes 65536 | tf_op jit(solution)/shard_map/own_contact/pallas_call | solution.py:413
  25.6 3.9 %far_contact.2 = f32[64,1,384]{2,1,0:T(1,128)} custom-call(s32[264]{0:T(512)S(1)} %get-tuple-element.59.refs_0_, s32[8]{0:T(128)S(1)} %compare_select_fusion.3.refs_1_.meta_ref, f32[8,1,768]{2,1,0:T(1,128)S(1)} %collective-permute-done.refs_2_, f32[8,1,768]{2,1,0:T(1,128)S(1)} %collective-permute-done.1.refs_3_, ...), custom_call_target="tpu_custom_call" | custom-call | flops 67108864 | bytes 65536 | tf_op jit(solution)/shard_map/far_contact/pallas_call | solution.py:442
  29.6 5.2 %all-to-all-start.1 = ((f32[64,1,384]{2,1,0:T(1,128)}), f32[64,1,384]{2,1,0:T(1,128)S(1)}, u32[]{:S(2)}, u32[]{:S(2)}) async-start(f32[64,1,384]{2,1,0:T(1,128)} %far_contact.2), calls=%async_computation.1 | async-start | bytes 196608 | tf_op jit(solution)/shard_map/all_to_all | solution.py:644
  34.8 5.2 %element.5.second_ref = f32[32,8,128]{2,1,0:T(8,128)S(1)} custom-call(f32[6,8192]{1,0:T(8,128)S(1)} %copy-done, s32[4,8192]{1,0:T(4,128)S(1)} %copy-done.1, bf16[24,24,8192]{2,1,0:T(8,128)(2,1)} %refs_2_.9, f32[64,128]{1,0:T(8,128)S(1)} %bitcast.2), custom_call_target="tpu_custom_call" | custom-call | flops 9437184 | bytes 9437184 | tf_op jit(solution)/shard_map/element/pallas_call | solution.py:197
  40.0 2.3 %all-to-all-done.1.back_ref = f32[64,1,384]{2,1,0:T(1,128)S(1)} async-done(((f32[64,1,384]{2,1,0:T(1,128)}), f32[64,1,384]{2,1,0:T(1,128)S(1)}, u32[]{:S(2)}, u32[]{:S(2)}) %all-to-all-start.1) | async-done | bytes 98336 | tf_op jit(solution)/shard_map/all_to_all | solution.py:644
  46.5 1.3 %collective-permute-done.6.near2_ref = f32[8,128]{1,0:T(8,128)S(1)} collective-permute-done((f32[8,128]{1,0:T(8,128)S(1)}, f32[8,128]{1,0:T(8,128)S(1)}, u32[]{:S(2)}, u32[]{:S(2)}) %collective-permute-start.6) | collective-permute-done | bytes 4128 | tf_op jit(solution)/shard_map/ppermute | solution.py:601
  47.8 1.8 %update.2 = (f32[6,8192]{1,0:T(8,128)S(1)}, f32[6,8192]{1,0:T(8,128)S(1)}, f32[64,1,384]{2,1,0:T(1,128)}) custom-call(s32[64]{0:T(128)S(1)} %copy-done.9, f32[64,8,128]{2,1,0:T(8,128)S(1)} %get-tuple-element.47.force_ref, f32[8,128]{1,0:T(8,128)S(1)} %collective-permute-done.4.near0_ref, f32[8,128]{1,0:T(8,128)S(1)} %collective-permute-done.5.near1_ref, ...), custom_call_target="tpu_custom_call" | custom-call | tf_op jit(solution)/shard_map/update/pallas_call | solution.py:576
  49.6 4.8 %all-to-all-start.2 = ((f32[64,1,384]{2,1,0:T(1,128)}), f32[64,1,384]{2,1,0:T(1,128)S(1)}, u32[]{:S(2)}, u32[]{:S(2)}) async-start(f32[64,1,384]{2,1,0:T(1,128)} %get-tuple-element.57), calls=%async_computation.2 | async-start | bytes 196608 | tf_op jit(solution)/shard_map/all_to_all | solution.py:644
  54.4 5.2 %element.6.first_ref = f32[32,8,128]{2,1,0:T(8,128)S(1)} custom-call(f32[6,8192]{1,0:T(8,128)S(1)} %get-tuple-element.65.refs_0_.disp_ref, s32[4,8192]{1,0:T(4,128)S(1)} %copy-done.1, bf16[24,24,8192]{2,1,0:T(8,128)(2,1)} %refs_2_.9, f32[64,128]{1,0:T(8,128)S(1)} %bitcast.3), custom_call_target="tpu_custom_call" | custom-call | flops 9437184 | bytes 9437184 | tf_op jit(solution)/shard_map/element/pallas_call | solution.py:197
  59.6 2.3 %all-to-all-done.2.recv_ref.refs_2_ = f32[64,1,384]{2,1,0:T(1,128)S(1)} async-done(((f32[64,1,384]{2,1,0:T(1,128)}), f32[64,1,384]{2,1,0:T(1,128)S(1)}, u32[]{:S(2)}, u32[]{:S(2)}) %all-to-all-start.2) | async-done | bytes 98336 | tf_op jit(solution)/shard_map/all_to_all | solution.py:644
  62.5 1.0 %collective-permute-start.10 = (f32[8,1,384]{2,1,0:T(1,128)S(1)}, f32[8,1,384]{2,1,0:T(1,128)S(1)}, u32[]{:S(2)}, u32[]{:S(2)}) collective-permute-start(f32[8,1,384]{2,1,0:T(1,128)S(1)} %edges.3), channel_id=1, source_target_pairs={{0,1},{1,0},{2,3},{3,2},{4,5},{5,4},{6,7},{7,6},{8,9},{9,8},{10,11... | collective-permute-start | bytes 36872 | tf_op jit(solution)/shard_map/ppermute | solution.py:601
  64.3 3.5 %own_contact.3 = (f32[64,8,128]{2,1,0:T(8,128)S(1)}, bf16[64,16,128]{2,1,0:T(8,128)(2,1)S(1)}) custom-call(s32[264]{0:T(512)S(1)} %get-tuple-element.59.refs_0_, f32[64,1,768]{2,1,0:T(1,128)S(1)} %all-to-all-done.recv_ref.refs_1_, f32[64,1,384]{2,1,0:T(1,128)S(1)} %all-to-all-done.2.recv_ref.refs_2_, s32[128,128]{1,0:T(8,128)S(1)} %copy-done.3, ...), custom_call_target="tpu_custom_call" | custom-call | flops 67108864 | bytes 65536 | tf_op jit(solution)/shard_map/own_contact/pallas_call | solution.py:413
  67.8 3.9 %far_contact.3 = f32[64,1,384]{2,1,0:T(1,128)} custom-call(s32[264]{0:T(512)S(1)} %get-tuple-element.59.refs_0_, s32[8]{0:T(128)S(1)} %compare_select_fusion.3.refs_1_.meta_ref, f32[8,1,768]{2,1,0:T(1,128)S(1)} %collective-permute-done.refs_2_, f32[8,1,768]{2,1,0:T(1,128)S(1)} %collective-permute-done.1.refs_3_, ...), custom_call_target="tpu_custom_call" | custom-call | flops 67108864 | bytes 65536 | tf_op jit(solution)/shard_map/far_contact/pallas_call | solution.py:442
  71.8 4.5 %all-to-all-start.3 = ((f32[64,1,384]{2,1,0:T(1,128)}), f32[64,1,384]{2,1,0:T(1,128)S(1)}, u32[]{:S(2)}, u32[]{:S(2)}) async-start(f32[64,1,384]{2,1,0:T(1,128)} %far_contact.3), calls=%async_computation.3 | async-start | bytes 196608 | tf_op jit(solution)/shard_map/all_to_all | solution.py:644
  76.3 5.2 %element.7.second_ref = f32[32,8,128]{2,1,0:T(8,128)S(1)} custom-call(f32[6,8192]{1,0:T(8,128)S(1)} %get-tuple-element.65.refs_0_.disp_ref, s32[4,8192]{1,0:T(4,128)S(1)} %copy-done.1, bf16[24,24,8192]{2,1,0:T(8,128)(2,1)} %refs_2_.9, f32[64,128]{1,0:T(8,128)S(1)} %bitcast.4), custom_call_target="tpu_custom_call" | custom-call | flops 9437184 | bytes 9437184 | tf_op jit(solution)/shard_map/element/pallas_call | solution.py:197
  81.5 2.3 %all-to-all-done.3.back_ref = f32[64,1,384]{2,1,0:T(1,128)S(1)} async-done(((f32[64,1,384]{2,1,0:T(1,128)}), f32[64,1,384]{2,1,0:T(1,128)S(1)}, u32[]{:S(2)}, u32[]{:S(2)}) %all-to-all-start.3) | async-done | bytes 98336 | tf_op jit(solution)/shard_map/all_to_all | solution.py:644
  86.6 1.4 %collective-permute-done.13.near1_ref = f32[8,128]{1,0:T(8,128)S(1)} collective-permute-done((f32[8,128]{1,0:T(8,128)S(1)}, f32[8,128]{1,0:T(8,128)S(1)}, u32[]{:S(2)}, u32[]{:S(2)}) %collective-permute-start.13) | collective-permute-done | bytes 4128 | tf_op jit(solution)/shard_map/ppermute | solution.py:601
  88.0 1.3 %collective-permute-done.14.near2_ref = f32[8,128]{1,0:T(8,128)S(1)} collective-permute-done((f32[8,128]{1,0:T(8,128)S(1)}, f32[8,128]{1,0:T(8,128)S(1)}, u32[]{:S(2)}, u32[]{:S(2)}) %collective-permute-start.14) | collective-permute-done | bytes 4128 | tf_op jit(solution)/shard_map/ppermute | solution.py:601
  89.3 1.9 %update.3 = (f32[6,8192]{1,0:T(8,128)}, f32[6,8192]{1,0:T(8,128)}) custom-call(s32[64]{0:T(128)S(1)} %copy-done.9, f32[64,8,128]{2,1,0:T(8,128)S(1)} %get-tuple-element.66.force_ref, f32[8,128]{1,0:T(8,128)S(1)} %collective-permute-done.12.near0_ref, f32[8,128]{1,0:T(8,128)S(1)} %collective-permute-done.13.near1_ref, ...), custom_call_target="tpu_custom_call" | custom-call | tf_op jit(solution)/shard_map/update/pallas_call | solution.py:576
  (55 shorter events, 9.4 us)
Async XLA Ops:
  0.6 34.1 %copy-start = (f32[6,8192]{1,0:T(8,128)S(1)}, f32[6,8192]{1,0:T(8,128)}, u32[]{:S(2)}) copy-start(f32[6,8192]{1,0:T(8,128)} %disp_ref.3) | copy-start | bytes 589828
  2.6 15.6 %all-to-all-start = ((f32[64,1,768]{2,1,0:T(1,128)}), f32[64,1,768]{2,1,0:T(1,128)S(1)}, u32[]{:S(2)}, u32[]{:S(2)}) async-start(f32[64,1,768]{2,1,0:T(1,128)} %prep.1), calls=%async_computation | async-start | bytes 393216 | tf_op jit(solution)/shard_map/all_to_all | solution.py:644
  10.7 37.1 %copy-start.2 = (f32[3,8192]{1,0:T(4,128)S(1)}, f32[3,8192]{1,0:T(4,128)}, u32[]{:S(2)}) copy-start(f32[3,8192]{1,0:T(4,128)} %pos_ref.5) | copy-start | bytes 294916
  10.7 37.1 %copy-start.5 = (f32[6,8192]{1,0:T(8,128)S(1)}, f32[6,8192]{1,0:T(8,128)}, u32[]{:S(2)}) copy-start(f32[6,8192]{1,0:T(8,128)} %mass_ref.3) | copy-start | bytes 589828
  10.7 37.1 %copy-start.7 = (f32[6,8192]{1,0:T(8,128)S(1)}, f32[6,8192]{1,0:T(8,128)}, u32[]{:S(2)}) copy-start(f32[6,8192]{1,0:T(8,128)} %vel_ref.1) | copy-start | bytes 589828
  18.8 6.8 %collective-permute-start = (f32[8,1,768]{2,1,0:T(1,128)S(1)}, f32[8,1,768]{2,1,0:T(1,128)S(1)}, u32[]{:S(2)}, u32[]{:S(2)}) collective-permute-start(f32[8,1,768]{2,1,0:T(1,128)S(1)} %edges.2), channel_id=1, source_target_pairs={{0,8},{8,0},{16,24},{24,16},{1,9},{9,1},{17,25},{25,17},{2,10},{10... | collective-permute-start | bytes 73736 | tf_op jit(solution)/shard_map/ppermute | solution.py:601
  19.3 6.3 %collective-permute-start.1 = (f32[8,1,768]{2,1,0:T(1,128)S(1)}, f32[8,1,768]{2,1,0:T(1,128)S(1)}, u32[]{:S(2)}, u32[]{:S(2)}) collective-permute-start(f32[8,1,768]{2,1,0:T(1,128)S(1)} %edges.2), channel_id=1, source_target_pairs={{0,24},{8,16},{16,8},{24,0},{1,25},{9,17},{17,9},{25,1},{2,26},{10... | collective-permute-start | bytes 73736 | tf_op jit(solution)/shard_map/ppermute | solution.py:601
  20.6 5.0 %collective-permute-start.2 = (f32[8,1,768]{2,1,0:T(1,128)S(1)}, f32[8,1,768]{2,1,0:T(1,128)S(1)}, u32[]{:S(2)}, u32[]{:S(2)}) collective-permute-start(f32[8,1,768]{2,1,0:T(1,128)S(1)} %edges.2), channel_id=1, source_target_pairs={{0,1},{1,0},{2,3},{3,2},{4,5},{5,4},{6,7},{7,6},{8,9},{9,8},{10,11... | collective-permute-start | bytes 73736 | tf_op jit(solution)/shard_map/ppermute | solution.py:601
  22.1 3.6 %collective-permute-start.3 = (f32[8,1,768]{2,1,0:T(1,128)S(1)}, f32[8,1,768]{2,1,0:T(1,128)S(1)}, u32[]{:S(2)}, u32[]{:S(2)}) collective-permute-start(f32[8,1,768]{2,1,0:T(1,128)S(1)} %edges.2), channel_id=1, source_target_pairs={{0,8},{1,2},{2,1},{3,4},{4,3},{5,6},{6,5},{7,15},{8,0},{9,10},{10,... | collective-permute-start | bytes 73736 | tf_op jit(solution)/shard_map/ppermute | solution.py:601
  29.6 12.8 %all-to-all-start.1 = ((f32[64,1,384]{2,1,0:T(1,128)}), f32[64,1,384]{2,1,0:T(1,128)S(1)}, u32[]{:S(2)}, u32[]{:S(2)}) async-start(f32[64,1,384]{2,1,0:T(1,128)} %far_contact.2), calls=%async_computation.1 | async-start | bytes 196608 | tf_op jit(solution)/shard_map/all_to_all | solution.py:644
  43.3 2.5 %collective-permute-start.4 = (f32[8,128]{1,0:T(8,128)S(1)}, f32[8,128]{1,0:T(8,128)S(1)}, u32[]{:S(2)}, u32[]{:S(2)}) collective-permute-start(f32[8,128]{1,0:T(8,128)S(1)} %get-tuple-element.52), channel_id=1, source_target_pairs={{0,8},{8,0},{16,24},{24,16},{1,9},{9,1},{17,25},{25,17},{2,10},{10... | collective-permute-start | bytes 12296 | tf_op jit(solution)/shard_map/ppermute | solution.py:601
  43.4 3.0 %collective-permute-start.5 = (f32[8,128]{1,0:T(8,128)S(1)}, f32[8,128]{1,0:T(8,128)S(1)}, u32[]{:S(2)}, u32[]{:S(2)}) collective-permute-start(f32[8,128]{1,0:T(8,128)S(1)} %get-tuple-element.53), channel_id=1, source_target_pairs={{0,24},{8,16},{16,8},{24,0},{1,25},{9,17},{17,9},{25,1},{2,26},{10... | collective-permute-start | bytes 12296 | tf_op jit(solution)/shard_map/ppermute | solution.py:601
  44.2 3.6 %collective-permute-start.6 = (f32[8,128]{1,0:T(8,128)S(1)}, f32[8,128]{1,0:T(8,128)S(1)}, u32[]{:S(2)}, u32[]{:S(2)}) collective-permute-start(f32[8,128]{1,0:T(8,128)S(1)} %get-tuple-element.54), channel_id=1, source_target_pairs={{0,1},{1,0},{2,3},{3,2},{4,5},{5,4},{6,7},{7,6},{8,9},{9,8},{10,11... | collective-permute-start | bytes 12296 | tf_op jit(solution)/shard_map/ppermute | solution.py:601
  45.0 2.8 %collective-permute-start.7 = (f32[8,128]{1,0:T(8,128)S(1)}, f32[8,128]{1,0:T(8,128)S(1)}, u32[]{:S(2)}, u32[]{:S(2)}) collective-permute-start(f32[8,128]{1,0:T(8,128)S(1)} %get-tuple-element.55), channel_id=1, source_target_pairs={{0,8},{1,2},{2,1},{3,4},{4,3},{5,6},{6,5},{7,15},{8,0},{9,10},{10,... | collective-permute-start | bytes 12296 | tf_op jit(solution)/shard_map/ppermute | solution.py:601
  49.6 12.4 %all-to-all-start.2 = ((f32[64,1,384]{2,1,0:T(1,128)}), f32[64,1,384]{2,1,0:T(1,128)S(1)}, u32[]{:S(2)}, u32[]{:S(2)}) async-start(f32[64,1,384]{2,1,0:T(1,128)} %get-tuple-element.57), calls=%async_computation.2 | async-start | bytes 196608 | tf_op jit(solution)/shard_map/all_to_all | solution.py:644
  62.5 5.3 %collective-permute-start.10 = (f32[8,1,384]{2,1,0:T(1,128)S(1)}, f32[8,1,384]{2,1,0:T(1,128)S(1)}, u32[]{:S(2)}, u32[]{:S(2)}) collective-permute-start(f32[8,1,384]{2,1,0:T(1,128)S(1)} %edges.3), channel_id=1, source_target_pairs={{0,1},{1,0},{2,3},{3,2},{4,5},{5,4},{6,7},{7,6},{8,9},{9,8},{10,11... | collective-permute-start | bytes 36872 | tf_op jit(solution)/shard_map/ppermute | solution.py:601
  63.5 4.3 %collective-permute-start.11 = (f32[8,1,384]{2,1,0:T(1,128)S(1)}, f32[8,1,384]{2,1,0:T(1,128)S(1)}, u32[]{:S(2)}, u32[]{:S(2)}) collective-permute-start(f32[8,1,384]{2,1,0:T(1,128)S(1)} %edges.3), channel_id=1, source_target_pairs={{0,8},{1,2},{2,1},{3,4},{4,3},{5,6},{6,5},{7,15},{8,0},{9,10},{10,... | collective-permute-start | bytes 36872 | tf_op jit(solution)/shard_map/ppermute | solution.py:601
  63.5 4.3 %collective-permute-start.8 = (f32[8,1,384]{2,1,0:T(1,128)S(1)}, f32[8,1,384]{2,1,0:T(1,128)S(1)}, u32[]{:S(2)}, u32[]{:S(2)}) collective-permute-start(f32[8,1,384]{2,1,0:T(1,128)S(1)} %edges.3), channel_id=1, source_target_pairs={{0,8},{8,0},{16,24},{24,16},{1,9},{9,1},{17,25},{25,17},{2,10},{10... | collective-permute-start | bytes 36872 | tf_op jit(solution)/shard_map/ppermute | solution.py:601
  64.0 3.8 %collective-permute-start.9 = (f32[8,1,384]{2,1,0:T(1,128)S(1)}, f32[8,1,384]{2,1,0:T(1,128)S(1)}, u32[]{:S(2)}, u32[]{:S(2)}) collective-permute-start(f32[8,1,384]{2,1,0:T(1,128)S(1)} %edges.3), channel_id=1, source_target_pairs={{0,24},{8,16},{16,8},{24,0},{1,25},{9,17},{17,9},{25,1},{2,26},{10... | collective-permute-start | bytes 36872 | tf_op jit(solution)/shard_map/ppermute | solution.py:601
  71.8 12.1 %all-to-all-start.3 = ((f32[64,1,384]{2,1,0:T(1,128)}), f32[64,1,384]{2,1,0:T(1,128)S(1)}, u32[]{:S(2)}, u32[]{:S(2)}) async-start(f32[64,1,384]{2,1,0:T(1,128)} %far_contact.3), calls=%async_computation.3 | async-start | bytes 196608 | tf_op jit(solution)/shard_map/all_to_all | solution.py:644
  84.8 1.8 %collective-permute-start.12 = (f32[8,128]{1,0:T(8,128)S(1)}, f32[8,128]{1,0:T(8,128)S(1)}, u32[]{:S(2)}, u32[]{:S(2)}) collective-permute-start(f32[8,128]{1,0:T(8,128)S(1)} %get-tuple-element.67), channel_id=1, source_target_pairs={{0,8},{8,0},{16,24},{24,16},{1,9},{9,1},{17,25},{25,17},{2,10},{10... | collective-permute-start | bytes 12296 | tf_op jit(solution)/shard_map/ppermute | solution.py:601
  85.0 3.0 %collective-permute-start.13 = (f32[8,128]{1,0:T(8,128)S(1)}, f32[8,128]{1,0:T(8,128)S(1)}, u32[]{:S(2)}, u32[]{:S(2)}) collective-permute-start(f32[8,128]{1,0:T(8,128)S(1)} %get-tuple-element.68), channel_id=1, source_target_pairs={{0,24},{8,16},{16,8},{24,0},{1,25},{9,17},{17,9},{25,1},{2,26},{10... | collective-permute-start | bytes 12296 | tf_op jit(solution)/shard_map/ppermute | solution.py:601
  85.7 3.6 %collective-permute-start.14 = (f32[8,128]{1,0:T(8,128)S(1)}, f32[8,128]{1,0:T(8,128)S(1)}, u32[]{:S(2)}, u32[]{:S(2)}) collective-permute-start(f32[8,128]{1,0:T(8,128)S(1)} %get-tuple-element.69), channel_id=1, source_target_pairs={{0,1},{1,0},{2,3},{3,2},{4,5},{5,4},{6,7},{7,6},{8,9},{9,8},{10,11... | collective-permute-start | bytes 12296 | tf_op jit(solution)/shard_map/ppermute | solution.py:601
  86.5 2.8 %collective-permute-start.15 = (f32[8,128]{1,0:T(8,128)S(1)}, f32[8,128]{1,0:T(8,128)S(1)}, u32[]{:S(2)}, u32[]{:S(2)}) collective-permute-start(f32[8,128]{1,0:T(8,128)S(1)} %get-tuple-element.70), channel_id=1, source_target_pairs={{0,8},{1,2},{2,1},{3,4},{4,3},{5,6},{6,5},{7,15},{8,0},{9,10},{10,... | collective-permute-start | bytes 12296 | tf_op jit(solution)/shard_map/ppermute | solution.py:601
  (7 other events, 192.0 us)

commit v7 on v6

--- a/solution.py
+++ b/solution.py
@@ -12,6 +12,8 @@
 EBLK = 8
 GROUP = 16
 FIELD = 10
+TAIL = 16
+PART = 16
 
 TIME_STEP = 0.5
 PENALTY = 32.0
@@ -100,13 +102,15 @@
 
 def element_kernel(*refs, origin, places):
     disp_ref, conn_ref, hbm_ref, yield_ref = refs[0:4]
-    out_ref = refs[6] if places else refs[4]
+    out_ref = refs[7] if places else refs[4]
     stiff_ref, sems = refs[-2:]
     wide = EBLK * BLK
     turns = out_ref.shape[0] // EBLK
     if places:
-        plan_ref = refs[7]
+        plan_ref = refs[8]
         sort = tile_sorter(*refs[4:6], plan_ref, places)
+        for i in range(refs[6].shape[0]):
+            plan_ref[plan_ref.shape[0] - TAIL + i] = refs[6][i]
         share = -(-refs[5].shape[1] // turns)
 
     def load(r):
@@ -176,8 +180,8 @@
 
     own = lax.fori_loop(0, turns, body, jnp.int32(0))
     if places:
-        plan_ref[plan_ref.shape[0] - 2] = own
-        plan_ref[plan_ref.shape[0] - 1] = refs[4][0] - own
+        plan_ref[plan_ref.shape[0] - TAIL - 2] = own
+        plan_ref[plan_ref.shape[0] - TAIL - 1] = refs[4][0] - own
 
 
 def element_forces(
@@ -192,7 +196,7 @@
     out = jax.ShapeDtypeStruct((blocks, ROWS, BLK), F32)
     out_spec = vspec()
     if places:
-        out = [out, jax.ShapeDtypeStruct((2 * tiles[1].shape[1] + 8,), jnp.int32)]
+        out = [out, jax.ShapeDtypeStruct((2 * tiles[1].shape[1] + 2 * TAIL,), jnp.int32)]
         out_spec = [out_spec, sspec()]
     return pl.pallas_call(
         kernel,
@@ -259,7 +263,7 @@
 
 
 def run_tiles(
-    plan_ref, first, number, base, start_ref, length_ref, slave_tab, master_tab, force_tab,
+    plan_ref, first, number, facet_entry, start_ref, length_ref, slave_tab, master_tab, force_tab,
     total_ref, depth_ref,
 ):
     facet = lax.broadcasted_iota(jnp.int32, (BLK, 2 * BLK), 0).astype(jnp.int16)
@@ -278,7 +282,7 @@
             for e in range(2):
                 entry, _ = at(group, d + e)
                 _, slave, master = unpacked(entry)
-                facets.append(master_tab[master - base])
+                facets.append(master_tab[facet_entry(master)[0]])
                 nodes.append(slave_tab[slave])
             left = jnp.concatenate([nodes[0], blank], axis=0)
             right = jnp.concatenate([blank, nodes[1]], axis=0)
@@ -296,9 +300,11 @@
             for e in range(2):
                 entry, live = at(group, d + e)
                 t, _, master = unpacked(entry)
+                where, known = facet_entry(master)
+                live = jnp.logical_and(live, known)
                 starts.append(start_ref[pl.ds(t, 1), :])
                 lengths.append(jnp.where(live, length_ref[pl.ds(t, 1), :], 0))
-                rows.append(force_tab[master - base])
+                rows.append(force_tab[where])
             start = jnp.concatenate(starts, axis=1).astype(small)
             length = jnp.concatenate(lengths, axis=1).astype(small)
             inside = ((facet - start) & (BLK - 1)) < length
@@ -327,10 +333,13 @@
     lax.fori_loop(0, (number + GROUP - 1) // GROUP, body, 0)
 
 
-def own_kernel(plan_ref, recv_ref, *refs, fresh):
+def own_kernel(table_ref, recv_ref, *refs, fresh):
     pos_ref = recv_ref if fresh else refs[0]
     refs = refs if fresh else refs[1:]
-    start_ref, length_ref, total_ref, slave_tab, master_tab, force_tab, depth_ref = refs
+    start_ref, length_ref, total_ref, slave_tab, master_tab, force_tab, depth_ref = refs[:7]
+    plan_ref, sem = refs[7:]
+    load = pltpu.make_async_copy(table_ref, plan_ref, sem)
+    load.start()
     ones = jnp.ones((3, BLK), F32)
     zero1 = jnp.zeros((1, BLK), F32)
     places = recv_ref.shape[0]
@@ -346,29 +355,41 @@
         return carry
 
     lax.fori_loop(0, places, entry, 0, unroll=8)
+    load.wait()
     run_tiles(
-        plan_ref, 0, plan_ref[plan_ref.shape[0] - 2], 0, start_ref, length_ref, slave_tab, master_tab, force_tab,
+        plan_ref, 0, plan_ref[plan_ref.shape[0] - TAIL - 2], lambda m: (m, True), start_ref, length_ref, slave_tab, master_tab, force_tab,
         total_ref, depth_ref,
     )
 
 
-def far_kernel(plan_ref, meta_ref, *refs, edges, fresh):
+def far_kernel(table_ref, *refs, edges, fresh):
     edge_refs = refs[0:4]
     pos_refs = edge_refs if fresh else refs[4:8]
     refs = refs[4:] if fresh else refs[8:]
     start_ref, length_ref, own_ref, slave_tab, out_ref = refs[0:5]
-    master_tab, force_tab, total_ref, depth_ref = refs[5:9]
+    master_tab, force_tab, total_ref, depth_ref, plan_ref, sem = refs[5:11]
+    load = pltpu.make_async_copy(table_ref, plan_ref, sem)
+    load.start()
+    tail = plan_ref.shape[0] - TAIL
     places = own_ref.shape[0]
     total_ref[...] = own_ref[...]
     for side in range(4):
-        valid = meta_ref[2 + side] > 0
-        base = (side ^ meta_ref[side // 2]) * edges
         for e in range(edges):
-            normal = jnp.where(valid, load_rows(edge_refs[side], e, 3, 3), 0.0)
-            position = jnp.where(valid, load_rows(pos_refs[side], e, 0, 3), 0.0)
-            master_entry(base + e, position, normal, master_tab, force_tab)
+            normal = load_rows(edge_refs[side], e, 3, 3)
+            position = load_rows(pos_refs[side], e, 0, 3)
+            master_entry(side * edges + e, position, normal, master_tab, force_tab)
+    load.wait()
+    log = edges.bit_length() - 1
+    power = edges == 1 << log
+
+    def facet_entry(master):
+        entry = master - places
+        side = entry >> log if power else entry // edges
+        pairing = side ^ jnp.where(side < 2, plan_ref[tail], plan_ref[tail + 1])
+        return entry + edges * (pairing - side), plan_ref[tail + 2 + pairing] > 0
+
     run_tiles(
-        plan_ref, start_ref.shape[0], plan_ref[plan_ref.shape[0] - 1], places, start_ref, length_ref,
+        plan_ref, start_ref.shape[0], plan_ref[tail - 1], facet_entry, start_ref, length_ref,
         slave_tab, master_tab, force_tab, total_ref, depth_ref,
     )
 
@@ -416,12 +437,14 @@
             jax.ShapeDtypeStruct((places, ROWS, BLK), F32),
             jax.ShapeDtypeStruct((places, 16, BLK), BF16),
         ],
-        in_specs=[sspec()] + [vspec()] * len(arrays),
+        in_specs=[pl.BlockSpec(memory_space=pl.ANY)] + [vspec()] * len(arrays),
         out_specs=[vspec()] * 2,
         scratch_shapes=[
             VMEM((places, 16, BLK), BF16),
             VMEM((places, 16, BLK), BF16),
             VMEM((GROUP // 2, BLK, 2 * BLK), F32),
+            SMEM(plan.shape, jnp.int32),
+            pltpu.SemaphoreType.DMA(()),
         ],
         cost_estimate=tile_cost(start.shape[0] // 2),
         compiler_params=limit(8),
@@ -429,7 +452,7 @@
     )(plan, *arrays)
 
 
-def far_contact(plan, meta, edges, edge_positions, start, length, total, slave_tab):
+def far_contact(plan, edges, edge_positions, start, length, total, slave_tab):
     places = total.shape[0]
     fresh = edge_positions is None
     edge_count = edges[0].shape[0]
@@ -442,18 +465,20 @@
     return pl.pallas_call(
         kernel,
         out_shape=jax.ShapeDtypeStruct((places, 1, 3 * BLK), F32),
-        in_specs=[sspec()] * 2 + [vspec()] * len(arrays),
+        in_specs=[pl.BlockSpec(memory_space=pl.ANY)] + [vspec()] * len(arrays),
         out_specs=vspec(),
         scratch_shapes=[
             VMEM((4 * edge_count, 16, BLK), BF16),
             VMEM((4 * edge_count, 16, BLK), BF16),
             VMEM((places, ROWS, BLK), F32),
             VMEM((GROUP // 2, BLK, 2 * BLK), F32),
+            SMEM(plan.shape, jnp.int32),
+            pltpu.SemaphoreType.DMA(()),
         ],
         cost_estimate=tile_cost(start.shape[0] // 2),
         compiler_params=limit(8),
         name="far_contact",
-    )(plan, meta, *arrays)
+    )(plan, *arrays)
 
 
 def side_list(list_ref, meta_ref, side):
@@ -531,26 +556,24 @@
     )(block_slot, meta, returned, *internal, lists)
 
 
-def update_kernel(
-    slot_ref,
-    force_ref,
-    near0_ref,
-    near1_ref,
-    near2_ref,
-    near3_ref,
-    code_ref,
-    mass_ref,
-    vel_ref,
-    disp_ref,
-    pos_ref,
-    vel_out,
-    disp_out,
-    *send_refs,
-):
+def update_kernel(*refs, send):
+    if send:
+        table_ref = refs[0]
+        slot_ref, sem = refs[-2:]
+        refs = refs[1:-2]
+        load = pltpu.make_async_copy(table_ref, slot_ref, sem)
+        load.start()
+    force_ref = refs[0]
+    near = [r[...] for r in refs[1:5]]
+    code_ref, mass_ref, vel_ref, disp_ref = refs[5:9]
+    if send:
+        pos_ref, vel_out, disp_out, send_ref = refs[9:]
+    else:
+        vel_hbm, disp_hbm, vel_out, disp_out, sems = refs[9:]
     blocks = force_ref.shape[0]
-    near = [r[...] for r in (near0_ref, near1_ref, near2_ref, near3_ref)]
-    if send_refs and send_refs[0].shape[0] != blocks:
-        send_refs[0][...] = jnp.zeros(send_refs[0].shape, F32)
+    if send and send_ref.shape[0] != blocks:
+        send_ref[...] = jnp.zeros(send_ref.shape, F32)
+    copies = []
     for k in range(blocks):
         lanes = slice(k * BLK, (k + 1) * BLK)
         code = jnp.broadcast_to(code_ref[k : k + 1, :], (ROWS, BLK))
@@ -564,23 +587,54 @@
         disp = disp_ref[:, lanes] + TIME_STEP * vel
         vel_out[:, lanes] = vel
         disp_out[:, lanes] = disp
-        if send_refs:
-            store_rows(send_refs[0], slot_ref[k], pos_ref[:, lanes] + disp[0:3])
+        if not send and (k + 1) % PART == 0:
+            span = slice((k + 1 - PART) * BLK, (k + 1) * BLK)
+            for i, (held, out) in enumerate(((vel_out, vel_hbm), (disp_out, disp_hbm))):
+                copies.append(
+                    pltpu.make_async_copy(
+                        held.at[:, span], out.at[:, span], sems.at[i, k // PART]
+                    )
+                )
+                copies[-1].start()
+    for copy in copies:
+        copy.wait()
+    if send:
+        load.wait()
+        for k in range(blocks):
+            lanes = slice(k * BLK, (k + 1) * BLK)
+            store_rows(send_ref, slot_ref[k], pos_ref[:, lanes] + disp_out[0:3, lanes])
 
 
 def update(block_slot, force, near, code, inv_mass, velocity, displacement, ref_pos, places):
     nodes = displacement.shape[1]
     out = [jax.ShapeDtypeStruct((6, nodes), F32)] * 2
+    arrays = [force, *near, code, inv_mass, velocity, displacement]
+    specs = [vspec()] * len(arrays)
+    out_specs = [vspec()] * 2
+    scratch = []
     if places:
+        arrays = [block_slot] + arrays + [ref_pos]
+        specs = [pl.BlockSpec(memory_space=pl.ANY)] + specs + [vspec()]
+        scratch = [SMEM(block_slot.shape, jnp.int32), pltpu.SemaphoreType.DMA(())]
         out = out + [jax.ShapeDtypeStruct((places, 1, 3 * BLK), F32)]
+        out_specs = [vspec()] * 3
+    else:
+        out_specs = [pl.BlockSpec(memory_space=pl.ANY)] * 2
+        scratch = [VMEM((6, nodes), F32)] * 2
+        scratch += [pltpu.SemaphoreType.DMA((2, nodes // BLK // PART))]
+
+    def kernel(*refs):
+        update_kernel(*refs, send=places > 0)
+
     return pl.pallas_call(
-        update_kernel,
+        kernel,
         out_shape=out,
-        in_specs=[sspec()] + [vspec()] * 10,
-        out_specs=[vspec()] * len(out),
+        in_specs=specs,
+        out_specs=out_specs,
+        scratch_shapes=scratch,
         compiler_params=limit(6),
         name="update",
-    )(block_slot, force, *near, code, inv_mass, velocity, displacement, ref_pos)
+    )(*arrays)
 
 
 def pair_lists(sizes):
@@ -659,7 +713,7 @@
                 left(levels),
                 0,
                 2,
-                (tile_count, left(tile_pairs)),
+                (tile_count, left(tile_pairs), meta),
                 places,
             )
         else:
@@ -672,7 +726,7 @@
             plan, first[0], None if fresh else received, win_start, win_len
         )
         box_force = far_contact(
-            plan, meta, first[1], None if fresh else near, win_start, win_len, total, slave_tab
+            plan, first[1], None if fresh else near, win_start, win_len, total, slave_tab
         )
         box_force, later = lax.optimization_barrier((box_force, displacement))
         returned = exchange(box_force)

time: 91.6 us -> 89.7 us (0.979)
  Pallas kernels: 47.2 us -> 45.1 us
    pallas_call x2, Pallas kernels: 3.65 us -> 2.59 us  [update(): pl.pallas_call(kernel, out_shape=out, in_specs=specs, out_specs=out_specs...]
    pallas_call x2, Pallas kernels: 6.98 us -> 6 us  [own_contact(): pl.pallas_call(kernel, out_shape=[jax.ShapeDtypeStruct((places, ROWS, BLK...]
  transfers between devices with their start and end apart: 20 -> 20, of which waited for: 8 -> 8; matrix products, arithmetic and copies ran while one was open for 0% -> 0% of each run, Pallas kernels for 34% -> 33%
where the time goes in v7:
time: 89.7 us; the launch traced here: 89.4 us
  Pallas kernels  45.1 us (50%)
  starting transfers between devices  30.7 us (34%)
  waiting for transfers between devices  11.9 us (13%)
  between operations  1.66 us (2%)
    pallas_call x4, Pallas kernels, element_forces(): pl.pallas_call(kernel, out_shape=out, in_specs=[vspec()] * 2 + [pl.BlockS...  23.1 us
    all_to_all x4, starting transfers between devices, exchange(): lax.all_to_all(blocks_out, AXES, split_axis=0, concat_axis=0, tiled=True)  22.1 us
    ppermute x16, starting transfers between devices, swap(): lax.ppermute(value, axis, pairs)  8.63 us
    pallas_call x2, Pallas kernels, far_contact(): pl.pallas_call(kernel, out_shape=jax.ShapeDtypeStruct((places, 1, 3 * BLK...  7.78 us
    all_to_all x4, waiting for transfers between devices, exchange(): lax.all_to_all(blocks_out, AXES, split_axis=0, concat_axis=0, tiled=True)  7.07 us
    pallas_call x2, Pallas kernels, own_contact(): pl.pallas_call(kernel, out_shape=[jax.ShapeDtypeStruct((places, ROWS, BLK...  6 us
    ppermute x16, waiting for transfers between devices, swap(): lax.ppermute(value, axis, pairs)  4.8 us
    pallas_call x2, Pallas kernels, update(): pl.pallas_call(kernel, out_shape=out, in_specs=specs, out_specs=out_specs...  2.59 us
  transfers between devices with their start and end apart: 20, of which 8 were waited for; matrix products, arithmetic and copies ran while one was open for 0% of the time, Pallas kernels for 33%

profile of v7, /device:TPU:0, one launch (start us, length us, event | category | flops | bytes accessed | tf_op | source)
XLA Modules:
  0.0 89.4 jit_solution(1746122153483260307)
XLA Ops:
  0.7 1.9 %prep.1 = f32[64,1,768]{2,1,0:T(1,128)} custom-call(s32[64]{0:T(128)} %slot_ref.9, f32[6,8192]{1,0:T(8,128)} %refs_9_.2, f32[3,8192]{1,0:T(4,128)} %refs_10_.2, f32[3,8192]{1,0:T(4,128)} %nrm_ref.1), custom_call_target="tpu_custom_call" | custom-call | tf_op jit(solution)/shard_map/prep/pallas_call | solution.py:77
  2.6 7.3 %all-to-all-start = ((f32[64,1,768]{2,1,0:T(1,128)}), f32[64,1,768]{2,1,0:T(1,128)S(1)}, u32[]{:S(2)}, u32[]{:S(2)}) async-start(f32[64,1,768]{2,1,0:T(1,128)} %prep.1), calls=%async_computation | async-start | bytes 393216 | tf_op jit(solution)/shard_map/all_to_all | solution.py:698
  10.7 7.4 %element.4 = (f32[32,8,128]{2,1,0:T(8,128)S(1)}, s32[288]{0:T(512)S(1)}) custom-call(f32[6,8192]{1,0:T(8,128)} %refs_9_.2, s32[4,8192]{1,0:T(4,128)} %refs_1_.7, bf16[24,24,8192]{2,1,0:T(8,128)(2,1)} %refs_2_.9, f32[64,128]{1,0:T(8,128)} %bitcast.1, s32[1]{0:T(128)S(6)} %copy.17.refs_4_, s32[2,128]{1,0:T(2,128)} %refs_5_.2, ...), custom_call_target="tpu_custom_call" | custom-call | flops 9437184 | bytes 9437184 | tf_op jit(solution)/shard_map/element/pallas_call | solution.py:201
  19.3 1.4 %collective-permute-start.1 = (f32[8,1,768]{2,1,0:T(1,128)S(1)}, f32[8,1,768]{2,1,0:T(1,128)S(1)}, u32[]{:S(2)}, u32[]{:S(2)}) collective-permute-start(f32[8,1,768]{2,1,0:T(1,128)S(1)} %edges.2), channel_id=1, source_target_pairs={{0,24},{8,16},{16,8},{24,0},{1,25},{9,17},{17,9},{25,1},{2,26},{10... | collective-permute-start | bytes 73736 | tf_op jit(solution)/shard_map/ppermute | solution.py:655
  20.6 1.4 %collective-permute-start.2 = (f32[8,1,768]{2,1,0:T(1,128)S(1)}, f32[8,1,768]{2,1,0:T(1,128)S(1)}, u32[]{:S(2)}, u32[]{:S(2)}) collective-permute-start(f32[8,1,768]{2,1,0:T(1,128)S(1)} %edges.2), channel_id=1, source_target_pairs={{0,1},{1,0},{2,3},{3,2},{4,5},{5,4},{6,7},{7,6},{8,9},{9,8},{10,11... | collective-permute-start | bytes 73736 | tf_op jit(solution)/shard_map/ppermute | solution.py:655
  22.1 3.0 %own_contact.2 = (f32[64,8,128]{2,1,0:T(8,128)S(1)}, bf16[64,16,128]{2,1,0:T(8,128)(2,1)S(1)}) custom-call(s32[288]{0:T(512)S(1)} %get-tuple-element.59.refs_0_, f32[64,1,768]{2,1,0:T(1,128)S(1)} %all-to-all-done.recv_ref.refs_1_, s32[128,128]{1,0:T(8,128)S(1)} %copy-done.2, s32[128,128]{1,0:T(8,128)S(1)} %copy-done.3), custom_call_target="tpu_custom_call" | custom-call | flops 67108864 | bytes 65536 | tf_op jit(solution)/shard_map/own_contact/pallas_call | solution.py:434
  25.1 3.9 %far_contact.2 = f32[64,1,384]{2,1,0:T(1,128)} custom-call(s32[288]{0:T(512)S(1)} %get-tuple-element.59.refs_0_, f32[8,1,768]{2,1,0:T(1,128)S(1)} %collective-permute-done.refs_1_, f32[8,1,768]{2,1,0:T(1,128)S(1)} %collective-permute-done.1.refs_2_, f32[8,1,768]{2,1,0:T(1,128)S(1)} %collective-permute-done.2.refs_3_, ...), custom_call_target="tpu_custom_call" | custom-call | flops 67108864 | bytes 65536 | tf_op jit(solution)/shard_map/far_contact/pallas_call | solution.py:465
  29.0 5.4 %all-to-all-start.1 = ((f32[64,1,384]{2,1,0:T(1,128)}), f32[64,1,384]{2,1,0:T(1,128)S(1)}, u32[]{:S(2)}, u32[]{:S(2)}) async-start(f32[64,1,384]{2,1,0:T(1,128)} %far_contact.2), calls=%async_computation.1 | async-start | bytes 196608 | tf_op jit(solution)/shard_map/all_to_all | solution.py:698
  34.5 5.2 %element.5.second_ref = f32[32,8,128]{2,1,0:T(8,128)S(1)} custom-call(f32[6,8192]{1,0:T(8,128)S(1)} %copy-done, s32[4,8192]{1,0:T(4,128)S(1)} %copy-done.1, bf16[24,24,8192]{2,1,0:T(8,128)(2,1)} %refs_2_.9, f32[64,128]{1,0:T(8,128)S(1)} %bitcast.2), custom_call_target="tpu_custom_call" | custom-call | flops 9437184 | bytes 9437184 | tf_op jit(solution)/shard_map/element/pallas_call | solution.py:201
  39.7 2.3 %all-to-all-done.1.back_ref = f32[64,1,384]{2,1,0:T(1,128)S(1)} async-done(((f32[64,1,384]{2,1,0:T(1,128)}), f32[64,1,384]{2,1,0:T(1,128)S(1)}, u32[]{:S(2)}, u32[]{:S(2)}) %all-to-all-start.1) | async-done | bytes 98336 | tf_op jit(solution)/shard_map/all_to_all | solution.py:698
  46.2 1.3 %collective-permute-done.6.refs_4_ = f32[8,128]{1,0:T(8,128)S(1)} collective-permute-done((f32[8,128]{1,0:T(8,128)S(1)}, f32[8,128]{1,0:T(8,128)S(1)}, u32[]{:S(2)}, u32[]{:S(2)}) %collective-permute-start.6) | collective-permute-done | bytes 4128 | tf_op jit(solution)/shard_map/ppermute | solution.py:655
  47.5 1.3 %update.2 = (f32[6,8192]{1,0:T(8,128)S(1)}, f32[6,8192]{1,0:T(8,128)S(1)}, f32[64,1,384]{2,1,0:T(1,128)}) custom-call(s32[64]{0:T(128)S(1)} %copy-done.9, f32[64,8,128]{2,1,0:T(8,128)S(1)} %get-tuple-element.47.refs_1_, f32[8,128]{1,0:T(8,128)S(1)} %collective-permute-done.4.refs_2_, f32[8,128]{1,0:T(8,128)S(1)} %collective-permute-done.5.refs_3_, ...), custom_call_target="tpu_custom_call" | custom-call | tf_op jit(solution)/shard_map/update/pallas_call | solution.py:629
  48.8 4.8 %all-to-all-start.2 = ((f32[64,1,384]{2,1,0:T(1,128)}), f32[64,1,384]{2,1,0:T(1,128)S(1)}, u32[]{:S(2)}, u32[]{:S(2)}) async-start(f32[64,1,384]{2,1,0:T(1,128)} %get-tuple-element.57), calls=%async_computation.2 | async-start | bytes 196608 | tf_op jit(solution)/shard_map/all_to_all | solution.py:698
  53.7 5.2 %element.6.first_ref = f32[32,8,128]{2,1,0:T(8,128)S(1)} custom-call(f32[6,8192]{1,0:T(8,128)S(1)} %get-tuple-element.65.refs_0_.refs_8_, s32[4,8192]{1,0:T(4,128)S(1)} %copy-done.1, bf16[24,24,8192]{2,1,0:T(8,128)(2,1)} %refs_2_.9, f32[64,128]{1,0:T(8,128)S(1)} %bitcast.3), custom_call_target="tpu_custom_call" | custom-call | flops 9437184 | bytes 9437184 | tf_op jit(solution)/shard_map/element/pallas_call | solution.py:201
  58.9 2.3 %all-to-all-done.2.recv_ref.refs_2_ = f32[64,1,384]{2,1,0:T(1,128)S(1)} async-done(((f32[64,1,384]{2,1,0:T(1,128)}), f32[64,1,384]{2,1,0:T(1,128)S(1)}, u32[]{:S(2)}, u32[]{:S(2)}) %all-to-all-start.2) | async-done | bytes 98336 | tf_op jit(solution)/shard_map/all_to_all | solution.py:698
  61.8 1.0 %collective-permute-start.10 = (f32[8,1,384]{2,1,0:T(1,128)S(1)}, f32[8,1,384]{2,1,0:T(1,128)S(1)}, u32[]{:S(2)}, u32[]{:S(2)}) collective-permute-start(f32[8,1,384]{2,1,0:T(1,128)S(1)} %edges.3), channel_id=1, source_target_pairs={{0,1},{1,0},{2,3},{3,2},{4,5},{5,4},{6,7},{7,6},{8,9},{9,8},{10,11... | collective-permute-start | bytes 36872 | tf_op jit(solution)/shard_map/ppermute | solution.py:655
  63.6 3.0 %own_contact.3 = (f32[64,8,128]{2,1,0:T(8,128)S(1)}, bf16[64,16,128]{2,1,0:T(8,128)(2,1)S(1)}) custom-call(s32[288]{0:T(512)S(1)} %get-tuple-element.59.refs_0_, f32[64,1,768]{2,1,0:T(1,128)S(1)} %all-to-all-done.recv_ref.refs_1_, f32[64,1,384]{2,1,0:T(1,128)S(1)} %all-to-all-done.2.recv_ref.refs_2_, s32[128,128]{1,0:T(8,128)S(1)} %copy-done.2, ...), custom_call_target="tpu_custom_call" | custom-call | flops 67108864 | bytes 65536 | tf_op jit(solution)/shard_map/own_contact/pallas_call | solution.py:434
  66.6 3.9 %far_contact.3 = f32[64,1,384]{2,1,0:T(1,128)} custom-call(s32[288]{0:T(512)S(1)} %get-tuple-element.59.refs_0_, f32[8,1,768]{2,1,0:T(1,128)S(1)} %collective-permute-done.refs_1_, f32[8,1,768]{2,1,0:T(1,128)S(1)} %collective-permute-done.1.refs_2_, f32[8,1,768]{2,1,0:T(1,128)S(1)} %collective-permute-done.2.refs_3_, ...), custom_call_target="tpu_custom_call" | custom-call | flops 67108864 | bytes 65536 | tf_op jit(solution)/shard_map/far_contact/pallas_call | solution.py:465
  70.5 4.5 %all-to-all-start.3 = ((f32[64,1,384]{2,1,0:T(1,128)}), f32[64,1,384]{2,1,0:T(1,128)S(1)}, u32[]{:S(2)}, u32[]{:S(2)}) async-start(f32[64,1,384]{2,1,0:T(1,128)} %far_contact.3), calls=%async_computation.3 | async-start | bytes 196608 | tf_op jit(solution)/shard_map/all_to_all | solution.py:698
  75.0 5.2 %element.7.second_ref = f32[32,8,128]{2,1,0:T(8,128)S(1)} custom-call(f32[6,8192]{1,0:T(8,128)S(1)} %get-tuple-element.65.refs_0_.refs_8_, s32[4,8192]{1,0:T(4,128)S(1)} %copy-done.1, bf16[24,24,8192]{2,1,0:T(8,128)(2,1)} %refs_2_.9, f32[64,128]{1,0:T(8,128)S(1)} %bitcast.4), custom_call_target="tpu_custom_call" | custom-call | flops 9437184 | bytes 9437184 | tf_op jit(solution)/shard_map/element/pallas_call | solution.py:201
  80.3 2.3 %all-to-all-done.3.back_ref = f32[64,1,384]{2,1,0:T(1,128)S(1)} async-done(((f32[64,1,384]{2,1,0:T(1,128)}), f32[64,1,384]{2,1,0:T(1,128)S(1)}, u32[]{:S(2)}, u32[]{:S(2)}) %all-to-all-start.3) | async-done | bytes 98336 | tf_op jit(solution)/shard_map/all_to_all | solution.py:698
  85.3 1.4 %collective-permute-done.13.refs_2_ = f32[8,128]{1,0:T(8,128)S(1)} collective-permute-done((f32[8,128]{1,0:T(8,128)S(1)}, f32[8,128]{1,0:T(8,128)S(1)}, u32[]{:S(2)}, u32[]{:S(2)}) %collective-permute-start.13) | collective-permute-done | bytes 4128 | tf_op jit(solution)/shard_map/ppermute | solution.py:655
  86.8 1.3 %collective-permute-done.14.refs_3_ = f32[8,128]{1,0:T(8,128)S(1)} collective-permute-done((f32[8,128]{1,0:T(8,128)S(1)}, f32[8,128]{1,0:T(8,128)S(1)}, u32[]{:S(2)}, u32[]{:S(2)}) %collective-permute-start.14) | collective-permute-done | bytes 4128 | tf_op jit(solution)/shard_map/ppermute | solution.py:655
  88.1 1.3 %update.3 = (f32[6,8192]{1,0:T(8,128)}, f32[6,8192]{1,0:T(8,128)}) custom-call(f32[64,8,128]{2,1,0:T(8,128)S(1)} %get-tuple-element.66.refs_0_, f32[8,128]{1,0:T(8,128)S(1)} %collective-permute-done.12.refs_1_, f32[8,128]{1,0:T(8,128)S(1)} %collective-permute-done.13.refs_2_, f32[8,128]{1,0:T(8,128)S(1)} %collective-permute-done.14.refs_3_, ...), custom_call_target="tpu_custom_call" | custom-call | tf_op jit(solution)/shard_map/update/pallas_call | solution.py:629
  (55 shorter events, 9.4 us)
Async XLA Ops:
  0.6 33.8 %copy-start = (f32[6,8192]{1,0:T(8,128)S(1)}, f32[6,8192]{1,0:T(8,128)}, u32[]{:S(2)}) copy-start(f32[6,8192]{1,0:T(8,128)} %refs_9_.2) | copy-start | bytes 589828
  2.6 15.6 %all-to-all-start = ((f32[64,1,768]{2,1,0:T(1,128)}), f32[64,1,768]{2,1,0:T(1,128)S(1)}, u32[]{:S(2)}, u32[]{:S(2)}) async-start(f32[64,1,768]{2,1,0:T(1,128)} %prep.1), calls=%async_computation | async-start | bytes 393216 | tf_op jit(solution)/shard_map/all_to_all | solution.py:698
  10.7 36.8 %copy-start.4 = (f32[6,8192]{1,0:T(8,128)S(1)}, f32[6,8192]{1,0:T(8,128)}, u32[]{:S(2)}) copy-start(f32[6,8192]{1,0:T(8,128)} %refs_6_.3) | copy-start | bytes 589828
  10.7 36.8 %copy-start.6 = (f32[3,8192]{1,0:T(4,128)S(1)}, f32[3,8192]{1,0:T(4,128)}, u32[]{:S(2)}) copy-start(f32[3,8192]{1,0:T(4,128)} %refs_10_.2) | copy-start | bytes 294916
  10.7 36.8 %copy-start.7 = (f32[6,8192]{1,0:T(8,128)S(1)}, f32[6,8192]{1,0:T(8,128)}, u32[]{:S(2)}) copy-start(f32[6,8192]{1,0:T(8,128)} %refs_8_.1) | copy-start | bytes 589828
  18.8 6.3 %collective-permute-start = (f32[8,1,768]{2,1,0:T(1,128)S(1)}, f32[8,1,768]{2,1,0:T(1,128)S(1)}, u32[]{:S(2)}, u32[]{:S(2)}) collective-permute-start(f32[8,1,768]{2,1,0:T(1,128)S(1)} %edges.2), channel_id=1, source_target_pairs={{0,8},{8,0},{16,24},{24,16},{1,9},{9,1},{17,25},{25,17},{2,10},{10... | collective-permute-start | bytes 73736 | tf_op jit(solution)/shard_map/ppermute | solution.py:655
  19.3 5.8 %collective-permute-start.1 = (f32[8,1,768]{2,1,0:T(1,128)S(1)}, f32[8,1,768]{2,1,0:T(1,128)S(1)}, u32[]{:S(2)}, u32[]{:S(2)}) collective-permute-start(f32[8,1,768]{2,1,0:T(1,128)S(1)} %edges.2), channel_id=1, source_target_pairs={{0,24},{8,16},{16,8},{24,0},{1,25},{9,17},{17,9},{25,1},{2,26},{10... | collective-permute-start | bytes 73736 | tf_op jit(solution)/shard_map/ppermute | solution.py:655
  20.6 4.5 %collective-permute-start.2 = (f32[8,1,768]{2,1,0:T(1,128)S(1)}, f32[8,1,768]{2,1,0:T(1,128)S(1)}, u32[]{:S(2)}, u32[]{:S(2)}) collective-permute-start(f32[8,1,768]{2,1,0:T(1,128)S(1)} %edges.2), channel_id=1, source_target_pairs={{0,1},{1,0},{2,3},{3,2},{4,5},{5,4},{6,7},{7,6},{8,9},{9,8},{10,11... | collective-permute-start | bytes 73736 | tf_op jit(solution)/shard_map/ppermute | solution.py:655
  22.1 3.1 %collective-permute-start.3 = (f32[8,1,768]{2,1,0:T(1,128)S(1)}, f32[8,1,768]{2,1,0:T(1,128)S(1)}, u32[]{:S(2)}, u32[]{:S(2)}) collective-permute-start(f32[8,1,768]{2,1,0:T(1,128)S(1)} %edges.2), channel_id=1, source_target_pairs={{0,8},{1,2},{2,1},{3,4},{4,3},{5,6},{6,5},{7,15},{8,0},{9,10},{10,... | collective-permute-start | bytes 73736 | tf_op jit(solution)/shard_map/ppermute | solution.py:655
  29.0 13.0 %all-to-all-start.1 = ((f32[64,1,384]{2,1,0:T(1,128)}), f32[64,1,384]{2,1,0:T(1,128)S(1)}, u32[]{:S(2)}, u32[]{:S(2)}) async-start(f32[64,1,384]{2,1,0:T(1,128)} %far_contact.2), calls=%async_computation.1 | async-start | bytes 196608 | tf_op jit(solution)/shard_map/all_to_all | solution.py:698
  43.0 2.5 %collective-permute-start.4 = (f32[8,128]{1,0:T(8,128)S(1)}, f32[8,128]{1,0:T(8,128)S(1)}, u32[]{:S(2)}, u32[]{:S(2)}) collective-permute-start(f32[8,128]{1,0:T(8,128)S(1)} %get-tuple-element.52), channel_id=1, source_target_pairs={{0,8},{8,0},{16,24},{24,16},{1,9},{9,1},{17,25},{25,17},{2,10},{10... | collective-permute-start | bytes 12296 | tf_op jit(solution)/shard_map/ppermute | solution.py:655
  43.1 3.0 %collective-permute-start.5 = (f32[8,128]{1,0:T(8,128)S(1)}, f32[8,128]{1,0:T(8,128)S(1)}, u32[]{:S(2)}, u32[]{:S(2)}) collective-permute-start(f32[8,128]{1,0:T(8,128)S(1)} %get-tuple-element.53), channel_id=1, source_target_pairs={{0,24},{8,16},{16,8},{24,0},{1,25},{9,17},{17,9},{25,1},{2,26},{10... | collective-permute-start | bytes 12296 | tf_op jit(solution)/shard_map/ppermute | solution.py:655
  43.9 3.6 %collective-permute-start.6 = (f32[8,128]{1,0:T(8,128)S(1)}, f32[8,128]{1,0:T(8,128)S(1)}, u32[]{:S(2)}, u32[]{:S(2)}) collective-permute-start(f32[8,128]{1,0:T(8,128)S(1)} %get-tuple-element.54), channel_id=1, source_target_pairs={{0,1},{1,0},{2,3},{3,2},{4,5},{5,4},{6,7},{7,6},{8,9},{9,8},{10,11... | collective-permute-start | bytes 12296 | tf_op jit(solution)/shard_map/ppermute | solution.py:655
  44.7 2.8 %collective-permute-start.7 = (f32[8,128]{1,0:T(8,128)S(1)}, f32[8,128]{1,0:T(8,128)S(1)}, u32[]{:S(2)}, u32[]{:S(2)}) collective-permute-start(f32[8,128]{1,0:T(8,128)S(1)} %get-tuple-element.55), channel_id=1, source_target_pairs={{0,8},{1,2},{2,1},{3,4},{4,3},{5,6},{6,5},{7,15},{8,0},{9,10},{10,... | collective-permute-start | bytes 12296 | tf_op jit(solution)/shard_map/ppermute | solution.py:655
  48.8 12.4 %all-to-all-start.2 = ((f32[64,1,384]{2,1,0:T(1,128)}), f32[64,1,384]{2,1,0:T(1,128)S(1)}, u32[]{:S(2)}, u32[]{:S(2)}) async-start(f32[64,1,384]{2,1,0:T(1,128)} %get-tuple-element.57), calls=%async_computation.2 | async-start | bytes 196608 | tf_op jit(solution)/shard_map/all_to_all | solution.py:698
  61.8 4.8 %collective-permute-start.10 = (f32[8,1,384]{2,1,0:T(1,128)S(1)}, f32[8,1,384]{2,1,0:T(1,128)S(1)}, u32[]{:S(2)}, u32[]{:S(2)}) collective-permute-start(f32[8,1,384]{2,1,0:T(1,128)S(1)} %edges.3), channel_id=1, source_target_pairs={{0,1},{1,0},{2,3},{3,2},{4,5},{5,4},{6,7},{7,6},{8,9},{9,8},{10,11... | collective-permute-start | bytes 36872 | tf_op jit(solution)/shard_map/ppermute | solution.py:655
  62.8 3.8 %collective-permute-start.11 = (f32[8,1,384]{2,1,0:T(1,128)S(1)}, f32[8,1,384]{2,1,0:T(1,128)S(1)}, u32[]{:S(2)}, u32[]{:S(2)}) collective-permute-start(f32[8,1,384]{2,1,0:T(1,128)S(1)} %edges.3), channel_id=1, source_target_pairs={{0,8},{1,2},{2,1},{3,4},{4,3},{5,6},{6,5},{7,15},{8,0},{9,10},{10,... | collective-permute-start | bytes 36872 | tf_op jit(solution)/shard_map/ppermute | solution.py:655
  62.8 3.8 %collective-permute-start.8 = (f32[8,1,384]{2,1,0:T(1,128)S(1)}, f32[8,1,384]{2,1,0:T(1,128)S(1)}, u32[]{:S(2)}, u32[]{:S(2)}) collective-permute-start(f32[8,1,384]{2,1,0:T(1,128)S(1)} %edges.3), channel_id=1, source_target_pairs={{0,8},{8,0},{16,24},{24,16},{1,9},{9,1},{17,25},{25,17},{2,10},{10... | collective-permute-start | bytes 36872 | tf_op jit(solution)/shard_map/ppermute | solution.py:655
  63.3 3.3 %collective-permute-start.9 = (f32[8,1,384]{2,1,0:T(1,128)S(1)}, f32[8,1,384]{2,1,0:T(1,128)S(1)}, u32[]{:S(2)}, u32[]{:S(2)}) collective-permute-start(f32[8,1,384]{2,1,0:T(1,128)S(1)} %edges.3), channel_id=1, source_target_pairs={{0,24},{8,16},{16,8},{24,0},{1,25},{9,17},{17,9},{25,1},{2,26},{10... | collective-permute-start | bytes 36872 | tf_op jit(solution)/shard_map/ppermute | solution.py:655
  70.5 12.1 %all-to-all-start.3 = ((f32[64,1,384]{2,1,0:T(1,128)}), f32[64,1,384]{2,1,0:T(1,128)S(1)}, u32[]{:S(2)}, u32[]{:S(2)}) async-start(f32[64,1,384]{2,1,0:T(1,128)} %far_contact.3), calls=%async_computation.3 | async-start | bytes 196608 | tf_op jit(solution)/shard_map/all_to_all | solution.py:698
  83.5 1.8 %collective-permute-start.12 = (f32[8,128]{1,0:T(8,128)S(1)}, f32[8,128]{1,0:T(8,128)S(1)}, u32[]{:S(2)}, u32[]{:S(2)}) collective-permute-start(f32[8,128]{1,0:T(8,128)S(1)} %get-tuple-element.67), channel_id=1, source_target_pairs={{0,8},{8,0},{16,24},{24,16},{1,9},{9,1},{17,25},{25,17},{2,10},{10... | collective-permute-start | bytes 12296 | tf_op jit(solution)/shard_map/ppermute | solution.py:655
  83.7 3.0 %collective-permute-start.13 = (f32[8,128]{1,0:T(8,128)S(1)}, f32[8,128]{1,0:T(8,128)S(1)}, u32[]{:S(2)}, u32[]{:S(2)}) collective-permute-start(f32[8,128]{1,0:T(8,128)S(1)} %get-tuple-element.68), channel_id=1, source_target_pairs={{0,24},{8,16},{16,8},{24,0},{1,25},{9,17},{17,9},{25,1},{2,26},{10... | collective-permute-start | bytes 12296 | tf_op jit(solution)/shard_map/ppermute | solution.py:655
  84.5 3.6 %collective-permute-start.14 = (f32[8,128]{1,0:T(8,128)S(1)}, f32[8,128]{1,0:T(8,128)S(1)}, u32[]{:S(2)}, u32[]{:S(2)}) collective-permute-start(f32[8,128]{1,0:T(8,128)S(1)} %get-tuple-element.69), channel_id=1, source_target_pairs={{0,1},{1,0},{2,3},{3,2},{4,5},{5,4},{6,7},{7,6},{8,9},{9,8},{10,11... | collective-permute-start | bytes 12296 | tf_op jit(solution)/shard_map/ppermute | solution.py:655
  85.3 2.8 %collective-permute-start.15 = (f32[8,128]{1,0:T(8,128)S(1)}, f32[8,128]{1,0:T(8,128)S(1)}, u32[]{:S(2)}, u32[]{:S(2)}) collective-permute-start(f32[8,128]{1,0:T(8,128)S(1)} %get-tuple-element.70), channel_id=1, source_target_pairs={{0,8},{1,2},{2,1},{3,4},{4,3},{5,6},{6,5},{7,15},{8,0},{9,10},{10,... | collective-permute-start | bytes 12296 | tf_op jit(solution)/shard_map/ppermute | solution.py:655
  (7 other events, 190.8 us)

commit v8 on v7

--- a/solution.py
+++ b/solution.py
@@ -9,7 +9,7 @@
 CAP = 2
 STEPS = 2
 ROWS = 8
-EBLK = 8
+EBLK = 16
 GROUP = 16
 FIELD = 10
 TAIL = 16

time: 89.7 us -> 89.5 us (level)
  no operation moved by 1% of the time
where the time goes in v8:
time: 89.5 us; the launch traced here: 89.2 us
  Pallas kernels  44.6 us (50%)
  starting transfers between devices  30.5 us (34%)
  waiting for transfers between devices  12.2 us (14%)
  between operations  1.83 us (2%)
    pallas_call x4, Pallas kernels, element_forces(): pl.pallas_call(kernel, out_shape=out, in_specs=[vspec()] * 2 + [pl.BlockS...  22.6 us
    all_to_all x4, starting transfers between devices, exchange(): lax.all_to_all(blocks_out, AXES, split_axis=0, concat_axis=0, tiled=True)  22 us
    ppermute x16, starting transfers between devices, swap(): lax.ppermute(value, axis, pairs)  8.51 us
    pallas_call x2, Pallas kernels, far_contact(): pl.pallas_call(kernel, out_shape=jax.ShapeDtypeStruct((places, 1, 3 * BLK...  7.76 us
    all_to_all x4, waiting for transfers between devices, exchange(): lax.all_to_all(blocks_out, AXES, split_axis=0, concat_axis=0, tiled=True)  7.39 us
    pallas_call x2, Pallas kernels, own_contact(): pl.pallas_call(kernel, out_shape=[jax.ShapeDtypeStruct((places, ROWS, BLK...  6.01 us
    ppermute x16, waiting for transfers between devices, swap(): lax.ppermute(value, axis, pairs)  4.79 us
    pallas_call x2, Pallas kernels, update(): pl.pallas_call(kernel, out_shape=out, in_specs=specs, out_specs=out_specs...  2.59 us
  transfers between devices with their start and end apart: 20, of which 8 were waited for; matrix products, arithmetic and copies ran while one was open for 0% of the time, Pallas kernels for 33%

profile of v8, /device:TPU:0, one launch (start us, length us, event | category | flops | bytes accessed | tf_op | source)
XLA Modules:
  0.0 89.2 jit_solution(12283729779489534355)
XLA Ops:
  0.7 1.9 %prep.1 = f32[64,1,768]{2,1,0:T(1,128)} custom-call(s32[64]{0:T(128)} %slot_ref.9, f32[6,8192]{1,0:T(8,128)} %refs_9_.2, f32[3,8192]{1,0:T(4,128)} %refs_10_.2, f32[3,8192]{1,0:T(4,128)} %nrm_ref.1), custom_call_target="tpu_custom_call" | custom-call | tf_op jit(solution)/shard_map/prep/pallas_call | solution.py:77
  2.6 7.3 %all-to-all-start = ((f32[64,1,768]{2,1,0:T(1,128)}), f32[64,1,768]{2,1,0:T(1,128)S(1)}, u32[]{:S(2)}, u32[]{:S(2)}) async-start(f32[64,1,768]{2,1,0:T(1,128)} %prep.1), calls=%async_computation | async-start | bytes 393216 | tf_op jit(solution)/shard_map/all_to_all | solution.py:698
  10.7 7.2 %element.4 = (f32[32,8,128]{2,1,0:T(8,128)S(1)}, s32[288]{0:T(512)S(1)}) custom-call(f32[6,8192]{1,0:T(8,128)} %refs_9_.2, s32[4,8192]{1,0:T(4,128)} %refs_1_.7, bf16[24,24,8192]{2,1,0:T(8,128)(2,1)} %refs_2_.9, f32[64,128]{1,0:T(8,128)} %bitcast.1, s32[1]{0:T(128)S(6)} %copy.17.refs_4_, s32[2,128]{1,0:T(2,128)} %refs_5_.2, ...), custom_call_target="tpu_custom_call" | custom-call | flops 9437184 | bytes 9437184 | tf_op jit(solution)/shard_map/element/pallas_call | solution.py:201
  19.3 1.2 %collective-permute-start.1 = (f32[8,1,768]{2,1,0:T(1,128)S(1)}, f32[8,1,768]{2,1,0:T(1,128)S(1)}, u32[]{:S(2)}, u32[]{:S(2)}) collective-permute-start(f32[8,1,768]{2,1,0:T(1,128)S(1)} %edges.2), channel_id=1, source_target_pairs={{0,24},{8,16},{16,8},{24,0},{1,25},{9,17},{17,9},{25,1},{2,26},{10... | collective-permute-start | bytes 73736 | tf_op jit(solution)/shard_map/ppermute | solution.py:655
  20.5 1.5 %collective-permute-start.2 = (f32[8,1,768]{2,1,0:T(1,128)S(1)}, f32[8,1,768]{2,1,0:T(1,128)S(1)}, u32[]{:S(2)}, u32[]{:S(2)}) collective-permute-start(f32[8,1,768]{2,1,0:T(1,128)S(1)} %edges.2), channel_id=1, source_target_pairs={{0,1},{1,0},{2,3},{3,2},{4,5},{5,4},{6,7},{7,6},{8,9},{9,8},{10,11... | collective-permute-start | bytes 73736 | tf_op jit(solution)/shard_map/ppermute | solution.py:655
  22.0 3.0 %own_contact.2 = (f32[64,8,128]{2,1,0:T(8,128)S(1)}, bf16[64,16,128]{2,1,0:T(8,128)(2,1)S(1)}) custom-call(s32[288]{0:T(512)S(1)} %get-tuple-element.59.refs_0_, f32[64,1,768]{2,1,0:T(1,128)S(1)} %all-to-all-done.recv_ref.refs_1_, s32[128,128]{1,0:T(8,128)S(1)} %copy-done.2, s32[128,128]{1,0:T(8,128)S(1)} %copy-done.3), custom_call_target="tpu_custom_call" | custom-call | flops 67108864 | bytes 65536 | tf_op jit(solution)/shard_map/own_contact/pallas_call | solution.py:434
  25.0 3.9 %far_contact.2 = f32[64,1,384]{2,1,0:T(1,128)} custom-call(s32[288]{0:T(512)S(1)} %get-tuple-element.59.refs_0_, f32[8,1,768]{2,1,0:T(1,128)S(1)} %collective-permute-done.refs_1_, f32[8,1,768]{2,1,0:T(1,128)S(1)} %collective-permute-done.1.refs_2_, f32[8,1,768]{2,1,0:T(1,128)S(1)} %collective-permute-done.2.refs_3_, ...), custom_call_target="tpu_custom_call" | custom-call | flops 67108864 | bytes 65536 | tf_op jit(solution)/shard_map/far_contact/pallas_call | solution.py:465
  28.9 5.4 %all-to-all-start.1 = ((f32[64,1,384]{2,1,0:T(1,128)}), f32[64,1,384]{2,1,0:T(1,128)S(1)}, u32[]{:S(2)}, u32[]{:S(2)}) async-start(f32[64,1,384]{2,1,0:T(1,128)} %far_contact.2), calls=%async_computation.1 | async-start | bytes 196608 | tf_op jit(solution)/shard_map/all_to_all | solution.py:698
  34.3 5.1 %element.5.second_ref = f32[32,8,128]{2,1,0:T(8,128)S(1)} custom-call(f32[6,8192]{1,0:T(8,128)S(1)} %copy-done, s32[4,8192]{1,0:T(4,128)S(1)} %copy-done.1, bf16[24,24,8192]{2,1,0:T(8,128)(2,1)} %refs_2_.9, f32[64,128]{1,0:T(8,128)S(1)} %bitcast.2), custom_call_target="tpu_custom_call" | custom-call | flops 9437184 | bytes 9437184 | tf_op jit(solution)/shard_map/element/pallas_call | solution.py:201
  39.5 2.4 %all-to-all-done.1.back_ref = f32[64,1,384]{2,1,0:T(1,128)S(1)} async-done(((f32[64,1,384]{2,1,0:T(1,128)}), f32[64,1,384]{2,1,0:T(1,128)S(1)}, u32[]{:S(2)}, u32[]{:S(2)}) %all-to-all-start.1) | async-done | bytes 98336 | tf_op jit(solution)/shard_map/all_to_all | solution.py:698
  46.0 1.3 %collective-permute-done.6.refs_4_ = f32[8,128]{1,0:T(8,128)S(1)} collective-permute-done((f32[8,128]{1,0:T(8,128)S(1)}, f32[8,128]{1,0:T(8,128)S(1)}, u32[]{:S(2)}, u32[]{:S(2)}) %collective-permute-start.6) | collective-permute-done | bytes 4128 | tf_op jit(solution)/shard_map/ppermute | solution.py:655
  47.4 1.3 %update.2 = (f32[6,8192]{1,0:T(8,128)S(1)}, f32[6,8192]{1,0:T(8,128)S(1)}, f32[64,1,384]{2,1,0:T(1,128)}) custom-call(s32[64]{0:T(128)S(1)} %copy-done.9, f32[64,8,128]{2,1,0:T(8,128)S(1)} %get-tuple-element.47.refs_1_, f32[8,128]{1,0:T(8,128)S(1)} %collective-permute-done.4.refs_2_, f32[8,128]{1,0:T(8,128)S(1)} %collective-permute-done.5.refs_3_, ...), custom_call_target="tpu_custom_call" | custom-call | tf_op jit(solution)/shard_map/update/pallas_call | solution.py:629
  48.7 4.7 %all-to-all-start.2 = ((f32[64,1,384]{2,1,0:T(1,128)}), f32[64,1,384]{2,1,0:T(1,128)S(1)}, u32[]{:S(2)}, u32[]{:S(2)}) async-start(f32[64,1,384]{2,1,0:T(1,128)} %get-tuple-element.57), calls=%async_computation.2 | async-start | bytes 196608 | tf_op jit(solution)/shard_map/all_to_all | solution.py:698
  53.4 5.1 %element.6.first_ref = f32[32,8,128]{2,1,0:T(8,128)S(1)} custom-call(f32[6,8192]{1,0:T(8,128)S(1)} %get-tuple-element.65.refs_0_.refs_8_, s32[4,8192]{1,0:T(4,128)S(1)} %copy-done.1, bf16[24,24,8192]{2,1,0:T(8,128)(2,1)} %refs_2_.9, f32[64,128]{1,0:T(8,128)S(1)} %bitcast.3), custom_call_target="tpu_custom_call" | custom-call | flops 9437184 | bytes 9437184 | tf_op jit(solution)/shard_map/element/pallas_call | solution.py:201
  58.5 2.5 %all-to-all-done.2.recv_ref.refs_2_ = f32[64,1,384]{2,1,0:T(1,128)S(1)} async-done(((f32[64,1,384]{2,1,0:T(1,128)}), f32[64,1,384]{2,1,0:T(1,128)S(1)}, u32[]{:S(2)}, u32[]{:S(2)}) %all-to-all-start.2) | async-done | bytes 98336 | tf_op jit(solution)/shard_map/all_to_all | solution.py:698
  61.5 1.0 %collective-permute-start.10 = (f32[8,1,384]{2,1,0:T(1,128)S(1)}, f32[8,1,384]{2,1,0:T(1,128)S(1)}, u32[]{:S(2)}, u32[]{:S(2)}) collective-permute-start(f32[8,1,384]{2,1,0:T(1,128)S(1)} %edges.3), channel_id=1, source_target_pairs={{0,1},{1,0},{2,3},{3,2},{4,5},{5,4},{6,7},{7,6},{8,9},{9,8},{10,11... | collective-permute-start | bytes 36872 | tf_op jit(solution)/shard_map/ppermute | solution.py:655
  63.3 3.0 %own_contact.3 = (f32[64,8,128]{2,1,0:T(8,128)S(1)}, bf16[64,16,128]{2,1,0:T(8,128)(2,1)S(1)}) custom-call(s32[288]{0:T(512)S(1)} %get-tuple-element.59.refs_0_, f32[64,1,768]{2,1,0:T(1,128)S(1)} %all-to-all-done.recv_ref.refs_1_, f32[64,1,384]{2,1,0:T(1,128)S(1)} %all-to-all-done.2.recv_ref.refs_2_, s32[128,128]{1,0:T(8,128)S(1)} %copy-done.2, ...), custom_call_target="tpu_custom_call" | custom-call | flops 67108864 | bytes 65536 | tf_op jit(solution)/shard_map/own_contact/pallas_call | solution.py:434
  66.4 3.9 %far_contact.3 = f32[64,1,384]{2,1,0:T(1,128)} custom-call(s32[288]{0:T(512)S(1)} %get-tuple-element.59.refs_0_, f32[8,1,768]{2,1,0:T(1,128)S(1)} %collective-permute-done.refs_1_, f32[8,1,768]{2,1,0:T(1,128)S(1)} %collective-permute-done.1.refs_2_, f32[8,1,768]{2,1,0:T(1,128)S(1)} %collective-permute-done.2.refs_3_, ...), custom_call_target="tpu_custom_call" | custom-call | flops 67108864 | bytes 65536 | tf_op jit(solution)/shard_map/far_contact/pallas_call | solution.py:465
  70.3 4.6 %all-to-all-start.3 = ((f32[64,1,384]{2,1,0:T(1,128)}), f32[64,1,384]{2,1,0:T(1,128)S(1)}, u32[]{:S(2)}, u32[]{:S(2)}) async-start(f32[64,1,384]{2,1,0:T(1,128)} %far_contact.3), calls=%async_computation.3 | async-start | bytes 196608 | tf_op jit(solution)/shard_map/all_to_all | solution.py:698
  74.9 5.1 %element.7.second_ref = f32[32,8,128]{2,1,0:T(8,128)S(1)} custom-call(f32[6,8192]{1,0:T(8,128)S(1)} %get-tuple-element.65.refs_0_.refs_8_, s32[4,8192]{1,0:T(4,128)S(1)} %copy-done.1, bf16[24,24,8192]{2,1,0:T(8,128)(2,1)} %refs_2_.9, f32[64,128]{1,0:T(8,128)S(1)} %bitcast.4), custom_call_target="tpu_custom_call" | custom-call | flops 9437184 | bytes 9437184 | tf_op jit(solution)/shard_map/element/pallas_call | solution.py:201
  80.0 2.3 %all-to-all-done.3.back_ref = f32[64,1,384]{2,1,0:T(1,128)S(1)} async-done(((f32[64,1,384]{2,1,0:T(1,128)}), f32[64,1,384]{2,1,0:T(1,128)S(1)}, u32[]{:S(2)}, u32[]{:S(2)}) %all-to-all-start.3) | async-done | bytes 98336 | tf_op jit(solution)/shard_map/all_to_all | solution.py:698
  85.0 1.4 %collective-permute-done.13.refs_2_ = f32[8,128]{1,0:T(8,128)S(1)} collective-permute-done((f32[8,128]{1,0:T(8,128)S(1)}, f32[8,128]{1,0:T(8,128)S(1)}, u32[]{:S(2)}, u32[]{:S(2)}) %collective-permute-start.13) | collective-permute-done | bytes 4128 | tf_op jit(solution)/shard_map/ppermute | solution.py:655
  86.4 1.3 %collective-permute-done.14.refs_3_ = f32[8,128]{1,0:T(8,128)S(1)} collective-permute-done((f32[8,128]{1,0:T(8,128)S(1)}, f32[8,128]{1,0:T(8,128)S(1)}, u32[]{:S(2)}, u32[]{:S(2)}) %collective-permute-start.14) | collective-permute-done | bytes 4128 | tf_op jit(solution)/shard_map/ppermute | solution.py:655
  87.7 1.3 %update.3 = (f32[6,8192]{1,0:T(8,128)}, f32[6,8192]{1,0:T(8,128)}) custom-call(f32[64,8,128]{2,1,0:T(8,128)S(1)} %get-tuple-element.66.refs_0_, f32[8,128]{1,0:T(8,128)S(1)} %collective-permute-done.12.refs_1_, f32[8,128]{1,0:T(8,128)S(1)} %collective-permute-done.13.refs_2_, f32[8,128]{1,0:T(8,128)S(1)} %collective-permute-done.14.refs_3_, ...), custom_call_target="tpu_custom_call" | custom-call | tf_op jit(solution)/shard_map/update/pallas_call | solution.py:629
  (55 shorter events, 9.6 us)
Async XLA Ops:
  0.6 33.7 %copy-start = (f32[6,8192]{1,0:T(8,128)S(1)}, f32[6,8192]{1,0:T(8,128)}, u32[]{:S(2)}) copy-start(f32[6,8192]{1,0:T(8,128)} %refs_9_.2) | copy-start | bytes 589828
  2.6 15.6 %all-to-all-start = ((f32[64,1,768]{2,1,0:T(1,128)}), f32[64,1,768]{2,1,0:T(1,128)S(1)}, u32[]{:S(2)}, u32[]{:S(2)}) async-start(f32[64,1,768]{2,1,0:T(1,128)} %prep.1), calls=%async_computation | async-start | bytes 393216 | tf_op jit(solution)/shard_map/all_to_all | solution.py:698
  10.7 36.7 %copy-start.4 = (f32[6,8192]{1,0:T(8,128)S(1)}, f32[6,8192]{1,0:T(8,128)}, u32[]{:S(2)}) copy-start(f32[6,8192]{1,0:T(8,128)} %refs_6_.3) | copy-start | bytes 589828
  10.7 36.7 %copy-start.6 = (f32[3,8192]{1,0:T(4,128)S(1)}, f32[3,8192]{1,0:T(4,128)}, u32[]{:S(2)}) copy-start(f32[3,8192]{1,0:T(4,128)} %refs_10_.2) | copy-start | bytes 294916
  10.7 36.7 %copy-start.7 = (f32[6,8192]{1,0:T(8,128)S(1)}, f32[6,8192]{1,0:T(8,128)}, u32[]{:S(2)}) copy-start(f32[6,8192]{1,0:T(8,128)} %refs_8_.1) | copy-start | bytes 589828
  18.8 6.2 %collective-permute-start = (f32[8,1,768]{2,1,0:T(1,128)S(1)}, f32[8,1,768]{2,1,0:T(1,128)S(1)}, u32[]{:S(2)}, u32[]{:S(2)}) collective-permute-start(f32[8,1,768]{2,1,0:T(1,128)S(1)} %edges.2), channel_id=1, source_target_pairs={{0,8},{8,0},{16,24},{24,16},{1,9},{9,1},{17,25},{25,17},{2,10},{10... | collective-permute-start | bytes 73736 | tf_op jit(solution)/shard_map/ppermute | solution.py:655
  19.3 5.7 %collective-permute-start.1 = (f32[8,1,768]{2,1,0:T(1,128)S(1)}, f32[8,1,768]{2,1,0:T(1,128)S(1)}, u32[]{:S(2)}, u32[]{:S(2)}) collective-permute-start(f32[8,1,768]{2,1,0:T(1,128)S(1)} %edges.2), channel_id=1, source_target_pairs={{0,24},{8,16},{16,8},{24,0},{1,25},{9,17},{17,9},{25,1},{2,26},{10... | collective-permute-start | bytes 73736 | tf_op jit(solution)/shard_map/ppermute | solution.py:655
  20.5 4.5 %collective-permute-start.2 = (f32[8,1,768]{2,1,0:T(1,128)S(1)}, f32[8,1,768]{2,1,0:T(1,128)S(1)}, u32[]{:S(2)}, u32[]{:S(2)}) collective-permute-start(f32[8,1,768]{2,1,0:T(1,128)S(1)} %edges.2), channel_id=1, source_target_pairs={{0,1},{1,0},{2,3},{3,2},{4,5},{5,4},{6,7},{7,6},{8,9},{9,8},{10,11... | collective-permute-start | bytes 73736 | tf_op jit(solution)/shard_map/ppermute | solution.py:655
  22.0 3.1 %collective-permute-start.3 = (f32[8,1,768]{2,1,0:T(1,128)S(1)}, f32[8,1,768]{2,1,0:T(1,128)S(1)}, u32[]{:S(2)}, u32[]{:S(2)}) collective-permute-start(f32[8,1,768]{2,1,0:T(1,128)S(1)} %edges.2), channel_id=1, source_target_pairs={{0,8},{1,2},{2,1},{3,4},{4,3},{5,6},{6,5},{7,15},{8,0},{9,10},{10,... | collective-permute-start | bytes 73736 | tf_op jit(solution)/shard_map/ppermute | solution.py:655
  28.9 13.0 %all-to-all-start.1 = ((f32[64,1,384]{2,1,0:T(1,128)}), f32[64,1,384]{2,1,0:T(1,128)S(1)}, u32[]{:S(2)}, u32[]{:S(2)}) async-start(f32[64,1,384]{2,1,0:T(1,128)} %far_contact.2), calls=%async_computation.1 | async-start | bytes 196608 | tf_op jit(solution)/shard_map/all_to_all | solution.py:698
  42.8 2.5 %collective-permute-start.4 = (f32[8,128]{1,0:T(8,128)S(1)}, f32[8,128]{1,0:T(8,128)S(1)}, u32[]{:S(2)}, u32[]{:S(2)}) collective-permute-start(f32[8,128]{1,0:T(8,128)S(1)} %get-tuple-element.52), channel_id=1, source_target_pairs={{0,8},{8,0},{16,24},{24,16},{1,9},{9,1},{17,25},{25,17},{2,10},{10... | collective-permute-start | bytes 12296 | tf_op jit(solution)/shard_map/ppermute | solution.py:655
  43.0 3.0 %collective-permute-start.5 = (f32[8,128]{1,0:T(8,128)S(1)}, f32[8,128]{1,0:T(8,128)S(1)}, u32[]{:S(2)}, u32[]{:S(2)}) collective-permute-start(f32[8,128]{1,0:T(8,128)S(1)} %get-tuple-element.53), channel_id=1, source_target_pairs={{0,24},{8,16},{16,8},{24,0},{1,25},{9,17},{17,9},{25,1},{2,26},{10... | collective-permute-start | bytes 12296 | tf_op jit(solution)/shard_map/ppermute | solution.py:655
  43.7 3.6 %collective-permute-start.6 = (f32[8,128]{1,0:T(8,128)S(1)}, f32[8,128]{1,0:T(8,128)S(1)}, u32[]{:S(2)}, u32[]{:S(2)}) collective-permute-start(f32[8,128]{1,0:T(8,128)S(1)} %get-tuple-element.54), channel_id=1, source_target_pairs={{0,1},{1,0},{2,3},{3,2},{4,5},{5,4},{6,7},{7,6},{8,9},{9,8},{10,11... | collective-permute-start | bytes 12296 | tf_op jit(solution)/shard_map/ppermute | solution.py:655
  44.6 2.8 %collective-permute-start.7 = (f32[8,128]{1,0:T(8,128)S(1)}, f32[8,128]{1,0:T(8,128)S(1)}, u32[]{:S(2)}, u32[]{:S(2)}) collective-permute-start(f32[8,128]{1,0:T(8,128)S(1)} %get-tuple-element.55), channel_id=1, source_target_pairs={{0,8},{1,2},{2,1},{3,4},{4,3},{5,6},{6,5},{7,15},{8,0},{9,10},{10,... | collective-permute-start | bytes 12296 | tf_op jit(solution)/shard_map/ppermute | solution.py:655
  48.7 12.3 %all-to-all-start.2 = ((f32[64,1,384]{2,1,0:T(1,128)}), f32[64,1,384]{2,1,0:T(1,128)S(1)}, u32[]{:S(2)}, u32[]{:S(2)}) async-start(f32[64,1,384]{2,1,0:T(1,128)} %get-tuple-element.57), calls=%async_computation.2 | async-start | bytes 196608 | tf_op jit(solution)/shard_map/all_to_all | solution.py:698
  61.5 4.8 %collective-permute-start.10 = (f32[8,1,384]{2,1,0:T(1,128)S(1)}, f32[8,1,384]{2,1,0:T(1,128)S(1)}, u32[]{:S(2)}, u32[]{:S(2)}) collective-permute-start(f32[8,1,384]{2,1,0:T(1,128)S(1)} %edges.3), channel_id=1, source_target_pairs={{0,1},{1,0},{2,3},{3,2},{4,5},{5,4},{6,7},{7,6},{8,9},{9,8},{10,11... | collective-permute-start | bytes 36872 | tf_op jit(solution)/shard_map/ppermute | solution.py:655
  62.5 3.8 %collective-permute-start.11 = (f32[8,1,384]{2,1,0:T(1,128)S(1)}, f32[8,1,384]{2,1,0:T(1,128)S(1)}, u32[]{:S(2)}, u32[]{:S(2)}) collective-permute-start(f32[8,1,384]{2,1,0:T(1,128)S(1)} %edges.3), channel_id=1, source_target_pairs={{0,8},{1,2},{2,1},{3,4},{4,3},{5,6},{6,5},{7,15},{8,0},{9,10},{10,... | collective-permute-start | bytes 36872 | tf_op jit(solution)/shard_map/ppermute | solution.py:655
  62.5 3.8 %collective-permute-start.8 = (f32[8,1,384]{2,1,0:T(1,128)S(1)}, f32[8,1,384]{2,1,0:T(1,128)S(1)}, u32[]{:S(2)}, u32[]{:S(2)}) collective-permute-start(f32[8,1,384]{2,1,0:T(1,128)S(1)} %edges.3), channel_id=1, source_target_pairs={{0,8},{8,0},{16,24},{24,16},{1,9},{9,1},{17,25},{25,17},{2,10},{10... | collective-permute-start | bytes 36872 | tf_op jit(solution)/shard_map/ppermute | solution.py:655
  63.0 3.4 %collective-permute-start.9 = (f32[8,1,384]{2,1,0:T(1,128)S(1)}, f32[8,1,384]{2,1,0:T(1,128)S(1)}, u32[]{:S(2)}, u32[]{:S(2)}) collective-permute-start(f32[8,1,384]{2,1,0:T(1,128)S(1)} %edges.3), channel_id=1, source_target_pairs={{0,24},{8,16},{16,8},{24,0},{1,25},{9,17},{17,9},{25,1},{2,26},{10... | collective-permute-start | bytes 36872 | tf_op jit(solution)/shard_map/ppermute | solution.py:655
  70.3 12.0 %all-to-all-start.3 = ((f32[64,1,384]{2,1,0:T(1,128)}), f32[64,1,384]{2,1,0:T(1,128)S(1)}, u32[]{:S(2)}, u32[]{:S(2)}) async-start(f32[64,1,384]{2,1,0:T(1,128)} %far_contact.3), calls=%async_computation.3 | async-start | bytes 196608 | tf_op jit(solution)/shard_map/all_to_all | solution.py:698
  83.2 1.8 %collective-permute-start.12 = (f32[8,128]{1,0:T(8,128)S(1)}, f32[8,128]{1,0:T(8,128)S(1)}, u32[]{:S(2)}, u32[]{:S(2)}) collective-permute-start(f32[8,128]{1,0:T(8,128)S(1)} %get-tuple-element.67), channel_id=1, source_target_pairs={{0,8},{8,0},{16,24},{24,16},{1,9},{9,1},{17,25},{25,17},{2,10},{10... | collective-permute-start | bytes 12296 | tf_op jit(solution)/shard_map/ppermute | solution.py:655
  83.4 3.0 %collective-permute-start.13 = (f32[8,128]{1,0:T(8,128)S(1)}, f32[8,128]{1,0:T(8,128)S(1)}, u32[]{:S(2)}, u32[]{:S(2)}) collective-permute-start(f32[8,128]{1,0:T(8,128)S(1)} %get-tuple-element.68), channel_id=1, source_target_pairs={{0,24},{8,16},{16,8},{24,0},{1,25},{9,17},{17,9},{25,1},{2,26},{10... | collective-permute-start | bytes 12296 | tf_op jit(solution)/shard_map/ppermute | solution.py:655
  84.1 3.6 %collective-permute-start.14 = (f32[8,128]{1,0:T(8,128)S(1)}, f32[8,128]{1,0:T(8,128)S(1)}, u32[]{:S(2)}, u32[]{:S(2)}) collective-permute-start(f32[8,128]{1,0:T(8,128)S(1)} %get-tuple-element.69), channel_id=1, source_target_pairs={{0,1},{1,0},{2,3},{3,2},{4,5},{5,4},{6,7},{7,6},{8,9},{9,8},{10,11... | collective-permute-start | bytes 12296 | tf_op jit(solution)/shard_map/ppermute | solution.py:655
  85.0 2.8 %collective-permute-start.15 = (f32[8,128]{1,0:T(8,128)S(1)}, f32[8,128]{1,0:T(8,128)S(1)}, u32[]{:S(2)}, u32[]{:S(2)}) collective-permute-start(f32[8,128]{1,0:T(8,128)S(1)} %get-tuple-element.70), channel_id=1, source_target_pairs={{0,8},{1,2},{2,1},{3,4},{4,3},{5,6},{6,5},{7,15},{8,0},{9,10},{10,... | collective-permute-start | bytes 12296 | tf_op jit(solution)/shard_map/ppermute | solution.py:655
  (7 other events, 189.9 us)

commit v9 on v8

--- a/solution.py
+++ b/solution.py
@@ -653,9 +653,9 @@
 def swap(values, sizes):
     moved = [
         lax.ppermute(value, axis, pairs)
-        for value, (axis, pairs) in reversed(list(zip(values, pair_lists(sizes))))
+        for value, (axis, pairs) in zip(values, pair_lists(sizes))
     ]
-    return moved[::-1]
+    return moved
 
 
 def body(

time: 89.5 us -> 89.5 us (level)
  no operation moved by 1% of the time
where the time goes in v9:
time: 89.5 us; the launch traced here: 89.2 us
  Pallas kernels  44.6 us (50%)
  starting transfers between devices  30.5 us (34%)
  waiting for transfers between devices  12.2 us (14%)
  between operations  1.83 us (2%)
    pallas_call x4, Pallas kernels, element_forces(): pl.pallas_call(kernel, out_shape=out, in_specs=[vspec()] * 2 + [pl.BlockS...  22.6 us
    all_to_all x4, starting transfers between devices, exchange(): lax.all_to_all(blocks_out, AXES, split_axis=0, concat_axis=0, tiled=True)  22 us
    ppermute x16, starting transfers between devices, swap(): lax.ppermute(value, axis, pairs)  8.5 us
    pallas_call x2, Pallas kernels, far_contact(): pl.pallas_call(kernel, out_shape=jax.ShapeDtypeStruct((places, 1, 3 * BLK...  7.75 us
    all_to_all x4, waiting for transfers between devices, exchange(): lax.all_to_all(blocks_out, AXES, split_axis=0, concat_axis=0, tiled=True)  7.4 us
    pallas_call x2, Pallas kernels, own_contact(): pl.pallas_call(kernel, out_shape=[jax.ShapeDtypeStruct((places, ROWS, BLK...  6.03 us
    ppermute x16, waiting for transfers between devices, swap(): lax.ppermute(value, axis, pairs)  4.79 us
    pallas_call x2, Pallas kernels, update(): pl.pallas_call(kernel, out_shape=out, in_specs=specs, out_specs=out_specs...  2.59 us
  transfers between devices with their start and end apart: 20, of which 8 were waited for; matrix products, arithmetic and copies ran while one was open for 0% of the time, Pallas kernels for 33%

profile of v9, /device:TPU:0, one launch (start us, length us, event | category | flops | bytes accessed | tf_op | source)
XLA Modules:
  0.0 89.2 jit_solution(12283729779489534355)
XLA Ops:
  0.7 1.9 %prep.1 = f32[64,1,768]{2,1,0:T(1,128)} custom-call(s32[64]{0:T(128)} %slot_ref.9, f32[6,8192]{1,0:T(8,128)} %refs_9_.2, f32[3,8192]{1,0:T(4,128)} %refs_10_.2, f32[3,8192]{1,0:T(4,128)} %nrm_ref.1), custom_call_target="tpu_custom_call" | custom-call | tf_op jit(solution)/shard_map/prep/pallas_call | solution.py:77
  2.6 7.3 %all-to-all-start = ((f32[64,1,768]{2,1,0:T(1,128)}), f32[64,1,768]{2,1,0:T(1,128)S(1)}, u32[]{:S(2)}, u32[]{:S(2)}) async-start(f32[64,1,768]{2,1,0:T(1,128)} %prep.1), calls=%async_computation | async-start | bytes 393216 | tf_op jit(solution)/shard_map/all_to_all | solution.py:698
  10.7 7.2 %element.4 = (f32[32,8,128]{2,1,0:T(8,128)S(1)}, s32[288]{0:T(512)S(1)}) custom-call(f32[6,8192]{1,0:T(8,128)} %refs_9_.2, s32[4,8192]{1,0:T(4,128)} %refs_1_.7, bf16[24,24,8192]{2,1,0:T(8,128)(2,1)} %refs_2_.9, f32[64,128]{1,0:T(8,128)} %bitcast.1, s32[1]{0:T(128)S(6)} %copy.17.refs_4_, s32[2,128]{1,0:T(2,128)} %refs_5_.2, ...), custom_call_target="tpu_custom_call" | custom-call | flops 9437184 | bytes 9437184 | tf_op jit(solution)/shard_map/element/pallas_call | solution.py:201
  19.3 1.2 %collective-permute-start.1 = (f32[8,1,768]{2,1,0:T(1,128)S(1)}, f32[8,1,768]{2,1,0:T(1,128)S(1)}, u32[]{:S(2)}, u32[]{:S(2)}) collective-permute-start(f32[8,1,768]{2,1,0:T(1,128)S(1)} %edges.2), channel_id=1, source_target_pairs={{0,24},{8,16},{16,8},{24,0},{1,25},{9,17},{17,9},{25,1},{2,26},{10... | collective-permute-start | bytes 73736 | tf_op jit(solution)/shard_map/ppermute | solution.py:655
  20.5 1.5 %collective-permute-start.2 = (f32[8,1,768]{2,1,0:T(1,128)S(1)}, f32[8,1,768]{2,1,0:T(1,128)S(1)}, u32[]{:S(2)}, u32[]{:S(2)}) collective-permute-start(f32[8,1,768]{2,1,0:T(1,128)S(1)} %edges.2), channel_id=1, source_target_pairs={{0,1},{1,0},{2,3},{3,2},{4,5},{5,4},{6,7},{7,6},{8,9},{9,8},{10,11... | collective-permute-start | bytes 73736 | tf_op jit(solution)/shard_map/ppermute | solution.py:655
  22.0 3.0 %own_contact.2 = (f32[64,8,128]{2,1,0:T(8,128)S(1)}, bf16[64,16,128]{2,1,0:T(8,128)(2,1)S(1)}) custom-call(s32[288]{0:T(512)S(1)} %get-tuple-element.59.refs_0_, f32[64,1,768]{2,1,0:T(1,128)S(1)} %all-to-all-done.recv_ref.refs_1_, s32[128,128]{1,0:T(8,128)S(1)} %copy-done.2, s32[128,128]{1,0:T(8,128)S(1)} %copy-done.3), custom_call_target="tpu_custom_call" | custom-call | flops 67108864 | bytes 65536 | tf_op jit(solution)/shard_map/own_contact/pallas_call | solution.py:434
  25.0 3.9 %far_contact.2 = f32[64,1,384]{2,1,0:T(1,128)} custom-call(s32[288]{0:T(512)S(1)} %get-tuple-element.59.refs_0_, f32[8,1,768]{2,1,0:T(1,128)S(1)} %collective-permute-done.refs_1_, f32[8,1,768]{2,1,0:T(1,128)S(1)} %collective-permute-done.1.refs_2_, f32[8,1,768]{2,1,0:T(1,128)S(1)} %collective-permute-done.2.refs_3_, ...), custom_call_target="tpu_custom_call" | custom-call | flops 67108864 | bytes 65536 | tf_op jit(solution)/shard_map/far_contact/pallas_call | solution.py:465
  28.9 5.4 %all-to-all-start.1 = ((f32[64,1,384]{2,1,0:T(1,128)}), f32[64,1,384]{2,1,0:T(1,128)S(1)}, u32[]{:S(2)}, u32[]{:S(2)}) async-start(f32[64,1,384]{2,1,0:T(1,128)} %far_contact.2), calls=%async_computation.1 | async-start | bytes 196608 | tf_op jit(solution)/shard_map/all_to_all | solution.py:698
  34.3 5.1 %element.5.second_ref = f32[32,8,128]{2,1,0:T(8,128)S(1)} custom-call(f32[6,8192]{1,0:T(8,128)S(1)} %copy-done, s32[4,8192]{1,0:T(4,128)S(1)} %copy-done.1, bf16[24,24,8192]{2,1,0:T(8,128)(2,1)} %refs_2_.9, f32[64,128]{1,0:T(8,128)S(1)} %bitcast.2), custom_call_target="tpu_custom_call" | custom-call | flops 9437184 | bytes 9437184 | tf_op jit(solution)/shard_map/element/pallas_call | solution.py:201
  39.5 2.4 %all-to-all-done.1.back_ref = f32[64,1,384]{2,1,0:T(1,128)S(1)} async-done(((f32[64,1,384]{2,1,0:T(1,128)}), f32[64,1,384]{2,1,0:T(1,128)S(1)}, u32[]{:S(2)}, u32[]{:S(2)}) %all-to-all-start.1) | async-done | bytes 98336 | tf_op jit(solution)/shard_map/all_to_all | solution.py:698
  46.0 1.3 %collective-permute-done.6.refs_4_ = f32[8,128]{1,0:T(8,128)S(1)} collective-permute-done((f32[8,128]{1,0:T(8,128)S(1)}, f32[8,128]{1,0:T(8,128)S(1)}, u32[]{:S(2)}, u32[]{:S(2)}) %collective-permute-start.6) | collective-permute-done | bytes 4128 | tf_op jit(solution)/shard_map/ppermute | solution.py:655
  47.4 1.3 %update.2 = (f32[6,8192]{1,0:T(8,128)S(1)}, f32[6,8192]{1,0:T(8,128)S(1)}, f32[64,1,384]{2,1,0:T(1,128)}) custom-call(s32[64]{0:T(128)S(1)} %copy-done.9, f32[64,8,128]{2,1,0:T(8,128)S(1)} %get-tuple-element.47.refs_1_, f32[8,128]{1,0:T(8,128)S(1)} %collective-permute-done.4.refs_2_, f32[8,128]{1,0:T(8,128)S(1)} %collective-permute-done.5.refs_3_, ...), custom_call_target="tpu_custom_call" | custom-call | tf_op jit(solution)/shard_map/update/pallas_call | solution.py:629
  48.7 4.7 %all-to-all-start.2 = ((f32[64,1,384]{2,1,0:T(1,128)}), f32[64,1,384]{2,1,0:T(1,128)S(1)}, u32[]{:S(2)}, u32[]{:S(2)}) async-start(f32[64,1,384]{2,1,0:T(1,128)} %get-tuple-element.57), calls=%async_computation.2 | async-start | bytes 196608 | tf_op jit(solution)/shard_map/all_to_all | solution.py:698
  53.4 5.1 %element.6.first_ref = f32[32,8,128]{2,1,0:T(8,128)S(1)} custom-call(f32[6,8192]{1,0:T(8,128)S(1)} %get-tuple-element.65.refs_0_.refs_8_, s32[4,8192]{1,0:T(4,128)S(1)} %copy-done.1, bf16[24,24,8192]{2,1,0:T(8,128)(2,1)} %refs_2_.9, f32[64,128]{1,0:T(8,128)S(1)} %bitcast.3), custom_call_target="tpu_custom_call" | custom-call | flops 9437184 | bytes 9437184 | tf_op jit(solution)/shard_map/element/pallas_call | solution.py:201
  58.5 2.4 %all-to-all-done.2.recv_ref.refs_2_ = f32[64,1,384]{2,1,0:T(1,128)S(1)} async-done(((f32[64,1,384]{2,1,0:T(1,128)}), f32[64,1,384]{2,1,0:T(1,128)S(1)}, u32[]{:S(2)}, u32[]{:S(2)}) %all-to-all-start.2) | async-done | bytes 98336 | tf_op jit(solution)/shard_map/all_to_all | solution.py:698
  61.5 1.0 %collective-permute-start.10 = (f32[8,1,384]{2,1,0:T(1,128)S(1)}, f32[8,1,384]{2,1,0:T(1,128)S(1)}, u32[]{:S(2)}, u32[]{:S(2)}) collective-permute-start(f32[8,1,384]{2,1,0:T(1,128)S(1)} %edges.3), channel_id=1, source_target_pairs={{0,1},{1,0},{2,3},{3,2},{4,5},{5,4},{6,7},{7,6},{8,9},{9,8},{10,11... | collective-permute-start | bytes 36872 | tf_op jit(solution)/shard_map/ppermute | solution.py:655
  63.3 3.0 %own_contact.3 = (f32[64,8,128]{2,1,0:T(8,128)S(1)}, bf16[64,16,128]{2,1,0:T(8,128)(2,1)S(1)}) custom-call(s32[288]{0:T(512)S(1)} %get-tuple-element.59.refs_0_, f32[64,1,768]{2,1,0:T(1,128)S(1)} %all-to-all-done.recv_ref.refs_1_, f32[64,1,384]{2,1,0:T(1,128)S(1)} %all-to-all-done.2.recv_ref.refs_2_, s32[128,128]{1,0:T(8,128)S(1)} %copy-done.2, ...), custom_call_target="tpu_custom_call" | custom-call | flops 67108864 | bytes 65536 | tf_op jit(solution)/shard_map/own_contact/pallas_call | solution.py:434
  66.4 3.9 %far_contact.3 = f32[64,1,384]{2,1,0:T(1,128)} custom-call(s32[288]{0:T(512)S(1)} %get-tuple-element.59.refs_0_, f32[8,1,768]{2,1,0:T(1,128)S(1)} %collective-permute-done.refs_1_, f32[8,1,768]{2,1,0:T(1,128)S(1)} %collective-permute-done.1.refs_2_, f32[8,1,768]{2,1,0:T(1,128)S(1)} %collective-permute-done.2.refs_3_, ...), custom_call_target="tpu_custom_call" | custom-call | flops 67108864 | bytes 65536 | tf_op jit(solution)/shard_map/far_contact/pallas_call | solution.py:465
  70.3 4.6 %all-to-all-start.3 = ((f32[64,1,384]{2,1,0:T(1,128)}), f32[64,1,384]{2,1,0:T(1,128)S(1)}, u32[]{:S(2)}, u32[]{:S(2)}) async-start(f32[64,1,384]{2,1,0:T(1,128)} %far_contact.3), calls=%async_computation.3 | async-start | bytes 196608 | tf_op jit(solution)/shard_map/all_to_all | solution.py:698
  74.8 5.1 %element.7.second_ref = f32[32,8,128]{2,1,0:T(8,128)S(1)} custom-call(f32[6,8192]{1,0:T(8,128)S(1)} %get-tuple-element.65.refs_0_.refs_8_, s32[4,8192]{1,0:T(4,128)S(1)} %copy-done.1, bf16[24,24,8192]{2,1,0:T(8,128)(2,1)} %refs_2_.9, f32[64,128]{1,0:T(8,128)S(1)} %bitcast.4), custom_call_target="tpu_custom_call" | custom-call | flops 9437184 | bytes 9437184 | tf_op jit(solution)/shard_map/element/pallas_call | solution.py:201
  80.0 2.3 %all-to-all-done.3.back_ref = f32[64,1,384]{2,1,0:T(1,128)S(1)} async-done(((f32[64,1,384]{2,1,0:T(1,128)}), f32[64,1,384]{2,1,0:T(1,128)S(1)}, u32[]{:S(2)}, u32[]{:S(2)}) %all-to-all-start.3) | async-done | bytes 98336 | tf_op jit(solution)/shard_map/all_to_all | solution.py:698
  84.9 1.4 %collective-permute-done.13.refs_2_ = f32[8,128]{1,0:T(8,128)S(1)} collective-permute-done((f32[8,128]{1,0:T(8,128)S(1)}, f32[8,128]{1,0:T(8,128)S(1)}, u32[]{:S(2)}, u32[]{:S(2)}) %collective-permute-start.13) | collective-permute-done | bytes 4128 | tf_op jit(solution)/shard_map/ppermute | solution.py:655
  86.4 1.3 %collective-permute-done.14.refs_3_ = f32[8,128]{1,0:T(8,128)S(1)} collective-permute-done((f32[8,128]{1,0:T(8,128)S(1)}, f32[8,128]{1,0:T(8,128)S(1)}, u32[]{:S(2)}, u32[]{:S(2)}) %collective-permute-start.14) | collective-permute-done | bytes 4128 | tf_op jit(solution)/shard_map/ppermute | solution.py:655
  87.7 1.3 %update.3 = (f32[6,8192]{1,0:T(8,128)}, f32[6,8192]{1,0:T(8,128)}) custom-call(f32[64,8,128]{2,1,0:T(8,128)S(1)} %get-tuple-element.66.refs_0_, f32[8,128]{1,0:T(8,128)S(1)} %collective-permute-done.12.refs_1_, f32[8,128]{1,0:T(8,128)S(1)} %collective-permute-done.13.refs_2_, f32[8,128]{1,0:T(8,128)S(1)} %collective-permute-done.14.refs_3_, ...), custom_call_target="tpu_custom_call" | custom-call | tf_op jit(solution)/shard_map/update/pallas_call | solution.py:629
  (55 shorter events, 9.6 us)
Async XLA Ops:
  0.6 33.7 %copy-start = (f32[6,8192]{1,0:T(8,128)S(1)}, f32[6,8192]{1,0:T(8,128)}, u32[]{:S(2)}) copy-start(f32[6,8192]{1,0:T(8,128)} %refs_9_.2) | copy-start | bytes 589828
  2.6 15.6 %all-to-all-start = ((f32[64,1,768]{2,1,0:T(1,128)}), f32[64,1,768]{2,1,0:T(1,128)S(1)}, u32[]{:S(2)}, u32[]{:S(2)}) async-start(f32[64,1,768]{2,1,0:T(1,128)} %prep.1), calls=%async_computation | async-start | bytes 393216 | tf_op jit(solution)/shard_map/all_to_all | solution.py:698
  10.7 36.7 %copy-start.4 = (f32[6,8192]{1,0:T(8,128)S(1)}, f32[6,8192]{1,0:T(8,128)}, u32[]{:S(2)}) copy-start(f32[6,8192]{1,0:T(8,128)} %refs_6_.3) | copy-start | bytes 589828
  10.7 36.7 %copy-start.6 = (f32[3,8192]{1,0:T(4,128)S(1)}, f32[3,8192]{1,0:T(4,128)}, u32[]{:S(2)}) copy-start(f32[3,8192]{1,0:T(4,128)} %refs_10_.2) | copy-start | bytes 294916
  10.7 36.7 %copy-start.7 = (f32[6,8192]{1,0:T(8,128)S(1)}, f32[6,8192]{1,0:T(8,128)}, u32[]{:S(2)}) copy-start(f32[6,8192]{1,0:T(8,128)} %refs_8_.1) | copy-start | bytes 589828
  18.8 6.2 %collective-permute-start = (f32[8,1,768]{2,1,0:T(1,128)S(1)}, f32[8,1,768]{2,1,0:T(1,128)S(1)}, u32[]{:S(2)}, u32[]{:S(2)}) collective-permute-start(f32[8,1,768]{2,1,0:T(1,128)S(1)} %edges.2), channel_id=1, source_target_pairs={{0,8},{8,0},{16,24},{24,16},{1,9},{9,1},{17,25},{25,17},{2,10},{10... | collective-permute-start | bytes 73736 | tf_op jit(solution)/shard_map/ppermute | solution.py:655
  19.3 5.7 %collective-permute-start.1 = (f32[8,1,768]{2,1,0:T(1,128)S(1)}, f32[8,1,768]{2,1,0:T(1,128)S(1)}, u32[]{:S(2)}, u32[]{:S(2)}) collective-permute-start(f32[8,1,768]{2,1,0:T(1,128)S(1)} %edges.2), channel_id=1, source_target_pairs={{0,24},{8,16},{16,8},{24,0},{1,25},{9,17},{17,9},{25,1},{2,26},{10... | collective-permute-start | bytes 73736 | tf_op jit(solution)/shard_map/ppermute | solution.py:655
  20.5 4.5 %collective-permute-start.2 = (f32[8,1,768]{2,1,0:T(1,128)S(1)}, f32[8,1,768]{2,1,0:T(1,128)S(1)}, u32[]{:S(2)}, u32[]{:S(2)}) collective-permute-start(f32[8,1,768]{2,1,0:T(1,128)S(1)} %edges.2), channel_id=1, source_target_pairs={{0,1},{1,0},{2,3},{3,2},{4,5},{5,4},{6,7},{7,6},{8,9},{9,8},{10,11... | collective-permute-start | bytes 73736 | tf_op jit(solution)/shard_map/ppermute | solution.py:655
  22.0 3.1 %collective-permute-start.3 = (f32[8,1,768]{2,1,0:T(1,128)S(1)}, f32[8,1,768]{2,1,0:T(1,128)S(1)}, u32[]{:S(2)}, u32[]{:S(2)}) collective-permute-start(f32[8,1,768]{2,1,0:T(1,128)S(1)} %edges.2), channel_id=1, source_target_pairs={{0,8},{1,2},{2,1},{3,4},{4,3},{5,6},{6,5},{7,15},{8,0},{9,10},{10,... | collective-permute-start | bytes 73736 | tf_op jit(solution)/shard_map/ppermute | solution.py:655
  28.9 13.0 %all-to-all-start.1 = ((f32[64,1,384]{2,1,0:T(1,128)}), f32[64,1,384]{2,1,0:T(1,128)S(1)}, u32[]{:S(2)}, u32[]{:S(2)}) async-start(f32[64,1,384]{2,1,0:T(1,128)} %far_contact.2), calls=%async_computation.1 | async-start | bytes 196608 | tf_op jit(solution)/shard_map/all_to_all | solution.py:698
  42.8 2.5 %collective-permute-start.4 = (f32[8,128]{1,0:T(8,128)S(1)}, f32[8,128]{1,0:T(8,128)S(1)}, u32[]{:S(2)}, u32[]{:S(2)}) collective-permute-start(f32[8,128]{1,0:T(8,128)S(1)} %get-tuple-element.52), channel_id=1, source_target_pairs={{0,8},{8,0},{16,24},{24,16},{1,9},{9,1},{17,25},{25,17},{2,10},{10... | collective-permute-start | bytes 12296 | tf_op jit(solution)/shard_map/ppermute | solution.py:655
  43.0 3.0 %collective-permute-start.5 = (f32[8,128]{1,0:T(8,128)S(1)}, f32[8,128]{1,0:T(8,128)S(1)}, u32[]{:S(2)}, u32[]{:S(2)}) collective-permute-start(f32[8,128]{1,0:T(8,128)S(1)} %get-tuple-element.53), channel_id=1, source_target_pairs={{0,24},{8,16},{16,8},{24,0},{1,25},{9,17},{17,9},{25,1},{2,26},{10... | collective-permute-start | bytes 12296 | tf_op jit(solution)/shard_map/ppermute | solution.py:655
  43.7 3.6 %collective-permute-start.6 = (f32[8,128]{1,0:T(8,128)S(1)}, f32[8,128]{1,0:T(8,128)S(1)}, u32[]{:S(2)}, u32[]{:S(2)}) collective-permute-start(f32[8,128]{1,0:T(8,128)S(1)} %get-tuple-element.54), channel_id=1, source_target_pairs={{0,1},{1,0},{2,3},{3,2},{4,5},{5,4},{6,7},{7,6},{8,9},{9,8},{10,11... | collective-permute-start | bytes 12296 | tf_op jit(solution)/shard_map/ppermute | solution.py:655
  44.6 2.8 %collective-permute-start.7 = (f32[8,128]{1,0:T(8,128)S(1)}, f32[8,128]{1,0:T(8,128)S(1)}, u32[]{:S(2)}, u32[]{:S(2)}) collective-permute-start(f32[8,128]{1,0:T(8,128)S(1)} %get-tuple-element.55), channel_id=1, source_target_pairs={{0,8},{1,2},{2,1},{3,4},{4,3},{5,6},{6,5},{7,15},{8,0},{9,10},{10,... | collective-permute-start | bytes 12296 | tf_op jit(solution)/shard_map/ppermute | solution.py:655
  48.7 12.3 %all-to-all-start.2 = ((f32[64,1,384]{2,1,0:T(1,128)}), f32[64,1,384]{2,1,0:T(1,128)S(1)}, u32[]{:S(2)}, u32[]{:S(2)}) async-start(f32[64,1,384]{2,1,0:T(1,128)} %get-tuple-element.57), calls=%async_computation.2 | async-start | bytes 196608 | tf_op jit(solution)/shard_map/all_to_all | solution.py:698
  61.5 4.8 %collective-permute-start.10 = (f32[8,1,384]{2,1,0:T(1,128)S(1)}, f32[8,1,384]{2,1,0:T(1,128)S(1)}, u32[]{:S(2)}, u32[]{:S(2)}) collective-permute-start(f32[8,1,384]{2,1,0:T(1,128)S(1)} %edges.3), channel_id=1, source_target_pairs={{0,1},{1,0},{2,3},{3,2},{4,5},{5,4},{6,7},{7,6},{8,9},{9,8},{10,11... | collective-permute-start | bytes 36872 | tf_op jit(solution)/shard_map/ppermute | solution.py:655
  62.5 3.9 %collective-permute-start.11 = (f32[8,1,384]{2,1,0:T(1,128)S(1)}, f32[8,1,384]{2,1,0:T(1,128)S(1)}, u32[]{:S(2)}, u32[]{:S(2)}) collective-permute-start(f32[8,1,384]{2,1,0:T(1,128)S(1)} %edges.3), channel_id=1, source_target_pairs={{0,8},{1,2},{2,1},{3,4},{4,3},{5,6},{6,5},{7,15},{8,0},{9,10},{10,... | collective-permute-start | bytes 36872 | tf_op jit(solution)/shard_map/ppermute | solution.py:655
  62.5 3.9 %collective-permute-start.8 = (f32[8,1,384]{2,1,0:T(1,128)S(1)}, f32[8,1,384]{2,1,0:T(1,128)S(1)}, u32[]{:S(2)}, u32[]{:S(2)}) collective-permute-start(f32[8,1,384]{2,1,0:T(1,128)S(1)} %edges.3), channel_id=1, source_target_pairs={{0,8},{8,0},{16,24},{24,16},{1,9},{9,1},{17,25},{25,17},{2,10},{10... | collective-permute-start | bytes 36872 | tf_op jit(solution)/shard_map/ppermute | solution.py:655
  63.0 3.4 %collective-permute-start.9 = (f32[8,1,384]{2,1,0:T(1,128)S(1)}, f32[8,1,384]{2,1,0:T(1,128)S(1)}, u32[]{:S(2)}, u32[]{:S(2)}) collective-permute-start(f32[8,1,384]{2,1,0:T(1,128)S(1)} %edges.3), channel_id=1, source_target_pairs={{0,24},{8,16},{16,8},{24,0},{1,25},{9,17},{17,9},{25,1},{2,26},{10... | collective-permute-start | bytes 36872 | tf_op jit(solution)/shard_map/ppermute | solution.py:655
  70.3 12.0 %all-to-all-start.3 = ((f32[64,1,384]{2,1,0:T(1,128)}), f32[64,1,384]{2,1,0:T(1,128)S(1)}, u32[]{:S(2)}, u32[]{:S(2)}) async-start(f32[64,1,384]{2,1,0:T(1,128)} %far_contact.3), calls=%async_computation.3 | async-start | bytes 196608 | tf_op jit(solution)/shard_map/all_to_all | solution.py:698
  83.2 1.8 %collective-permute-start.12 = (f32[8,128]{1,0:T(8,128)S(1)}, f32[8,128]{1,0:T(8,128)S(1)}, u32[]{:S(2)}, u32[]{:S(2)}) collective-permute-start(f32[8,128]{1,0:T(8,128)S(1)} %get-tuple-element.67), channel_id=1, source_target_pairs={{0,8},{8,0},{16,24},{24,16},{1,9},{9,1},{17,25},{25,17},{2,10},{10... | collective-permute-start | bytes 12296 | tf_op jit(solution)/shard_map/ppermute | solution.py:655
  83.3 3.0 %collective-permute-start.13 = (f32[8,128]{1,0:T(8,128)S(1)}, f32[8,128]{1,0:T(8,128)S(1)}, u32[]{:S(2)}, u32[]{:S(2)}) collective-permute-start(f32[8,128]{1,0:T(8,128)S(1)} %get-tuple-element.68), channel_id=1, source_target_pairs={{0,24},{8,16},{16,8},{24,0},{1,25},{9,17},{17,9},{25,1},{2,26},{10... | collective-permute-start | bytes 12296 | tf_op jit(solution)/shard_map/ppermute | solution.py:655
  84.1 3.6 %collective-permute-start.14 = (f32[8,128]{1,0:T(8,128)S(1)}, f32[8,128]{1,0:T(8,128)S(1)}, u32[]{:S(2)}, u32[]{:S(2)}) collective-permute-start(f32[8,128]{1,0:T(8,128)S(1)} %get-tuple-element.69), channel_id=1, source_target_pairs={{0,1},{1,0},{2,3},{3,2},{4,5},{5,4},{6,7},{7,6},{8,9},{9,8},{10,11... | collective-permute-start | bytes 12296 | tf_op jit(solution)/shard_map/ppermute | solution.py:655
  84.9 2.8 %collective-permute-start.15 = (f32[8,128]{1,0:T(8,128)S(1)}, f32[8,128]{1,0:T(8,128)S(1)}, u32[]{:S(2)}, u32[]{:S(2)}) collective-permute-start(f32[8,128]{1,0:T(8,128)S(1)} %get-tuple-element.70), channel_id=1, source_target_pairs={{0,8},{1,2},{2,1},{3,4},{4,3},{5,6},{6,5},{7,15},{8,0},{9,10},{10,... | collective-permute-start | bytes 12296 | tf_op jit(solution)/shard_map/ppermute | solution.py:655
  (7 other events, 189.9 us)
